TPU v7x, 32 devices: a whole 2x2x4 slice. The times are simulated.
32 devices in a mesh: tok: 8 (over z, y), feat: 4 (over x, core).
Axes of the slice: x: 2, y: 2, z: 4, core: 2. Of those that a mesh axis runs over, the one named last changes fastest.
Arguments:
- tokens: bfloat16 [8192, 2048], P('tok', 'feat'), as said below
- gain_attn: float32 [2048], P('feat'), may hold values from 0.5 to 1.5
- w_query: bfloat16 [2048, 2048], P('tok', 'feat'), may hold values from -0.125 to 0.125
- w_key: bfloat16 [2048, 2048], P('tok', 'feat'), may hold values from -0.125 to 0.125
- w_value: bfloat16 [2048, 2048], P('tok', 'feat'), may hold values from -0.125 to 0.125
- w_out: bfloat16 [2048, 2048], P('feat', 'tok'), may hold values from -1.5 to 1.5
- gain_ffn: float32 [2048], P('feat'), may hold values from 0.5 to 1.5
- w_gate: bfloat16 [2048, 8192], P('tok', 'feat'), may hold values from -0.125 to 0.125
- w_up: bfloat16 [2048, 8192], P('tok', 'feat'), may hold values from -0.125 to 0.125
- w_down: bfloat16 [8192, 2048], P('feat', 'tok'), may hold values from -0.125 to 0.125
- cotangent: bfloat16 [8192, 2048], P('tok', 'feat'), as said below
Outputs:
- result: bfloat16 [8192, 2048], P('tok', 'feat')
- input_grad: bfloat16 [8192, 2048], P('tok', 'feat')
- gain_attn_grad: float32 [2048], P('feat')
- gain_ffn_grad: float32 [2048], P('feat')
- query_grad: float32 [2048, 2048], P('tok', 'feat')
- key_grad: float32 [2048, 2048], P('tok', 'feat')
- value_grad: float32 [2048, 2048], P('tok', 'feat')
- out_grad: float32 [2048, 2048], P('feat', 'tok')
- gate_grad: float32 [2048, 8192], P('tok', 'feat')
- up_grad: float32 [2048, 8192], P('tok', 'feat')
- down_grad: float32 [8192, 2048], P('feat', 'tok')
Inputs may be any that keep to these rules, and one draw needn't show every extreme that they name: `tokens`: real-valued activations. `cotangent`: real-valued output gradients.
All inputs are finite; a program needn't handle non-finite values.
Results may differ from a plain program's by a relative error of at most 0.019.
Values may be sent and summed in bfloat16 or wider, within the bound.
A program may use at most 256 MiB of HBM per device.

v0:
```python
import jax
import jax.numpy as jnp
from jax import lax
from jax.sharding import PartitionSpec as P

D = 2048
HD = 64
LEN = 1024


EPSILON = 1e-05


def left_trans(left, right):
    return lax.dot_general(
        left, right, (((0,), (0,)), ((), ())), preferred_element_type=jnp.float32
    )


def right_trans(left, right):
    return lax.dot_general(
        left, right, (((1,), (1,)), ((), ())), preferred_element_type=jnp.float32
    )


def product(left, right):
    return jnp.dot(left, right, preferred_element_type=jnp.float32)


def feature_sum(values):
    return lax.psum(values, "feat")


def whole_rows(shard):
    return lax.all_gather(shard, "feat", axis=1, tiled=True)


def split_sums(partial_value):
    return lax.psum_scatter(partial_value, "feat", scatter_dimension=1, tiled=True)


def normalize(values, gain):
    squares = feature_sum(jnp.sum(values * values, axis=1))
    factor = lax.rsqrt(squares / D + EPSILON)
    return ((values * factor[:, None] * gain).astype(jnp.bfloat16), factor)


def norm_back(values, factor, gain, grad_normed):
    weighted = gain * grad_normed
    inner = feature_sum(jnp.sum(weighted * values, axis=1))
    grad_values = (
        factor[:, None] * weighted - values * (factor * factor * factor * inner / D)[:, None]
    )
    grad_gain = jnp.sum(grad_normed * values * factor[:, None], axis=0)
    return (grad_values, grad_gain)


def split_heads(values):
    return values.reshape(values.shape[0] // LEN, LEN, values.shape[1] // HD, HD)


def causal_scores(query_block, key_block, offset):
    block_rows = query_block.shape[1]
    key_count = key_block.shape[1]
    scores = jnp.einsum(
        "sqhd,skhd->shqk", query_block, key_block, preferred_element_type=jnp.float32
    ) * HD ** (-0.5)
    allowed = (offset + jnp.arange(block_rows))[:, None] >= jnp.arange(key_count)[None, :]
    return jnp.where(allowed, scores, -1e30)


def attend(queries, key_rows, value_rows):
    query_heads, key_heads, value_heads = (
        split_heads(queries),
        split_heads(key_rows),
        split_heads(value_rows),
    )
    block_rows = min(512, LEN)
    outputs = []
    log_sums = []
    for offset in range(0, LEN, block_rows):
        block_end = offset + block_rows
        scores = causal_scores(query_heads[:, offset:block_end], key_heads[:, :block_end], offset)
        highest = jnp.max(scores, axis=-1, keepdims=True)
        exponent = jnp.exp(scores - highest)
        denominator = jnp.sum(exponent, axis=-1, keepdims=True)
        probs = (exponent / denominator).astype(jnp.bfloat16)
        outputs.append(
            jnp.einsum(
                "shqk,skhd->sqhd",
                probs,
                value_heads[:, :block_end],
                preferred_element_type=jnp.float32,
            )
        )
        log_sums.append((highest + jnp.log(denominator))[..., 0])
    attended = jnp.concatenate(outputs, axis=1).astype(jnp.bfloat16).reshape(queries.shape)
    return (attended, jnp.concatenate(log_sums, axis=2))


def attend_back(queries, key_rows, value_rows, log_sums, grad_attended):
    query_heads, key_heads, value_heads = (
        split_heads(queries),
        split_heads(key_rows),
        split_heads(value_rows),
    )
    grad_heads = split_heads(grad_attended)
    block_rows = min(512, LEN)
    factor = HD ** (-0.5)
    query_parts = []
    grad_keys = jnp.zeros(key_heads.shape, jnp.float32)
    grad_values = jnp.zeros(value_heads.shape, jnp.float32)
    for offset in range(0, LEN, block_rows):
        block_end = offset + block_rows
        query_block = query_heads[:, offset:block_end]
        grad_block = grad_heads[:, offset:block_end]
        scores = causal_scores(query_block, key_heads[:, :block_end], offset)
        probs = jnp.exp(scores - log_sums[:, :, offset:block_end, None])
        grad_probs = jnp.einsum(
            "sqhd,skhd->shqk",
            grad_block,
            value_heads[:, :block_end],
            preferred_element_type=jnp.float32,
        )
        inner = jnp.sum(probs * grad_probs, axis=-1, keepdims=True)
        grad_scores = (probs * (grad_probs - inner)).astype(jnp.bfloat16)
        query_parts.append(
            jnp.einsum(
                "shqk,skhd->sqhd",
                grad_scores,
                key_heads[:, :block_end],
                preferred_element_type=jnp.float32,
            )
            * factor
        )
        key_term = (
            jnp.einsum(
                "shqk,sqhd->skhd", grad_scores, query_block, preferred_element_type=jnp.float32
            )
            * factor
        )
        grad_keys = grad_keys.at[:, :block_end].add(key_term)
        value_term = jnp.einsum(
            "shqk,sqhd->skhd",
            probs.astype(jnp.bfloat16),
            grad_block,
            preferred_element_type=jnp.float32,
        )
        grad_values = grad_values.at[:, :block_end].add(value_term)
    shape = queries.shape
    grad_queries = jnp.concatenate(query_parts, axis=1).astype(jnp.bfloat16).reshape(shape)
    return (
        grad_queries,
        grad_keys.astype(jnp.bfloat16).reshape(shape),
        grad_values.astype(jnp.bfloat16).reshape(shape),
    )


def on_device(
    tokens, gain_attn, w_query, w_key, w_value, w_out, gain_ffn, w_gate, w_up, w_down, cotangent
):
    residual = tokens.astype(jnp.float32)
    normed, factor_one = normalize(residual, gain_attn)
    gathered_in = whole_rows(normed)
    query_proj, key_proj, value_proj, out_proj = (
        lax.all_gather(w_query, "tok", axis=0, tiled=True),
        lax.all_gather(w_key, "tok", axis=0, tiled=True),
        lax.all_gather(w_value, "tok", axis=0, tiled=True),
        lax.all_gather(w_out, "tok", axis=1, tiled=True),
    )
    queries = product(gathered_in, query_proj).astype(jnp.bfloat16)
    key_rows = product(gathered_in, key_proj).astype(jnp.bfloat16)
    value_rows = product(gathered_in, value_proj).astype(jnp.bfloat16)
    attended, log_sums = attend(queries, key_rows, value_rows)
    middle = residual + split_sums(product(attended, out_proj))
    normed_two, factor_two = normalize(middle, gain_ffn)
    gathered_mid = whole_rows(normed_two)
    gate_proj, up_proj, down_proj = (
        lax.all_gather(w_gate, "tok", axis=0, tiled=True),
        lax.all_gather(w_up, "tok", axis=0, tiled=True),
        lax.all_gather(w_down, "tok", axis=1, tiled=True),
    )
    gate = product(gathered_mid, gate_proj)
    upward = product(gathered_mid, up_proj)
    sigma = jax.nn.sigmoid(gate)
    hidden = (gate * sigma * upward).astype(jnp.bfloat16)
    outcome = middle + split_sums(product(hidden, down_proj))
    grad_result = cotangent.astype(jnp.float32)
    grad_rows = whole_rows(cotangent)
    grad_hidden = right_trans(grad_rows, down_proj)
    term_down = left_trans(hidden, grad_rows)
    grad_gate = (grad_hidden * upward * sigma * (1.0 + gate * (1.0 - sigma))).astype(jnp.bfloat16)
    grad_up = (grad_hidden * gate * sigma).astype(jnp.bfloat16)
    term_gate = left_trans(gathered_mid, grad_gate)
    term_up = left_trans(gathered_mid, grad_up)
    gate_grad, up_grad, down_grad = (term_gate, term_up, term_down)
    grad_normed_two = split_sums(right_trans(grad_gate, gate_proj) + right_trans(grad_up, up_proj))
    grad_middle_norm, gain_ffn_part = norm_back(middle, factor_two, gain_ffn, grad_normed_two)
    grad_middle = grad_result + grad_middle_norm
    grad_mid_rows = whole_rows(grad_middle.astype(jnp.bfloat16))
    grad_attended = right_trans(grad_mid_rows, out_proj).astype(jnp.bfloat16)
    term_out = left_trans(attended, grad_mid_rows)
    grad_queries, grad_keys, grad_values = attend_back(
        queries, key_rows, value_rows, log_sums, grad_attended
    )
    term_query = left_trans(gathered_in, grad_queries)
    term_key = left_trans(gathered_in, grad_keys)
    term_value = left_trans(gathered_in, grad_values)
    grad_normed = split_sums(
        right_trans(grad_queries, query_proj)
        + right_trans(grad_keys, key_proj)
        + right_trans(grad_values, value_proj)
    )
    grad_input_norm, gain_attn_part = norm_back(residual, factor_one, gain_attn, grad_normed)
    input_grad = (grad_middle + grad_input_norm).astype(jnp.bfloat16)
    gain_attn_grad, gain_ffn_grad = lax.psum((gain_attn_part, gain_ffn_part), "tok")
    query_grad, key_grad, value_grad, out_grad, gate_grad, up_grad, down_grad = (
        lax.psum_scatter(
            term_query.astype(jnp.bfloat16), "tok", scatter_dimension=0, tiled=True
        ).astype(jnp.float32),
        lax.psum_scatter(
            term_key.astype(jnp.bfloat16), "tok", scatter_dimension=0, tiled=True
        ).astype(jnp.float32),
        lax.psum_scatter(
            term_value.astype(jnp.bfloat16), "tok", scatter_dimension=0, tiled=True
        ).astype(jnp.float32),
        lax.psum_scatter(
            term_out.astype(jnp.bfloat16), "tok", scatter_dimension=1, tiled=True
        ).astype(jnp.float32),
        lax.psum_scatter(
            gate_grad.astype(jnp.bfloat16), "tok", scatter_dimension=0, tiled=True
        ).astype(jnp.float32),
        lax.psum_scatter(
            up_grad.astype(jnp.bfloat16), "tok", scatter_dimension=0, tiled=True
        ).astype(jnp.float32),
        lax.psum_scatter(
            down_grad.astype(jnp.bfloat16), "tok", scatter_dimension=1, tiled=True
        ).astype(jnp.float32),
    )
    return (
        outcome.astype(jnp.bfloat16),
        input_grad,
        gain_attn_grad,
        gain_ffn_grad,
        query_grad,
        key_grad,
        value_grad,
        out_grad,
        gate_grad,
        up_grad,
        down_grad,
    )


def solution(mesh):
    in_specs = (
        P("tok", "feat"),
        P("feat"),
        P("tok", "feat"),
        P("tok", "feat"),
        P("tok", "feat"),
        P("feat", "tok"),
        P("feat"),
        P("tok", "feat"),
        P("tok", "feat"),
        P("feat", "tok"),
        P("tok", "feat"),
    )
    out_specs = (
        P("tok", "feat"),
        P("tok", "feat"),
        P("feat"),
        P("feat"),
        P("tok", "feat"),
        P("tok", "feat"),
        P("tok", "feat"),
        P("feat", "tok"),
        P("tok", "feat"),
        P("tok", "feat"),
        P("feat", "tok"),
    )
    return jax.shard_map(
        on_device, mesh=mesh, in_specs=in_specs, out_specs=out_specs, check_vma=False
    )
```

profile of v0, /device:TPU:0, one launch (start us, length us, event | category | flops | bytes accessed | tf_op | source)
XLA Modules:
  0.0 1844.4 jit_solution(2995573513767249965)
XLA Ops:
  23.4 38.8 %all-gather.18.cloned.1.call-done = bf16[2048,512]{1,0:T(8,128)(2,1)} async-done(((bf16[256,512]{1,0:T(8,128)(2,1)}), bf16[2048,512]{1,0:T(8,128)(2,1)}) %all-gather.18.cloned.1.call-update) | async-done | bytes 2097168 | tf_op jit(solution)/shard_map/all_gather | solution.py:167
  62.2 35.1 %all-gather.12.cloned.1.call-done = bf16[1024,2048]{1,0:T(8,128)(2,1)} async-done(((bf16[1024,512]{1,0:T(8,128)(2,1)}), bf16[1024,2048]{1,0:T(8,128)(2,1)}) %all-gather.12.cloned.1.call-update) | async-done | bytes 4194320 | tf_op jit(solution)/shard_map/all_gather | solution.py:35
  102.5 46.2 %all-gather.16.cloned.1.call-done = bf16[2048,512]{1,0:T(8,128)(2,1)} async-done(((bf16[256,512]{1,0:T(8,128)(2,1)}), bf16[2048,512]{1,0:T(8,128)(2,1)}) %all-gather.16.cloned.1.call-update) | async-done | bytes 2097168 | tf_op jit(solution)/shard_map/all_gather | solution.py:166
  171.9 26.6 %all-gather.14.cloned.1.call-done = bf16[2048,512]{1,0:T(8,128)(2,1)} async-done(((bf16[256,512]{1,0:T(8,128)(2,1)}), bf16[2048,512]{1,0:T(8,128)(2,1)}) %all-gather.14.cloned.1.call-update) | async-done | bytes 2097168 | tf_op jit(solution)/shard_map/all_gather | solution.py:168
  220.0 30.0 %all-gather.20.cloned.1.call-done = bf16[512,2048]{1,0:T(8,128)(2,1)} async-done(((bf16[512,256]{1,0:T(8,128)(2,1)}), bf16[512,2048]{1,0:T(8,128)(2,1)}) %all-gather.20.cloned.1.call-update) | async-done | bytes 2097168 | tf_op jit(solution)/shard_map/all_gather | solution.py:169
  258.1 69.2 %reduce-scatter.12.cloned.1.call-done = f32[1024,512]{1,0:T(8,128)} async-done(((f32[1024,2048]{1,0:T(8,128)}), f32[1024,512]{1,0:T(8,128)}) %reduce-scatter.12.cloned.1.call-update) | async-done | bytes 2097168 | tf_op jit(solution)/shard_map/reduce_scatter | solution.py:39
  338.4 116.2 %all-gather.26.cloned.1.call-done = bf16[2048,2048]{1,0:T(8,128)(2,1)} async-done(((bf16[256,2048]{1,0:T(8,128)(2,1)}), bf16[2048,2048]{1,0:T(8,128)(2,1)}) %all-gather.26.cloned.1.call-update) | async-done | bytes 8388624 | tf_op jit(solution)/shard_map/all_gather | solution.py:180
  454.7 34.9 %all-gather.22.cloned.1.call-done = bf16[1024,2048]{1,0:T(8,128)(2,1)} async-done(((bf16[1024,512]{1,0:T(8,128)(2,1)}), bf16[1024,2048]{1,0:T(8,128)(2,1)}) %all-gather.22.cloned.1.call-update) | async-done | bytes 4194320 | tf_op jit(solution)/shard_map/all_gather | solution.py:35
  489.6 14.6 fusion.49
  504.2 112.8 %all-gather.24.cloned.1.call-done = bf16[2048,2048]{1,0:T(8,128)(2,1)} async-done(((bf16[256,2048]{1,0:T(8,128)(2,1)}), bf16[2048,2048]{1,0:T(8,128)(2,1)}) %all-gather.24.cloned.1.call-update) | async-done | bytes 8388624 | tf_op jit(solution)/shard_map/all_gather | solution.py:179
  616.9 14.5 fusion.48
  631.4 19.7 %all-gather.30.cloned.1.call-done = bf16[1024,2048]{1,0:T(8,128)(2,1)} async-done(((bf16[1024,512]{1,0:T(8,128)(2,1)}), bf16[1024,2048]{1,0:T(8,128)(2,1)}) %all-gather.30.cloned.1.call-update) | async-done | bytes 4194320 | tf_op jit(solution)/shard_map/all_gather | solution.py:35
  651.1 127.7 %all-gather.28.cloned.1.call-done = bf16[2048,2048]{1,0:T(8,128)(2,1)} async-done(((bf16[2048,256]{1,0:T(8,128)(2,1)}), bf16[2048,2048]{1,0:T(8,128)(2,1)}) %all-gather.28.cloned.1.call-update) | async-done | bytes 8388624 | tf_op jit(solution)/shard_map/all_gather | solution.py:181
  778.8 21.9 %multiply_convert_fusion.2 = (bf16[1024,2048]{1,0:T(8,128)(2,1)}, bf16[1024,2048]{1,0:T(8,128)(2,1)}, bf16[1024,2048]{1,0:T(8,128)(2,1)}) fusion(f32[1024,2048]{1,0:T(8,128)} %fusion.48, f32[1024,2048]{1,0:T(8,128)} %fusion.49, bf16[1024,2048]{1,0:T(8,128)(2,1)} %all-gather.30.cloned.1.call-done, bf16[2048,2048]{1,0:T(8,128)(2,1)} %all-gather.28.cloned.1.call-done), kind=kOutput, calls=%fused_computation.14 | convolution fusion | flops 8623489024 | bytes 41943040 | tf_op jit(solution)/shard_map/dot_general | solution.py:21
  800.7 12.9 fusion.51
  813.6 13.5 convolution_add_fusion
  827.2 70.0 %reduce-scatter.16.cloned.1.call-done = f32[1024,512]{1,0:T(8,128)} async-done(((f32[1024,2048]{1,0:T(8,128)}), f32[1024,512]{1,0:T(8,128)}) %reduce-scatter.16.cloned.1.call-update) | async-done | bytes 2097168 | tf_op jit(solution)/shard_map/reduce_scatter | solution.py:39
  909.4 14.5 convolution_convert_fusion
  924.0 14.1 convolution_convert_fusion.1
  938.2 14.3 convolution_convert_fusion.2
  998.6 9.0 multiply_reduce_fusion
  1050.7 14.5 fusion.50
  1065.2 32.9 %reduce-scatter.32.cloned.1.call-done = bf16[2048,256]{1,0:T(8,128)(2,1)} async-done(((bf16[2048,2048]{1,0:T(8,128)(2,1)}), bf16[2048,256]{1,0:T(8,128)(2,1)}) %reduce-scatter.32.cloned.1.call-update) | async-done | bytes 1048592 | tf_op jit(solution)/shard_map/reduce_scatter | solution.py:236
  1100.7 149.2 %reduce-scatter.30.cloned.1.call-done = bf16[256,2048]{1,0:T(8,128)(2,1)} async-done(((bf16[2048,2048]{1,0:T(8,128)(2,1)}), bf16[256,2048]{1,0:T(8,128)(2,1)}) %reduce-scatter.30.cloned.1.call-update) | async-done | bytes 1048592 | tf_op jit(solution)/shard_map/reduce_scatter | solution.py:233
  1252.8 148.7 %reduce-scatter.28.cloned.1.call-done = bf16[256,2048]{1,0:T(8,128)(2,1)} async-done(((bf16[2048,2048]{1,0:T(8,128)(2,1)}), bf16[256,2048]{1,0:T(8,128)(2,1)}) %reduce-scatter.28.cloned.1.call-update) | async-done | bytes 1048592 | tf_op jit(solution)/shard_map/reduce_scatter | solution.py:230
  1404.3 68.4 %reduce-scatter.26.cloned.1.call-done = bf16[512,256]{1,0:T(8,128)(2,1)} async-done(((bf16[512,2048]{1,0:T(8,128)(2,1)}), bf16[512,256]{1,0:T(8,128)(2,1)}) %reduce-scatter.26.cloned.1.call-update) | async-done | bytes 262160 | tf_op jit(solution)/shard_map/reduce_scatter | solution.py:227
  1474.4 69.0 %reduce-scatter.24.cloned.1.call-done = bf16[256,512]{1,0:T(8,128)(2,1)} async-done(((bf16[2048,512]{1,0:T(8,128)(2,1)}), bf16[256,512]{1,0:T(8,128)(2,1)}) %reduce-scatter.24.cloned.1.call-update) | async-done | bytes 262160 | tf_op jit(solution)/shard_map/reduce_scatter | solution.py:224
  1545.3 68.8 %reduce-scatter.22.cloned.1.call-done = bf16[256,512]{1,0:T(8,128)(2,1)} async-done(((bf16[2048,512]{1,0:T(8,128)(2,1)}), bf16[256,512]{1,0:T(8,128)(2,1)}) %reduce-scatter.22.cloned.1.call-update) | async-done | bytes 262160 | tf_op jit(solution)/shard_map/reduce_scatter | solution.py:221
  1615.9 68.9 %reduce-scatter.20.cloned.1.call-done = bf16[256,512]{1,0:T(8,128)(2,1)} async-done(((bf16[2048,512]{1,0:T(8,128)(2,1)}), bf16[256,512]{1,0:T(8,128)(2,1)}) %reduce-scatter.20.cloned.1.call-update) | async-done | bytes 262160 | tf_op jit(solution)/shard_map/reduce_scatter | solution.py:218
  1686.6 71.7 %reduce-scatter.18.cloned.1.call-done = f32[1024,512]{1,0:T(8,128)} async-done(((f32[1024,2048]{1,0:T(8,128)}), f32[1024,512]{1,0:T(8,128)}) %reduce-scatter.18.cloned.1.call-update) | async-done | bytes 2097168 | tf_op jit(solution)/shard_map/reduce_scatter | solution.py:39
  1760.7 22.0 %all-reduce.2 = (f32[512]{0:T(512)}, f32[512]{0:T(512)}) all-reduce(f32[512]{0:T(512)S(1)} %get-tuple-element.77, f32[512]{0:T(512)S(1)} %copy-done.38), channel_id=1, replica_groups=mesh['tok'=8,'feat'=4] {'tok'}, use_global_device_ids=true, to_apply=%region_19.20 | all-reduce | flops 1024 | bytes 8192 | tf_op jit(solution)/shard_map/psum | solution.py:216
  1788.8 43.9 %reduce-scatter.14.cloned.1.call-done = f32[1024,512]{1,0:T(8,128)} async-done(((f32[1024,2048]{1,0:T(8,128)}), f32[1024,512]{1,0:T(8,128)}) %reduce-scatter.14.cloned.1.call-update) | async-done | bytes 2097168 | tf_op jit(solution)/shard_map/reduce_scatter | solution.py:39
  (217 shorter events, 214.7 us)
Async XLA Ops:
  7.2 55.0 %all-gather.18.cloned.1.call-start = ((), (), s32[]{:S(2)}) async-start(), calls=%async_computation.14 | async-start | bytes 2359296 | tf_op jit(solution)/shard_map/all_gather | solution.py:167
  7.9 89.4 %all-gather.12.cloned.1.call-start = ((), (), s32[]{:S(2)}) async-start(), calls=%async_computation.11 | async-start | bytes 5242880 | tf_op jit(solution)/shard_map/all_gather | solution.py:35
  20.9 127.8 %all-gather.16.cloned.1.call-start = ((), (), s32[]{:S(2)}) async-start(), calls=%async_computation.13 | async-start | bytes 2359296 | tf_op jit(solution)/shard_map/all_gather | solution.py:166
  21.7 176.9 %all-gather.14.cloned.1.call-start = ((), (), s32[]{:S(2)}) async-start(), calls=%async_computation.12 | async-start | bytes 2359296 | tf_op jit(solution)/shard_map/all_gather | solution.py:168
  22.3 227.8 %all-gather.20.cloned.1.call-start = ((), (), s32[]{:S(2)}) async-start(), calls=%async_computation.15 | async-start | bytes 2359296 | tf_op jit(solution)/shard_map/all_gather | solution.py:169
  22.8 304.5 %reduce-scatter.12.cloned.1.call-start = ((), (), s32[]{:S(2)}) async-start(), calls=%async_computation.16 | async-start | bytes 10485760 | tf_op jit(solution)/shard_map/reduce_scatter | solution.py:39
  257.3 197.3 %all-gather.26.cloned.1.call-start = ((), (), s32[]{:S(2)}) async-start(), calls=%async_computation.19 | async-start | bytes 9437184 | tf_op jit(solution)/shard_map/all_gather | solution.py:180
  258.1 231.5 %all-gather.22.cloned.1.call-start = ((), (), s32[]{:S(2)}) async-start(), calls=%async_computation.17 | async-start | bytes 5242880 | tf_op jit(solution)/shard_map/all_gather | solution.py:35
  329.3 576.4 %copy-start.2 = (f32[1024,512]{1,0:T(8,128)}, f32[1024,512]{1,0:T(8,128)S(1)}, u32[]{:S(2)}) copy-start(f32[1024,512]{1,0:T(8,128)S(1)} %get-tuple-element.82) | copy-start | bytes 6291460
  335.1 570.6 %copy-start.23 = (f32[1024]{0:T(1024)}, f32[1024]{0:T(1024)S(1)}, u32[]{:S(2)}) copy-start(f32[1024]{0:T(1024)S(1)} %add_rsqrt_fusion) | copy-start | bytes 12292
  336.3 280.6 %all-gather.24.cloned.1.call-start = ((), (), s32[]{:S(2)}) async-start(), calls=%async_computation.18 | async-start | bytes 9437184 | tf_op jit(solution)/shard_map/all_gather | solution.py:179
  337.1 314.0 %all-gather.30.cloned.1.call-start = ((), (), s32[]{:S(2)}) async-start(), calls=%async_computation.22 | async-start | bytes 5242880 | tf_op jit(solution)/shard_map/all_gather | solution.py:35
  337.6 441.1 %all-gather.28.cloned.1.call-start = ((), (), s32[]{:S(2)}) async-start(), calls=%async_computation.20 | async-start | bytes 9437184 | tf_op jit(solution)/shard_map/all_gather | solution.py:181
  338.4 558.8 %reduce-scatter.16.cloned.1.call-start = ((), (), s32[]{:S(2)}) async-start(), calls=%async_computation.23 | async-start | bytes 10485760 | tf_op jit(solution)/shard_map/reduce_scatter | solution.py:39
  827.2 126.1 %all-gather.32.cloned.1.call-start = ((), (), s32[]{:S(2)}) async-start(), calls=%async_computation.24 | async-start | bytes 5242880 | tf_op jit(solution)/shard_map/all_gather | solution.py:35
  909.4 188.7 %reduce-scatter.32.cloned.1.call-start = ((), (), s32[]{:S(2)}) async-start(), calls=%async_computation.32 | async-start | bytes 9437184 | tf_op jit(solution)/shard_map/reduce_scatter | solution.py:236
  923.9 326.0 %reduce-scatter.30.cloned.1.call-start = ((), (), s32[]{:S(2)}) async-start(), calls=%async_computation.31 | async-start | bytes 9437184 | tf_op jit(solution)/shard_map/reduce_scatter | solution.py:233
  938.1 463.4 %reduce-scatter.28.cloned.1.call-start = ((), (), s32[]{:S(2)}) async-start(), calls=%async_computation.30 | async-start | bytes 9437184 | tf_op jit(solution)/shard_map/reduce_scatter | solution.py:230
  952.5 520.2 %reduce-scatter.26.cloned.1.call-start = ((), (), s32[]{:S(2)}) async-start(), calls=%async_computation.29 | async-start | bytes 2359296 | tf_op jit(solution)/shard_map/reduce_scatter | solution.py:227
  959.7 583.7 %reduce-scatter.24.cloned.1.call-start = ((), (), s32[]{:S(2)}) async-start(), calls=%async_computation.28 | async-start | bytes 2359296 | tf_op jit(solution)/shard_map/reduce_scatter | solution.py:224
  998.6 615.5 %reduce-scatter.22.cloned.1.call-start = ((), (), s32[]{:S(2)}) async-start(), calls=%async_computation.27 | async-start | bytes 2359296 | tf_op jit(solution)/shard_map/reduce_scatter | solution.py:221
  1024.8 660.0 %reduce-scatter.20.cloned.1.call-start = ((), (), s32[]{:S(2)}) async-start(), calls=%async_computation.26 | async-start | bytes 2359296 | tf_op jit(solution)/shard_map/reduce_scatter | solution.py:218
  1037.9 720.3 %reduce-scatter.18.cloned.1.call-start = ((), (), s32[]{:S(2)}) async-start(), calls=%async_computation.25 | async-start | bytes 10485760 | tf_op jit(solution)/shard_map/reduce_scatter | solution.py:39
  1050.6 782.1 %reduce-scatter.14.cloned.1.call-start = ((), (), s32[]{:S(2)}) async-start(), calls=%async_computation.21 | async-start | bytes 10485760 | tf_op jit(solution)/shard_map/reduce_scatter | solution.py:39
  1100.7 657.5 %copy-start.6 = (bf16[1024,512]{1,0:T(8,128)(2,1)S(1)}, bf16[1024,512]{1,0:T(8,128)(2,1)}, u32[]{:S(2)}) copy-start(bf16[1024,512]{1,0:T(8,128)(2,1)} %param.23) | copy-start | bytes 3145732
  1100.7 657.5 %copy-start.26 = (f32[1024]{0:T(1024)S(1)}, f32[1024]{0:T(1024)}, u32[]{:S(2)}) copy-start(f32[1024]{0:T(1024)} %copy-done.25) | copy-start | bytes 12292
  1100.7 657.5 %copy-start.37 = (f32[512]{0:T(512)S(1)}, f32[512]{0:T(512)}, u32[]{:S(2)}) copy-start(f32[512]{0:T(512)} %param.24) | copy-start | bytes 6148
  1252.7 536.0 %copy-start.32 = (f32[1024]{0:T(1024)S(1)}, f32[1024]{0:T(1024)}, u32[]{:S(2)}) copy-start(f32[1024]{0:T(1024)} %copy-done.31) | copy-start | bytes 12292
  1252.7 580.0 %copy-start.3 = (f32[1024,512]{1,0:T(8,128)S(1)}, f32[1024,512]{1,0:T(8,128)}, u32[]{:S(2)}) copy-start(f32[1024,512]{1,0:T(8,128)} %copy-done.2) | copy-start | bytes 6291460
  1252.7 580.0 %copy-start.24 = (f32[1024]{0:T(1024)S(1)}, f32[1024]{0:T(1024)}, u32[]{:S(2)}) copy-start(f32[1024]{0:T(1024)} %copy-done.23) | copy-start | bytes 12292
  1252.7 580.0 %copy-start.34 = (f32[1024]{0:T(1024)S(1)}, f32[1024]{0:T(1024)}, u32[]{:S(2)}) copy-start(f32[1024]{0:T(1024)} %copy-done.33) | copy-start | bytes 12292
  1252.8 580.0 %copy-start.36 = (f32[512]{0:T(512)S(1)}, f32[512]{0:T(512)}, u32[]{:S(2)}) copy-start(f32[512]{0:T(512)} %param.29) | copy-start | bytes 6148
  (47 other events, 1268.6 us)
Sparse Core Ops, SparseCore 0:
  10.1 51.9 all-gather.17
  64.3 32.9 all-gather.11
  99.4 49.2 all-gather.15
  150.7 47.7 all-gather.13
  200.4 49.5 all-gather.19
  257.4 69.8 reduce-scatter.11
  329.7 124.9 all-gather.25
  456.9 32.6 all-gather.21
  491.9 124.9 all-gather.23
  618.4 32.6 all-gather.29
  653.3 125.3 all-gather.27
  827.3 69.8 reduce-scatter.15
  909.5 35.5 all-gather.31
  948.6 149.4 reduce-scatter.31
  1102.0 147.9 reduce-scatter.29
  1253.4 147.9 reduce-scatter.27
  1405.3 67.3 reduce-scatter.25
  1476.5 66.9 reduce-scatter.23
  1547.4 66.6 reduce-scatter.21
  1617.9 66.8 reduce-scatter.19
  1687.6 70.6 reduce-scatter.17
  1760.8 71.8 reduce-scatter.13
where the time goes:
time: 1850 us; the launch traced here: 1840 us
  waiting for transfers between devices  1450 us (78%)
  matrix products  253 us (14%)
  other arithmetic  58 us (3%)
  blocking collectives  47.9 us (3%)
    reduce_scatter x4, waiting for transfers between devices, split_sums(): lax.psum_scatter(partial_value, 'feat', scatter_dimension=1, tiled=True)  255 us
    reduce_scatter x1, waiting for transfers between devices, on_device(): lax.psum_scatter(up_grad.astype(jnp.bfloat16), 'tok', scatter_dimension=0...  149 us
    reduce_scatter x1, waiting for transfers between devices, on_device(): lax.psum_scatter(gate_grad.astype(jnp.bfloat16), 'tok', scatter_dimension...  149 us
    all_gather x1, waiting for transfers between devices, on_device(): lax.all_gather(w_down, 'tok', axis=1, tiled=True)  128 us
    all_gather x1, waiting for transfers between devices, on_device(): lax.all_gather(w_up, 'tok', axis=0, tiled=True)  116 us
    all_gather x1, waiting for transfers between devices, on_device(): lax.all_gather(w_gate, 'tok', axis=0, tiled=True)  113 us
    all_gather x4, waiting for transfers between devices, whole_rows(): return lax.all_gather(shard, 'feat', axis=1, tiled=True)  89.8 us
    reduce_scatter x1, waiting for transfers between devices, on_device(): lax.psum_scatter(term_value.astype(jnp.bfloat16), 'tok', scatter_dimensio...  69 us
  transfers between devices with their start and end apart: 22, of which 21 were waited for; matrix products, arithmetic and copies ran while one was open for 13% of the time, Pallas kernels for 0%

commit v1 on v0

v1 whole, which is shorter than its diff:
```python
import jax
import jax.numpy as jnp
from jax import lax
from jax.sharding import PartitionSpec as P

HD = 64
LEN = 1024
EPSILON = 1e-05
BF16 = jnp.bfloat16
F32 = jnp.float32


def left_trans(left, right):
    return lax.dot_general(
        left, right, (((0,), (0,)), ((), ())), preferred_element_type=F32
    )


def right_trans(left, right):
    return lax.dot_general(
        left, right, (((1,), (1,)), ((), ())), preferred_element_type=F32
    )


def product(left, right):
    return jnp.dot(left, right, preferred_element_type=F32)


class Tok:
    def __init__(self, size):
        self.size = size
        self.ring = size // 2

    def coords(self):
        me = lax.axis_index("tok")
        return me // 2, me % 2

    def up(self, value):
        pairs = [(i, (i + 2) % self.size) for i in range(self.size)]
        return lax.ppermute(value, "tok", pairs)

    def down(self, value):
        pairs = [(i, (i - 2) % self.size) for i in range(self.size)]
        return lax.ppermute(value, "tok", pairs)

    def swap(self, value):
        return lax.ppermute(value, "tok", [(i, i ^ 1) for i in range(self.size)])

    def gather(self, shard):
        pieces = []
        for step in range(self.ring):
            pieces += [shard, self.swap(shard)]
            if step < self.ring - 1:
                shard = self.up(shard)
        return pieces

    def scatter(self, piece):
        total = None
        for step in reversed(range(self.ring)):
            arrived = self.swap(piece(2 * step + 1).astype(BF16))
            mine = piece(2 * step) + arrived.astype(F32)
            if total is not None:
                mine = mine + self.down(total.astype(BF16)).astype(F32)
            total = mine
        return total


def x_swap(value):
    return lax.ppermute(value, "feat", [(i, i ^ 2) for i in range(4)])


def core_swap(value):
    return lax.ppermute(value, "feat", [(i, i ^ 1) for i in range(4)])


def feat_gather(shard):
    far = x_swap(shard)
    return [shard, core_swap(shard), far, core_swap(far)]


def feat_scatter(piece):
    third = core_swap(piece(3).astype(BF16)).astype(F32)
    far = (piece(2) + third).astype(BF16)
    far = x_swap(far).astype(F32)
    first = core_swap(piece(1).astype(BF16)).astype(F32)
    return piece(0) + first + far


def split_heads(values):
    return values.reshape(values.shape[0] // LEN, LEN, values.shape[1] // HD, HD)


def causal_scores(query_block, key_block, offset):
    block_rows = query_block.shape[1]
    key_count = key_block.shape[1]
    scores = jnp.einsum(
        "sqhd,skhd->shqk", query_block, key_block, preferred_element_type=F32
    ) * HD ** (-0.5)
    allowed = (offset + jnp.arange(block_rows))[:, None] >= jnp.arange(key_count)[None, :]
    return jnp.where(allowed, scores, -1e30)


def attend(queries, key_rows, value_rows):
    query_heads, key_heads, value_heads = (
        split_heads(queries),
        split_heads(key_rows),
        split_heads(value_rows),
    )
    block_rows = min(512, LEN)
    outputs = []
    log_sums = []
    for offset in range(0, LEN, block_rows):
        block_end = offset + block_rows
        scores = causal_scores(query_heads[:, offset:block_end], key_heads[:, :block_end], offset)
        highest = jnp.max(scores, axis=-1, keepdims=True)
        exponent = jnp.exp(scores - highest)
        denominator = jnp.sum(exponent, axis=-1, keepdims=True)
        probs = (exponent / denominator).astype(BF16)
        outputs.append(
            jnp.einsum(
                "shqk,skhd->sqhd",
                probs,
                value_heads[:, :block_end],
                preferred_element_type=F32,
            )
        )
        log_sums.append((highest + jnp.log(denominator))[..., 0])
    attended = jnp.concatenate(outputs, axis=1).astype(BF16).reshape(queries.shape)
    return (attended, jnp.concatenate(log_sums, axis=2))


def attend_back(queries, key_rows, value_rows, log_sums, grad_attended):
    query_heads, key_heads, value_heads = (
        split_heads(queries),
        split_heads(key_rows),
        split_heads(value_rows),
    )
    grad_heads = split_heads(grad_attended)
    block_rows = min(512, LEN)
    factor = HD ** (-0.5)
    query_parts = []
    grad_keys = jnp.zeros(key_heads.shape, F32)
    grad_values = jnp.zeros(value_heads.shape, F32)
    for offset in range(0, LEN, block_rows):
        block_end = offset + block_rows
        query_block = query_heads[:, offset:block_end]
        grad_block = grad_heads[:, offset:block_end]
        scores = causal_scores(query_block, key_heads[:, :block_end], offset)
        probs = jnp.exp(scores - log_sums[:, :, offset:block_end, None])
        grad_probs = jnp.einsum(
            "sqhd,skhd->shqk",
            grad_block,
            value_heads[:, :block_end],
            preferred_element_type=F32,
        )
        inner = jnp.sum(probs * grad_probs, axis=-1, keepdims=True)
        grad_scores = (probs * (grad_probs - inner)).astype(BF16)
        query_parts.append(
            jnp.einsum(
                "shqk,skhd->sqhd",
                grad_scores,
                key_heads[:, :block_end],
                preferred_element_type=F32,
            )
            * factor
        )
        key_term = (
            jnp.einsum(
                "shqk,sqhd->skhd", grad_scores, query_block, preferred_element_type=F32
            )
            * factor
        )
        grad_keys = grad_keys.at[:, :block_end].add(key_term)
        value_term = jnp.einsum(
            "shqk,sqhd->skhd",
            probs.astype(BF16),
            grad_block,
            preferred_element_type=F32,
        )
        grad_values = grad_values.at[:, :block_end].add(value_term)
    shape = queries.shape
    grad_queries = jnp.concatenate(query_parts, axis=1).astype(BF16).reshape(shape)
    return (
        grad_queries,
        grad_keys.astype(BF16).reshape(shape),
        grad_values.astype(BF16).reshape(shape),
    )


def program(
    tok_size,
    tokens, gain_attn, w_query, w_key, w_value, w_out, gain_ffn, w_gate, w_up, w_down, cotangent
):
    tok = Tok(tok_size)
    ring = tok.ring
    place, member = tok.coords()
    feat = lax.axis_index("feat")
    rows, wide = tokens.shape
    model = 4 * wide
    unit = model // ring
    half = unit // 2
    per = wide // unit
    quarter = rows // 4
    hidden_wide = w_gate.shape[1]

    def swap_halves(block):
        turned = jnp.concatenate([block[..., half:], block[..., :half]], axis=-1)
        return jnp.where(member == 0, block, turned)

    def to_rotated(slots):
        stacked = jnp.stack(slots)
        if per > 1:
            lead = stacked.reshape(4, -1, per, unit)
            stacked = jnp.moveaxis(lead, 2, 1).reshape(4 * per, -1, unit)
        blocks = []
        for step in range(ring):
            source = (place - step) % ring
            index = ((source // per) ^ feat) * per + source % per
            block = lax.dynamic_index_in_dim(stacked, index, 0, keepdims=False)
            blocks.append(swap_halves(block))
        return jnp.concatenate(blocks, axis=-1)

    def slot_of(rotated, r):
        lead = rotated.reshape(-1, ring, unit)
        blocks = []
        for inside in range(per):
            source = (feat ^ r) * per + inside
            step = (place - source) % ring
            block = lax.dynamic_index_in_dim(lead, step, 1, keepdims=False)
            blocks.append(swap_halves(block))
        return jnp.concatenate(blocks, axis=-1)

    def row_block(values, r):
        return lax.dynamic_slice_in_dim(values, (feat ^ r) * quarter, quarter, 0)

    def natural_rows(blocks):
        stacked = jnp.stack(blocks)
        return jnp.concatenate(
            [lax.dynamic_index_in_dim(stacked, feat ^ j, 0, keepdims=False) for j in range(4)]
        )

    qkv = jnp.concatenate(tok.gather(jnp.concatenate([w_query, w_key, w_value], axis=1)), axis=0)
    out_proj = jnp.concatenate(tok.gather(w_out), axis=1)
    gate_up = jnp.concatenate(tok.gather(jnp.concatenate([w_gate, w_up], axis=1)), axis=0)
    down_proj = jnp.concatenate(tok.gather(w_down), axis=1)

    gains = lax.all_gather(jnp.stack([gain_attn, gain_ffn]), "feat")
    gains_slots = [lax.dynamic_index_in_dim(gains, feat ^ r, 0, keepdims=False) for r in range(4)]
    gains_rot = to_rotated(gains_slots)
    gain_one, gain_two = gains_rot[0], gains_rot[1]
    x_all = to_rotated(feat_gather(tokens)).astype(F32)
    cot_slots = feat_gather(cotangent)
    cot_nat = to_rotated(cot_slots)
    cot_rows = jnp.concatenate([row_block(cot_nat, r) for r in range(4)])

    factor_one = lax.rsqrt(jnp.mean(x_all * x_all, axis=1, keepdims=True) + EPSILON)
    normed = (x_all * factor_one * gain_one).astype(BF16)
    projected = product(normed, qkv).astype(BF16)
    queries = projected[:, :wide]
    key_rows = projected[:, wide : 2 * wide]
    value_rows = projected[:, 2 * wide :]
    attended, log_sums = attend(queries, key_rows, value_rows)
    mixed = feat_scatter(lambda r: product(row_block(attended, r), out_proj))
    middle = row_block(x_all, 0) + mixed
    factor_two = lax.rsqrt(jnp.mean(middle * middle, axis=1, keepdims=True) + EPSILON)
    normed_own = (middle * factor_two * gain_two).astype(BF16)
    normed_two = jnp.concatenate(feat_gather(normed_own))

    both = product(normed_two, gate_up)
    gate, upward = both[:, :hidden_wide], both[:, hidden_wide:]
    sigma = jax.nn.sigmoid(gate)
    hidden = (gate * sigma * upward).astype(BF16)
    grad_hidden = right_trans(cot_rows, down_proj)
    grad_gate = (grad_hidden * upward * sigma * (1.0 + gate * (1.0 - sigma))).astype(BF16)
    grad_up = (grad_hidden * gate * sigma).astype(BF16)
    grad_both = jnp.concatenate([grad_gate, grad_up], axis=1)

    def columns(values, i):
        return values[:, i * half : (i + 1) * half]

    down_grad = tok.scatter(lambda i: left_trans(hidden, columns(cot_rows, i)))
    both_grad = tok.scatter(lambda i: left_trans(columns(normed_two, i), grad_both))
    gate_grad, up_grad = both_grad[:, :hidden_wide], both_grad[:, hidden_wide:]

    grad_normed_two = feat_scatter(
        lambda r: right_trans(grad_both[r * quarter : (r + 1) * quarter], gate_up)
    )
    weighted = gain_two * grad_normed_two
    inner = jnp.mean(weighted * middle, axis=1, keepdims=True)
    grad_middle = (
        cot_rows[:quarter].astype(F32)
        + factor_two * weighted
        - middle * (factor_two * factor_two * factor_two * inner)
    )
    gain_ffn_part = jnp.sum(grad_normed_two * middle * factor_two, axis=0)

    out_rows = product(hidden, down_proj)
    out_rows = jnp.concatenate([out_rows[:quarter] + middle, out_rows[quarter:]])
    out_blocks = [out_rows[r * quarter : (r + 1) * quarter] for r in range(4)]
    outcome = feat_scatter(lambda r: natural_rows([slot_of(block, r) for block in out_blocks]))

    grad_mid_rows = natural_rows(feat_gather(grad_middle.astype(BF16)))
    grad_attended = right_trans(grad_mid_rows, out_proj).astype(BF16)
    out_grad = tok.scatter(lambda i: left_trans(attended, columns(grad_mid_rows, i)))
    grad_queries, grad_keys, grad_values = attend_back(
        queries, key_rows, value_rows, log_sums, grad_attended
    )
    grad_proj = jnp.concatenate([grad_queries, grad_keys, grad_values], axis=1)
    qkv_grad = tok.scatter(lambda i: left_trans(columns(normed, i), grad_proj))

    grad_normed = right_trans(grad_proj, qkv)
    inner_part = jnp.sum(grad_normed * gain_one * x_all, axis=1)
    inner_one = lax.psum(inner_part, "feat")
    gain_attn_part = jnp.sum(grad_normed * x_all * factor_one, axis=0)
    carried = grad_normed * gain_one * factor_one
    own_rows = jax.nn.one_hot(feat, 4, dtype=F32)
    spread = jnp.concatenate([own_rows[j] * grad_middle for j in range(4)])
    carried = carried + spread
    gathered_grad = feat_scatter(lambda r: slot_of(carried, r))
    one = factor_one[:, 0]
    input_grad = gathered_grad - tokens.astype(F32) * (one * one * one * inner_one / model)[:, None]

    parts = jnp.stack([gain_attn_part, gain_ffn_part])
    owned = jnp.stack([slot_of(parts, r) for r in range(4)])
    own_all = jnp.concatenate(
        [lax.dynamic_index_in_dim(owned, feat ^ j, 0, keepdims=False) for j in range(4)], axis=-1
    )
    gain_sums = lax.psum(own_all, ("tok", "feat"))
    gain_grads = lax.dynamic_slice_in_dim(gain_sums, feat * wide, wide, 1)
    return (
        outcome.astype(BF16),
        input_grad.astype(BF16),
        gain_grads[0],
        gain_grads[1],
        qkv_grad[:, :wide],
        qkv_grad[:, wide : 2 * wide],
        qkv_grad[:, 2 * wide :],
        out_grad,
        gate_grad,
        up_grad,
        down_grad,
    )


def solution(mesh):
    in_specs = (
        P("tok", "feat"),
        P("feat"),
        P("tok", "feat"),
        P("tok", "feat"),
        P("tok", "feat"),
        P("feat", "tok"),
        P("feat"),
        P("tok", "feat"),
        P("tok", "feat"),
        P("feat", "tok"),
        P("tok", "feat"),
    )
    out_specs = (
        P("tok", "feat"),
        P("tok", "feat"),
        P("feat"),
        P("feat"),
        P("tok", "feat"),
        P("tok", "feat"),
        P("tok", "feat"),
        P("feat", "tok"),
        P("tok", "feat"),
        P("tok", "feat"),
        P("feat", "tok"),
    )

    def on_device(*arrays):
        return program(mesh.shape["tok"], *arrays)

    return jax.shard_map(
        on_device, mesh=mesh, in_specs=in_specs, out_specs=out_specs, check_vma=False
    )
```

time: 1850 us -> 1160 us (0.63)
  waiting for transfers between devices: 1450 us -> 421 us
  local copies, waits for them, and re-layouts: 15 us -> 162 us
  starting transfers between devices: 1.06 us -> 73.7 us
  matrix products: 253 us -> 322 us
  blocking collectives: 47.9 us -> 92 us
  other arithmetic: 58 us -> 77.8 us
    reduce_scatter x11 -> x0, waiting for transfers between devices: 861 us -> none  [the longest x4 255 us: split_sums(): lax.psum_scatter(partial_value, 'feat', scatter_dimension=1, tiled=True)]
    all_gather x11 -> x0, waiting for transfers between devices: 588 us -> none  [the longest x1 128 us: on_device(): lax.all_gather(w_down, 'tok', axis=1, tiled=True)]
    ppermute x0 -> x80, waiting for transfers between devices: none -> 421 us  [the longest x32 226 us: swap(): return lax.ppermute(value, 'tok', [(i, i ^ 1) for i in range(self.size)])]
    ppermute x0 -> x80, starting transfers between devices: none -> 73.7 us  [the longest x32 33.9 us: swap(): return lax.ppermute(value, 'tok', [(i, i ^ 1) for i in range(self.size)])]
    dot_general x7 -> x32, matrix products: 62.3 us -> 128 us  [left_trans(): lax.dot_general(left, right, (((0,), (0,)), ((), ())), preferred_element_...]
    dynamic_slice x0 -> x12, local copies, waits for them, and re-layouts: none -> 50.9 us  [the longest x10 50.5 us: slot_of(): block = lax.dynamic_index_in_dim(lead, step, 1, keepdims=False)]
    unnamed x114 -> x329, local copies, waits for them, and re-layouts: 15 us -> 62.1 us
    psum x5 -> x2, blocking collectives: 47.9 us -> 86.8 us  [the longest x1 79.8 us: program(): gain_sums = lax.psum(own_all, ('tok', 'feat'))]
  transfers between devices with their start and end apart: 22 -> 80, of which waited for: 21 -> 30; matrix products, arithmetic and copies ran while one was open for 13% -> 37% of each run, Pallas kernels for 0% -> 0%
where the time goes in v1:
time: 1160 us; the launch traced here: 1150 us
  waiting for transfers between devices  421 us (36%)
  matrix products  322 us (28%)
  local copies, waits for them, and re-layouts  162 us (14%)
  blocking collectives  92 us (8%)
  other arithmetic  77.8 us (7%)
  starting transfers between devices  73.7 us (6%)
    ppermute x32, waiting for transfers between devices, swap(): return lax.ppermute(value, 'tok', [(i, i ^ 1) for i in range(self.size)])  226 us
    dot_general x32, matrix products, left_trans(): lax.dot_general(left, right, (((0,), (0,)), ((), ())), preferred_element_...  128 us
    dot_general x7, matrix products, right_trans(): lax.dot_general(left, right, (((1,), (1,)), ((), ())), preferred_element_...  93.7 us
    ppermute x12, waiting for transfers between devices, up(): return lax.ppermute(value, 'tok', pairs)  85.8 us
    psum x1, blocking collectives, program(): gain_sums = lax.psum(own_all, ('tok', 'feat'))  79.8 us
    ppermute x12, waiting for transfers between devices, down(): return lax.ppermute(value, 'tok', pairs)  74.4 us
    unnamed x329, local copies, waits for them, and re-layouts  62.1 us
    dynamic_slice x10, local copies, waits for them, and re-layouts, slot_of(): block = lax.dynamic_index_in_dim(lead, step, 1, keepdims=False)  50.5 us
  transfers between devices with their start and end apart: 80, of which 30 were waited for; matrix products, arithmetic and copies ran while one was open for 37% of the time, Pallas kernels for 0%

profile of v1, /device:TPU:0, one launch (start us, length us, event | category | flops | bytes accessed | tf_op | source)
XLA Modules:
  0.0 1152.3 jit_solution(1211388668994720829)
XLA Ops:
  52.8 9.6 collective-permute-done.4
  73.8 11.2 collective-permute-done.31
  90.0 9.9 collective-permute-done.6
  109.8 27.2 %collective-permute-done.23 = bf16[256,4096]{1,0:T(8,128)(2,1)S(1)} collective-permute-done((bf16[256,4096]{1,0:T(8,128)(2,1)S(1)}, bf16[256,4096]{1,0:T(8,128)(2,1)S(1)}, u32[]{:S(2)}, u32[]{:S(2)}) %collective-permute-start.23) | collective-permute-done | bytes 2097184 | tf_op jit(solution)/shard_map/ppermute | solution.py:47
  138.4 12.0 %collective-permute-done.24 = bf16[256,4096]{1,0:T(8,128)(2,1)} collective-permute-done((bf16[256,4096]{1,0:T(8,128)(2,1)S(1)}, bf16[256,4096]{1,0:T(8,128)(2,1)}, u32[]{:S(2)}, u32[]{:S(2)}) %collective-permute-start.24) | collective-permute-done | bytes 2097184 | tf_op jit(solution)/shard_map/ppermute | solution.py:40
  155.2 17.7 %collective-permute-done.33 = bf16[2048,256]{1,0:T(8,128)(2,1)} collective-permute-done((bf16[2048,256]{1,0:T(8,128)(2,1)}, bf16[2048,256]{1,0:T(8,128)(2,1)}, u32[]{:S(2)}, u32[]{:S(2)}) %collective-permute-start.33) | collective-permute-done | bytes 1048608 | tf_op jit(solution)/shard_map/ppermute | solution.py:40
  177.6 12.1 %collective-permute-done.8 = bf16[256,1536]{1,0:T(8,128)(2,1)S(1)} collective-permute-done((bf16[256,1536]{1,0:T(8,128)(2,1)S(1)}, bf16[256,1536]{1,0:T(8,128)(2,1)S(1)}, u32[]{:S(2)}, u32[]{:S(2)}) %collective-permute-start.8) | collective-permute-done | bytes 786464 | tf_op jit(solution)/shard_map/ppermute | solution.py:40
  194.5 20.8 %collective-permute-done.9 = bf16[256,1536]{1,0:T(8,128)(2,1)S(1)} collective-permute-done((bf16[256,1536]{1,0:T(8,128)(2,1)S(1)}, bf16[256,1536]{1,0:T(8,128)(2,1)S(1)}, u32[]{:S(2)}, u32[]{:S(2)}) %collective-permute-start.9) | collective-permute-done | bytes 786464 | tf_op jit(solution)/shard_map/ppermute | solution.py:47
  272.1 13.9 %collective-permute-done.19 = bf16[256,2048]{1,0:T(8,128)(2,1)S(1)} collective-permute-done((bf16[256,2048]{1,0:T(8,128)(2,1)S(1)}, bf16[256,2048]{1,0:T(8,128)(2,1)S(1)}, u32[]{:S(2)}, u32[]{:S(2)}) %collective-permute-start.19) | collective-permute-done | bytes 1048608 | tf_op jit(solution)/shard_map/ppermute | solution.py:69
  292.4 20.6 %collective-permute-done.25 = bf16[256,4096]{1,0:T(8,128)(2,1)S(1)} collective-permute-done((bf16[256,4096]{1,0:T(8,128)(2,1)}, bf16[256,4096]{1,0:T(8,128)(2,1)S(1)}, u32[]{:S(2)}, u32[]{:S(2)}) %collective-permute-start.25) | collective-permute-done | bytes 2097184 | tf_op jit(solution)/shard_map/ppermute | solution.py:47
  324.3 11.1 collective-permute-done.36
  336.6 43.8 %collective-permute-done.27 = bf16[256,4096]{1,0:T(8,128)(2,1)S(1)} collective-permute-done((bf16[256,4096]{1,0:T(8,128)(2,1)}, bf16[256,4096]{1,0:T(8,128)(2,1)S(1)}, u32[]{:S(2)}, u32[]{:S(2)}) %collective-permute-start.27) | collective-permute-done | bytes 2097184 | tf_op jit(solution)/shard_map/ppermute | solution.py:47
  385.9 38.7 %collective-permute-done.29 = bf16[256,4096]{1,0:T(8,128)(2,1)S(1)} collective-permute-done((bf16[256,4096]{1,0:T(8,128)(2,1)S(1)}, bf16[256,4096]{1,0:T(8,128)(2,1)S(1)}, u32[]{:S(2)}, u32[]{:S(2)}) %collective-permute-start.29) | collective-permute-done | bytes 2097184 | tf_op jit(solution)/shard_map/ppermute | solution.py:47
  426.2 22.4 %fusion.178 = f32[1024,4096]{1,0:T(8,128)} fusion(bf16[2048,4096]{1,0:T(8,128)(2,1)} %constant_dynamic-update-slice_fusion.23, bf16[256,2048]{1,0:T(8,128)(2,1)S(1)} %collective-permute-done.22, bf16[256,2048]{1,0:T(8,128)(2,1)S(1)} %collective-permute-done.21, bf16[256,2048]{1,0:T(8,128)(2,1)S(1)} %collective-permute-done.20, ...), kind=kOutput, calls=%fused_computation.479 | convolution fusion | flops 17196646400 | bytes 37748736 | tf_op jit(solution)/shard_map/dot_general | solution.py:26
  448.6 22.3 %multiply_convert_fusion.2 = (bf16[1024,2048]{1,0:T(8,128)(2,1)}, bf16[1024,2048]{1,0:T(8,128)(2,1)}, bf16[1024,2048]{1,0:T(8,128)(2,1)}) fusion(f32[1024,4096]{1,0:T(8,128)} %fusion.178, bf16[2048,2048]{1,0:T(8,128)(2,1)} %constant_dynamic-update-slice_fusion.32, bf16[256,2048]{1,0:T(8,128)(2,1)S(1)} %get-tuple-element.100, ...), kind=kOutput, calls=%fused_computation.24 | convolution fusion | flops 8640266240 | bytes 41943040 | tf_op jit(solution)/shard_map/dot_general | solution.py:20
  471.0 10.9 convolution_convert_fusion.5
  481.9 12.0 %convolution_convert_fusion.6 = bf16[256,2048]{1,0:T(8,128)(2,1)} fusion(bf16[2048,4096]{1,0:T(8,128)(2,1)} %constant_dynamic-update-slice_fusion.23, bf16[1024,2048]{1,0:T(8,128)(2,1)} %get-tuple-element.82, bf16[1024,2048]{1,0:T(8,128)(2,1)} %get-tuple-element.81), kind=kOutput, calls=%fused_computation.74 | convolution fusion | flops 4299685888 | bytes 26214400 | tf_op jit(solution)/shard_map/dot_general | solution.py:20
  514.9 11.5 fusion.206
  546.6 11.9 %fusion.21 = bf16[256,2048]{1,0:T(8,128)(2,1)} fusion(bf16[2048,4096]{1,0:T(8,128)(2,1)} %constant_dynamic-update-slice_fusion.23, bf16[1024,2048]{1,0:T(8,128)(2,1)} %get-tuple-element.82, bf16[1024,2048]{1,0:T(8,128)(2,1)} %get-tuple-element.81, bf16[256,2048]{1,0:T(8,128)(2,1)S(1)} %collective-permute-done.44), kind=kOutput, calls=%fused_computation.71 | convolution fusion | flops 4300734464 | bytes 27262976 | tf_op jit(solution)/shard_map/dot_general | solution.py:20
  583.7 14.0 %multiply_reduce_fusion.5 = (f32[2048]{0:T(1024)}, f32[256]{0:T(256)S(1)}, f32[256,2048]{1,0:T(8,128)}) fusion(f32[256,2048]{1,0:T(8,128)S(1)} %copy-done.7, f32[256]{0:T(256)S(1)} %copy-done.112, f32[2048]{0:T(1024)S(1)} %bitcast.521, bf16[256,2048]{1,0:T(8,128)(2,1)} %collective-permute-done.45, bf16[256,2048]{1,0:T(8,128)(2,1)} %collective-permute-done.43, ...), kind=kOutput, calls=%fused_computation.123 | convolution fusion | flops 4304402432 | bytes 31475712 | tf_op jit(solution)/shard_map/dot_general | solution.py:20
  666.6 10.7 collective-permute-done.47
  735.9 10.2 multiply_convert_fusion
  757.1 17.2 %multiply_reduce_fusion.1 = (f32[2048]{0:T(1024)S(1)}, f32[1024]{0:T(1024)S(1)}, f32[1024,2048]{1,0:T(8,128)}) fusion(f32[1024]{0:T(1024)S(1)} %copy-done.110, bf16[1024,512]{1,0:T(8,128)(2,1)S(1)} %copy-done.14, bf16[1024,512]{1,0:T(8,128)(2,1)S(1)} %copy-done.16, bf16[1024,512]{1,0:T(8,128)(2,1)S(1)} %copy-done.18, bf16[1024,512]{1,0:T(8,128)(2,1)} %copy-done.19, ...), kind=kOutput, calls=%fused_computation.19 | convolution fusion | flops 6494876672 | bytes 30433280 | tf_op jit(solution)/shard_map/dot_general | solution.py:20
  774.3 11.2 reshape.1193
  785.5 11.5 constant_dynamic-slice_fusion.10
  797.0 11.6 %constant_dynamic-slice_fusion.11 = (bf16[1024,1,512]{2,1,0:T(2,128)(2,1)}, bf16[1024,1,512]{2,1,0:T(2,128)(2,1)}) fusion(f32[1024,4,512]{2,1,0:T(4,128)} %reshape.1193, s32[]{:T(128)S(6)} %select_n.600, s32[]{:T(128)S(6)} %select_n.612), kind=kLoop, calls=%fused_computation.391 | loop fusion | bytes 4194312 | tf_op jit(solution)/shard_map/jit(dynamic_index_in_dim)/dynamic_slice | solution.py:229
  855.4 79.8 %psum.15 = f32[2,2048]{1,0:T(2,128)S(1)} all-reduce(f32[2,2048]{1,0:T(2,128)S(1)} %pad_maximum_fusion.20), channel_id=1, replica_groups=mesh['tok'=8,'feat'=4] {'tok','feat'}, use_global_device_ids=true, to_apply=%region_13.14 | all-reduce | flops 4096 | bytes 32768 | tf_op jit(solution)/shard_map/psum | solution.py:328
  970.2 11.7 %collective-permute-done.61 = bf16[512,256]{1,0:T(8,128)(2,1)S(1)} collective-permute-done((bf16[512,256]{1,0:T(8,128)(2,1)S(1)}, bf16[512,256]{1,0:T(8,128)(2,1)S(1)}, u32[]{:S(2)}, u32[]{:S(2)}) %collective-permute-start.61) | collective-permute-done | bytes 262176 | tf_op jit(solution)/shard_map/ppermute | solution.py:47
  990.4 44.9 %collective-permute-done.64 = bf16[512,256]{1,0:T(8,128)(2,1)S(1)} collective-permute-done((bf16[512,256]{1,0:T(8,128)(2,1)S(1)}, bf16[512,256]{1,0:T(8,128)(2,1)S(1)}, u32[]{:S(2)}, u32[]{:S(2)}) %collective-permute-start.64) | collective-permute-done | bytes 262176 | tf_op jit(solution)/shard_map/ppermute | solution.py:44
  1041.7 11.9 %collective-permute-done.56 = bf16[256,1536]{1,0:T(8,128)(2,1)S(1)} collective-permute-done((bf16[256,1536]{1,0:T(8,128)(2,1)S(1)}, bf16[256,1536]{1,0:T(8,128)(2,1)S(1)}, u32[]{:S(2)}, u32[]{:S(2)}) %collective-permute-start.56) | collective-permute-done | bytes 786464 | tf_op jit(solution)/shard_map/ppermute | solution.py:44
  1091.7 39.1 %collective-permute-done.52 = bf16[256,1536]{1,0:T(8,128)(2,1)S(1)} collective-permute-done((bf16[256,1536]{1,0:T(8,128)(2,1)S(1)}, bf16[256,1536]{1,0:T(8,128)(2,1)S(1)}, u32[]{:S(2)}, u32[]{:S(2)}) %collective-permute-start.52) | collective-permute-done | bytes 786464 | tf_op jit(solution)/shard_map/ppermute | solution.py:47
  1130.8 10.0 collective-permute-done.58
  (674 shorter events, 525.4 us)
Async XLA Ops:
  99.9 50.5 %collective-permute-start.24 = (bf16[256,4096]{1,0:T(8,128)(2,1)S(1)}, bf16[256,4096]{1,0:T(8,128)(2,1)}, u32[]{:S(2)}, u32[]{:S(2)}) collective-permute-start(bf16[256,4096]{1,0:T(8,128)(2,1)S(1)} %copy-done.95), channel_id=1, source_target_pairs={{0,8},{4,12},{8,16},{12,20},{16,24},{20,28},{24,0},{28,4},{1,9},{5... | collective-permute-start | bytes 6291464 | tf_op jit(solution)/shard_map/ppermute | solution.py:40
  100.9 151.8 %collective-permute-start.32 = (bf16[2048,256]{1,0:T(8,128)(2,1)}, bf16[2048,256]{1,0:T(8,128)(2,1)}, u32[]{:S(2)}, u32[]{:S(2)}) collective-permute-start(bf16[2048,256]{1,0:T(8,128)(2,1)} %collective-permute-done.31), channel_id=1, source_target_pairs={{0,4},{4,0},{8,12},{12,8},{16,20},{20,16},{24,28},{28,24},{1,5},{5... | collective-permute-start | bytes 3145736 | tf_op jit(solution)/shard_map/ppermute | solution.py:47
  103.6 69.3 %collective-permute-start.33 = (bf16[2048,256]{1,0:T(8,128)(2,1)}, bf16[2048,256]{1,0:T(8,128)(2,1)}, u32[]{:S(2)}, u32[]{:S(2)}) collective-permute-start(bf16[2048,256]{1,0:T(8,128)(2,1)} %collective-permute-done.31), channel_id=1, source_target_pairs={{0,8},{4,12},{8,16},{12,20},{16,24},{20,28},{24,0},{28,4},{1,9},{5... | collective-permute-start | bytes 3145736 | tf_op jit(solution)/shard_map/ppermute | solution.py:40
  105.1 87.3 %collective-permute-start.7 = (bf16[256,1536]{1,0:T(8,128)(2,1)S(1)}, bf16[256,1536]{1,0:T(8,128)(2,1)S(1)}, u32[]{:S(2)}, u32[]{:S(2)}) collective-permute-start(bf16[256,1536]{1,0:T(8,128)(2,1)S(1)} %collective-permute-done.6), channel_id=1, source_target_pairs={{0,4},{4,0},{8,12},{12,8},{16,20},{20,16},{24,28},{28,24},{1,5},{5... | collective-permute-start | bytes 2359304 | tf_op jit(solution)/shard_map/ppermute | solution.py:47
  137.0 52.7 %collective-permute-start.8 = (bf16[256,1536]{1,0:T(8,128)(2,1)S(1)}, bf16[256,1536]{1,0:T(8,128)(2,1)S(1)}, u32[]{:S(2)}, u32[]{:S(2)}) collective-permute-start(bf16[256,1536]{1,0:T(8,128)(2,1)S(1)} %collective-permute-done.6), channel_id=1, source_target_pairs={{0,8},{4,12},{8,16},{12,20},{16,24},{20,28},{24,0},{28,4},{1,9},{5... | collective-permute-start | bytes 2359304 | tf_op jit(solution)/shard_map/ppermute | solution.py:40
  155.1 115.8 %collective-permute-start.26 = (bf16[256,4096]{1,0:T(8,128)(2,1)}, bf16[256,4096]{1,0:T(8,128)(2,1)}, u32[]{:S(2)}, u32[]{:S(2)}) collective-permute-start(bf16[256,4096]{1,0:T(8,128)(2,1)} %collective-permute-done.24), channel_id=1, source_target_pairs={{0,8},{4,12},{8,16},{12,20},{16,24},{20,28},{24,0},{28,4},{1,9},{5... | collective-permute-start | bytes 6291464 | tf_op jit(solution)/shard_map/ppermute | solution.py:40
  172.9 91.4 %collective-permute-start.34 = (bf16[2048,256]{1,0:T(8,128)(2,1)}, bf16[2048,256]{1,0:T(8,128)(2,1)}, u32[]{:S(2)}, u32[]{:S(2)}) collective-permute-start(bf16[2048,256]{1,0:T(8,128)(2,1)} %collective-permute-done.33), channel_id=1, source_target_pairs={{0,4},{4,0},{8,12},{12,8},{16,20},{20,16},{24,28},{28,24},{1,5},{5... | collective-permute-start | bytes 3145736 | tf_op jit(solution)/shard_map/ppermute | solution.py:47
  192.3 72.5 %collective-permute-start.35 = (bf16[2048,256]{1,0:T(8,128)(2,1)}, bf16[2048,256]{1,0:T(8,128)(2,1)}, u32[]{:S(2)}, u32[]{:S(2)}) collective-permute-start(bf16[2048,256]{1,0:T(8,128)(2,1)} %collective-permute-done.33), channel_id=1, source_target_pairs={{0,8},{4,12},{8,16},{12,20},{16,24},{20,28},{24,0},{28,4},{1,9},{5... | collective-permute-start | bytes 3145736 | tf_op jit(solution)/shard_map/ppermute | solution.py:40
  264.8 70.6 %collective-permute-start.36 = (bf16[2048,256]{1,0:T(8,128)(2,1)}, bf16[2048,256]{1,0:T(8,128)(2,1)S(1)}, u32[]{:S(2)}, u32[]{:S(2)}) collective-permute-start(bf16[2048,256]{1,0:T(8,128)(2,1)} %collective-permute-done.35), channel_id=1, source_target_pairs={{0,4},{4,0},{8,12},{12,8},{16,20},{20,16},{24,28},{28,24},{1,5},{5... | collective-permute-start | bytes 3145736 | tf_op jit(solution)/shard_map/ppermute | solution.py:47
  271.0 49.2 %collective-permute-start.28 = (bf16[256,4096]{1,0:T(8,128)(2,1)}, bf16[256,4096]{1,0:T(8,128)(2,1)S(1)}, u32[]{:S(2)}, u32[]{:S(2)}) collective-permute-start(bf16[256,4096]{1,0:T(8,128)(2,1)} %collective-permute-done.26), channel_id=1, source_target_pairs={{0,8},{4,12},{8,16},{12,20},{16,24},{20,28},{24,0},{28,4},{1,9},{5... | collective-permute-start | bytes 6291464 | tf_op jit(solution)/shard_map/ppermute | solution.py:40
  271.6 108.8 %collective-permute-start.27 = (bf16[256,4096]{1,0:T(8,128)(2,1)}, bf16[256,4096]{1,0:T(8,128)(2,1)S(1)}, u32[]{:S(2)}, u32[]{:S(2)}) collective-permute-start(bf16[256,4096]{1,0:T(8,128)(2,1)} %collective-permute-done.26), channel_id=1, source_target_pairs={{0,4},{4,0},{8,12},{12,8},{16,20},{20,16},{24,28},{28,24},{1,5},{5... | collective-permute-start | bytes 6291464 | tf_op jit(solution)/shard_map/ppermute | solution.py:47
  320.2 104.5 %collective-permute-start.29 = (bf16[256,4096]{1,0:T(8,128)(2,1)S(1)}, bf16[256,4096]{1,0:T(8,128)(2,1)S(1)}, u32[]{:S(2)}, u32[]{:S(2)}) collective-permute-start(bf16[256,4096]{1,0:T(8,128)(2,1)S(1)} %collective-permute-done.28), channel_id=1, source_target_pairs={{0,4},{4,0},{8,12},{12,8},{16,20},{20,16},{24,28},{28,24},{1,5},{5... | collective-permute-start | bytes 6291464 | tf_op jit(solution)/shard_map/ppermute | solution.py:47
  323.8 59.6 %collective-permute-start.20 = (bf16[256,2048]{1,0:T(8,128)(2,1)S(1)}, bf16[256,2048]{1,0:T(8,128)(2,1)S(1)}, u32[]{:S(2)}, u32[]{:S(2)}) collective-permute-start(bf16[256,2048]{1,0:T(8,128)(2,1)S(1)} %multiply_convert_fusion.6), channel_id=1, source_target_pairs={{0,1},{1,0},{2,3},{3,2},{4,5},{5,4},{6,7},{7,6},{8,9},{9,8},{10,11... | collective-permute-start | bytes 3145736 | tf_op jit(solution)/shard_map/ppermute | solution.py:73
  323.8 59.6 %collective-permute-start.22 = (bf16[256,2048]{1,0:T(8,128)(2,1)S(1)}, bf16[256,2048]{1,0:T(8,128)(2,1)S(1)}, u32[]{:S(2)}, u32[]{:S(2)}) collective-permute-start(bf16[256,2048]{1,0:T(8,128)(2,1)S(1)} %collective-permute-done.21), channel_id=1, source_target_pairs={{0,1},{1,0},{2,3},{3,2},{4,5},{5,4},{6,7},{7,6},{8,9},{9,8},{10,11... | collective-permute-start | bytes 3145736 | tf_op jit(solution)/shard_map/ppermute | solution.py:73
  564.3 102.3 %collective-permute-start.69 = (bf16[256,4096]{1,0:T(8,128)(2,1)}, bf16[256,4096]{1,0:T(8,128)(2,1)}, u32[]{:S(2)}, u32[]{:S(2)}) collective-permute-start(bf16[256,4096]{1,0:T(8,128)(2,1)} %convolution_convert_fusion), channel_id=1, source_target_pairs={{0,4},{4,0},{8,12},{12,8},{16,20},{20,16},{24,28},{28,24},{1,5},{5... | collective-permute-start | bytes 6291464 | tf_op jit(solution)/shard_map/ppermute | solution.py:47
  565.9 85.8 %collective-permute-start.75 = (bf16[2048,256]{1,0:T(8,128)(2,1)}, bf16[2048,256]{1,0:T(8,128)(2,1)}, u32[]{:S(2)}, u32[]{:S(2)}) collective-permute-start(bf16[2048,256]{1,0:T(8,128)(2,1)} %convolution_convert_fusion.10), channel_id=1, source_target_pairs={{0,4},{4,0},{8,12},{12,8},{16,20},{20,16},{24,28},{28,24},{1,5},{5... | collective-permute-start | bytes 3145736 | tf_op jit(solution)/shard_map/ppermute | solution.py:47
  569.8 117.5 %collective-permute-start.74 = (bf16[2048,256]{1,0:T(8,128)(2,1)}, bf16[2048,256]{1,0:T(8,128)(2,1)}, u32[]{:S(2)}, u32[]{:S(2)}) collective-permute-start(bf16[2048,256]{1,0:T(8,128)(2,1)} %convolution_convert_fusion.11), channel_id=1, source_target_pairs={{0,4},{4,0},{8,12},{12,8},{16,20},{20,16},{24,28},{28,24},{1,5},{5... | collective-permute-start | bytes 3145736 | tf_op jit(solution)/shard_map/ppermute | solution.py:47
  575.2 77.9 %collective-permute-start.77 = (bf16[2048,256]{1,0:T(8,128)(2,1)}, bf16[2048,256]{1,0:T(8,128)(2,1)}, u32[]{:S(2)}, u32[]{:S(2)}) collective-permute-start(bf16[2048,256]{1,0:T(8,128)(2,1)} %add_convert_fusion.2), channel_id=1, source_target_pairs={{0,24},{4,28},{8,0},{12,4},{16,8},{20,12},{24,16},{28,20},{1,25},{... | collective-permute-start | bytes 3145736 | tf_op jit(solution)/shard_map/ppermute | solution.py:44
  684.3 275.0 %collective-permute-start.68 = (bf16[256,4096]{1,0:T(8,128)(2,1)}, bf16[256,4096]{1,0:T(8,128)(2,1)}, u32[]{:S(2)}, u32[]{:S(2)}) collective-permute-start(bf16[256,4096]{1,0:T(8,128)(2,1)} %convolution_convert_fusion.1), channel_id=1, source_target_pairs={{0,4},{4,0},{8,12},{12,8},{16,20},{20,16},{24,28},{28,24},{1,5},{5... | collective-permute-start | bytes 6291464 | tf_op jit(solution)/shard_map/ppermute | solution.py:47
  687.3 367.7 %collective-permute-start.67 = (bf16[256,4096]{1,0:T(8,128)(2,1)}, bf16[256,4096]{1,0:T(8,128)(2,1)}, u32[]{:S(2)}, u32[]{:S(2)}) collective-permute-start(bf16[256,4096]{1,0:T(8,128)(2,1)} %convolution_convert_fusion.2), channel_id=1, source_target_pairs={{0,4},{4,0},{8,12},{12,8},{16,20},{20,16},{24,28},{28,24},{1,5},{5... | collective-permute-start | bytes 6291464 | tf_op jit(solution)/shard_map/ppermute | solution.py:47
  687.8 259.9 %collective-permute-start.73 = (bf16[2048,256]{1,0:T(8,128)(2,1)}, bf16[2048,256]{1,0:T(8,128)(2,1)}, u32[]{:S(2)}, u32[]{:S(2)}) collective-permute-start(bf16[2048,256]{1,0:T(8,128)(2,1)} %convolution_convert_fusion.12), channel_id=1, source_target_pairs={{0,4},{4,0},{8,12},{12,8},{16,20},{20,16},{24,28},{28,24},{1,5},{5... | collective-permute-start | bytes 3145736 | tf_op jit(solution)/shard_map/ppermute | solution.py:47
  691.8 153.1 %collective-permute-start.37 = (bf16[1024,512]{1,0:T(8,128)(2,1)}, bf16[1024,512]{1,0:T(8,128)(2,1)}, u32[]{:S(2)}, u32[]{:S(2)}) collective-permute-start(bf16[1024,512]{1,0:T(8,128)(2,1)} %pad_maximum_fusion.15), channel_id=1, source_target_pairs={{0,1},{1,0},{2,3},{3,2},{4,5},{5,4},{6,7},{7,6},{8,9},{9,8},{10,11... | collective-permute-start | bytes 3145736 | tf_op jit(solution)/shard_map/ppermute | solution.py:73
  691.8 153.1 %collective-permute-start.39 = (bf16[1024,512]{1,0:T(8,128)(2,1)}, bf16[1024,512]{1,0:T(8,128)(2,1)}, u32[]{:S(2)}, u32[]{:S(2)}) collective-permute-start(bf16[1024,512]{1,0:T(8,128)(2,1)} %fusion.33), channel_id=1, source_target_pairs={{0,2},{1,3},{2,0},{3,1},{4,6},{5,7},{6,4},{7,5},{8,10},{9,11},{10,... | collective-permute-start | bytes 3145736 | tf_op jit(solution)/shard_map/ppermute | solution.py:69
  844.9 114.7 %collective-permute-start.70 = (bf16[256,4096]{1,0:T(8,128)(2,1)}, bf16[256,4096]{1,0:T(8,128)(2,1)}, u32[]{:S(2)}, u32[]{:S(2)}) collective-permute-start(bf16[256,4096]{1,0:T(8,128)(2,1)} %fusion.13), channel_id=1, source_target_pairs={{0,24},{4,28},{8,0},{12,4},{16,8},{20,12},{24,16},{28,20},{1,25},{... | collective-permute-start | bytes 6291464 | tf_op jit(solution)/shard_map/ppermute | solution.py:44
  844.9 102.8 %collective-permute-start.79 = (bf16[2048,256]{1,0:T(8,128)(2,1)}, bf16[2048,256]{1,0:T(8,128)(2,1)}, u32[]{:S(2)}, u32[]{:S(2)}) collective-permute-start(bf16[2048,256]{1,0:T(8,128)(2,1)} %add_convert_fusion), channel_id=1, source_target_pairs={{0,24},{4,28},{8,0},{12,4},{16,8},{20,12},{24,16},{28,20},{1,25},{... | collective-permute-start | bytes 3145736 | tf_op jit(solution)/shard_map/ppermute | solution.py:44
  947.7 92.6 %collective-permute-start.50 = (bf16[1024,512]{1,0:T(8,128)(2,1)S(1)}, bf16[1024,512]{1,0:T(8,128)(2,1)S(1)}, u32[]{:S(2)}, u32[]{:S(2)}) collective-permute-start(bf16[1024,512]{1,0:T(8,128)(2,1)S(1)} %copy-done.91), channel_id=1, source_target_pairs={{0,1},{1,0},{2,3},{3,2},{4,5},{5,4},{6,7},{7,6},{8,9},{9,8},{10,11... | collective-permute-start | bytes 3145736 | tf_op jit(solution)/shard_map/ppermute | solution.py:73
  983.5 72.5 %collective-permute-start.71 = (bf16[256,4096]{1,0:T(8,128)(2,1)}, bf16[256,4096]{1,0:T(8,128)(2,1)}, u32[]{:S(2)}, u32[]{:S(2)}) collective-permute-start(bf16[256,4096]{1,0:T(8,128)(2,1)} %fusion.11), channel_id=1, source_target_pairs={{0,24},{4,28},{8,0},{12,4},{16,8},{20,12},{24,16},{28,20},{1,25},{... | collective-permute-start | bytes 6291464 | tf_op jit(solution)/shard_map/ppermute | solution.py:44
  985.8 49.6 %collective-permute-start.64 = (bf16[512,256]{1,0:T(8,128)(2,1)S(1)}, bf16[512,256]{1,0:T(8,128)(2,1)S(1)}, u32[]{:S(2)}, u32[]{:S(2)}) collective-permute-start(bf16[512,256]{1,0:T(8,128)(2,1)S(1)} %fusion.94), channel_id=1, source_target_pairs={{0,24},{4,28},{8,0},{12,4},{16,8},{20,12},{24,16},{28,20},{1,25},{... | collective-permute-start | bytes 786440 | tf_op jit(solution)/shard_map/ppermute | solution.py:44
  989.1 51.7 %collective-permute-start.54 = (bf16[256,1536]{1,0:T(8,128)(2,1)S(1)}, bf16[256,1536]{1,0:T(8,128)(2,1)S(1)}, u32[]{:S(2)}, u32[]{:S(2)}) collective-permute-start(bf16[256,1536]{1,0:T(8,128)(2,1)S(1)} %copy-done.119), channel_id=1, source_target_pairs={{0,4},{4,0},{8,12},{12,8},{16,20},{20,16},{24,28},{28,24},{1,5},{5... | collective-permute-start | bytes 2359304 | tf_op jit(solution)/shard_map/ppermute | solution.py:47
  1069.2 73.0 %collective-permute-start.66 = (bf16[256,4096]{1,0:T(8,128)(2,1)S(1)}, bf16[256,4096]{1,0:T(8,128)(2,1)S(1)}, u32[]{:S(2)}, u32[]{:S(2)}) collective-permute-start(bf16[256,4096]{1,0:T(8,128)(2,1)S(1)} %copy-done.116), channel_id=1, source_target_pairs={{0,4},{4,0},{8,12},{12,8},{16,20},{20,16},{24,28},{28,24},{1,5},{5... | collective-permute-start | bytes 6291464 | tf_op jit(solution)/shard_map/ppermute | solution.py:47
  1078.3 65.2 %collective-permute-start.72 = (bf16[256,4096]{1,0:T(8,128)(2,1)}, bf16[256,4096]{1,0:T(8,128)(2,1)S(1)}, u32[]{:S(2)}, u32[]{:S(2)}) collective-permute-start(bf16[256,4096]{1,0:T(8,128)(2,1)} %fusion.12), channel_id=1, source_target_pairs={{0,24},{4,28},{8,0},{12,4},{16,8},{20,12},{24,16},{28,20},{1,25},{... | collective-permute-start | bytes 6291464 | tf_op jit(solution)/shard_map/ppermute | solution.py:44
  1084.5 56.3 %collective-permute-start.58 = (bf16[256,1536]{1,0:T(8,128)(2,1)S(1)}, bf16[256,1536]{1,0:T(8,128)(2,1)S(1)}, u32[]{:S(2)}, u32[]{:S(2)}) collective-permute-start(bf16[256,1536]{1,0:T(8,128)(2,1)S(1)} %add_convert_fusion.3), channel_id=1, source_target_pairs={{0,24},{4,28},{8,0},{12,4},{16,8},{20,12},{24,16},{28,20},{1,25},{... | collective-permute-start | bytes 2359304 | tf_op jit(solution)/shard_map/ppermute | solution.py:44
  (188 other events, 3333.9 us)

commit v2 on v0

v2 whole, which is shorter than its diff:
```python
import jax
import jax.numpy as jnp
from jax import lax
from jax.experimental import pallas as pl
from jax.experimental.pallas import tpu as pltpu
from jax.sharding import PartitionSpec as P

HD = 64
LEN = 1024
EPSILON = 1e-05
BF16 = jnp.bfloat16
F32 = jnp.float32
MESH = pl.DeviceIdType.MESH
VMEM = 48 << 20
CHUNKS = 2
FORWARD_BLOCK = 512
BACK_BLOCK = 256


def left_trans(left, right):
    return lax.dot_general(
        left, right, (((0,), (0,)), ((), ())), preferred_element_type=F32
    )


def right_trans(left, right):
    return lax.dot_general(
        left, right, (((1,), (1,)), ((), ())), preferred_element_type=F32
    )


def product(left, right):
    return jnp.dot(left, right, preferred_element_type=F32)


def causal_tile(scores):
    size = scores.shape[0]
    key = lax.broadcasted_iota(jnp.int32, scores.shape, 0)
    query = lax.broadcasted_iota(jnp.int32, scores.shape, 1)
    return jnp.where(key <= query, scores, -1e30)


def head_parts(packed_ref, head, width):
    columns = [slice(part * width + head * HD, part * width + (head + 1) * HD) for part in range(3)]
    query, key, value = [packed_ref[:, part] for part in columns]
    return query * HD ** (-0.5), key, value


def attend_kernel(packed_ref, out_ref, lse_ref):
    width = out_ref.shape[1]
    for head in range(width // HD):
        query, key, value = head_parts(packed_ref, head, width)
        query = query.astype(BF16)
        value_t = value.T
        for top in range(0, LEN, FORWARD_BLOCK):
            keys = top + FORWARD_BLOCK
            scores = right_trans(key[:keys], query[top:keys])
            last = causal_tile(scores[top:])
            scores = jnp.concatenate([scores[:top], last]) if top else last
            highest = jnp.max(scores, axis=0, keepdims=True)
            exponent = jnp.exp(scores - highest)
            total = jnp.sum(exponent, axis=0, keepdims=True)
            mixed = product(value_t[:, :keys], exponent.astype(BF16)) / total
            out_ref[top:keys, head * HD : (head + 1) * HD] = mixed.T.astype(BF16)
            lse_ref[0, 0, head : head + 1, top:keys] = highest + jnp.log(total)


def attend_back_kernel(packed_ref, out_ref, grad_ref, lse_ref, grads_ref, key_acc, value_acc):
    width = out_ref.shape[1]
    for head in range(width // HD):
        lanes = slice(head * HD, (head + 1) * HD)
        query, key, value = head_parts(packed_ref, head, width)
        query = query.astype(BF16)
        key_t = key.T
        grad = grad_ref[:, lanes]
        inner = (out_ref[:, lanes].astype(F32) * grad.astype(F32)).T
        inner = jnp.sum(inner, axis=0, keepdims=True)
        for top in reversed(range(0, LEN, BACK_BLOCK)):
            keys = top + BACK_BLOCK
            scores = right_trans(key[:keys], query[top:keys])
            last = causal_tile(scores[top:])
            scores = jnp.concatenate([scores[:top], last]) if top else last
            probs = jnp.exp(scores - lse_ref[0, 0, head : head + 1, top:keys])
            grad_probs = right_trans(value[:keys], grad[top:keys])
            grad_scores = (probs * (grad_probs - inner[:, top:keys])).astype(BF16)
            value_term = product(probs.astype(BF16), grad[top:keys])
            key_term = product(grad_scores, query[top:keys])
            if keys == LEN:
                value_acc[...] = value_term
                key_acc[...] = key_term
            else:
                value_acc[:keys] += value_term
                key_acc[:keys] += key_term
            grad_query = product(key_t[:, :keys], grad_scores) * HD ** (-0.5)
            grads_ref[top:keys, lanes] = grad_query.T.astype(BF16)
        grads_ref[:, width + head * HD : width + (head + 1) * HD] = key_acc[...].astype(BF16)
        grads_ref[:, 2 * width + head * HD : 2 * width + (head + 1) * HD] = value_acc[...].astype(
            BF16
        )


def attend(packed):
    rows, columns = packed.shape
    width = 2 * HD
    sequences, pairs = rows // LEN, columns // (3 * width)
    return pl.pallas_call(
        attend_kernel,
        grid=(sequences, pairs),
        out_shape=(
            jax.ShapeDtypeStruct((rows, pairs * width), BF16),
            jax.ShapeDtypeStruct((sequences, pairs, 2, LEN), F32),
        ),
        in_specs=[pl.BlockSpec((LEN, 3 * width), lambda s, p: (s, p))],
        out_specs=(
            pl.BlockSpec((LEN, width), lambda s, p: (s, p)),
            pl.BlockSpec((1, 1, 2, LEN), lambda s, p: (s, p, 0, 0)),
        ),
        compiler_params=pltpu.CompilerParams(vmem_limit_bytes=VMEM),
        cost_estimate=pl.CostEstimate(
            flops=4 * rows * LEN * pairs * width // 2,
            transcendentals=rows * LEN * pairs,
            bytes_accessed=2 * rows * columns * 2,
        ),
        name="attend",
    )(packed)


def attend_back(packed, attended, grad_attended, lse):
    rows, columns = packed.shape
    width = 2 * HD
    sequences, pairs = rows // LEN, columns // (3 * width)
    narrow = pl.BlockSpec((LEN, width), lambda s, p: (s, p))
    return pl.pallas_call(
        attend_back_kernel,
        grid=(sequences, pairs),
        out_shape=jax.ShapeDtypeStruct((rows, columns), BF16),
        in_specs=[
            pl.BlockSpec((LEN, 3 * width), lambda s, p: (s, p)),
            narrow,
            narrow,
            pl.BlockSpec((1, 1, 2, LEN), lambda s, p: (s, p, 0, 0)),
        ],
        out_specs=pl.BlockSpec((LEN, 3 * width), lambda s, p: (s, p)),
        scratch_shapes=[pltpu.VMEM((LEN, HD), F32)] * 2,
        compiler_params=pltpu.CompilerParams(vmem_limit_bytes=VMEM),
        cost_estimate=pl.CostEstimate(
            flops=10 * rows * LEN * pairs * width // 2,
            transcendentals=rows * LEN * pairs,
            bytes_accessed=3 * rows * columns * 2,
        ),
        name="attend_back",
    )(packed, attended, grad_attended, lse)


SPREAD = (
    (0, 0, "y", None),
    (0, 1, "x", None),
    (0, 0, "x", None),
    (0, 1, "y", None),
    (0, 0, "core", None),
    (0, 1, "core", None),
    (4, 0, "x", 0),
    (2, 1, "y", 1),
    (4, 0, "core", 0),
    (2, 1, "core", 1),
    (2, 0, "core", 2),
    (4, 1, "core", 3),
    (6, 0, "core", 6),
    (6, 1, "core", 7),
)
BIT = {"y": 4, "x": 2, "core": 1}


def neighbours():
    token, feat = lax.axis_index("tok"), lax.axis_index("feat")
    return {
        "y": (token + 1 - 2 * lax.rem(token, 2), feat),
        "x": (token, lax.rem(feat + 2, 4)),
        "core": (token, feat + 1 - 2 * lax.rem(feat, 2)),
    }


def owner(r):
    member, slot = lax.rem(lax.axis_index("tok"), 2), lax.axis_index("feat")
    if r & 4:
        member = 1 - member
    if r & 2:
        slot = lax.rem(slot + 2, 4)
    if r & 1:
        slot = slot + 1 - 2 * lax.rem(slot, 2)
    return member, slot


def greet():
    barrier = pltpu.get_barrier_semaphore()
    for peer in neighbours().values():
        pl.semaphore_signal(barrier, inc=1, device_id=peer, device_id_type=MESH)
    pl.semaphore_wait(barrier, 3)


class Spread:
    def __init__(self, own, region, send, recv):
        self.own, self.region, self.send, self.recv = own, region, send, recv
        self.peers = neighbours()

    def copy(self, k):
        r, half, way, _ = SPREAD[k]
        source = self.own(half) if r == 0 else self.region(r, half)
        return pltpu.make_async_remote_copy(
            source, self.region(r, half), self.send.at[k], self.recv.at[k],
            device_id=self.peers[way], device_id_type=MESH,
        )

    def arrival(self, k):
        r, half, way, _ = SPREAD[k]
        place = self.region(r ^ BIT[way], half)
        return pltpu.make_async_remote_copy(
            place, place, self.send.at[k], self.recv.at[k],
            device_id=self.peers[way], device_id_type=MESH,
        )

    def start(self, half):
        for k, (r, which, _, after) in enumerate(SPREAD):
            if after is None and which == half:
                self.copy(k).start()

    def forward(self):
        for first in range(8):
            if first in (4, 5):
                continue
            self.arrival(first).wait_recv()
            for k, (_, _, _, after) in enumerate(SPREAD):
                if after == first:
                    self.copy(k).start()

    def finish(self):
        for k, (_, _, way, _) in enumerate(SPREAD):
            if way == "core":
                self.arrival(k).wait_recv()
        for k in range(len(SPREAD)):
            self.copy(k).wait_send()


SPREAD_SEMS = [pltpu.SemaphoreType.DMA((len(SPREAD),))] * 2


class Collect:
    def __init__(self, part, size, parts, near, from_x, from_y, last_y, last_x, sems):
        self.part, self.size, self.half = part, size, size // 2
        self.parts, self.near = parts, near
        self.from_x, self.from_y, self.last_y, self.last_x = from_x, from_y, last_y, last_x
        self.load, self.send, self.recv = sems
        self.peers = neighbours()

    @staticmethod
    def scratch(size, columns):
        half = size // 2
        return [
            pltpu.VMEM((4, size, columns), BF16),
            pltpu.VMEM((4, size, columns), BF16),
            pltpu.VMEM((2, half, columns), BF16),
            pltpu.VMEM((2, half, columns), BF16),
            pltpu.VMEM((half, columns), BF16),
            pltpu.VMEM((half, columns), BF16),
            pltpu.SemaphoreType.DMA((4,)),
            pltpu.SemaphoreType.DMA((10,)),
            pltpu.SemaphoreType.DMA((10,)),
        ]

    def remote(self, k, source, target, way):
        return pltpu.make_async_remote_copy(
            source, target, self.send.at[k], self.recv.at[k],
            device_id=self.peers[way], device_id_type=MESH,
        )

    def copy(self, k):
        low, high = pl.ds(0, self.half), pl.ds(self.half, self.half)
        if k < 4:
            return self.remote(k, self.part(2 * k + 1), self.near.at[k], "core")
        if k < 6:
            return self.remote(k, self.parts.at[(1, 3)[k - 4], low], self.from_x.at[k - 4], "x")
        if k < 8:
            return self.remote(k, self.parts.at[(2, 3)[k - 6], high], self.from_y.at[k - 6], "y")
        if k == 8:
            return self.remote(k, self.parts.at[2, low], self.last_y, "y")
        return self.remote(k, self.parts.at[1, high], self.last_x, "x")

    def add(self, index, start, count, other):
        step = 32

        def body(i, carry):
            here = pl.ds(pl.multiple_of(start + i * step, step), step)
            there = pl.ds(pl.multiple_of(i * step, step), step)
            total = self.parts[index, here].astype(F32) + other[there].astype(F32)
            self.parts[index, here] = total.astype(BF16)
            return carry

        lax.fori_loop(0, count // step, body, 0)

    def run(self):
        for k in (3, 1, 2, 0):
            self.copy(k).start()
        loads = [
            pltpu.make_async_copy(self.part(2 * k), self.parts.at[k], self.load.at[k])
            for k in range(4)
        ]
        for k in (3, 1, 2, 0):
            loads[k].start()
        for k, following in ((3, (5, 7)), (1, (4,)), (2, (6,)), (0, ())):
            loads[k].wait()
            self.copy(k).wait_recv()
            self.add(k, 0, self.size, self.near.at[k])
            for after in following:
                self.copy(after).start()
        self.copy(5).wait_recv()
        self.add(2, 0, self.half, self.from_x.at[1])
        self.copy(8).start()
        self.copy(7).wait_recv()
        self.add(1, self.half, self.half, self.from_y.at[1])
        self.copy(9).start()

    def total(self, half, rows):
        first, last = (self.from_x, self.last_y) if half == 0 else (self.from_y, self.last_x)
        own = self.parts[0, pl.ds(pl.multiple_of(half * self.half + rows.start, 32), rows.size)]
        return own.astype(F32) + first[0, rows].astype(F32) + last[rows].astype(F32)

    def ready(self, half):
        for k in ((4, 8) if half == 0 else (6, 9)):
            self.copy(k).wait_recv()

    def finish(self):
        for k in range(10):
            self.copy(k).wait_send()


def loop_rows(count, body):
    def step(i, carry):
        body(pl.ds(pl.multiple_of(i * 32, 32), 32))
        return carry

    lax.fori_loop(0, count // 32, step, 0)


def call(kernel, identity, operands, spaces, outputs, out_spaces, scratch, cost):
    return pl.pallas_call(
        kernel,
        out_shape=outputs,
        in_specs=[pl.BlockSpec(memory_space=space) for space in spaces],
        out_specs=jax.tree.map(lambda space: pl.BlockSpec(memory_space=space), out_spaces),
        scratch_shapes=scratch,
        compiler_params=pltpu.CompilerParams(
            collective_id=identity, has_side_effects=True, vmem_limit_bytes=VMEM
        ),
        cost_estimate=pl.CostEstimate(flops=cost, bytes_accessed=cost // 100, transcendentals=0),
        name=kernel.__name__,
    )(*operands)


def gather_block(identity, shard):
    rows, wide = shard.shape
    half = rows // 2

    def gather_input(shard_ref, out_ref, local, send, recv):
        greet()

        def region(r, which):
            member, slot = owner(r)
            return out_ref.at[
                pl.ds(pl.multiple_of(member * rows + which * half, half), half),
                pl.ds(pl.multiple_of(slot * wide, wide), wide),
            ]

        spread = Spread(
            lambda which: shard_ref.at[pl.ds(which * half, half)], region, send, recv
        )
        spread.start(0)
        spread.start(1)
        copies = [
            pltpu.make_async_copy(
                shard_ref.at[pl.ds(which * half, half)], region(0, which), local.at[which]
            )
            for which in range(2)
        ]
        for copy in copies:
            copy.start()
        spread.forward()
        spread.finish()
        for copy in copies:
            copy.wait()

    return call(
        gather_input, identity, (shard,), (pl.ANY,),
        jax.ShapeDtypeStruct((2 * rows, 4 * wide), shard.dtype), pl.ANY,
        [pltpu.SemaphoreType.DMA((2,))] + SPREAD_SEMS, 40_000_000_000,
    )


def scatter_block(identity, terms):
    rows, wide = terms.shape[0] // 2, terms.shape[1] // 4

    def scatter_output(terms_ref, out_ref, *scratch):
        greet()

        def part(r):
            member, slot = owner(r)
            return terms_ref.at[
                pl.ds(pl.multiple_of(member * rows, rows), rows),
                pl.ds(pl.multiple_of(slot * wide, wide), wide),
            ]

        collect = Collect(part, rows, *scratch[:6], scratch[6:])
        collect.run()
        for which in range(2):
            collect.ready(which)

            def body(here):
                there = pl.ds(pl.multiple_of(which * (rows // 2) + here.start, 32), 32)
                out_ref[there] = collect.total(which, here).astype(BF16)

            loop_rows(rows // 2, body)
        collect.finish()

    return call(
        scatter_output, identity, (terms,), (pl.ANY,),
        jax.ShapeDtypeStruct((rows, wide), BF16), pltpu.VMEM,
        Collect.scratch(rows, wide), 30_000_000_000,
    )


def row_parts(terms_ref, quarter):
    def part(r):
        member, slot = owner(r)
        return terms_ref.at[pl.ds(pl.multiple_of((member * 4 + slot) * quarter, quarter), quarter)]

    return part


def row_region(out_ref, quarter):
    half = quarter // 2

    def region(r, which):
        member, slot = owner(r)
        start = (member * 4 + slot) * quarter + which * half
        return out_ref.at[pl.ds(pl.multiple_of(start, half), half)]

    return region


def middle_norm(identity, terms, x_all, gain):
    total, model = terms.shape
    quarter = total // 8
    half = quarter // 2

    def middle_step(
        terms_ref, x_ref, gain_ref, out_ref, middle_ref, factor_ref,
        x_own, normed, local, send, recv, *scratch
    ):
        greet()
        x_copy = pltpu.make_async_copy(row_parts(x_ref, quarter)(0), x_own, local.at[0])
        x_copy.start()
        collect = Collect(row_parts(terms_ref, quarter), quarter, *scratch[:6], scratch[6:])
        region = row_region(out_ref, quarter)
        spread = Spread(
            lambda which: normed.at[pl.ds(which * half, half)], region, send, recv
        )
        collect.run()
        x_copy.wait()
        copies = []
        for which in range(2):
            collect.ready(which)

            def body(here):
                there = pl.ds(pl.multiple_of(which * half + here.start, 32), 32)
                middle = collect.total(which, here) + x_own[there].astype(F32)
                mean = jnp.mean(middle * middle, axis=1, keepdims=True)
                factor = lax.rsqrt(mean + EPSILON)
                middle_ref[there] = middle
                factor_ref[there] = jnp.broadcast_to(factor, (32, 128))
                normed[there] = (middle * factor * gain_ref[...]).astype(BF16)

            loop_rows(half, body)
            spread.start(which)
            copy = pltpu.make_async_copy(
                normed.at[pl.ds(which * half, half)], region(0, which), local.at[1 + which]
            )
            copy.start()
            copies.append(copy)
        spread.forward()
        spread.finish()
        collect.finish()
        for copy in copies:
            copy.wait()

    return call(
        middle_step, identity, (terms, x_all, gain), (pl.ANY, pl.ANY, pltpu.VMEM),
        (
            jax.ShapeDtypeStruct((total, model), BF16),
            jax.ShapeDtypeStruct((quarter, model), F32),
            jax.ShapeDtypeStruct((quarter, 128), F32),
        ),
        (pl.ANY, pltpu.VMEM, pltpu.VMEM),
        [
            pltpu.VMEM((quarter, model), BF16),
            pltpu.VMEM((quarter, model), BF16),
            pltpu.SemaphoreType.DMA((3,)),
        ]
        + SPREAD_SEMS
        + Collect.scratch(quarter, model),
        70_000_000_000,
    )


def middle_back(identity, terms, cot, middle, factor, gain):
    total, model = terms.shape
    quarter = total // 8
    half = quarter // 2

    def middle_back_step(
        terms_ref, cot_ref, middle_ref, factor_ref, gain_ref, out_ref, grad_ref, gain_grad_ref,
        cot_own, rounded, local, send, recv, *scratch
    ):
        greet()
        cot_copy = pltpu.make_async_copy(row_parts(cot_ref, quarter)(0), cot_own, local.at[0])
        cot_copy.start()
        collect = Collect(row_parts(terms_ref, quarter), quarter, *scratch[:6], scratch[6:])
        region = row_region(out_ref, quarter)
        spread = Spread(
            lambda which: rounded.at[pl.ds(which * half, half)], region, send, recv
        )
        collect.run()
        cot_copy.wait()
        gain_grad_ref[...] = jnp.zeros_like(gain_grad_ref)
        copies = []
        for which in range(2):
            collect.ready(which)

            def body(here):
                there = pl.ds(pl.multiple_of(which * half + here.start, 32), 32)
                grad_normed = collect.total(which, here)
                values = middle_ref[there]
                factor = factor_ref[there][:, :1]
                weighted = gain_ref[...] * grad_normed
                inner = jnp.mean(weighted * values, axis=1, keepdims=True)
                grad = (
                    cot_own[there].astype(F32)
                    + factor * weighted
                    - values * (factor * factor * factor * inner)
                )
                grad_ref[there] = grad
                rounded[there] = grad.astype(BF16)
                gain_grad_ref[...] += jnp.sum(grad_normed * values * factor, axis=0, keepdims=True)

            loop_rows(half, body)
            spread.start(which)
            copy = pltpu.make_async_copy(
                rounded.at[pl.ds(which * half, half)], region(0, which), local.at[1 + which]
            )
            copy.start()
            copies.append(copy)
        spread.forward()
        spread.finish()
        collect.finish()
        for copy in copies:
            copy.wait()

    return call(
        middle_back_step, identity, (terms, cot, middle, factor, gain),
        (pl.ANY, pl.ANY, pltpu.VMEM, pltpu.VMEM, pltpu.VMEM),
        (
            jax.ShapeDtypeStruct((total, model), BF16),
            jax.ShapeDtypeStruct((quarter, model), F32),
            jax.ShapeDtypeStruct((1, model), F32),
        ),
        (pl.ANY, pltpu.VMEM, pltpu.VMEM),
        [
            pltpu.VMEM((quarter, model), BF16),
            pltpu.VMEM((quarter, model), BF16),
            pltpu.SemaphoreType.DMA((3,)),
        ]
        + SPREAD_SEMS
        + Collect.scratch(quarter, model),
        70_000_000_000,
    )


def input_terms(grad_packed, qkv, x_all, gain, grad_middle, own):
    total, columns = grad_packed.shape
    model = x_all.shape[1]
    tile = grad_middle.shape[0]

    def input_terms_step(own_ref, grad_ref, qkv_ref, x_ref, gain_ref, middle_ref, out_ref, gain_grad_ref):
        step = pl.program_id(0)
        grad_normed = right_trans(grad_ref[...], qkv_ref[...])
        values = x_ref[...].astype(F32)
        factor = lax.rsqrt(jnp.mean(values * values, axis=1, keepdims=True) + EPSILON)
        weighted = grad_normed * gain_ref[...]
        inner = jnp.mean(weighted * values, axis=1, keepdims=True)
        terms = factor * weighted - values * (factor * factor * factor * inner)

        @pl.when(step == own_ref[0])
        def _():
            out_ref[...] = (terms + middle_ref[...]).astype(BF16)

        @pl.when(step != own_ref[0])
        def _():
            out_ref[...] = terms.astype(BF16)

        @pl.when(step == 0)
        def _():
            gain_grad_ref[...] = jnp.zeros_like(gain_grad_ref)

        gain_grad_ref[...] += jnp.sum(grad_normed * values * factor, axis=0, keepdims=True)

    return pl.pallas_call(
        input_terms_step,
        grid_spec=pltpu.PrefetchScalarGridSpec(
            num_scalar_prefetch=1,
            grid=(total // tile,),
            in_specs=[
                pl.BlockSpec((tile, columns), lambda i, own: (i, 0)),
                pl.BlockSpec((model, columns), lambda i, own: (0, 0)),
                pl.BlockSpec((tile, model), lambda i, own: (i, 0)),
                pl.BlockSpec((1, model), lambda i, own: (0, 0)),
                pl.BlockSpec((tile, model), lambda i, own: (0, 0)),
            ],
            out_specs=[
                pl.BlockSpec((tile, model), lambda i, own: (i, 0)),
                pl.BlockSpec((1, model), lambda i, own: (0, 0)),
            ],
        ),
        out_shape=[
            jax.ShapeDtypeStruct((total, model), BF16),
            jax.ShapeDtypeStruct((1, model), F32),
        ],
        compiler_params=pltpu.CompilerParams(vmem_limit_bytes=VMEM),
        cost_estimate=pl.CostEstimate(
            flops=2 * total * columns * model,
            transcendentals=total,
            bytes_accessed=6 * total * model,
        ),
        name="input_terms",
    )(own, grad_packed, qkv, x_all, gain, grad_middle)


def program(
    tok_size,
    tokens, gain_attn, w_query, w_key, w_value, w_out, gain_ffn, w_gate, w_up, w_down, cotangent
):
    token = lax.axis_index("tok")
    feat = lax.axis_index("feat")
    member = token % 2
    rows, wide = tokens.shape
    model = 4 * wide
    quarter = rows // 4
    groups = [list(range(i, tok_size, 2)) for i in range(2)]
    pair_width = 2 * HD

    def swap(value):
        return lax.ppermute(value, "tok", [(i, i ^ 1) for i in range(tok_size)])

    def x_swap(value):
        return lax.ppermute(value, "feat", [(i, i ^ 2) for i in range(4)])

    def core_swap(value):
        return lax.ppermute(value, "feat", [(i, i ^ 1) for i in range(4)])

    def mine(values, axis):
        size = values.shape[axis] // 2
        return lax.dynamic_slice_in_dim(values, member * size, size, axis)

    def theirs(values, axis):
        size = values.shape[axis] // 2
        return lax.dynamic_slice_in_dim(values, (1 - member) * size, size, axis)

    def ordered(own, other, axis):
        first = jnp.where(member == 0, own, other)
        second = jnp.where(member == 0, other, own)
        return jnp.concatenate([first, second], axis=axis)

    def weight_start(shard, hidden_axis):
        return ordered(
            mine(shard, hidden_axis), swap(theirs(shard, hidden_axis)), 1 - hidden_axis
        )

    def ring_gather(shard, axis):
        return lax.all_gather(shard, "tok", axis=axis, tiled=True, axis_index_groups=groups)

    def ring_scatter(terms, axis):
        return lax.psum_scatter(
            terms, "tok", scatter_dimension=axis, tiled=True, axis_index_groups=groups
        )

    def weight_finish(total, hidden_axis):
        axis = 1 - hidden_axis
        other = swap(theirs(total, axis))
        return ordered(mine(total, axis), other, hidden_axis).astype(F32)

    def add_own_rows(values, own):
        start = (member * 4 + feat) * quarter
        here = lax.dynamic_slice_in_dim(values, start, quarter, 0)
        here = (here.astype(F32) + own).astype(BF16)
        return lax.dynamic_update_slice_in_dim(values, here, start, 0)

    packed_weights = []
    starts = [weight_start(w, 1) for w in (w_query, w_key, w_value)]
    heads_wide = starts[0].shape[1]
    for left in range(0, heads_wide, pair_width):
        packed_weights += [w[:, left : left + pair_width] for w in starts]
    qkv_start = jnp.concatenate(packed_weights, axis=1)
    out_start = weight_start(w_out, 0)
    tokens_after, qkv_start, out_start = lax.optimization_barrier((tokens, qkv_start, out_start))
    qkv = ring_gather(qkv_start, 0)
    out_proj = ring_gather(out_start, 1)
    x_all = gather_block(0, tokens_after)
    w_gate, w_up, w_down, cotangent, x_all = lax.optimization_barrier(
        (w_gate, w_up, w_down, cotangent, x_all)
    )
    gate_start = weight_start(w_gate, 1)
    up_start = weight_start(w_up, 1)
    down_start = weight_start(w_down, 0)
    hidden_wide = down_start.shape[0]
    chunk = hidden_wide // CHUNKS
    gate_up, down_proj = [], []
    for c in range(CHUNKS):
        part = slice(c * chunk, (c + 1) * chunk)
        gate_up.append(
            ring_gather(jnp.concatenate([gate_start[:, part], up_start[:, part]], axis=1), 0)
        )
        down_proj.append(ring_gather(down_start[part], 1))
    cot_rows = gather_block(1, cotangent)

    gains = jnp.stack([gain_attn, gain_ffn])
    gains = jnp.stack([gains, core_swap(gains)])
    gains = jnp.concatenate([gains, x_swap(gains)])
    gains = jnp.concatenate(
        [lax.dynamic_index_in_dim(gains, feat ^ j, 0, keepdims=False) for j in range(4)], axis=1
    )
    gain_one, gain_two = gains[:1], gains[1:]

    x_wide = x_all.astype(F32)
    factor_one = lax.rsqrt(jnp.mean(x_wide * x_wide, axis=1, keepdims=True) + EPSILON)
    normed = (x_wide * factor_one * gain_one).astype(BF16)
    packed = product(normed, qkv).astype(BF16)
    attended, log_sums = attend(packed)
    normed_two, middle, factor_two = middle_norm(
        2, product(attended, out_proj).astype(BF16), x_all, gain_two
    )

    out_rows = 0.0
    grad_normed_two = 0.0
    gate_grads, up_grads, down_grads = [], [], []
    for c in range(CHUNKS):
        both = product(normed_two, gate_up[c])
        gate, upward = both[:, :chunk], both[:, chunk:]
        sigma = jax.nn.sigmoid(gate)
        hidden = (gate * sigma * upward).astype(BF16)
        grad_hidden = right_trans(cot_rows, down_proj[c])
        grad_gate = (grad_hidden * upward * sigma * (1.0 + gate * (1.0 - sigma))).astype(BF16)
        grad_up = (grad_hidden * gate * sigma).astype(BF16)
        grad_both = jnp.concatenate([grad_gate, grad_up], axis=1)
        grad_normed_two = grad_normed_two + right_trans(grad_both, gate_up[c])
        down_grads.append(ring_scatter(left_trans(hidden, cot_rows).astype(BF16), 1))
        both_grad = ring_scatter(left_trans(normed_two, grad_both).astype(BF16), 0)
        gate_grads.append(both_grad[:, :chunk])
        up_grads.append(both_grad[:, chunk:])
        out_rows = out_rows + product(hidden, down_proj[c])
    gate_grad = weight_finish(jnp.concatenate(gate_grads, axis=1), 1)
    up_grad = weight_finish(jnp.concatenate(up_grads, axis=1), 1)
    down_grad = weight_finish(jnp.concatenate(down_grads, axis=0), 0)
    grad_mid_rows, grad_middle, gain_ffn_part = middle_back(
        3, grad_normed_two.astype(BF16), cot_rows, middle, factor_two, gain_two
    )
    outcome = scatter_block(4, add_own_rows(out_rows.astype(BF16), middle))

    grad_attended = right_trans(grad_mid_rows, out_proj).astype(BF16)
    out_grad = weight_finish(
        ring_scatter(left_trans(attended, grad_mid_rows).astype(BF16), 1), 0
    )
    grad_packed = attend_back(packed, attended, grad_attended, log_sums)
    qkv_grad = ring_scatter(left_trans(normed, grad_packed).astype(BF16), 0)
    part_grads = []
    for part in range(3):
        columns = [
            qkv_grad[:, left + part * pair_width : left + (part + 1) * pair_width]
            for left in range(0, 3 * heads_wide, 3 * pair_width)
        ]
        part_grads.append(weight_finish(jnp.concatenate(columns, axis=1), 1))
    own = (member * 4 + feat).astype(jnp.int32).reshape(1)
    terms, gain_attn_part = input_terms(grad_packed, qkv, x_all, gain_one, grad_middle, own)
    input_grad = scatter_block(5, terms)

    sums = jnp.concatenate([gain_attn_part, gain_ffn_part])
    for change in (core_swap, x_swap):
        sums = sums + change(sums)
    bit = 1
    while bit < tok_size:
        sums = sums + lax.ppermute(sums, "tok", [(i, i ^ bit) for i in range(tok_size)])
        bit *= 2
    gain_grads = lax.dynamic_slice_in_dim(sums, feat * wide, wide, 1)
    return (
        outcome,
        input_grad,
        gain_grads[0],
        gain_grads[1],
        *part_grads,
        out_grad,
        gate_grad,
        up_grad,
        down_grad,
    )


def solution(mesh):
    in_specs = (
        P("tok", "feat"),
        P("feat"),
        P("tok", "feat"),
        P("tok", "feat"),
        P("tok", "feat"),
        P("feat", "tok"),
        P("feat"),
        P("tok", "feat"),
        P("tok", "feat"),
        P("feat", "tok"),
        P("tok", "feat"),
    )
    out_specs = (
        P("tok", "feat"),
        P("tok", "feat"),
        P("feat"),
        P("feat"),
        P("tok", "feat"),
        P("tok", "feat"),
        P("tok", "feat"),
        P("feat", "tok"),
        P("tok", "feat"),
        P("tok", "feat"),
        P("feat", "tok"),
    )

    def on_device(*arrays):
        return program(mesh.shape["tok"], *arrays)

    return jax.shard_map(
        on_device, mesh=mesh, in_specs=in_specs, out_specs=out_specs, check_vma=False
    )
```

time: 1850 us -> 820 us (0.44)
  waiting for transfers between devices: 1450 us -> 143 us
  Pallas kernels: 0 us -> 377 us
  matrix products: 253 us -> 200 us
  blocking collectives: 47.9 us -> 0 us
  other arithmetic: 58 us -> 32.8 us
  starting transfers between devices: 1.06 us -> 19.7 us
    reduce_scatter x11 -> x6, waiting for transfers between devices: 861 us -> 28.4 us  [ring_scatter(): lax.psum_scatter(terms, 'tok', scatter_dimension=axis, tiled=True, axis_i...]
    all_gather x11 -> x6, waiting for transfers between devices: 588 us -> 46.2 us  [ring_gather(): lax.all_gather(shard, 'tok', axis=axis, tiled=True, axis_index_groups=gro...]
    pallas_call x0 -> x9, Pallas kernels: none -> 377 us  [the longest x6 330 us: call(): pl.pallas_call(kernel, out_shape=outputs, in_specs=[pl.BlockSpec(memory_s...]
    ppermute x0 -> x21, waiting for transfers between devices: none -> 67.4 us  [the longest x14 59.5 us: swap(): return lax.ppermute(value, 'tok', [(i, i ^ 1) for i in range(tok_size)])]
    dot_general x19 -> x6, matrix products: 125 us -> 70.7 us  [product(): return jnp.dot(left, right, preferred_element_type=F32)]
    psum x5 -> x0, blocking collectives: 47.9 us -> none  [the longest x4 25.9 us: feature_sum(): return lax.psum(values, 'feat')]
    convert_element_type x13 -> x7, other arithmetic: 39.6 us -> 7.99 us  [weight_finish(): return ordered(mine(total, axis), other, hidden_axis).astype(F32)]
    dot_general x7 -> x5, matrix products: 66 us -> 66.7 us  [right_trans(): lax.dot_general(left, right, (((1,), (1,)), ((), ())), preferred_element_...]
  transfers between devices with their start and end apart: 22 -> 33, of which waited for: 21 -> 15; matrix products, arithmetic and copies ran while one was open for 13% -> 30% of each run, Pallas kernels for 0% -> 46%
where the time goes in v2:
time: 820 us; the launch traced here: 815 us
  Pallas kernels  377 us (46%)
  matrix products  200 us (24%)
  waiting for transfers between devices  143 us (17%)
  other arithmetic  32.8 us (4%)
  local copies, waits for them, and re-layouts  27.6 us (3%)
  starting transfers between devices  19.7 us (2%)
  between operations  15.2 us (2%)
    pallas_call x6, Pallas kernels, call(): pl.pallas_call(kernel, out_shape=outputs, in_specs=[pl.BlockSpec(memory_s...  330 us
    dot_general x6, matrix products, product(): return jnp.dot(left, right, preferred_element_type=F32)  70.7 us
    dot_general x5, matrix products, right_trans(): lax.dot_general(left, right, (((1,), (1,)), ((), ())), preferred_element_...  66.7 us
    dot_general x6, matrix products, left_trans(): lax.dot_general(left, right, (((0,), (0,)), ((), ())), preferred_element_...  62.2 us
    ppermute x14, waiting for transfers between devices, swap(): return lax.ppermute(value, 'tok', [(i, i ^ 1) for i in range(tok_size)])  59.5 us
    all_gather x6, waiting for transfers between devices, ring_gather(): lax.all_gather(shard, 'tok', axis=axis, tiled=True, axis_index_groups=gro...  46.2 us
    reduce_scatter x6, waiting for transfers between devices, ring_scatter(): lax.psum_scatter(terms, 'tok', scatter_dimension=axis, tiled=True, axis_i...  28.4 us
    pallas_call x1, Pallas kernels, input_terms(): pl.pallas_call(input_terms_step, grid_spec=pltpu.PrefetchScalarGridSpec(n...  18 us
  transfers between devices with their start and end apart: 33, of which 15 were waited for; matrix products, arithmetic and copies ran while one was open for 30% of the time, Pallas kernels for 46%

profile of v2, /device:TPU:0, one launch (start us, length us, event | category | flops | bytes accessed | tf_op | source)
XLA Modules:
  0.0 815.1 jit_solution(17164673837616662395)
XLA Ops:
  24.9 41.2 %gather_input.2.x_ref = bf16[2048,2048]{1,0:T(8,128)(2,1)} custom-call(bf16[1024,512]{1,0:T(8,128)(2,1)S(1)} %copy-done.4), custom_call_target="tpu_custom_call" | custom-call | flops 40000000000 | bytes 400000000 | tf_op jit(solution)/shard_map/gather_input/pallas_call | solution.py:345
  69.1 12.0 %collective-permute-done.6 = bf16[256,1024]{1,0:T(8,128)(2,1)} collective-permute-done((bf16[256,1024]{1,0:T(8,128)(2,1)S(1)}, bf16[256,1024]{1,0:T(8,128)(2,1)}, u32[]{:S(2)}, u32[]{:S(2)}) %collective-permute-start.6) | collective-permute-done | bytes 524320 | tf_op jit(solution)/shard_map/ppermute | solution.py:659
  82.5 9.3 %collective-permute-done.7 = bf16[256,1024]{1,0:T(8,128)(2,1)} collective-permute-done((bf16[256,1024]{1,0:T(8,128)(2,1)}, bf16[256,1024]{1,0:T(8,128)(2,1)}, u32[]{:S(2)}, u32[]{:S(2)}) %collective-permute-start.7) | collective-permute-done | bytes 524320 | tf_op jit(solution)/shard_map/ppermute | solution.py:659
  95.8 13.1 %collective-permute-done.8 = bf16[1024,256]{1,0:T(8,128)(2,1)S(1)} collective-permute-done((bf16[1024,256]{1,0:T(8,128)(2,1)S(1)}, bf16[1024,256]{1,0:T(8,128)(2,1)S(1)}, u32[]{:S(2)}, u32[]{:S(2)}) %collective-permute-start.8) | collective-permute-done | bytes 524320 | tf_op jit(solution)/shard_map/ppermute | solution.py:659
  122.6 38.7 %gather_input.3.cot_ref = bf16[2048,2048]{1,0:T(8,128)(2,1)} custom-call(bf16[1024,512]{1,0:T(8,128)(2,1)S(1)} %copy-done.5), custom_call_target="tpu_custom_call" | custom-call | flops 40000000000 | bytes 400000000 | tf_op jit(solution)/shard_map/gather_input/pallas_call | solution.py:345
  161.8 10.2 %convolution_convert_fusion.3.packed_ref = bf16[2048,768]{1,0:T(8,128)(2,1)S(1)} fusion(bf16[2048,768]{1,0:T(8,128)(2,1)} %all-gather.7.cloned.1.call-done.qkv_ref, bf16[2048,2048]{1,0:T(8,128)(2,1)} %gather_input.2.x_ref, f32[2048]{0:T(1024)S(1)} %bitcast.45, f32[2048]{0:T(1024)S(1)} %add_rsqrt_fusion), kind=kOutput, calls=%fused_computation.20 | convolution fusion | flops 6460801024 | bytes 14696448 | tf_op jit(solution)/shard_map/dot_general | solution.py:33
  172.0 11.3 %attend.1 = (bf16[2048,256]{1,0:T(8,128)(2,1)S(1)}, f32[2,2,2,1024]{3,2,1,0:T(2,128)S(1)}) custom-call(bf16[2048,768]{1,0:T(8,128)(2,1)S(1)} %convolution_convert_fusion.3.packed_ref), custom_call_target="tpu_custom_call" | custom-call | flops 1073741824 | bytes 6291456 | tf_op jit(solution)/shard_map/attend/pallas_call | solution.py:106
  184.9 7.3 convolution_convert_fusion.terms_ref
  192.2 81.4 %middle_step.1 = (bf16[2048,2048]{1,0:T(8,128)(2,1)}, f32[256,2048]{1,0:T(8,128)S(1)}, f32[256,128]{1,0:T(8,128)S(1)}) custom-call(bf16[2048,2048]{1,0:T(8,128)(2,1)} %convolution_convert_fusion.terms_ref, bf16[2048,2048]{1,0:T(8,128)(2,1)} %gather_input.2.x_ref, f32[1,2048]{1,0:T(1,128)S(1)} %get-tuple-element.93.gain_ref), custom_call_target="tpu_custom_call" | custom-call | flops 70000001024 | bytes 700000000 | tf_op jit(solution)/shard_map/middle_step/pallas_call | solution.py:345
  273.7 15.2 %fusion.49 = f32[2048,1024]{0,1:T(8,128)} fusion(bf16[2048,2048]{1,0:T(8,128)(2,1)} %get-tuple-element.34, bf16[2048,1024]{1,0:T(8,128)(2,1)} %all-gather.11.cloned.1.call-done), kind=kOutput, calls=%fused_computation.169 | convolution fusion | flops 8589934592 | bytes 20971520 | tf_op jit(solution)/shard_map/dot_general | solution.py:33
  288.9 14.4 %multiply_convert_fusion.3 = (bf16[2048,512]{0,1:T(8,128)(2,1)}, bf16[2048,512]{0,1:T(8,128)(2,1)}, bf16[2048,512]{0,1:T(8,128)(2,1)S(1)}) fusion(f32[2048,1024]{0,1:T(8,128)} %fusion.49, bf16[2048,2048]{1,0:T(8,128)(2,1)} %gather_input.3.cot_ref, bf16[512,2048]{1,0:T(8,128)(2,1)} %all-gather.13.cloned.1.call-done), kind=kOutput, calls=%fused_computation.13 | convolution fusion | flops 4311744512 | bytes 25165824 | tf_op jit(solution)/shard_map/dot_general | solution.py:27
  304.6 9.2 %convolution_convert_fusion.6 = bf16[512,2048]{1,0:T(8,128)(2,1)} fusion(bf16[2048,512]{0,1:T(8,128)(2,1)S(1)} %get-tuple-element.52, bf16[2048,2048]{1,0:T(8,128)(2,1)} %gather_input.3.cot_ref), kind=kOutput, calls=%fused_computation.23 | convolution fusion | flops 4296015872 | bytes 12582912 | tf_op jit(solution)/shard_map/dot_general | solution.py:21
  313.9 14.5 %all-gather.15.cloned.1.call-done = bf16[2048,1024]{1,0:T(8,128)(2,1)} async-done(((bf16[512,1024]{1,0:T(8,128)(2,1)}), bf16[2048,1024]{1,0:T(8,128)(2,1)}) %all-gather.15.cloned.1.call-update) | async-done | bytes 4194320 | tf_op jit(solution)/shard_map/all_gather | solution.py:686
  328.4 14.8 %fusion.51 = f32[2048,1024]{0,1:T(8,128)} fusion(bf16[2048,2048]{1,0:T(8,128)(2,1)} %get-tuple-element.34, bf16[2048,1024]{1,0:T(8,128)(2,1)} %all-gather.15.cloned.1.call-done), kind=kOutput, calls=%fused_computation.171 | convolution fusion | flops 8589934592 | bytes 20971520 | tf_op jit(solution)/shard_map/dot_general | solution.py:33
  343.2 31.7 %all-gather.17.cloned.1.call-done = bf16[512,2048]{1,0:T(8,128)(2,1)} async-done(((bf16[512,512]{1,0:T(8,128)(2,1)}), bf16[512,2048]{1,0:T(8,128)(2,1)}) %all-gather.17.cloned.1.call-update) | async-done | bytes 2097168 | tf_op jit(solution)/shard_map/all_gather | solution.py:686
  374.9 14.3 %multiply_convert_fusion.1 = (bf16[2048,512]{0,1:T(8,128)(2,1)}, bf16[2048,512]{0,1:T(8,128)(2,1)}, bf16[2048,512]{0,1:T(8,128)(2,1)S(1)}) fusion(f32[2048,1024]{0,1:T(8,128)} %fusion.51, bf16[2048,2048]{1,0:T(8,128)(2,1)} %gather_input.3.cot_ref, bf16[512,2048]{1,0:T(8,128)(2,1)} %all-gather.17.cloned.1.call-done), kind=kOutput, calls=%fused_computation.11 | convolution fusion | flops 4311744512 | bytes 25165824 | tf_op jit(solution)/shard_map/dot_general | solution.py:27
  390.6 9.2 %convolution_convert_fusion.5 = bf16[512,2048]{1,0:T(8,128)(2,1)} fusion(bf16[2048,512]{0,1:T(8,128)(2,1)S(1)} %get-tuple-element.51, bf16[2048,2048]{1,0:T(8,128)(2,1)} %gather_input.3.cot_ref), kind=kOutput, calls=%fused_computation.22 | convolution fusion | flops 4296015872 | bytes 12582912 | tf_op jit(solution)/shard_map/dot_general | solution.py:21
  399.8 15.5 %fusion.3 = f32[2048,2048]{1,0:T(8,128)} fusion(bf16[2048,1024]{1,0:T(8,128)(2,1)} %all-gather.11.cloned.1.call-done, bf16[2048,512]{0,1:T(8,128)(2,1)} %get-tuple-element.50, bf16[2048,512]{0,1:T(8,128)(2,1)} %get-tuple-element.49), kind=kOutput, calls=%fused_computation.24 | convolution fusion | flops 8598323200 | bytes 25165824 | tf_op jit(solution)/shard_map/dot_general | solution.py:27
  415.3 16.4 %add_convert_fusion.terms_ref = bf16[2048,2048]{1,0:T(8,128)(2,1)} fusion(f32[2048,2048]{1,0:T(8,128)} %fusion.3, bf16[2048,1024]{1,0:T(8,128)(2,1)} %all-gather.15.cloned.1.call-done, bf16[2048,512]{0,1:T(8,128)(2,1)} %get-tuple-element.48, bf16[2048,512]{0,1:T(8,128)(2,1)} %get-tuple-element.47), kind=kOutput, calls=%fused_computation.5 | convolution fusion | flops 8606711808 | bytes 33554432 | tf_op jit(solution)/shard_map/dot_general | solution.py:27
  431.7 81.0 %middle_back_step.1 = (bf16[2048,2048]{1,0:T(8,128)(2,1)}, f32[256,2048]{1,0:T(8,128)S(1)}, f32[1,2048]{1,0:T(1,128)S(1)}) custom-call(bf16[2048,2048]{1,0:T(8,128)(2,1)} %add_convert_fusion.terms_ref, bf16[2048,2048]{1,0:T(8,128)(2,1)} %gather_input.3.cot_ref, f32[256,2048]{1,0:T(8,128)S(1)} %get-tuple-element.38.middle_ref, ...), custom_call_target="tpu_custom_call" | custom-call | flops 70000001024 | bytes 700000000 | tf_op jit(solution)/shard_map/middle_back_step/pallas_call | solution.py:345
  527.3 17.7 %attend_back.1.grad_ref = bf16[2048,768]{1,0:T(8,128)(2,1)S(1)} custom-call(bf16[2048,768]{1,0:T(8,128)(2,1)} %copy-done.6, bf16[2048,256]{1,0:T(8,128)(2,1)S(1)} %copy-done.1, bf16[2048,256]{1,0:T(8,128)(2,1)S(1)} %convolution_convert_fusion.8.grad_ref, f32[2,2,2,1024]{3,2,1,0:T(2,128)S(1)} %get-tuple-element.42.lse_ref), custom_call_target="tpu_custom_call" | custom-call | flops 2684354560 | bytes 9437184 | tf_op jit(solution)/shard_map/attend_back/pallas_call | solution.py:133
  545.0 11.1 %convolution_convert_fusion.4 = bf16[2048,768]{1,0:T(8,128)(2,1)} fusion(bf16[2048,768]{1,0:T(8,128)(2,1)S(1)} %attend_back.1.grad_ref, bf16[2048,2048]{1,0:T(8,128)(2,1)} %gather_input.2.x_ref, f32[2048]{0:T(1024)S(1)} %bitcast.46, f32[2048]{0:T(1024)S(1)} %copy-done.21), kind=kOutput, calls=%fused_computation.21 | convolution fusion | flops 6460801024 | bytes 14696448 | tf_op jit(solution)/shard_map/dot_general | solution.py:21
  558.0 13.9 %convolution_convert_fusion.1 = bf16[2048,1024]{1,0:T(8,128)(2,1)} fusion(bf16[2048,2048]{1,0:T(8,128)(2,1)} %get-tuple-element.34, bf16[2048,512]{0,1:T(8,128)(2,1)} %get-tuple-element.48, bf16[2048,512]{0,1:T(8,128)(2,1)} %get-tuple-element.47), kind=kOutput, calls=%fused_computation.18 | convolution fusion | flops 8600420352 | bytes 16777216 | tf_op jit(solution)/shard_map/dot_general | solution.py:21
  575.6 18.0 %input_terms.1 = (bf16[2048,2048]{1,0:T(8,128)(2,1)}, f32[1,2048]{1,0:T(1,128)S(1)}) custom-call(s32[1]{0:T(128)} %bitcast.9.own_ref, bf16[2048,768]{1,0:T(8,128)(2,1)S(1)} %copy-done.8, bf16[2048,768]{1,0:T(8,128)(2,1)} %all-gather.7.cloned.1.call-done.qkv_ref, bf16[2048,2048]{1,0:T(8,128)(2,1)} %gather_input.2.x_ref, f32[1,2048]{1,0:T(1,128)S(1)} %copy-done.3, ...), custom_call_target="tpu_custom_call" | custom-call | flops 6442450944 | bytes 25165824 | tf_op jit(solution)/shard_map/input_terms/pallas_call | solution.py:614
  594.0 40.7 %scatter_output.3 = bf16[1024,512]{1,0:T(8,128)(2,1)S(1)} custom-call(bf16[2048,2048]{1,0:T(8,128)(2,1)} %get-tuple-element.44.terms_ref), custom_call_target="tpu_custom_call" | custom-call | flops 30000001024 | bytes 300000000 | tf_op jit(solution)/shard_map/scatter_output/pallas_call | solution.py:345
  634.7 12.2 %convolution_convert_fusion.2 = bf16[2048,1024]{1,0:T(8,128)(2,1)} fusion(bf16[2048,2048]{1,0:T(8,128)(2,1)S(1)} %bitcast.54, bf16[2048,512]{0,1:T(8,128)(2,1)} %get-tuple-element.50, bf16[2048,512]{0,1:T(8,128)(2,1)S(1)} %copy-done.28), kind=kOutput, calls=%fused_computation.19 | convolution fusion | flops 8600420352 | bytes 16777216 | tf_op jit(solution)/shard_map/dot_general | solution.py:21
  648.1 12.7 %fusion.50 = f32[2048,2048]{1,0:T(8,128)} fusion(bf16[2048,512]{0,1:T(8,128)(2,1)} %copy-done.25, bf16[512,2048]{1,0:T(8,128)(2,1)} %all-gather.13.cloned.1.call-done), kind=kOutput, calls=%fused_computation.170 | convolution fusion | flops 4294967296 | bytes 20971520 | tf_op jit(solution)/shard_map/dot_general | solution.py:33
  662.0 10.4 %add_convert_fusion.1 = bf16[2048,2048]{1,0:T(8,128)(2,1)} fusion(f32[2048,2048]{1,0:T(8,128)} %fusion.50, bf16[2048,512]{0,1:T(8,128)(2,1)S(1)} %copy-done.27, bf16[512,2048]{1,0:T(8,128)(2,1)S(1)} %copy-done.24), kind=kOutput, calls=%fused_computation.6 | convolution fusion | flops 4303355904 | bytes 29360128 | tf_op jit(solution)/shard_map/dot_general | solution.py:33
  682.6 47.4 %scatter_output.2 = bf16[1024,512]{1,0:T(8,128)(2,1)S(1)} custom-call(bf16[2048,2048]{1,0:T(8,128)(2,1)} %fusion.8.terms_ref), custom_call_target="tpu_custom_call" | custom-call | flops 30000001024 | bytes 300000000 | tf_op jit(solution)/shard_map/scatter_output/pallas_call | solution.py:345
  747.8 28.3 %reduce-scatter.11.cloned.1.call-done = bf16[512,1024]{1,0:T(8,128)(2,1)} async-done(((bf16[2048,1024]{1,0:T(8,128)(2,1)}), bf16[512,1024]{1,0:T(8,128)(2,1)}) %reduce-scatter.11.cloned.1.call-update) | async-done | bytes 1048592 | tf_op jit(solution)/shard_map/reduce_scatter | solution.py:689
  783.3 9.0 %collective-permute-done.18 = bf16[256,1024]{1,0:T(8,128)(2,1)S(1)} collective-permute-done((bf16[256,1024]{1,0:T(8,128)(2,1)S(1)}, bf16[256,1024]{1,0:T(8,128)(2,1)S(1)}, u32[]{:S(2)}, u32[]{:S(2)}) %collective-permute-start.18) | collective-permute-done | bytes 524320 | tf_op jit(solution)/shard_map/ppermute | solution.py:659
  792.3 10.1 %collective-permute-done.19 = bf16[256,1024]{1,0:T(8,128)(2,1)S(1)} collective-permute-done((bf16[256,1024]{1,0:T(8,128)(2,1)S(1)}, bf16[256,1024]{1,0:T(8,128)(2,1)S(1)}, u32[]{:S(2)}, u32[]{:S(2)}) %collective-permute-start.19) | collective-permute-done | bytes 524320 | tf_op jit(solution)/shard_map/ppermute | solution.py:659
  (202 shorter events, 107.7 us)
Async XLA Ops:
  7.2 154.5 %all-gather.7.cloned.1.call-start = ((), (), s32[]{:S(2)}) async-start(), calls=%async_computation.6 | async-start | bytes 3932160 | tf_op jit(solution)/shard_map/all_gather | solution.py:686
  8.3 8.0 collective-permute-start
  12.2 6.5 collective-permute-start.1
  13.2 8.3 %collective-permute-start.2 = (bf16[256,256]{1,0:T(8,128)(2,1)S(1)}, bf16[256,256]{1,0:T(8,128)(2,1)S(1)}, u32[]{:S(2)}, u32[]{:S(2)}) collective-permute-start(bf16[256,256]{1,0:T(8,128)(2,1)S(1)} %constant_dynamic-slice_fusion.12), channel_id=1, source_target_pairs={{0,4},{4,0},{8,12},{12,8},{16,20},{20,16},{24,28},{28,24},{1,5},{5... | collective-permute-start | bytes 393224 | tf_op jit(solution)/shard_map/ppermute | solution.py:659
  16.2 7.0 collective-permute-start.3
  24.1 160.8 %all-gather.9.cloned.1.call-start = ((), (), s32[]{:S(2)}) async-start(), calls=%async_computation.7 | async-start | bytes 1310720 | tf_op jit(solution)/shard_map/all_gather | solution.py:686
  24.8 248.8 %all-gather.11.cloned.1.call-start = ((), (), s32[]{:S(2)}) async-start(), calls=%async_computation.8 | async-start | bytes 5242880 | tf_op jit(solution)/shard_map/all_gather | solution.py:686
  66.2 14.9 %collective-permute-start.6 = (bf16[256,1024]{1,0:T(8,128)(2,1)S(1)}, bf16[256,1024]{1,0:T(8,128)(2,1)}, u32[]{:S(2)}, u32[]{:S(2)}) collective-permute-start(bf16[256,1024]{1,0:T(8,128)(2,1)S(1)} %constant_dynamic-slice_fusion.6), channel_id=1, source_target_pairs={{0,4},{4,0},{8,12},{12,8},{16,20},{20,16},{24,28},{28,24},{1,5},{5... | collective-permute-start | bytes 1572872 | tf_op jit(solution)/shard_map/ppermute | solution.py:659
  67.2 24.5 %collective-permute-start.7 = (bf16[256,1024]{1,0:T(8,128)(2,1)}, bf16[256,1024]{1,0:T(8,128)(2,1)}, u32[]{:S(2)}, u32[]{:S(2)}) collective-permute-start(bf16[256,1024]{1,0:T(8,128)(2,1)} %constant_dynamic-slice_fusion.5), channel_id=1, source_target_pairs={{0,4},{4,0},{8,12},{12,8},{16,20},{20,16},{24,28},{28,24},{1,5},{5... | collective-permute-start | bytes 1572872 | tf_op jit(solution)/shard_map/ppermute | solution.py:659
  94.3 194.6 %all-gather.13.cloned.1.call-start = ((), (), s32[]{:S(2)}) async-start(), calls=%async_computation.9 | async-start | bytes 2621440 | tf_op jit(solution)/shard_map/all_gather | solution.py:686
  95.4 13.5 %collective-permute-start.8 = (bf16[1024,256]{1,0:T(8,128)(2,1)S(1)}, bf16[1024,256]{1,0:T(8,128)(2,1)S(1)}, u32[]{:S(2)}, u32[]{:S(2)}) collective-permute-start(bf16[1024,256]{1,0:T(8,128)(2,1)S(1)} %constant_dynamic-slice_fusion.4), channel_id=1, source_target_pairs={{0,4},{4,0},{8,12},{12,8},{16,20},{20,16},{24,28},{28,24},{1,5},{5... | collective-permute-start | bytes 1572872 | tf_op jit(solution)/shard_map/ppermute | solution.py:659
  111.2 217.2 %all-gather.15.cloned.1.call-start = ((), (), s32[]{:S(2)}) async-start(), calls=%async_computation.10 | async-start | bytes 5242880 | tf_op jit(solution)/shard_map/all_gather | solution.py:686
  112.3 262.6 %all-gather.17.cloned.1.call-start = ((), (), s32[]{:S(2)}) async-start(), calls=%async_computation.11 | async-start | bytes 2621440 | tf_op jit(solution)/shard_map/all_gather | solution.py:686
  113.6 3.7 collective-permute-start.5
  161.4 516.8 %reduce-scatter.15.cloned.1.call-start = ((), (), s32[]{:S(2)}) async-start(), calls=%async_computation.16 | async-start | bytes 2621440 | tf_op jit(solution)/shard_map/reduce_scatter | solution.py:689
  313.8 365.5 %reduce-scatter.17.cloned.1.call-start = ((), (), s32[]{:S(2)}) async-start(), calls=%async_computation.17 | async-start | bytes 2621440 | tf_op jit(solution)/shard_map/reduce_scatter | solution.py:689
  399.7 330.9 %reduce-scatter.9.cloned.1.call-start = ((), (), s32[]{:S(2)}) async-start(), calls=%async_computation.13 | async-start | bytes 1310720 | tf_op jit(solution)/shard_map/reduce_scatter | solution.py:689
  520.7 215.5 %reduce-scatter.7.cloned.1.call-start = ((), (), s32[]{:S(2)}) async-start(), calls=%async_computation.12 | async-start | bytes 3932160 | tf_op jit(solution)/shard_map/reduce_scatter | solution.py:689
  557.8 188.7 %reduce-scatter.13.cloned.1.call-start = ((), (), s32[]{:S(2)}) async-start(), calls=%async_computation.15 | async-start | bytes 5242880 | tf_op jit(solution)/shard_map/reduce_scatter | solution.py:689
  572.0 204.1 %reduce-scatter.11.cloned.1.call-start = ((), (), s32[]{:S(2)}) async-start(), calls=%async_computation.14 | async-start | bytes 5242880 | tf_op jit(solution)/shard_map/reduce_scatter | solution.py:689
  593.6 53.3 %collective-permute-start.9 = (f32[2,2048]{1,0:T(2,128)S(1)}, f32[2,2048]{1,0:T(2,128)S(1)}, u32[]{:S(2)}, u32[]{:S(2)}) collective-permute-start(f32[2,2048]{1,0:T(2,128)S(1)} %pad_maximum_fusion.15), channel_id=1, source_target_pairs={{0,1},{1,0},{2,3},{3,2},{4,5},{5,4},{6,7},{7,6},{8,9},{9,8},{10,11... | collective-permute-start | bytes 49160 | tf_op jit(solution)/shard_map/ppermute | solution.py:665
  647.0 13.9 %collective-permute-start.10 = (f32[2,2048]{1,0:T(2,128)S(1)}, f32[2,2048]{1,0:T(2,128)S(1)}, u32[]{:S(2)}, u32[]{:S(2)}) collective-permute-start(f32[2,2048]{1,0:T(2,128)S(1)} %fusion.43), channel_id=1, source_target_pairs={{0,2},{1,3},{2,0},{3,1},{4,6},{5,7},{6,4},{7,5},{8,10},{9,11},{10,... | collective-permute-start | bytes 49160 | tf_op jit(solution)/shard_map/ppermute | solution.py:662
  660.9 11.5 %collective-permute-start.11 = (f32[2,2048]{1,0:T(2,128)S(1)}, f32[2,2048]{1,0:T(2,128)S(1)}, u32[]{:S(2)}, u32[]{:S(2)}) collective-permute-start(f32[2,2048]{1,0:T(2,128)S(1)} %fusion.80), channel_id=1, source_target_pairs={{0,4},{4,0},{8,12},{12,8},{16,20},{20,16},{24,28},{28,24},{1,5},{5... | collective-permute-start | bytes 49160 | tf_op jit(solution)/shard_map/ppermute | solution.py:797
  672.4 5.7 collective-permute-start.12
  678.1 51.9 %collective-permute-start.13 = (f32[2,2048]{1,0:T(2,128)S(1)}, f32[2,2048]{1,0:T(2,128)S(1)}, u32[]{:S(2)}, u32[]{:S(2)}) collective-permute-start(f32[2,2048]{1,0:T(2,128)S(1)} %add.146), channel_id=1, source_target_pairs={{0,16},{4,20},{8,24},{12,28},{16,0},{20,4},{24,8},{28,12},{1,17},{... | collective-permute-start | bytes 49160 | tf_op jit(solution)/shard_map/ppermute | solution.py:797
  681.3 52.2 %collective-permute-start.20 = (bf16[1024,256]{1,0:T(8,128)(2,1)}, bf16[1024,256]{1,0:T(8,128)(2,1)}, u32[]{:S(2)}, u32[]{:S(2)}) collective-permute-start(bf16[1024,256]{1,0:T(8,128)(2,1)} %constant_dynamic-slice_fusion.1), channel_id=1, source_target_pairs={{0,4},{4,0},{8,12},{12,8},{16,20},{20,16},{24,28},{28,24},{1,5},{5... | collective-permute-start | bytes 1572872 | tf_op jit(solution)/shard_map/ppermute | solution.py:659
  732.2 9.6 %collective-permute-start.17 = (bf16[256,256]{1,0:T(8,128)(2,1)}, bf16[256,256]{1,0:T(8,128)(2,1)}, u32[]{:S(2)}, u32[]{:S(2)}) collective-permute-start(bf16[256,256]{1,0:T(8,128)(2,1)} %constant_dynamic-slice_fusion.2), channel_id=1, source_target_pairs={{0,4},{4,0},{8,12},{12,8},{16,20},{20,16},{24,28},{28,24},{1,5},{5... | collective-permute-start | bytes 393224 | tf_op jit(solution)/shard_map/ppermute | solution.py:659
  737.6 6.4 collective-permute-start.16
  739.1 41.5 %collective-permute-start.14 = (bf16[256,256]{1,0:T(8,128)(2,1)}, bf16[256,256]{1,0:T(8,128)(2,1)}, u32[]{:S(2)}, u32[]{:S(2)}) collective-permute-start(bf16[256,256]{1,0:T(8,128)(2,1)} %fusion.28), channel_id=1, source_target_pairs={{0,4},{4,0},{8,12},{12,8},{16,20},{20,16},{24,28},{28,24},{1,5},{5... | collective-permute-start | bytes 393224 | tf_op jit(solution)/shard_map/ppermute | solution.py:659
  741.0 39.5 %collective-permute-start.15 = (bf16[256,256]{1,0:T(8,128)(2,1)}, bf16[256,256]{1,0:T(8,128)(2,1)}, u32[]{:S(2)}, u32[]{:S(2)}) collective-permute-start(bf16[256,256]{1,0:T(8,128)(2,1)} %fusion.26), channel_id=1, source_target_pairs={{0,4},{4,0},{8,12},{12,8},{16,20},{20,16},{24,28},{28,24},{1,5},{5... | collective-permute-start | bytes 393224 | tf_op jit(solution)/shard_map/ppermute | solution.py:659
  777.5 14.9 %collective-permute-start.18 = (bf16[256,1024]{1,0:T(8,128)(2,1)S(1)}, bf16[256,1024]{1,0:T(8,128)(2,1)S(1)}, u32[]{:S(2)}, u32[]{:S(2)}) collective-permute-start(bf16[256,1024]{1,0:T(8,128)(2,1)S(1)} %fusion.15), channel_id=1, source_target_pairs={{0,4},{4,0},{8,12},{12,8},{16,20},{20,16},{24,28},{28,24},{1,5},{5... | collective-permute-start | bytes 1572872 | tf_op jit(solution)/shard_map/ppermute | solution.py:659
  779.1 23.4 %collective-permute-start.19 = (bf16[256,1024]{1,0:T(8,128)(2,1)S(1)}, bf16[256,1024]{1,0:T(8,128)(2,1)S(1)}, u32[]{:S(2)}, u32[]{:S(2)}) collective-permute-start(bf16[256,1024]{1,0:T(8,128)(2,1)S(1)} %fusion.13), channel_id=1, source_target_pairs={{0,4},{4,0},{8,12},{12,8},{16,20},{20,16},{24,28},{28,24},{1,5},{5... | collective-permute-start | bytes 1572872 | tf_op jit(solution)/shard_map/ppermute | solution.py:659
  (32 other events, 578.3 us)
Sparse Core Ops, SparseCore 0:
  24.2 64.9 all-gather.6
  91.3 26.5 all-gather.8
  120.1 80.2 all-gather.10
  202.4 44.4 all-gather.12
  248.9 79.4 all-gather.14
  330.4 44.4 all-gather.16
  377.2 42.4 reduce-scatter.14
  422.1 43.1 reduce-scatter.16
  520.9 25.5 reduce-scatter.8
  557.9 58.7 reduce-scatter.6
  619.1 77.4 reduce-scatter.12
  698.8 77.2 reduce-scatter.10

commit v3 on v2

--- a/solution.py
+++ b/solution.py
@@ -356,42 +356,53 @@
     )(*operands)
 
 
-def gather_block(identity, shard):
-    rows, wide = shard.shape
+def gather_blocks(identity, *shards):
+    rows, wide = shards[0].shape
     half = rows // 2
-
-    def gather_input(shard_ref, out_ref, local, send, recv):
+    count = len(shards)
+
+    def gather_inputs(*refs):
         greet()
-
-        def region(r, which):
-            member, slot = owner(r)
-            return out_ref.at[
-                pl.ds(pl.multiple_of(member * rows + which * half, half), half),
-                pl.ds(pl.multiple_of(slot * wide, wide), wide),
-            ]
-
-        spread = Spread(
-            lambda which: shard_ref.at[pl.ds(which * half, half)], region, send, recv
-        )
-        spread.start(0)
-        spread.start(1)
-        copies = [
-            pltpu.make_async_copy(
-                shard_ref.at[pl.ds(which * half, half)], region(0, which), local.at[which]
-            )
-            for which in range(2)
-        ]
+        local = refs[2 * count]
+        spreads, copies = [], []
+        for i in range(count):
+            shard_ref, out_ref = refs[i], refs[count + i]
+
+            def own(which, shard_ref=shard_ref):
+                return shard_ref.at[pl.ds(which * half, half)]
+
+            def region(r, which, out_ref=out_ref):
+                member, slot = owner(r)
+                return out_ref.at[
+                    pl.ds(pl.multiple_of(member * rows + which * half, half), half),
+                    pl.ds(pl.multiple_of(slot * wide, wide), wide),
+                ]
+
+            sems = refs[2 * count + 1 + 2 * i : 2 * count + 3 + 2 * i]
+            spreads.append(Spread(own, region, *sems))
+            for which in range(2):
+                copies.append(
+                    pltpu.make_async_copy(own(which), region(0, which), local.at[i, which])
+                )
+        spreads[0].start(0)
+        spreads[0].start(1)
         for copy in copies:
             copy.start()
-        spread.forward()
-        spread.finish()
+        for i in range(count):
+            spreads[i].forward()
+            if i + 1 < count:
+                spreads[i + 1].start(0)
+                spreads[i + 1].start(1)
+        for spread in spreads:
+            spread.finish()
         for copy in copies:
             copy.wait()
 
     return call(
-        gather_input, identity, (shard,), (pl.ANY,),
-        jax.ShapeDtypeStruct((2 * rows, 4 * wide), shard.dtype), pl.ANY,
-        [pltpu.SemaphoreType.DMA((2,))] + SPREAD_SEMS, 40_000_000_000,
+        gather_inputs, identity, shards, (pl.ANY,) * count,
+        [jax.ShapeDtypeStruct((2 * rows, 4 * wide), shard.dtype) for shard in shards],
+        [pl.ANY] * count,
+        [pltpu.SemaphoreType.DMA((count, 2))] + SPREAD_SEMS * count, 80_000_000_000,
     )
 
 
@@ -583,7 +594,7 @@
     )
 
 
-def input_terms(grad_packed, qkv, x_all, gain, grad_middle, own):
+def input_terms(grad_packed, weights, x_all, gain, grad_middle, own):
     total, columns = grad_packed.shape
     model = x_all.shape[1]
     tile = grad_middle.shape[0]
@@ -639,7 +650,7 @@
             bytes_accessed=6 * total * model,
         ),
         name="input_terms",
-    )(own, grad_packed, qkv, x_all, gain, grad_middle)
+    )(own, grad_packed, weights, x_all, gain, grad_middle)
 
 
 def program(
@@ -664,36 +675,35 @@
     def core_swap(value):
         return lax.ppermute(value, "feat", [(i, i ^ 1) for i in range(4)])
 
-    def mine(values, axis):
-        size = values.shape[axis] // 2
-        return lax.dynamic_slice_in_dim(values, member * size, size, axis)
-
-    def theirs(values, axis):
-        size = values.shape[axis] // 2
-        return lax.dynamic_slice_in_dim(values, (1 - member) * size, size, axis)
-
-    def ordered(own, other, axis):
+    def halves(weight, own):
+        size = weight.shape[1] // 2
+        start = member if own else 1 - member
+        return lax.dynamic_slice_in_dim(weight, start * size, size, 1)
+
+    def pair_blocks(weights, select):
+        own = select([halves(w, True) for w in weights])
+        other = swap(select([halves(w, False) for w in weights]))
+        return jnp.where(
+            member == 0,
+            jnp.concatenate([own, other]),
+            jnp.concatenate([other, own]),
+        )
+
+    def ring_gather(shard):
+        return lax.all_gather(shard, "tok", axis=0, tiled=True, axis_index_groups=groups)
+
+    def ring_scatter(terms):
+        return lax.psum_scatter(
+            terms, "tok", scatter_dimension=0, tiled=True, axis_index_groups=groups
+        )
+
+    def pair_finish(total):
+        size = total.shape[0] // 2
+        own = lax.dynamic_slice_in_dim(total, member * size, size, 0)
+        other = swap(lax.dynamic_slice_in_dim(total, (1 - member) * size, size, 0))
         first = jnp.where(member == 0, own, other)
         second = jnp.where(member == 0, other, own)
-        return jnp.concatenate([first, second], axis=axis)
-
-    def weight_start(shard, hidden_axis):
-        return ordered(
-            mine(shard, hidden_axis), swap(theirs(shard, hidden_axis)), 1 - hidden_axis
-        )
-
-    def ring_gather(shard, axis):
-        return lax.all_gather(shard, "tok", axis=axis, tiled=True, axis_index_groups=groups)
-
-    def ring_scatter(terms, axis):
-        return lax.psum_scatter(
-            terms, "tok", scatter_dimension=axis, tiled=True, axis_index_groups=groups
-        )
-
-    def weight_finish(total, hidden_axis):
-        axis = 1 - hidden_axis
-        other = swap(theirs(total, axis))
-        return ordered(mine(total, axis), other, hidden_axis).astype(F32)
+        return first, second
 
     def add_own_rows(values, own):
         start = (member * 4 + feat) * quarter
@@ -701,33 +711,32 @@
         here = (here.astype(F32) + own).astype(BF16)
         return lax.dynamic_update_slice_in_dim(values, here, start, 0)
 
-    packed_weights = []
-    starts = [weight_start(w, 1) for w in (w_query, w_key, w_value)]
-    heads_wide = starts[0].shape[1]
-    for left in range(0, heads_wide, pair_width):
-        packed_weights += [w[:, left : left + pair_width] for w in starts]
-    qkv_start = jnp.concatenate(packed_weights, axis=1)
-    out_start = weight_start(w_out, 0)
-    tokens_after, qkv_start, out_start = lax.optimization_barrier((tokens, qkv_start, out_start))
-    qkv = ring_gather(qkv_start, 0)
-    out_proj = ring_gather(out_start, 1)
-    x_all = gather_block(0, tokens_after)
-    w_gate, w_up, w_down, cotangent, x_all = lax.optimization_barrier(
-        (w_gate, w_up, w_down, cotangent, x_all)
-    )
-    gate_start = weight_start(w_gate, 1)
-    up_start = weight_start(w_up, 1)
-    down_start = weight_start(w_down, 0)
-    hidden_wide = down_start.shape[0]
-    chunk = hidden_wide // CHUNKS
-    gate_up, down_proj = [], []
-    for c in range(CHUNKS):
-        part = slice(c * chunk, (c + 1) * chunk)
-        gate_up.append(
-            ring_gather(jnp.concatenate([gate_start[:, part], up_start[:, part]], axis=1), 0)
-        )
-        down_proj.append(ring_gather(down_start[part], 1))
-    cot_rows = gather_block(1, cotangent)
+    def attention_columns(parts):
+        heads_wide = parts[0].shape[1]
+        packed = []
+        for left in range(0, heads_wide, pair_width):
+            packed += [part[:, left : left + pair_width] for part in parts[:3]]
+        return jnp.concatenate(packed + [parts[3]], axis=1)
+
+    def chunk_columns(c):
+        def select(parts):
+            size = parts[0].shape[1] // CHUNKS
+            return jnp.concatenate([part[:, c * size : (c + 1) * size] for part in parts], axis=1)
+
+        return select
+
+    attention_start = pair_blocks((w_query, w_key, w_value, w_out.T), attention_columns)
+    feed_starts = [
+        pair_blocks((w_gate, w_up, w_down.T), chunk_columns(c)) for c in range(CHUNKS)
+    ]
+    tokens_after, attention_start = lax.optimization_barrier((tokens, attention_start))
+    attention_weights = ring_gather(attention_start)
+    x_all, cot_rows = gather_blocks(0, tokens_after, cotangent)
+    feed_weights = [ring_gather(start) for start in feed_starts]
+    heads_wide = w_query.shape[1] // 2
+    qkv = attention_weights[:, : 3 * heads_wide]
+    out_proj = attention_weights[:, 3 * heads_wide :]
+    chunk = w_gate.shape[1] // 2 // CHUNKS
 
     gains = jnp.stack([gain_attn, gain_ffn])
     gains = jnp.stack([gains, core_swap(gains)])
@@ -743,51 +752,84 @@
     packed = product(normed, qkv).astype(BF16)
     attended, log_sums = attend(packed)
     normed_two, middle, factor_two = middle_norm(
-        2, product(attended, out_proj).astype(BF16), x_all, gain_two
+        2, right_trans(attended, out_proj).astype(BF16), x_all, gain_two
     )
 
     out_rows = 0.0
     grad_normed_two = 0.0
-    gate_grads, up_grads, down_grads = [], [], []
+    feed_sums = []
     for c in range(CHUNKS):
-        both = product(normed_two, gate_up[c])
+        if c:
+            feed_weights[c], feed_terms = lax.optimization_barrier((feed_weights[c], feed_terms))
+            feed_sums.append(ring_scatter(feed_terms))
+        gate_up, down_proj = feed_weights[c][:, : 2 * chunk], feed_weights[c][:, 2 * chunk :]
+        both = product(normed_two, gate_up)
         gate, upward = both[:, :chunk], both[:, chunk:]
         sigma = jax.nn.sigmoid(gate)
         hidden = (gate * sigma * upward).astype(BF16)
-        grad_hidden = right_trans(cot_rows, down_proj[c])
+        grad_hidden = product(cot_rows, down_proj)
         grad_gate = (grad_hidden * upward * sigma * (1.0 + gate * (1.0 - sigma))).astype(BF16)
         grad_up = (grad_hidden * gate * sigma).astype(BF16)
         grad_both = jnp.concatenate([grad_gate, grad_up], axis=1)
-        grad_normed_two = grad_normed_two + right_trans(grad_both, gate_up[c])
-        down_grads.append(ring_scatter(left_trans(hidden, cot_rows).astype(BF16), 1))
-        both_grad = ring_scatter(left_trans(normed_two, grad_both).astype(BF16), 0)
-        gate_grads.append(both_grad[:, :chunk])
-        up_grads.append(both_grad[:, chunk:])
-        out_rows = out_rows + product(hidden, down_proj[c])
-    gate_grad = weight_finish(jnp.concatenate(gate_grads, axis=1), 1)
-    up_grad = weight_finish(jnp.concatenate(up_grads, axis=1), 1)
-    down_grad = weight_finish(jnp.concatenate(down_grads, axis=0), 0)
+        grad_normed_two = grad_normed_two + right_trans(grad_both, gate_up)
+        if c + 1 == CHUNKS:
+            grad_normed_two = grad_normed_two.astype(BF16)
+        feed_terms = jnp.concatenate(
+            [
+                left_trans(normed_two, grad_both).astype(BF16),
+                left_trans(cot_rows, hidden).astype(BF16),
+            ],
+            axis=1,
+        )
+        out_rows = out_rows + right_trans(hidden, down_proj)
+    grad_normed_two, feed_terms = lax.optimization_barrier((grad_normed_two, feed_terms))
+    feed_sums.append(ring_scatter(feed_terms))
+
     grad_mid_rows, grad_middle, gain_ffn_part = middle_back(
-        3, grad_normed_two.astype(BF16), cot_rows, middle, factor_two, gain_two
-    )
-    outcome = scatter_block(4, add_own_rows(out_rows.astype(BF16), middle))
-
-    grad_attended = right_trans(grad_mid_rows, out_proj).astype(BF16)
-    out_grad = weight_finish(
-        ring_scatter(left_trans(attended, grad_mid_rows).astype(BF16), 1), 0
-    )
+        3, grad_normed_two, cot_rows, middle, factor_two, gain_two
+    )
+
+    grad_mid_rows, feed_sums[0] = lax.optimization_barrier((grad_mid_rows, feed_sums[0]))
+    grad_attended = product(grad_mid_rows, out_proj).astype(BF16)
     grad_packed = attend_back(packed, attended, grad_attended, log_sums)
-    qkv_grad = ring_scatter(left_trans(normed, grad_packed).astype(BF16), 0)
+    attention_terms = jnp.concatenate(
+        [
+            left_trans(normed, grad_packed).astype(BF16),
+            left_trans(grad_mid_rows, attended).astype(BF16),
+        ],
+        axis=1,
+    )
+    attention_terms, grad_packed = lax.optimization_barrier((attention_terms, grad_packed))
+    attention_grads = pair_finish(ring_scatter(attention_terms))
     part_grads = []
     for part in range(3):
         columns = [
-            qkv_grad[:, left + part * pair_width : left + (part + 1) * pair_width]
+            grads[:, left + part * pair_width : left + (part + 1) * pair_width]
+            for grads in attention_grads
             for left in range(0, 3 * heads_wide, 3 * pair_width)
         ]
-        part_grads.append(weight_finish(jnp.concatenate(columns, axis=1), 1))
+        part_grads.append(jnp.concatenate(columns, axis=1).astype(F32))
+    out_grad = (
+        jnp.concatenate([grads[:, 3 * heads_wide :] for grads in attention_grads], axis=1)
+        .astype(F32)
+        .T
+    )
     own = (member * 4 + feat).astype(jnp.int32).reshape(1)
-    terms, gain_attn_part = input_terms(grad_packed, qkv, x_all, gain_one, grad_middle, own)
+    terms, gain_attn_part = input_terms(grad_packed, attention_weights, x_all, gain_one, grad_middle, own)
     input_grad = scatter_block(5, terms)
+    out_rows = add_own_rows(out_rows.astype(BF16), middle)
+    out_rows, feed_sums[1] = lax.optimization_barrier((out_rows, feed_sums[1]))
+    outcome = scatter_block(4, out_rows)
+    feed_grads = [pair_finish(total) for total in feed_sums]
+
+    def feed_grad(part):
+        columns = slice(part * chunk, (part + 1) * chunk)
+        return jnp.concatenate(
+            [feed_grads[c][which][:, columns] for which in range(2) for c in range(CHUNKS)],
+            axis=1,
+        ).astype(F32)
+
+    gate_grad, up_grad, down_grad = feed_grad(0), feed_grad(1), feed_grad(2).T
 
     sums = jnp.concatenate([gain_attn_part, gain_ffn_part])
     for change in (core_swap, x_swap):

time: 820 us -> 756 us (0.922)
  waiting for transfers between devices: 143 us -> 60.3 us
  matrix products: 200 us -> 181 us
  other arithmetic: 32.8 us -> 47.1 us
  Pallas kernels: 377 us -> 391 us
  local copies, waits for them, and re-layouts: 27.6 us -> 40.6 us
    ppermute x14 -> x6, waiting for transfers between devices: 59.5 us -> 29.1 us  [swap(): return lax.ppermute(value, 'tok', [(i, i ^ 1) for i in range(tok_size)])]
    reduce_scatter x6 -> x3, waiting for transfers between devices: 28.4 us -> 0.02 us  [ring_scatter(): lax.psum_scatter(terms, 'tok', scatter_dimension=0, tiled=True, axis_inde...]
    all_gather x6 -> x3, waiting for transfers between devices: 46.2 us -> 28 us  [ring_gather(): lax.all_gather(shard, 'tok', axis=0, tiled=True, axis_index_groups=groups)]
    unnamed x65 -> x98, local copies, waits for them, and re-layouts: 13.9 us -> 29.6 us
    pallas_call x6 -> x5, Pallas kernels: 330 us -> 344 us  [call(): pl.pallas_call(kernel, out_shape=outputs, in_specs=[pl.BlockSpec(memory_s...]
    select_n x11 -> x5, other arithmetic: 11.4 us -> 21.8 us  [the longest x3 18.7 us: pair_blocks(): jnp.where(member == 0, jnp.concatenate([own, other]), jnp.concatenate([ot...]
    dot_general x6, matrix products: 70.7 us -> 60.6 us  [product(): return jnp.dot(left, right, preferred_element_type=F32)]
  transfers between devices with their start and end apart: 33 -> 19, of which waited for: 15 -> 6; matrix products, arithmetic and copies ran while one was open for 30% -> 32% of each run, Pallas kernels for 46% -> 52%
where the time goes in v3:
time: 756 us; the launch traced here: 750 us
  Pallas kernels  391 us (52%)
  matrix products  181 us (24%)
  waiting for transfers between devices  60.3 us (8%)
  other arithmetic  47.1 us (6%)
  local copies, waits for them, and re-layouts  40.6 us (5%)
  between operations  15.3 us (2%)
  starting transfers between devices  14.1 us (2%)
    pallas_call x5, Pallas kernels, call(): pl.pallas_call(kernel, out_shape=outputs, in_specs=[pl.BlockSpec(memory_s...  344 us
    dot_general x5, matrix products, right_trans(): lax.dot_general(left, right, (((1,), (1,)), ((), ())), preferred_element_...  63.3 us
    dot_general x6, matrix products, product(): return jnp.dot(left, right, preferred_element_type=F32)  60.6 us
    dot_general x6, matrix products, left_trans(): lax.dot_general(left, right, (((0,), (0,)), ((), ())), preferred_element_...  57.4 us
    unnamed x98, local copies, waits for them, and re-layouts  29.6 us
    ppermute x6, waiting for transfers between devices, swap(): return lax.ppermute(value, 'tok', [(i, i ^ 1) for i in range(tok_size)])  29.1 us
    all_gather x3, waiting for transfers between devices, ring_gather(): lax.all_gather(shard, 'tok', axis=0, tiled=True, axis_index_groups=groups)  28 us
    select_n x3, other arithmetic, pair_blocks(): jnp.where(member == 0, jnp.concatenate([own, other]), jnp.concatenate([ot...  18.7 us
  transfers between devices with their start and end apart: 19, of which 6 were waited for; matrix products, arithmetic and copies ran while one was open for 32% of the time, Pallas kernels for 52%

profile of v3, /device:TPU:0, one launch (start us, length us, event | category | flops | bytes accessed | tf_op | source)
XLA Modules:
  0.0 750.1 jit_solution(11948423321432340141)
XLA Ops:
  23.9 12.0 %collective-permute-done = bf16[256,1024]{1,0:T(8,128)(2,1)S(1)} collective-permute-done((bf16[256,1024]{1,0:T(8,128)(2,1)}, bf16[256,1024]{1,0:T(8,128)(2,1)S(1)}, u32[]{:S(2)}, u32[]{:S(2)}) %collective-permute-start) | collective-permute-done | bytes 524320 | tf_op jit(solution)/shard_map/ppermute | solution.py:670
  49.2 13.2 %collective-permute-done.3 = bf16[256,1536]{0,1:T(8,128)(2,1)} collective-permute-done((bf16[256,1536]{0,1:T(8,128)(2,1)}, bf16[256,1536]{0,1:T(8,128)(2,1)}, u32[]{:S(2)}, u32[]{:S(2)}) %collective-permute-start.3) | collective-permute-done | bytes 786464 | tf_op jit(solution)/shard_map/ppermute | solution.py:670
  62.4 7.5 %maximum_select_fusion = bf16[512,1536]{0,1:T(8,128)(2,1)} fusion(bf16[256,1536]{0,1:T(8,128)(2,1)} %collective-permute-done.3, bf16[256,512]{0,1:T(8,128)(2,1)} %get-tuple-element.117, bf16[256,512]{0,1:T(8,128)(2,1)S(1)} %copy.38, bf16[256,512]{0,1:T(8,128)(2,1)S(1)} %copy.36, pred[]{:T(512)S(6)} %eq.4), kind=kLoop, calls=%fused_computation.46 | loop fusion | flops 13369344 | bytes 3145729 | tf_op jit(solution)/shard_map/jit(_where)/select_n | solution.py:686
  70.4 82.5 %gather_inputs.1 = (bf16[2048,2048]{1,0:T(8,128)(2,1)}, bf16[2048,2048]{1,0:T(8,128)(2,1)}) custom-call(bf16[1024,512]{1,0:T(8,128)(2,1)S(1)} %copy-done.6, bf16[1024,512]{1,0:T(8,128)(2,1)S(1)} %copy-done.7), custom_call_target="tpu_custom_call" | custom-call | flops 80000000000 | bytes 800000000 | tf_op jit(solution)/shard_map/gather_inputs/pallas_call | solution.py:345
  152.8 5.2 fusion
  158.1 9.7 %maximum_select_fusion.1 = bf16[512,1536]{0,1:T(8,128)(2,1)} fusion(bf16[256,1536]{0,1:T(8,128)(2,1)} %collective-permute-done.4, bf16[256,512]{0,1:T(8,128)(2,1)S(1)} %copy-done.20, bf16[256,512]{0,1:T(8,128)(2,1)S(1)} %copy.44, bf16[256,512]{0,1:T(8,128)(2,1)S(1)} %copy.43, pred[]{:T(512)S(6)} %eq.4), kind=kLoop, calls=%fused_computation.47 | loop fusion | flops 13369344 | bytes 3145729 | tf_op jit(solution)/shard_map/jit(_where)/select_n | solution.py:686
  168.1 10.2 %convolution_convert_fusion.3.packed_ref = bf16[2048,768]{1,0:T(8,128)(2,1)S(1)} fusion(bf16[2048,1024]{1,0:T(8,128)(2,1)} %all-gather.4.cloned.1.call-done.qkv_ref, bf16[2048,2048]{1,0:T(8,128)(2,1)} %get-tuple-element.36.x_ref, f32[2048]{0:T(1024)S(1)} %bitcast.46, f32[2048]{0:T(1024)S(1)} %add_rsqrt_fusion), kind=kOutput, calls=%fused_computation.30 | convolution fusion | flops 6460801024 | bytes 14696448 | tf_op jit(solution)/shard_map/dot_general | solution.py:33
  178.3 11.3 %attend.1 = (bf16[2048,256]{1,0:T(8,128)(2,1)S(1)}, f32[2,2,2,1024]{3,2,1,0:T(2,128)S(1)}) custom-call(bf16[2048,768]{1,0:T(8,128)(2,1)S(1)} %convolution_convert_fusion.3.packed_ref), custom_call_target="tpu_custom_call" | custom-call | flops 1073741824 | bytes 6291456 | tf_op jit(solution)/shard_map/attend/pallas_call | solution.py:106
  189.6 7.3 convolution_convert_fusion.terms_ref
  196.9 79.9 %middle_step.1 = (bf16[2048,2048]{1,0:T(8,128)(2,1)}, f32[256,2048]{1,0:T(8,128)S(1)}, f32[256,128]{1,0:T(8,128)S(1)}) custom-call(bf16[2048,2048]{1,0:T(8,128)(2,1)} %convolution_convert_fusion.terms_ref, bf16[2048,2048]{1,0:T(8,128)(2,1)} %get-tuple-element.36.x_ref, f32[1,2048]{1,0:T(1,128)S(1)} %get-tuple-element.128.gain_ref), custom_call_target="tpu_custom_call" | custom-call | flops 70000001024 | bytes 700000000 | tf_op jit(solution)/shard_map/middle_step/pallas_call | solution.py:345
  276.9 12.6 %fusion.5 = f32[2048,1024]{0,1:T(8,128)S(1)} fusion(bf16[2048,2048]{1,0:T(8,128)(2,1)} %get-tuple-element.39, bf16[2048,1536]{0,1:T(8,128)(2,1)} %all-gather.6.cloned.1.call-done), kind=kOutput, calls=%fused_computation.25 | convolution fusion | flops 8589934592 | bytes 20971520 | tf_op jit(solution)/shard_map/dot_general | solution.py:33
  289.6 9.7 %multiply_convert_fusion.4 = (bf16[2048,512]{0,1:T(8,128)(2,1)S(1)}, bf16[2048,512]{0,1:T(8,128)(2,1)S(1)}, bf16[2048,512]{0,1:T(8,128)(2,1)S(1)}) fusion(f32[2048,1024]{0,1:T(8,128)S(1)} %fusion.5, bf16[2048,2048]{1,0:T(8,128)(2,1)} %get-tuple-element.40.cot_ref, bf16[2048,1536]{0,1:T(8,128)(2,1)} %all-gather.6.cloned.1.call-done), kind=kOutput, calls=%fused_computation.18 | convolution fusion | flops 4311744512 | bytes 25165824 | tf_op jit(solution)/shard_map/dot_general | solution.py:33
  299.3 10.4 %convolution_convert_fusion.6 = bf16[2048,512]{0,1:T(8,128)(2,1)S(1)} fusion(bf16[2048,512]{0,1:T(8,128)(2,1)S(1)} %get-tuple-element.75, bf16[2048,2048]{1,0:T(8,128)(2,1)} %get-tuple-element.40.cot_ref), kind=kOutput, calls=%fused_computation.34 | convolution fusion | flops 4296015872 | bytes 12582912 | tf_op jit(solution)/shard_map/dot_general | solution.py:21
  309.8 10.3 %convolution_convert_fusion.2 = bf16[2048,1024]{0,1:T(8,128)(2,1)S(1)} fusion(bf16[2048,2048]{1,0:T(8,128)(2,1)S(1)} %copy-done.28, bf16[2048,512]{0,1:T(8,128)(2,1)S(1)} %get-tuple-element.73, bf16[2048,512]{0,1:T(8,128)(2,1)S(1)} %get-tuple-element.72), kind=kOutput, calls=%fused_computation.22 | convolution fusion | flops 8600420352 | bytes 16777216 | tf_op jit(solution)/shard_map/dot_general | solution.py:21
  323.6 28.0 %all-gather.8.cloned.1.call-done = bf16[2048,1536]{0,1:T(8,128)(2,1)} async-done(((bf16[512,1536]{0,1:T(8,128)(2,1)}), bf16[2048,1536]{0,1:T(8,128)(2,1)}) %all-gather.8.cloned.1.call-update) | async-done | bytes 6291472 | tf_op jit(solution)/shard_map/all_gather | solution.py:693
  351.6 12.7 %fusion.8 = f32[2048,1024]{0,1:T(8,128)S(1)} fusion(bf16[2048,2048]{1,0:T(8,128)(2,1)} %get-tuple-element.39, bf16[2048,1536]{0,1:T(8,128)(2,1)} %all-gather.8.cloned.1.call-done), kind=kOutput, calls=%fused_computation.28 | convolution fusion | flops 8589934592 | bytes 20971520 | tf_op jit(solution)/shard_map/dot_general | solution.py:33
  364.4 9.2 %multiply_convert_fusion.1 = (bf16[2048,512]{0,1:T(8,128)(2,1)S(1)}, bf16[2048,512]{0,1:T(8,128)(2,1)S(1)}, bf16[2048,512]{0,1:T(8,128)(2,1)S(1)}) fusion(f32[2048,1024]{0,1:T(8,128)S(1)} %fusion.8, bf16[2048,2048]{1,0:T(8,128)(2,1)} %get-tuple-element.40.cot_ref, bf16[2048,1536]{0,1:T(8,128)(2,1)} %all-gather.8.cloned.1.call-done), kind=kOutput, calls=%fused_computation.14 | convolution fusion | flops 4311744512 | bytes 25165824 | tf_op jit(solution)/shard_map/dot_general | solution.py:33
  373.6 10.4 %convolution_convert_fusion.5 = bf16[2048,512]{0,1:T(8,128)(2,1)S(1)} fusion(bf16[2048,512]{0,1:T(8,128)(2,1)S(1)} %get-tuple-element.74, bf16[2048,2048]{1,0:T(8,128)(2,1)} %get-tuple-element.40.cot_ref), kind=kOutput, calls=%fused_computation.33 | convolution fusion | flops 4296015872 | bytes 12582912 | tf_op jit(solution)/shard_map/dot_general | solution.py:21
  384.1 11.3 %convolution_convert_fusion.1 = bf16[2048,1024]{0,1:T(8,128)(2,1)S(1)} fusion(bf16[2048,2048]{1,0:T(8,128)(2,1)} %get-tuple-element.39, bf16[2048,512]{0,1:T(8,128)(2,1)S(1)} %get-tuple-element.71, bf16[2048,512]{0,1:T(8,128)(2,1)S(1)} %get-tuple-element.70), kind=kOutput, calls=%fused_computation.21 | convolution fusion | flops 8600420352 | bytes 16777216 | tf_op jit(solution)/shard_map/dot_general | solution.py:21
  398.8 16.0 %fusion.3 = f32[2048,2048]{1,0:T(8,128)} fusion(bf16[2048,1536]{0,1:T(8,128)(2,1)} %all-gather.6.cloned.1.call-done, bf16[2048,512]{0,1:T(8,128)(2,1)} %copy-done.33, bf16[2048,512]{0,1:T(8,128)(2,1)} %copy-done.32), kind=kOutput, calls=%fused_computation.23 | convolution fusion | flops 8598323200 | bytes 25165824 | tf_op jit(solution)/shard_map/dot_general | solution.py:27
  414.8 16.2 %add_convert_fusion.terms_ref = bf16[2048,2048]{1,0:T(8,128)(2,1)} fusion(f32[2048,2048]{1,0:T(8,128)} %fusion.3, bf16[2048,1536]{0,1:T(8,128)(2,1)} %all-gather.8.cloned.1.call-done, bf16[2048,512]{0,1:T(8,128)(2,1)} %copy-done.31, bf16[2048,512]{0,1:T(8,128)(2,1)S(1)} %copy-done.30), kind=kOutput, calls=%fused_computation.5 | convolution fusion | flops 8606711808 | bytes 33554432 | tf_op jit(solution)/shard_map/dot_general | solution.py:27
  431.1 12.8 %fusion.15 = f32[2048,2048]{1,0:T(8,128)} fusion(bf16[2048,512]{0,1:T(8,128)(2,1)} %copy-done.25, bf16[2048,1536]{0,1:T(8,128)(2,1)} %all-gather.6.cloned.1.call-done), kind=kOutput, calls=%fused_computation.41 | convolution fusion | flops 4294967296 | bytes 20971520 | tf_op jit(solution)/shard_map/dot_general | solution.py:27
  443.9 11.1 %add_convert_fusion.1 = bf16[2048,2048]{1,0:T(8,128)(2,1)} fusion(f32[2048,2048]{1,0:T(8,128)} %fusion.15, bf16[2048,512]{0,1:T(8,128)(2,1)S(1)} %copy-done.27, bf16[2048,1536]{0,1:T(8,128)(2,1)} %all-gather.8.cloned.1.call-done), kind=kOutput, calls=%fused_computation.6 | convolution fusion | flops 4303355904 | bytes 29360128 | tf_op jit(solution)/shard_map/dot_general | solution.py:27
  454.9 81.7 %middle_back_step.1 = (bf16[2048,2048]{1,0:T(8,128)(2,1)}, f32[256,2048]{1,0:T(8,128)S(1)}, f32[1,2048]{1,0:T(1,128)S(1)}) custom-call(bf16[2048,2048]{1,0:T(8,128)(2,1)} %add_convert_fusion.terms_ref, bf16[2048,2048]{1,0:T(8,128)(2,1)} %get-tuple-element.40.cot_ref, f32[256,2048]{1,0:T(8,128)S(1)} %get-tuple-element.42.middle_ref, ...), custom_call_target="tpu_custom_call" | custom-call | flops 70000001024 | bytes 700000000 | tf_op jit(solution)/shard_map/middle_back_step/pallas_call | solution.py:345
  538.0 6.2 convolution_convert_fusion.8.grad_ref
  544.2 17.9 %attend_back.1.grad_ref = bf16[2048,768]{1,0:T(8,128)(2,1)S(1)} custom-call(bf16[2048,768]{1,0:T(8,128)(2,1)} %copy-done.8, bf16[2048,256]{1,0:T(8,128)(2,1)S(1)} %copy-done.1, bf16[2048,256]{1,0:T(8,128)(2,1)S(1)} %convolution_convert_fusion.8.grad_ref, f32[2,2,2,1024]{3,2,1,0:T(2,128)S(1)} %get-tuple-element.50.lse_ref), custom_call_target="tpu_custom_call" | custom-call | flops 2684354560 | bytes 9437184 | tf_op jit(solution)/shard_map/attend_back/pallas_call | solution.py:133
  562.1 6.9 convolution_convert_fusion.7
  569.1 7.9 %convolution_convert_fusion.4 = bf16[2048,768]{0,1:T(8,128)(2,1)S(1)} fusion(bf16[2048,768]{1,0:T(8,128)(2,1)S(1)} %attend_back.1.grad_ref, bf16[2048,2048]{1,0:T(8,128)(2,1)S(1)} %bitcast.49, f32[2048]{0:T(1024)S(1)} %bitcast.47, f32[2048]{0:T(1024)S(1)} %copy-done.22), kind=kOutput, calls=%fused_computation.31 | convolution fusion | flops 6460801024 | bytes 14696448 | tf_op jit(solution)/shard_map/dot_general | solution.py:21
  582.9 17.9 %input_terms.1 = (bf16[2048,2048]{1,0:T(8,128)(2,1)}, f32[1,2048]{1,0:T(1,128)S(1)}) custom-call(s32[1]{0:T(128)} %bitcast.13.own_ref, bf16[2048,768]{1,0:T(8,128)(2,1)S(1)} %copy-done.10, bf16[2048,1024]{1,0:T(8,128)(2,1)} %all-gather.4.cloned.1.call-done.qkv_ref, bf16[2048,2048]{1,0:T(8,128)(2,1)} %get-tuple-element.36.x_ref, f32[1,2048]{1,0:T(1,128)S(1)} %copy-done.3, ...), custom_call_target="tpu_custom_call" | custom-call | flops 6442450944 | bytes 25165824 | tf_op jit(solution)/shard_map/input_terms/pallas_call | solution.py:625
  608.0 50.7 %scatter_output.3 = bf16[1024,512]{1,0:T(8,128)(2,1)S(1)} custom-call(bf16[2048,2048]{1,0:T(8,128)(2,1)} %get-tuple-element.53.terms_ref), custom_call_target="tpu_custom_call" | custom-call | flops 30000001024 | bytes 300000000 | tf_op jit(solution)/shard_map/scatter_output/pallas_call | solution.py:345
  663.5 49.6 %scatter_output.2 = bf16[1024,512]{1,0:T(8,128)(2,1)S(1)} custom-call(bf16[2048,2048]{1,0:T(8,128)(2,1)} %fusion.20.terms_ref), custom_call_target="tpu_custom_call" | custom-call | flops 30000001024 | bytes 300000000 | tf_op jit(solution)/shard_map/scatter_output/pallas_call | solution.py:345
  731.8 3.9 collective-permute-done.10
  (187 shorter events, 82.6 us)
Async XLA Ops:
  7.2 30.3 %copy-start.23 = (f32[512]{0:T(512)S(1)}, f32[512]{0:T(512)}, u32[]{:S(2)}) copy-start(f32[512]{0:T(512)} %param.17) | copy-start | bytes 6148
  7.2 30.3 %copy-start.24 = (f32[512]{0:T(512)S(1)}, f32[512]{0:T(512)}, u32[]{:S(2)}) copy-start(f32[512]{0:T(512)} %param.12) | copy-start | bytes 6148
  7.2 30.4 %copy-start.16 = (bf16[256,2048]{1,0:T(8,128)(2,1)S(1)}, bf16[256,2048]{1,0:T(8,128)(2,1)}, u32[]{:S(2)}) copy-start(bf16[256,2048]{1,0:T(8,128)(2,1)} %param.18) | copy-start | bytes 3145732
  7.2 160.9 %all-gather.4.cloned.1.call-start = ((), (), s32[]{:S(2)}) async-start(), calls=%async_computation.3 | async-start | bytes 5242880 | tf_op jit(solution)/shard_map/all_gather | solution.py:693
  8.3 30.2 %copy-start.17 = (bf16[256,2048]{1,0:T(8,128)(2,1)S(1)}, bf16[256,2048]{1,0:T(8,128)(2,1)}, u32[]{:S(2)}) copy-start(bf16[256,2048]{1,0:T(8,128)(2,1)} %param.19) | copy-start | bytes 3145732
  20.8 15.1 %collective-permute-start = (bf16[256,1024]{1,0:T(8,128)(2,1)}, bf16[256,1024]{1,0:T(8,128)(2,1)S(1)}, u32[]{:S(2)}, u32[]{:S(2)}) collective-permute-start(bf16[256,1024]{1,0:T(8,128)(2,1)} %bitcast_dynamic-update-slice_fusion), channel_id=1, source_target_pairs={{0,4},{4,0},{8,12},{12,8},{16,20},{20,16},{24,28},{28,24},{1,5},{5... | collective-permute-start | bytes 1572872 | tf_op jit(solution)/shard_map/ppermute | solution.py:670
  37.4 239.5 %all-gather.6.cloned.1.call-start = ((), (), s32[]{:S(2)}) async-start(), calls=%async_computation.4 | async-start | bytes 7864320 | tf_op jit(solution)/shard_map/all_gather | solution.py:693
  37.5 7.5 %collective-permute-start.1 = (f32[2,512]{1,0:T(2,128)S(1)}, f32[2,512]{1,0:T(2,128)S(1)}, u32[]{:S(2)}, u32[]{:S(2)}) collective-permute-start(f32[2,512]{1,0:T(2,128)S(1)} %get-tuple-element.137), channel_id=1, source_target_pairs={{0,1},{1,0},{2,3},{3,2},{4,5},{5,4},{6,7},{7,6},{8,9},{9,8},{10,11... | collective-permute-start | bytes 12296 | tf_op jit(solution)/shard_map/ppermute | solution.py:676
  41.8 20.7 %collective-permute-start.3 = (bf16[256,1536]{0,1:T(8,128)(2,1)}, bf16[256,1536]{0,1:T(8,128)(2,1)}, u32[]{:S(2)}, u32[]{:S(2)}) collective-permute-start(bf16[256,1536]{0,1:T(8,128)(2,1)} %pad_maximum_fusion.9), channel_id=1, source_target_pairs={{0,4},{4,0},{8,12},{12,8},{16,20},{20,16},{24,28},{28,24},{1,5},{5... | collective-permute-start | bytes 2359304 | tf_op jit(solution)/shard_map/ppermute | solution.py:670
  44.7 25.6 %copy-start.6 = (bf16[1024,512]{1,0:T(8,128)(2,1)S(1)}, bf16[1024,512]{1,0:T(8,128)(2,1)}, u32[]{:S(2)}) copy-start(bf16[1024,512]{1,0:T(8,128)(2,1)} %refs_0_) | copy-start | bytes 3145732
  44.7 25.6 %copy-start.7 = (bf16[1024,512]{1,0:T(8,128)(2,1)S(1)}, bf16[1024,512]{1,0:T(8,128)(2,1)}, u32[]{:S(2)}) copy-start(bf16[1024,512]{1,0:T(8,128)(2,1)} %refs_1_.1) | copy-start | bytes 3145732
  44.7 113.3 %collective-permute-start.4 = (bf16[256,1536]{0,1:T(8,128)(2,1)}, bf16[256,1536]{0,1:T(8,128)(2,1)}, u32[]{:S(2)}, u32[]{:S(2)}) collective-permute-start(bf16[256,1536]{0,1:T(8,128)(2,1)} %pad_maximum_fusion.10), channel_id=1, source_target_pairs={{0,4},{4,0},{8,12},{12,8},{16,20},{20,16},{24,28},{28,24},{1,5},{5... | collective-permute-start | bytes 2359304 | tf_op jit(solution)/shard_map/ppermute | solution.py:670
  45.0 4.2 collective-permute-start.2
  70.0 281.6 %all-gather.8.cloned.1.call-start = ((), (), s32[]{:S(2)}) async-start(), calls=%async_computation.5 | async-start | bytes 7864320 | tf_op jit(solution)/shard_map/all_gather | solution.py:693
  70.3 97.8 %copy-start.2 = (f32[1,2048]{1,0:T(1,128)}, f32[1,2048]{1,0:T(1,128)S(1)}, u32[]{:S(2)}) copy-start(f32[1,2048]{1,0:T(1,128)S(1)} %get-tuple-element.129.gain_ref) | copy-start | bytes 24580
  70.3 126.6 %copy-start.4 = (f32[1,2048]{1,0:T(1,128)}, f32[1,2048]{1,0:T(1,128)S(1)}, u32[]{:S(2)}) copy-start(f32[1,2048]{1,0:T(1,128)S(1)} %get-tuple-element.128.gain_ref) | copy-start | bytes 24580
  158.0 20.3 %copy-start.21 = (f32[2048]{0:T(1024)}, f32[2048]{0:T(1024)S(1)}, u32[]{:S(2)}) copy-start(f32[2048]{0:T(1024)S(1)} %add_rsqrt_fusion) | copy-start | bytes 24580
  167.8 370.2 %reduce-scatter.6.cloned.1.call-start = ((), (), s32[]{:S(2)}) async-start(), calls=%async_computation.7 | async-start | bytes 7864320 | tf_op jit(solution)/shard_map/reduce_scatter | solution.py:696
  178.3 18.6 %copy-start.8 = (bf16[2048,768]{1,0:T(8,128)(2,1)}, bf16[2048,768]{1,0:T(8,128)(2,1)S(1)}, u32[]{:S(2)}) copy-start(bf16[2048,768]{1,0:T(8,128)(2,1)S(1)} %convolution_convert_fusion.3.packed_ref) | copy-start | bytes 9437188
  351.6 307.1 %reduce-scatter.4.cloned.1.call-start = ((), (), s32[]{:S(2)}) async-start(), calls=%async_computation.6 | async-start | bytes 7864320 | tf_op jit(solution)/shard_map/reduce_scatter | solution.py:696
  431.0 290.5 %reduce-scatter.8.cloned.1.call-start = ((), (), s32[]{:S(2)}) async-start(), calls=%async_computation.8 | async-start | bytes 5242880 | tf_op jit(solution)/shard_map/reduce_scatter | solution.py:696
  544.2 24.9 %slice-start = ((s8[8388608]{0:T(1024)(128)(4,1)}), s8[4194304]{0:T(1024)(128)(4,1)S(1)}, s32[]{:S(2)}) async-start(s8[8388608]{0:T(1024)(128)(4,1)} %bitcast.48), calls=%async_computation.9 | async-start | bytes 8388608
  600.8 2.9 collective-permute-start.5
  603.8 3.8 collective-permute-start.6
  604.5 109.2 %collective-permute-start.11 = (bf16[256,1536]{0,1:T(8,128)(2,1)S(1)}, bf16[256,1536]{0,1:T(8,128)(2,1)}, u32[]{:S(2)}, u32[]{:S(2)}) collective-permute-start(bf16[256,1536]{0,1:T(8,128)(2,1)S(1)} %constant_dynamic-slice_fusion.5), channel_id=1, source_target_pairs={{0,4},{4,0},{8,12},{12,8},{16,20},{20,16},{24,28},{28,24},{1,5},{5... | collective-permute-start | bytes 2359304 | tf_op jit(solution)/shard_map/ppermute | solution.py:670
  607.6 51.1 %collective-permute-start.7 = (f32[2,2048]{1,0:T(2,128)S(1)}, f32[2,2048]{1,0:T(2,128)S(1)}, u32[]{:S(2)}, u32[]{:S(2)}) collective-permute-start(f32[2,2048]{1,0:T(2,128)S(1)} %fusion.61), channel_id=1, source_target_pairs={{0,4},{4,0},{8,12},{12,8},{16,20},{20,16},{24,28},{28,24},{1,5},{5... | collective-permute-start | bytes 49160 | tf_op jit(solution)/shard_map/ppermute | solution.py:839
  658.7 4.3 collective-permute-start.8
  660.0 53.7 %collective-permute-start.12 = (bf16[256,1536]{0,1:T(8,128)(2,1)S(1)}, bf16[256,1536]{0,1:T(8,128)(2,1)S(1)}, u32[]{:S(2)}, u32[]{:S(2)}) collective-permute-start(bf16[256,1536]{0,1:T(8,128)(2,1)S(1)} %constant_dynamic-slice_fusion.4), channel_id=1, source_target_pairs={{0,4},{4,0},{8,12},{12,8},{16,20},{20,16},{24,28},{28,24},{1,5},{5... | collective-permute-start | bytes 2359304 | tf_op jit(solution)/shard_map/ppermute | solution.py:670
  663.1 50.7 %copy-start.14 = (bf16[512,1536]{0,1:T(8,128)(2,1)S(1)}, bf16[512,1536]{0,1:T(8,128)(2,1)}, u32[]{:S(2)}) copy-start(bf16[512,1536]{0,1:T(8,128)(2,1)} %reduce-scatter.6.cloned.1.call-done) | copy-start | bytes 4718596
  663.1 50.6 %copy-start.15 = (bf16[512,1536]{0,1:T(8,128)(2,1)S(1)}, bf16[512,1536]{0,1:T(8,128)(2,1)}, u32[]{:S(2)}) copy-start(bf16[512,1536]{0,1:T(8,128)(2,1)} %reduce-scatter.4.cloned.1.call-done) | copy-start | bytes 4718596
  663.1 50.0 %collective-permute-start.9 = (f32[2,2048]{1,0:T(2,128)S(1)}, f32[2,2048]{1,0:T(2,128)S(1)}, u32[]{:S(2)}, u32[]{:S(2)}) collective-permute-start(f32[2,2048]{1,0:T(2,128)S(1)} %add.138), channel_id=1, source_target_pairs={{0,16},{4,20},{8,24},{12,28},{16,0},{20,4},{24,8},{28,12},{1,17},{... | collective-permute-start | bytes 49160 | tf_op jit(solution)/shard_map/ppermute | solution.py:839
  723.4 12.3 %collective-permute-start.10 = (bf16[256,1024]{0,1:T(8,128)(2,1)}, bf16[256,1024]{0,1:T(8,128)(2,1)}, u32[]{:S(2)}, u32[]{:S(2)}) collective-permute-start(bf16[256,1024]{0,1:T(8,128)(2,1)} %constant_dynamic-slice_fusion.6), channel_id=1, source_target_pairs={{0,4},{4,0},{8,12},{12,8},{16,20},{20,16},{24,28},{28,24},{1,5},{5... | collective-permute-start | bytes 1572872 | tf_op jit(solution)/shard_map/ppermute | solution.py:670
  (23 other events, 176.4 us)
Sparse Core Ops, SparseCore 0:
  37.5 82.2 all-gather.3
  121.9 113.8 all-gather.5
  238.0 113.5 all-gather.7
  353.7 108.9 reduce-scatter.5
  464.9 111.2 reduce-scatter.3
  606.2 74.6 reduce-scatter.7

commit v4 on v3

--- a/solution.py
+++ b/solution.py
@@ -191,11 +191,77 @@
     return member, slot
 
 
-def greet():
+def greet(others=()):
     barrier = pltpu.get_barrier_semaphore()
-    for peer in neighbours().values():
+    peers = [*neighbours().values(), *others]
+    for peer in peers:
         pl.semaphore_signal(barrier, inc=1, device_id=peer, device_id_type=MESH)
-    pl.semaphore_wait(barrier, 3)
+    pl.semaphore_wait(barrier, len(peers))
+
+
+def ring_peer(ring, distance):
+    token = lax.axis_index("tok")
+    return lax.rem(token + 2 * distance, 2 * ring), lax.axis_index("feat")
+
+
+class SumAll:
+    def __init__(self, ring, ref, steps, arrived, slots, send, recv):
+        self.ring, self.ref = ring, ref
+        self.steps, self.arrived, self.slots = steps, arrived, slots
+        self.send, self.recv = send, recv
+        self.place = lax.div(lax.axis_index("tok"), 2)
+        self.peers = neighbours()
+
+    @staticmethod
+    def scratch(ring, shape):
+        return [
+            pltpu.VMEM((3, *shape), F32),
+            pltpu.VMEM((3, *shape), F32),
+            pltpu.VMEM((ring, *shape), F32),
+            pltpu.SemaphoreType.DMA((2 + ring,)),
+            pltpu.SemaphoreType.DMA((2 + ring,)),
+        ]
+
+    def copy(self, k):
+        if k < 3:
+            source = self.ref if k == 0 else self.steps.at[k - 1]
+            target, peer = self.arrived.at[k], self.peers[("core", "x", "y")[k]]
+        else:
+            source, target = self.steps.at[2], self.slots.at[self.place]
+            peer = ring_peer(self.ring, k - 2)
+        return pltpu.make_async_remote_copy(
+            source, target, self.send.at[k], self.recv.at[k],
+            device_id=peer, device_id_type=MESH,
+        )
+
+    def start(self):
+        self.copy(0).start()
+
+    def step(self, k):
+        self.copy(k).wait_recv()
+        before = self.ref[...] if k == 0 else self.steps[k - 1]
+        self.steps[k] = before + self.arrived[k]
+        if k < 2:
+            self.copy(k + 1).start()
+        else:
+            for distance in range(1, self.ring):
+                self.copy(2 + distance).start()
+            self.slots[self.place] = self.steps[2]
+
+    def finish(self):
+        for distance in range(1, self.ring):
+            source = lax.rem(self.place + self.ring - distance, self.ring)
+            k = 2 + distance
+            pltpu.make_async_remote_copy(
+                self.slots.at[source], self.slots.at[source], self.send.at[k], self.recv.at[k],
+                device_id=ring_peer(self.ring, distance), device_id_type=MESH,
+            ).wait_recv()
+        for k in range(2 + self.ring):
+            self.copy(k).wait_send()
+        total = self.slots[0]
+        for place in range(1, self.ring):
+            total = total + self.slots[place]
+        return total
 
 
 class Spread:
@@ -297,21 +363,24 @@
 
         lax.fori_loop(0, count // step, body, 0)
 
-    def run(self):
+    def loads(self, k):
+        return pltpu.make_async_copy(self.part(2 * k), self.parts.at[k], self.load.at[k])
+
+    def start(self):
         for k in (3, 1, 2, 0):
             self.copy(k).start()
-        loads = [
-            pltpu.make_async_copy(self.part(2 * k), self.parts.at[k], self.load.at[k])
-            for k in range(4)
-        ]
         for k in (3, 1, 2, 0):
-            loads[k].start()
+            self.loads(k).start()
+
+    def first(self):
         for k, following in ((3, (5, 7)), (1, (4,)), (2, (6,)), (0, ())):
-            loads[k].wait()
+            self.loads(k).wait()
             self.copy(k).wait_recv()
             self.add(k, 0, self.size, self.near.at[k])
             for after in following:
                 self.copy(after).start()
+
+    def second(self):
         self.copy(5).wait_recv()
         self.add(2, 0, self.half, self.from_x.at[1])
         self.copy(8).start()
@@ -356,85 +425,164 @@
     )(*operands)
 
 
-def gather_blocks(identity, *shards):
-    rows, wide = shards[0].shape
-    half = rows // 2
-    count = len(shards)
-
-    def gather_inputs(*refs):
+class PairSwap:
+    def __init__(self, sources, out_ref, pieces, local, send, recv):
+        self.sources, self.out, self.pieces = sources, out_ref, pieces
+        self.local, self.send, self.recv = local, send, recv
+        self.peer = neighbours()["y"]
+        self.member = lax.rem(lax.axis_index("tok"), 2)
+
+    def block(self, i, half):
+        source, start, width, _ = self.pieces[i]
+        ref = self.sources[source]
+        offset = half * (ref.shape[1] // 2) + start
+        return ref.at[:, pl.ds(pl.multiple_of(offset, 128), width)]
+
+    def place(self, i, member):
+        _, _, width, column = self.pieces[i]
+        rows = self.out.shape[0] // 2
+        return self.out.at[pl.ds(pl.multiple_of(member * rows, rows), rows), pl.ds(column, width)]
+
+    def remote(self, i, source, member):
+        return pltpu.make_async_remote_copy(
+            source, self.place(i, member), self.send.at[i], self.recv.at[i],
+            device_id=self.peer, device_id_type=MESH,
+        )
+
+    def own(self, i):
+        return pltpu.make_async_copy(
+            self.block(i, self.member), self.place(i, self.member), self.local.at[i]
+        )
+
+    def away(self, i):
+        return self.remote(i, self.block(i, 1 - self.member), self.member)
+
+    def start(self):
+        for i in range(len(self.pieces)):
+            self.away(i).start()
+        for i in range(len(self.pieces)):
+            self.own(i).start()
+
+    def finish(self):
+        for i in range(len(self.pieces)):
+            other = 1 - self.member
+            self.remote(i, self.place(i, other), other).wait_recv()
+            self.away(i).wait_send()
+            self.own(i).wait()
+
+
+def swap_and_gather(identity, weights, pieces, shard=None):
+    count = len(weights)
+    size = weights[0].shape[0]
+    columns = sum(piece[2] for piece in pieces)
+    operands = tuple(weights)
+    outputs = [jax.ShapeDtypeStruct((2 * size, columns), weights[0].dtype)]
+    scratch = [pltpu.SemaphoreType.DMA((len(pieces),))] * 3
+    if shard is not None:
+        rows, wide = shard.shape
+        half = rows // 2
+        operands += (shard,)
+        outputs.append(jax.ShapeDtypeStruct((2 * rows, 4 * wide), shard.dtype))
+        scratch += [pltpu.SemaphoreType.DMA((2,))] + SPREAD_SEMS
+
+    def swap_gather(*refs):
+        sources, refs = refs[:count], refs[count:]
+        if shard is not None:
+            shard_ref, start_ref, out_ref, *sems = refs
+        else:
+            start_ref, *sems = refs
         greet()
-        local = refs[2 * count]
-        spreads, copies = [], []
+        pair = PairSwap(sources, start_ref, pieces, *sems[:3])
+        pair.start()
+        if shard is None:
+            pair.finish()
+            return
+
+        def own(which):
+            return shard_ref.at[pl.ds(which * half, half)]
+
+        def region(r, which):
+            member, slot = owner(r)
+            return out_ref.at[
+                pl.ds(pl.multiple_of(member * rows + which * half, half), half),
+                pl.ds(pl.multiple_of(slot * wide, wide), wide),
+            ]
+
+        spread = Spread(own, region, *sems[4:])
+        spread.start(0)
+        spread.start(1)
+        copies = [
+            pltpu.make_async_copy(own(which), region(0, which), sems[3].at[which])
+            for which in range(2)
+        ]
+        for copy in copies:
+            copy.start()
+        spread.forward()
+        spread.finish()
+        pair.finish()
+        for copy in copies:
+            copy.wait()
+
+    return call(
+        swap_gather, identity, operands, (pl.ANY,) * len(operands),
+        outputs, [pl.ANY] * len(outputs), scratch,
+        15_000_000_000 if shard is None else 50_000_000_000,
+    )
+
+
+def scatter_blocks(identity, ring, vector, *terms):
+    rows, wide = terms[0].shape[0] // 2, terms[0].shape[1] // 4
+    count = len(terms)
+
+    def scatter_outputs(vector_ref, *refs):
+        greet([ring_peer(ring, distance) for distance in range(1, ring)])
+        small_ref = refs[2 * count]
+        scratch = refs[2 * count + 1 :]
+        small = SumAll(ring, vector_ref, *scratch[:5])
+        collects = []
         for i in range(count):
-            shard_ref, out_ref = refs[i], refs[count + i]
-
-            def own(which, shard_ref=shard_ref):
-                return shard_ref.at[pl.ds(which * half, half)]
-
-            def region(r, which, out_ref=out_ref):
+
+            def part(r, terms_ref=refs[i]):
                 member, slot = owner(r)
-                return out_ref.at[
-                    pl.ds(pl.multiple_of(member * rows + which * half, half), half),
+                return terms_ref.at[
+                    pl.ds(pl.multiple_of(member * rows, rows), rows),
                     pl.ds(pl.multiple_of(slot * wide, wide), wide),
                 ]
 
-            sems = refs[2 * count + 1 + 2 * i : 2 * count + 3 + 2 * i]
-            spreads.append(Spread(own, region, *sems))
+            mine = scratch[5 + 9 * i : 5 + 9 * (i + 1)]
+            collects.append(Collect(part, rows, *mine[:6], mine[6:]))
+        small.start()
+        for collect in collects:
+            collect.start()
+        small.step(0)
+        for collect in collects:
+            collect.first()
+        small.step(1)
+        for collect in collects:
+            collect.second()
+        small.step(2)
+        for collect, out_ref in zip(collects, refs[count:]):
             for which in range(2):
-                copies.append(
-                    pltpu.make_async_copy(own(which), region(0, which), local.at[i, which])
-                )
-        spreads[0].start(0)
-        spreads[0].start(1)
-        for copy in copies:
-            copy.start()
-        for i in range(count):
-            spreads[i].forward()
-            if i + 1 < count:
-                spreads[i + 1].start(0)
-                spreads[i + 1].start(1)
-        for spread in spreads:
-            spread.finish()
-        for copy in copies:
-            copy.wait()
+                collect.ready(which)
+
+                def body(here, collect=collect, out_ref=out_ref):
+                    there = pl.ds(pl.multiple_of(which * (rows // 2) + here.start, 32), 32)
+                    out_ref[there] = collect.total(which, here).astype(BF16)
+
+                loop_rows(rows // 2, body)
+        for collect in collects:
+            collect.finish()
+        scratch[1][0] = small.finish()
+        start = pl.multiple_of(lax.axis_index("feat") * wide, wide)
+        small_ref[...] = scratch[1][0, :, pl.ds(start, wide)]
 
     return call(
-        gather_inputs, identity, shards, (pl.ANY,) * count,
-        [jax.ShapeDtypeStruct((2 * rows, 4 * wide), shard.dtype) for shard in shards],
-        [pl.ANY] * count,
-        [pltpu.SemaphoreType.DMA((count, 2))] + SPREAD_SEMS * count, 80_000_000_000,
-    )
-
-
-def scatter_block(identity, terms):
-    rows, wide = terms.shape[0] // 2, terms.shape[1] // 4
-
-    def scatter_output(terms_ref, out_ref, *scratch):
-        greet()
-
-        def part(r):
-            member, slot = owner(r)
-            return terms_ref.at[
-                pl.ds(pl.multiple_of(member * rows, rows), rows),
-                pl.ds(pl.multiple_of(slot * wide, wide), wide),
-            ]
-
-        collect = Collect(part, rows, *scratch[:6], scratch[6:])
-        collect.run()
-        for which in range(2):
-            collect.ready(which)
-
-            def body(here):
-                there = pl.ds(pl.multiple_of(which * (rows // 2) + here.start, 32), 32)
-                out_ref[there] = collect.total(which, here).astype(BF16)
-
-            loop_rows(rows // 2, body)
-        collect.finish()
-
-    return call(
-        scatter_output, identity, (terms,), (pl.ANY,),
-        jax.ShapeDtypeStruct((rows, wide), BF16), pltpu.VMEM,
-        Collect.scratch(rows, wide), 30_000_000_000,
+        scatter_outputs, identity, (vector, *terms), (pltpu.VMEM,) + (pl.ANY,) * count,
+        [jax.ShapeDtypeStruct((rows, wide), BF16)] * count
+        + [jax.ShapeDtypeStruct((vector.shape[0], wide), F32)],
+        [pltpu.VMEM] * (count + 1),
+        SumAll.scratch(ring, vector.shape) + Collect.scratch(rows, wide) * count,
+        30_000_000_000 * count,
     )
 
 
@@ -474,7 +622,9 @@
         spread = Spread(
             lambda which: normed.at[pl.ds(which * half, half)], region, send, recv
         )
-        collect.run()
+        collect.start()
+        collect.first()
+        collect.second()
         x_copy.wait()
         copies = []
         for which in range(2):
@@ -538,7 +688,9 @@
         spread = Spread(
             lambda which: rounded.at[pl.ds(which * half, half)], region, send, recv
         )
-        collect.run()
+        collect.start()
+        collect.first()
+        collect.second()
         cot_copy.wait()
         gain_grad_ref[...] = jnp.zeros_like(gain_grad_ref)
         copies = []
@@ -592,6 +744,43 @@
         + Collect.scratch(quarter, model),
         70_000_000_000,
     )
+
+
+def assemble(plan, flipped_out, totals, others):
+    count = len(totals)
+    size = others[0].shape[0]
+    shapes = []
+    for index, pieces in enumerate(plan):
+        wide = 2 * sum(piece[2] for piece in pieces)
+        shapes.append((size, wide) if index < flipped_out else (wide, size))
+
+    def assemble_grads(*refs):
+        member = lax.rem(lax.axis_index("tok"), 2)
+        outs = refs[2 * count :]
+        for index, pieces in enumerate(plan):
+            half = sum(piece[2] for piece in pieces)
+            for source, column, width, target in pieces:
+                own_rows = pl.ds(pl.multiple_of(member * size, size), size)
+                own = refs[source][own_rows, column : column + width]
+                other = refs[count + source][:, column : column + width]
+                for which, block in ((member, own), (1 - member, other)):
+                    start = pl.multiple_of(which * half + target, 128)
+                    if index < flipped_out:
+                        outs[index][:, pl.ds(start, width)] = block.astype(F32)
+                    else:
+                        outs[index][pl.ds(start, width), :] = block.astype(F32).T
+
+    return pl.pallas_call(
+        assemble_grads,
+        out_shape=[jax.ShapeDtypeStruct(shape, F32) for shape in shapes],
+        in_specs=[pl.BlockSpec(memory_space=pltpu.VMEM)] * (2 * count),
+        out_specs=[pl.BlockSpec(memory_space=pltpu.VMEM)] * len(plan),
+        compiler_params=pltpu.CompilerParams(vmem_limit_bytes=VMEM),
+        cost_estimate=pl.CostEstimate(
+            flops=0, transcendentals=0, bytes_accessed=8 * size * 2 * sum(t.shape[1] for t in totals)
+        ),
+        name="assemble_grads",
+    )(*totals, *others)
 
 
 def input_terms(grad_packed, weights, x_all, gain, grad_middle, own):
@@ -653,6 +842,105 @@
     )(own, grad_packed, weights, x_all, gain, grad_middle)
 
 
+def feed_forward(normed, cot, weights, chunk):
+    total, model = normed.shape
+    tile = 512
+    part = 256 if chunk % 256 == 0 else 128
+
+    def feed_step(normed_ref, cot_ref, gate_ref, up_ref, down_ref, hidden_ref, grads_ref):
+        for left in range(0, chunk, part):
+            here = slice(left, left + part)
+            gate = product(normed_ref[...], gate_ref[:, here])
+            upward = product(normed_ref[...], up_ref[:, here])
+            grad_hidden = product(cot_ref[...], down_ref[:, here])
+            sigma = jax.nn.sigmoid(gate)
+            active = gate * sigma
+            hidden_ref[:, here] = (active * upward).astype(BF16)
+            grads_ref[:, here] = (
+                grad_hidden * upward * (sigma + active * (1.0 - sigma))
+            ).astype(BF16)
+            grads_ref[:, chunk + left : chunk + left + part] = (grad_hidden * active).astype(BF16)
+
+    rows = pl.BlockSpec((tile, model), lambda i: (i, 0))
+
+    def weight(part):
+        return pl.BlockSpec((model, chunk), lambda i: (0, part), pipeline_mode=pl.Buffered(1))
+
+    return pl.pallas_call(
+        feed_step,
+        grid=(total // tile,),
+        in_specs=[rows, rows, weight(0), weight(1), weight(2)],
+        out_specs=[
+            pl.BlockSpec((tile, chunk), lambda i: (i, 0)),
+            pl.BlockSpec((tile, 2 * chunk), lambda i: (i, 0)),
+        ],
+        out_shape=[
+            jax.ShapeDtypeStruct((total, chunk), BF16),
+            jax.ShapeDtypeStruct((total, 2 * chunk), BF16),
+        ],
+        compiler_params=pltpu.CompilerParams(vmem_limit_bytes=VMEM),
+        cost_estimate=pl.CostEstimate(
+            flops=6 * total * chunk * model,
+            transcendentals=total * chunk,
+            bytes_accessed=4 * total * model + 6 * chunk * (model + total),
+        ),
+        name="feed_forward",
+    )(normed, cot, weights, weights, weights)
+
+
+def columns_back(left, weights, place, base=None, own=None, middle=None):
+    total, inner = left.shape
+    model = weights.shape[0]
+    tile, part = 512, 512
+
+    def columns_step(own_ref, left_ref, right_ref, *refs):
+        out_ref = refs[-1]
+        for start in range(0, model, part):
+            here = slice(start, start + part)
+            value = right_trans(left_ref[...], right_ref[here, :])
+            if base is not None:
+                value = value + refs[0][:, here].astype(F32)
+            out_ref[:, here] = value.astype(BF16)
+        if middle is not None:
+            middle_ref = refs[-2]
+            size = middle_ref.shape[0]
+            inside = own_ref[0] * size - pl.program_id(0) * tile
+
+            @pl.when((inside >= 0) & (inside < tile))
+            def _():
+                rows = pl.ds(pl.multiple_of(inside, size), size)
+                out_ref[rows, :] = (out_ref[rows, :].astype(F32) + middle_ref[...]).astype(BF16)
+
+    in_specs = [
+        pl.BlockSpec((tile, inner), lambda i, own: (i, 0)),
+        pl.BlockSpec((model, inner), lambda i, own: (0, place), pipeline_mode=pl.Buffered(1)),
+    ]
+    operands = [own, left, weights]
+    if base is not None:
+        in_specs.append(pl.BlockSpec((tile, model), lambda i, own: (i, 0)))
+        operands.append(base)
+    if middle is not None:
+        in_specs.append(pl.BlockSpec(middle.shape, lambda i, own: (0, 0)))
+        operands.append(middle)
+    return pl.pallas_call(
+        columns_step,
+        grid_spec=pltpu.PrefetchScalarGridSpec(
+            num_scalar_prefetch=1,
+            grid=(total // tile,),
+            in_specs=in_specs,
+            out_specs=pl.BlockSpec((tile, model), lambda i, own: (i, 0)),
+        ),
+        out_shape=jax.ShapeDtypeStruct((total, model), BF16),
+        compiler_params=pltpu.CompilerParams(vmem_limit_bytes=VMEM),
+        cost_estimate=pl.CostEstimate(
+            flops=2 * total * model * inner,
+            transcendentals=0,
+            bytes_accessed=2 * total * model + 2 * (total + model) * inner,
+        ),
+        name="columns_back",
+    )(*operands)
+
+
 def program(
     tok_size,
     tokens, gain_attn, w_query, w_key, w_value, w_out, gain_ffn, w_gate, w_up, w_down, cotangent
@@ -675,20 +963,6 @@
     def core_swap(value):
         return lax.ppermute(value, "feat", [(i, i ^ 1) for i in range(4)])
 
-    def halves(weight, own):
-        size = weight.shape[1] // 2
-        start = member if own else 1 - member
-        return lax.dynamic_slice_in_dim(weight, start * size, size, 1)
-
-    def pair_blocks(weights, select):
-        own = select([halves(w, True) for w in weights])
-        other = swap(select([halves(w, False) for w in weights]))
-        return jnp.where(
-            member == 0,
-            jnp.concatenate([own, other]),
-            jnp.concatenate([other, own]),
-        )
-
     def ring_gather(shard):
         return lax.all_gather(shard, "tok", axis=0, tiled=True, axis_index_groups=groups)
 
@@ -697,46 +971,34 @@
             terms, "tok", scatter_dimension=0, tiled=True, axis_index_groups=groups
         )
 
-    def pair_finish(total):
+    def other_half(total):
         size = total.shape[0] // 2
-        own = lax.dynamic_slice_in_dim(total, member * size, size, 0)
-        other = swap(lax.dynamic_slice_in_dim(total, (1 - member) * size, size, 0))
-        first = jnp.where(member == 0, own, other)
-        second = jnp.where(member == 0, other, own)
-        return first, second
-
-    def add_own_rows(values, own):
-        start = (member * 4 + feat) * quarter
-        here = lax.dynamic_slice_in_dim(values, start, quarter, 0)
-        here = (here.astype(F32) + own).astype(BF16)
-        return lax.dynamic_update_slice_in_dim(values, here, start, 0)
-
-    def attention_columns(parts):
-        heads_wide = parts[0].shape[1]
-        packed = []
-        for left in range(0, heads_wide, pair_width):
-            packed += [part[:, left : left + pair_width] for part in parts[:3]]
-        return jnp.concatenate(packed + [parts[3]], axis=1)
-
-    def chunk_columns(c):
-        def select(parts):
-            size = parts[0].shape[1] // CHUNKS
-            return jnp.concatenate([part[:, c * size : (c + 1) * size] for part in parts], axis=1)
-
-        return select
-
-    attention_start = pair_blocks((w_query, w_key, w_value, w_out.T), attention_columns)
-    feed_starts = [
-        pair_blocks((w_gate, w_up, w_down.T), chunk_columns(c)) for c in range(CHUNKS)
+        return swap(lax.dynamic_slice_in_dim(total, (1 - member) * size, size, 0))
+
+    heads_wide = w_query.shape[1] // 2
+    chunk = w_gate.shape[1] // 2 // CHUNKS
+    attention_pieces = [
+        (part, left, pair_width, 3 * left + part * pair_width)
+        for left in range(0, heads_wide, pair_width)
+        for part in range(3)
     ]
+    attention_pieces.append((3, 0, heads_wide, 3 * heads_wide))
+    (attention_start,) = swap_and_gather(0, (w_query, w_key, w_value, w_out.T), attention_pieces)
+    feed = (w_gate, w_up, w_down.T)
     tokens_after, attention_start = lax.optimization_barrier((tokens, attention_start))
     attention_weights = ring_gather(attention_start)
-    x_all, cot_rows = gather_blocks(0, tokens_after, cotangent)
-    feed_weights = [ring_gather(start) for start in feed_starts]
-    heads_wide = w_query.shape[1] // 2
+    feed_weights = []
+    wholes = []
+    for c, shard in enumerate((tokens_after, cotangent)):
+        if c:
+            shard, wholes[0] = lax.optimization_barrier((shard, wholes[0]))
+        pieces = [(part, c * chunk, chunk, part * chunk) for part in range(3)]
+        start, whole = swap_and_gather(1 + c, feed, pieces, shard)
+        wholes.append(whole)
+        feed_weights.append(ring_gather(start))
+    x_all, cot_rows = wholes
     qkv = attention_weights[:, : 3 * heads_wide]
     out_proj = attention_weights[:, 3 * heads_wide :]
-    chunk = w_gate.shape[1] // 2 // CHUNKS
 
     gains = jnp.stack([gain_attn, gain_ffn])
     gains = jnp.stack([gains, core_swap(gains)])
@@ -752,28 +1014,20 @@
     packed = product(normed, qkv).astype(BF16)
     attended, log_sums = attend(packed)
     normed_two, middle, factor_two = middle_norm(
-        2, right_trans(attended, out_proj).astype(BF16), x_all, gain_two
-    )
-
-    out_rows = 0.0
-    grad_normed_two = 0.0
+        3, right_trans(attended, out_proj).astype(BF16), x_all, gain_two
+    )
+
+    own = (member * 4 + feat).astype(jnp.int32).reshape(1)
     feed_sums = []
+    grad_normed_two = out_rows = None
     for c in range(CHUNKS):
         if c:
-            feed_weights[c], feed_terms = lax.optimization_barrier((feed_weights[c], feed_terms))
+            feed_weights[c], feed_terms, grad_normed_two, out_rows = lax.optimization_barrier(
+                (feed_weights[c], feed_terms, grad_normed_two, out_rows)
+            )
             feed_sums.append(ring_scatter(feed_terms))
-        gate_up, down_proj = feed_weights[c][:, : 2 * chunk], feed_weights[c][:, 2 * chunk :]
-        both = product(normed_two, gate_up)
-        gate, upward = both[:, :chunk], both[:, chunk:]
-        sigma = jax.nn.sigmoid(gate)
-        hidden = (gate * sigma * upward).astype(BF16)
-        grad_hidden = product(cot_rows, down_proj)
-        grad_gate = (grad_hidden * upward * sigma * (1.0 + gate * (1.0 - sigma))).astype(BF16)
-        grad_up = (grad_hidden * gate * sigma).astype(BF16)
-        grad_both = jnp.concatenate([grad_gate, grad_up], axis=1)
-        grad_normed_two = grad_normed_two + right_trans(grad_both, gate_up)
-        if c + 1 == CHUNKS:
-            grad_normed_two = grad_normed_two.astype(BF16)
+        hidden, grad_both = feed_forward(normed_two, cot_rows, feed_weights[c], chunk)
+        grad_normed_two = columns_back(grad_both, feed_weights[c], 0, grad_normed_two, own)
         feed_terms = jnp.concatenate(
             [
                 left_trans(normed_two, grad_both).astype(BF16),
@@ -781,17 +1035,19 @@
             ],
             axis=1,
         )
-        out_rows = out_rows + right_trans(hidden, down_proj)
+        if c + 1 < CHUNKS:
+            out_rows = columns_back(hidden, feed_weights[c], 2, out_rows, own)
     grad_normed_two, feed_terms = lax.optimization_barrier((grad_normed_two, feed_terms))
     feed_sums.append(ring_scatter(feed_terms))
-
     grad_mid_rows, grad_middle, gain_ffn_part = middle_back(
-        3, grad_normed_two, cot_rows, middle, factor_two, gain_two
+        4, grad_normed_two, cot_rows, middle, factor_two, gain_two
     )
 
     grad_mid_rows, feed_sums[0] = lax.optimization_barrier((grad_mid_rows, feed_sums[0]))
     grad_attended = product(grad_mid_rows, out_proj).astype(BF16)
     grad_packed = attend_back(packed, attended, grad_attended, log_sums)
+    first_other = other_half(feed_sums[0])
+    grad_packed, first_other = lax.optimization_barrier((grad_packed, first_other))
     attention_terms = jnp.concatenate(
         [
             left_trans(normed, grad_packed).astype(BF16),
@@ -800,52 +1056,37 @@
         axis=1,
     )
     attention_terms, grad_packed = lax.optimization_barrier((attention_terms, grad_packed))
-    attention_grads = pair_finish(ring_scatter(attention_terms))
-    part_grads = []
-    for part in range(3):
-        columns = [
-            grads[:, left + part * pair_width : left + (part + 1) * pair_width]
-            for grads in attention_grads
-            for left in range(0, 3 * heads_wide, 3 * pair_width)
+    attention_sum = ring_scatter(attention_terms)
+    terms, gain_attn_part = input_terms(grad_packed, attention_weights, x_all, gain_one, grad_middle, own)
+    hidden, terms = lax.optimization_barrier((hidden, terms))
+    out_rows = columns_back(hidden, feed_weights[-1], 2, out_rows, own, middle)
+    out_rows, feed_sums[1] = lax.optimization_barrier((out_rows, feed_sums[1]))
+    outcome, input_grad, gain_grads = scatter_blocks(
+        5, tok_size // 2, jnp.concatenate([gain_attn_part, gain_ffn_part]), out_rows, terms
+    )
+    outcome, attention_sum = lax.optimization_barrier((outcome, attention_sum))
+
+    feed_plan = [
+        [(c, part * chunk, chunk, c * chunk) for c in range(CHUNKS)] for part in range(3)
+    ]
+    gate_grad, up_grad, down_grad = assemble(
+        feed_plan, 2, feed_sums, [first_other, other_half(feed_sums[1])]
+    )
+    attention_plan = [
+        [
+            (0, 3 * left + part * pair_width, pair_width, left)
+            for left in range(0, heads_wide, pair_width)
         ]
-        part_grads.append(jnp.concatenate(columns, axis=1).astype(F32))
-    out_grad = (
-        jnp.concatenate([grads[:, 3 * heads_wide :] for grads in attention_grads], axis=1)
-        .astype(F32)
-        .T
-    )
-    own = (member * 4 + feat).astype(jnp.int32).reshape(1)
-    terms, gain_attn_part = input_terms(grad_packed, attention_weights, x_all, gain_one, grad_middle, own)
-    input_grad = scatter_block(5, terms)
-    out_rows = add_own_rows(out_rows.astype(BF16), middle)
-    out_rows, feed_sums[1] = lax.optimization_barrier((out_rows, feed_sums[1]))
-    outcome = scatter_block(4, out_rows)
-    feed_grads = [pair_finish(total) for total in feed_sums]
-
-    def feed_grad(part):
-        columns = slice(part * chunk, (part + 1) * chunk)
-        return jnp.concatenate(
-            [feed_grads[c][which][:, columns] for which in range(2) for c in range(CHUNKS)],
-            axis=1,
-        ).astype(F32)
-
-    gate_grad, up_grad, down_grad = feed_grad(0), feed_grad(1), feed_grad(2).T
-
-    sums = jnp.concatenate([gain_attn_part, gain_ffn_part])
-    for change in (core_swap, x_swap):
-        sums = sums + change(sums)
-    bit = 1
-    while bit < tok_size:
-        sums = sums + lax.ppermute(sums, "tok", [(i, i ^ bit) for i in range(tok_size)])
-        bit *= 2
-    gain_grads = lax.dynamic_slice_in_dim(sums, feat * wide, wide, 1)
+        for part in range(3)
+    ]
+    attention_plan.append([(0, 3 * heads_wide, heads_wide, 0)])
+    part_grads = assemble(attention_plan, 3, [attention_sum], [other_half(attention_sum)])
     return (
         outcome,
         input_grad,
         gain_grads[0],
         gain_grads[1],
         *part_grads,
-        out_grad,
         gate_grad,
         up_grad,
         down_grad,

time: 756 us -> 685 us (0.906)
  Pallas kernels: 391 us -> 513 us
  matrix products: 181 us -> 82.2 us
  waiting for transfers between devices: 60.3 us -> 22.8 us
  other arithmetic: 47.1 us -> 14.1 us
  local copies, waits for them, and re-layouts: 40.6 us -> 28.5 us
  starting transfers between devices: 14.1 us -> 5.63 us
    pallas_call x0 -> x8, Pallas kernels: none -> 89.5 us  [the longest x4 45.3 us: columns_back(): pl.pallas_call(columns_step, grid_spec=pltpu.PrefetchScalarGridSpec(num_s...]
    dot_general x5 -> x1, matrix products: 63.3 us -> 7.31 us  [right_trans(): lax.dot_general(left, right, (((1,), (1,)), ((), ())), preferred_element_...]
    dot_general x6 -> x2, matrix products: 60.6 us -> 16.6 us  [product(): return jnp.dot(left, right, preferred_element_type=F32)]
    pallas_call x5 -> x6, Pallas kernels: 344 us -> 377 us  [call(): pl.pallas_call(kernel, out_shape=outputs, in_specs=[pl.BlockSpec(memory_s...]
    ppermute x6 -> x3, waiting for transfers between devices: 29.1 us -> 5.38 us  [swap(): return lax.ppermute(value, 'tok', [(i, i ^ 1) for i in range(tok_size)])]
    select_n x5 -> x0, other arithmetic: 21.8 us -> none  [the longest x3 18.7 us: pair_blocks(): jnp.where(member == 0, jnp.concatenate([own, other]), jnp.concatenate([ot...]
    all_gather x3, waiting for transfers between devices: 28 us -> 10.1 us  [ring_gather(): lax.all_gather(shard, 'tok', axis=0, tiled=True, axis_index_groups=groups)]
    unnamed x98 -> x76, local copies, waits for them, and re-layouts: 29.6 us -> 23.4 us
  transfers between devices with their start and end apart: 19 -> 11, of which waited for: 6 -> 4; matrix products, arithmetic and copies ran while one was open for 32% -> 15% of each run, Pallas kernels for 52% -> 73%
where the time goes in v4:
time: 685 us; the launch traced here: 681 us
  Pallas kernels  513 us (75%)
  matrix products  82.2 us (12%)
  local copies, waits for them, and re-layouts  28.5 us (4%)
  waiting for transfers between devices  22.8 us (3%)
  between operations  14.8 us (2%)
  other arithmetic  14.1 us (2%)
    pallas_call x6, Pallas kernels, call(): pl.pallas_call(kernel, out_shape=outputs, in_specs=[pl.BlockSpec(memory_s...  377 us
    dot_general x6, matrix products, left_trans(): lax.dot_general(left, right, (((0,), (0,)), ((), ())), preferred_element_...  58.2 us
    pallas_call x4, Pallas kernels, columns_back(): pl.pallas_call(columns_step, grid_spec=pltpu.PrefetchScalarGridSpec(num_s...  45.3 us
    pallas_call x2, Pallas kernels, feed_forward(): pl.pallas_call(feed_step, grid=(total // tile,), in_specs=[rows, rows, we...  38.5 us
    unnamed x76, local copies, waits for them, and re-layouts  23.4 us
    pallas_call x1, Pallas kernels, input_terms(): pl.pallas_call(input_terms_step, grid_spec=pltpu.PrefetchScalarGridSpec(n...  18 us
    pallas_call x1, Pallas kernels, attend_back(): pl.pallas_call(attend_back_kernel, grid=(sequences, pairs), out_shape=jax...  17.7 us
    dot_general x2, matrix products, product(): return jnp.dot(left, right, preferred_element_type=F32)  16.6 us
  transfers between devices with their start and end apart: 11, of which 4 were waited for; matrix products, arithmetic and copies ran while one was open for 15% of the time, Pallas kernels for 73%

profile of v4, /device:TPU:0, one launch (start us, length us, event | category | flops | bytes accessed | tf_op | source)
XLA Modules:
  0.0 681.1 jit_solution(15459511764821410954)
XLA Ops:
  11.2 16.4 %swap_gather.3 = bf16[512,1024]{1,0:T(8,128)(2,1)} custom-call(bf16[256,512]{1,0:T(8,128)(2,1)S(1)} %copy-done.20, bf16[256,512]{1,0:T(8,128)(2,1)S(1)} %copy-done.21, bf16[256,512]{1,0:T(8,128)(2,1)S(1)} %copy-done.22, bf16[256,512]{1,0:T(8,128)(2,1)S(1)} %bitcast.34), custom_call_target="tpu_custom_call" | custom-call | flops 15000000512 | bytes 150000000 | tf_op jit(solution)/shard_map/swap_gather/pallas_call | solution.py:414
  30.4 54.8 %swap_gather.4 = (bf16[512,1536]{1,0:T(8,128)(2,1)}, bf16[2048,2048]{1,0:T(8,128)(2,1)}) custom-call(bf16[256,2048]{1,0:T(8,128)(2,1)S(1)} %copy-done.16, bf16[256,2048]{1,0:T(8,128)(2,1)S(1)} %copy-done.17, bf16[256,2048]{1,0:T(8,128)(2,1)S(1)} %bitcast.32, bf16[1024,512]{1,0:T(8,128)(2,1)S(1)} %copy-done.15), custom_call_target="tpu_custom_call" | custom-call | flops 49999998976 | bytes 500000000 | tf_op jit(solution)/shard_map/swap_gather/pallas_call | solution.py:414
  88.2 56.0 %swap_gather.5 = (bf16[512,1536]{1,0:T(8,128)(2,1)}, bf16[2048,2048]{1,0:T(8,128)(2,1)}) custom-call(bf16[256,2048]{1,0:T(8,128)(2,1)S(1)} %copy-done.16, bf16[256,2048]{1,0:T(8,128)(2,1)S(1)} %copy-done.18, bf16[256,2048]{1,0:T(8,128)(2,1)S(1)} %bitcast.33, bf16[1024,512]{1,0:T(8,128)(2,1)S(1)} %copy-done.19), custom_call_target="tpu_custom_call" | custom-call | flops 49999998976 | bytes 500000000 | tf_op jit(solution)/shard_map/swap_gather/pallas_call | solution.py:414
  144.4 5.1 fusion
  150.7 2.6 collective-permute-done.1
  153.3 10.7 %convolution_convert_fusion.3.packed_ref = bf16[2048,768]{1,0:T(8,128)(2,1)S(1)} fusion(bf16[2048,1024]{1,0:T(8,128)(2,1)} %all-gather.4.cloned.1.call-done.qkv_ref, bf16[2048,2048]{1,0:T(8,128)(2,1)} %get-tuple-element.63.x_ref, f32[2048]{0:T(1024)S(1)} %bitcast.35, f32[2048]{0:T(1024)S(1)} %add_rsqrt_fusion), kind=kOutput, calls=%fused_computation.11 | convolution fusion | flops 6460801024 | bytes 14696448 | tf_op jit(solution)/shard_map/dot_general | solution.py:33
  164.0 11.3 %attend.1 = (bf16[2048,256]{1,0:T(8,128)(2,1)S(1)}, f32[2,2,2,1024]{3,2,1,0:T(2,128)S(1)}) custom-call(bf16[2048,768]{1,0:T(8,128)(2,1)S(1)} %convolution_convert_fusion.3.packed_ref), custom_call_target="tpu_custom_call" | custom-call | flops 1073741824 | bytes 6291456 | tf_op jit(solution)/shard_map/attend/pallas_call | solution.py:106
  175.4 7.3 %convolution_convert_fusion.terms_ref = bf16[2048,2048]{1,0:T(8,128)(2,1)} fusion(bf16[2048,256]{1,0:T(8,128)(2,1)S(1)} %get-tuple-element.65.out_ref, bf16[2048,1024]{1,0:T(8,128)(2,1)} %all-gather.4.cloned.1.call-done.qkv_ref), kind=kOutput, calls=%fused_computation.5 | convolution fusion | flops 2151677952 | bytes 10485760 | tf_op jit(solution)/shard_map/dot_general | solution.py:27
  182.7 80.6 %middle_step.1 = (bf16[2048,2048]{1,0:T(8,128)(2,1)}, f32[256,2048]{1,0:T(8,128)S(1)}, f32[256,128]{1,0:T(8,128)S(1)}) custom-call(bf16[2048,2048]{1,0:T(8,128)(2,1)} %convolution_convert_fusion.terms_ref, bf16[2048,2048]{1,0:T(8,128)(2,1)} %get-tuple-element.63.x_ref, f32[1,2048]{1,0:T(1,128)S(1)} %get-tuple-element.111.gain_ref), custom_call_target="tpu_custom_call" | custom-call | flops 70000001024 | bytes 700000000 | tf_op jit(solution)/shard_map/middle_step/pallas_call | solution.py:414
  263.3 19.2 %feed_forward.2 = (bf16[2048,512]{1,0:T(8,128)(2,1)S(1)}, bf16[2048,1024]{1,0:T(8,128)(2,1)}) custom-call(bf16[2048,2048]{1,0:T(8,128)(2,1)} %get-tuple-element.66.normed_ref, bf16[2048,2048]{1,0:T(8,128)(2,1)} %get-tuple-element.68.cot_ref, bf16[2048,1536]{1,0:T(8,128)(2,1)} %all-gather.8.cloned.1.call-done.gate_ref.up_ref.down_ref.right_ref, ...), custom_call_target="tpu_custom_call" | custom-call | flops 12884901888 | bytes 29360128 | tf_op jit(solution)/shard_map/feed_forward/pallas_call | solution.py:869
  282.5 8.2 %columns_back.5.refs_0_ = bf16[2048,2048]{1,0:T(8,128)(2,1)} custom-call(s32[1]{0:T(128)} %bitcast.own_ref, bf16[2048,512]{1,0:T(8,128)(2,1)S(1)} %get-tuple-element.72.left_ref, bf16[2048,1536]{1,0:T(8,128)(2,1)} %all-gather.8.cloned.1.call-done.gate_ref.up_ref.down_ref.right_ref), custom_call_target="tpu_custom_call" | custom-call | flops 4294967296 | bytes 12582912 | tf_op jit(solution)/shard_map/columns_back/pallas_call | solution.py:925
  290.7 8.8 %convolution_convert_fusion.6 = bf16[2048,512]{1,0:T(8,128)(2,1)S(1)} fusion(bf16[2048,2048]{1,0:T(8,128)(2,1)} %get-tuple-element.68.cot_ref, bf16[2048,512]{1,0:T(8,128)(2,1)S(1)} %get-tuple-element.72.left_ref), kind=kOutput, calls=%fused_computation.15 | convolution fusion | flops 4296015872 | bytes 12582912 | tf_op jit(solution)/shard_map/dot_general | solution.py:21
  299.5 11.4 %convolution_convert_fusion.2 = bf16[2048,1024]{1,0:T(8,128)(2,1)S(1)} fusion(bf16[2048,2048]{1,0:T(8,128)(2,1)} %get-tuple-element.66.normed_ref, bf16[2048,1024]{1,0:T(8,128)(2,1)S(1)} %copy-done.30), kind=kOutput, calls=%fused_computation.10 | convolution fusion | flops 8592031744 | bytes 16777216 | tf_op jit(solution)/shard_map/dot_general | solution.py:21
  311.0 3.2 pad_maximum_fusion
  316.3 13.1 %columns_back.4.refs_0_ = bf16[2048,2048]{1,0:T(8,128)(2,1)} custom-call(s32[1]{0:T(128)} %bitcast.own_ref, bf16[2048,1024]{1,0:T(8,128)(2,1)S(1)} %copy-done.31, bf16[2048,1536]{1,0:T(8,128)(2,1)} %all-gather.8.cloned.1.call-done.gate_ref.up_ref.down_ref.right_ref), custom_call_target="tpu_custom_call" | custom-call | flops 8589934592 | bytes 16777216 | tf_op jit(solution)/shard_map/columns_back/pallas_call | solution.py:925
  329.4 10.1 %all-gather.6.cloned.1.call-done.gate_ref.up_ref.down_ref.right_ref = bf16[2048,1536]{1,0:T(8,128)(2,1)} async-done(((bf16[512,1536]{1,0:T(8,128)(2,1)}), bf16[2048,1536]{1,0:T(8,128)(2,1)}) %all-gather.6.cloned.1.call-update) | async-done | bytes 6291472 | tf_op jit(solution)/shard_map/all_gather | solution.py:967
  339.5 19.3 %feed_forward.3 = (bf16[2048,512]{1,0:T(8,128)(2,1)S(1)}, bf16[2048,1024]{1,0:T(8,128)(2,1)}) custom-call(bf16[2048,2048]{1,0:T(8,128)(2,1)} %get-tuple-element.66.normed_ref, bf16[2048,2048]{1,0:T(8,128)(2,1)} %get-tuple-element.68.cot_ref, bf16[2048,1536]{1,0:T(8,128)(2,1)} %all-gather.6.cloned.1.call-done.gate_ref.up_ref.down_ref.right_ref, ...), custom_call_target="tpu_custom_call" | custom-call | flops 12884901888 | bytes 29360128 | tf_op jit(solution)/shard_map/feed_forward/pallas_call | solution.py:869
  358.9 9.3 %convolution_convert_fusion.5 = bf16[2048,512]{1,0:T(8,128)(2,1)S(1)} fusion(bf16[2048,2048]{1,0:T(8,128)(2,1)} %get-tuple-element.68.cot_ref, bf16[2048,512]{1,0:T(8,128)(2,1)S(1)} %get-tuple-element.91.left_ref), kind=kOutput, calls=%fused_computation.14 | convolution fusion | flops 4296015872 | bytes 12582912 | tf_op jit(solution)/shard_map/dot_general | solution.py:21
  368.1 11.4 %convolution_convert_fusion.1 = bf16[2048,1024]{1,0:T(8,128)(2,1)S(1)} fusion(bf16[2048,2048]{1,0:T(8,128)(2,1)} %get-tuple-element.66.normed_ref, bf16[2048,1024]{1,0:T(8,128)(2,1)S(1)} %copy-done.26), kind=kOutput, calls=%fused_computation.9 | convolution fusion | flops 8592031744 | bytes 16777216 | tf_op jit(solution)/shard_map/dot_general | solution.py:21
  379.5 3.2 pad_maximum_fusion.1
  384.9 13.7 %columns_back.6.terms_ref = bf16[2048,2048]{1,0:T(8,128)(2,1)} custom-call(s32[1]{0:T(128)} %bitcast.own_ref, bf16[2048,1024]{1,0:T(8,128)(2,1)S(1)} %copy-done.27, bf16[2048,1536]{1,0:T(8,128)(2,1)} %all-gather.6.cloned.1.call-done.gate_ref.up_ref.down_ref.right_ref, bf16[2048,2048]{1,0:T(8,128)(2,1)} %columns_back.4.refs_0_), custom_call_target="tpu_custom_call" | custom-call | flops 8589934592 | bytes 16777216 | tf_op jit(solution)/shard_map/columns_back/pallas_call | solution.py:925
  399.1 81.8 %middle_back_step.1 = (bf16[2048,2048]{1,0:T(8,128)(2,1)}, f32[256,2048]{1,0:T(8,128)S(1)}, f32[1,2048]{1,0:T(1,128)S(1)}) custom-call(bf16[2048,2048]{1,0:T(8,128)(2,1)} %columns_back.6.terms_ref, bf16[2048,2048]{1,0:T(8,128)(2,1)} %get-tuple-element.68.cot_ref, f32[256,2048]{1,0:T(8,128)S(1)} %get-tuple-element.78.middle_ref.refs_1_, ...), custom_call_target="tpu_custom_call" | custom-call | flops 70000001024 | bytes 700000000 | tf_op jit(solution)/shard_map/middle_back_step/pallas_call | solution.py:414
  483.8 6.0 convolution_convert_fusion.8.grad_ref
  489.8 17.7 %attend_back.1.grad_ref = bf16[2048,768]{1,0:T(8,128)(2,1)S(1)} custom-call(bf16[2048,768]{1,0:T(8,128)(2,1)} %copy-done.23, bf16[2048,256]{1,0:T(8,128)(2,1)S(1)} %copy-done.6, bf16[2048,256]{1,0:T(8,128)(2,1)S(1)} %convolution_convert_fusion.8.grad_ref, f32[2,2,2,1024]{3,2,1,0:T(2,128)S(1)} %get-tuple-element.83.lse_ref), custom_call_target="tpu_custom_call" | custom-call | flops 2684354560 | bytes 9437184 | tf_op jit(solution)/shard_map/attend_back/pallas_call | solution.py:133
  507.6 7.2 %convolution_convert_fusion.7 = bf16[2048,256]{1,0:T(8,128)(2,1)S(1)} fusion(bf16[2048,2048]{1,0:T(8,128)(2,1)} %get-tuple-element.82, bf16[2048,256]{1,0:T(8,128)(2,1)S(1)} %copy-done.6), kind=kOutput, calls=%fused_computation.16 | convolution fusion | flops 2148007936 | bytes 10485760 | tf_op jit(solution)/shard_map/dot_general | solution.py:21
  514.8 10.1 %convolution_convert_fusion.4 = bf16[2048,768]{1,0:T(8,128)(2,1)S(1)} fusion(bf16[2048,768]{1,0:T(8,128)(2,1)S(1)} %attend_back.1.grad_ref, bf16[2048,2048]{1,0:T(8,128)(2,1)} %get-tuple-element.63.x_ref, f32[2048]{0:T(1024)S(1)} %bitcast.36, f32[2048]{0:T(1024)S(1)} %copy-done.33), kind=kOutput, calls=%fused_computation.12 | convolution fusion | flops 6460801024 | bytes 14696448 | tf_op jit(solution)/shard_map/dot_general | solution.py:21
  531.1 18.0 %input_terms.1 = (bf16[2048,2048]{1,0:T(8,128)(2,1)}, f32[1,2048]{1,0:T(1,128)S(1)}) custom-call(s32[1]{0:T(128)} %bitcast.own_ref, bf16[2048,768]{1,0:T(8,128)(2,1)S(1)} %copy-done.25, bf16[2048,1024]{1,0:T(8,128)(2,1)} %all-gather.4.cloned.1.call-done.qkv_ref, bf16[2048,2048]{1,0:T(8,128)(2,1)} %get-tuple-element.63.x_ref, f32[1,2048]{1,0:T(1,128)S(1)} %copy-done.14, ...), custom_call_target="tpu_custom_call" | custom-call | flops 6442450944 | bytes 25165824 | tf_op jit(solution)/shard_map/input_terms/pallas_call | solution.py:814
  549.1 10.3 %columns_back.7.refs_0_ = bf16[2048,2048]{1,0:T(8,128)(2,1)} custom-call(s32[1]{0:T(128)} %bitcast.own_ref, bf16[2048,512]{1,0:T(8,128)(2,1)S(1)} %copy-done.4, bf16[2048,1536]{1,0:T(8,128)(2,1)} %all-gather.6.cloned.1.call-done.gate_ref.up_ref.down_ref.right_ref, bf16[2048,2048]{1,0:T(8,128)(2,1)} %columns_back.5.refs_0_, ...), custom_call_target="tpu_custom_call" | custom-call | flops 4294967296 | bytes 12582912 | tf_op jit(solution)/shard_map/columns_back/pallas_call | solution.py:925
  559.4 4.7 reduce-scatter.6.cloned.1.call-done.refs_1_
  567.7 86.9 %scatter_outputs.1 = (bf16[1024,512]{1,0:T(8,128)(2,1)S(1)}, bf16[1024,512]{1,0:T(8,128)(2,1)S(1)}, f32[2,512]{1,0:T(2,128)S(1)}) custom-call(f32[2,2048]{1,0:T(2,128)S(1)} %pad_maximum_fusion.5.vector_ref, bf16[2048,2048]{1,0:T(8,128)(2,1)} %columns_back.7.refs_0_, bf16[2048,2048]{1,0:T(8,128)(2,1)} %get-tuple-element.95.refs_1_), custom_call_target="tpu_custom_call" | custom-call | flops 60000002048 | bytes 600000000 | tf_op jit(solution)/shard_map/scatter_outputs/pallas_call | solution.py:414
  661.1 4.3 assemble_grads.3
  665.4 5.4 collective-permute-done.3.refs_1_
  (114 shorter events, 38.4 us)
Async XLA Ops:
  7.2 146.2 %all-gather.4.cloned.1.call-start = ((), (), s32[]{:S(2)}) async-start(), calls=%async_computation.3 | async-start | bytes 5242880 | tf_op jit(solution)/shard_map/all_gather | solution.py:967
  11.2 18.0 %copy-start.15 = (bf16[1024,512]{1,0:T(8,128)(2,1)S(1)}, bf16[1024,512]{1,0:T(8,128)(2,1)}, u32[]{:S(2)}) copy-start(bf16[1024,512]{1,0:T(8,128)(2,1)} %refs_3_) | copy-start | bytes 3145732
  11.2 18.0 %copy-start.16 = (bf16[256,2048]{1,0:T(8,128)(2,1)S(1)}, bf16[256,2048]{1,0:T(8,128)(2,1)}, u32[]{:S(2)}) copy-start(bf16[256,2048]{1,0:T(8,128)(2,1)} %refs_0_.5) | copy-start | bytes 3145732
  27.6 235.7 %all-gather.8.cloned.1.call-start = ((), (), s32[]{:S(2)}) async-start(), calls=%async_computation.5 | async-start | bytes 7864320 | tf_op jit(solution)/shard_map/all_gather | solution.py:967
  30.4 54.9 %copy-start.34 = (f32[512]{0:T(512)S(1)}, f32[512]{0:T(512)}, u32[]{:S(2)}) copy-start(f32[512]{0:T(512)} %param.17) | copy-start | bytes 6148
  30.4 54.9 %copy-start.35 = (f32[512]{0:T(512)S(1)}, f32[512]{0:T(512)}, u32[]{:S(2)}) copy-start(f32[512]{0:T(512)} %param.12) | copy-start | bytes 6148
  85.2 254.2 %all-gather.6.cloned.1.call-start = ((), (), s32[]{:S(2)}) async-start(), calls=%async_computation.4 | async-start | bytes 7864320 | tf_op jit(solution)/shard_map/all_gather | solution.py:967
  85.3 64.1 %collective-permute-start = (f32[2,512]{1,0:T(2,128)S(1)}, f32[2,512]{1,0:T(2,128)S(1)}, u32[]{:S(2)}, u32[]{:S(2)}) collective-permute-start(f32[2,512]{1,0:T(2,128)S(1)} %get-tuple-element.120), channel_id=1, source_target_pairs={{0,1},{1,0},{2,3},{3,2},{4,5},{5,4},{6,7},{7,6},{8,9},{9,8},{10,11... | collective-permute-start | bytes 12296 | tf_op jit(solution)/shard_map/ppermute | solution.py:964
  144.3 338.0 %reduce-scatter.4.cloned.1.call-start = ((), (), s32[]{:S(2)}) async-start(), calls=%async_computation.6 | async-start | bytes 7864320 | tf_op jit(solution)/shard_map/reduce_scatter | solution.py:970
  149.5 3.7 collective-permute-start.1
  153.3 10.7 %copy-start.13 = (f32[1,2048]{1,0:T(1,128)}, f32[1,2048]{1,0:T(1,128)S(1)}, u32[]{:S(2)}) copy-start(f32[1,2048]{1,0:T(1,128)S(1)} %get-tuple-element.112.gain_ref) | copy-start | bytes 24580
  164.0 18.6 %copy-start.23 = (bf16[2048,768]{1,0:T(8,128)(2,1)}, bf16[2048,768]{1,0:T(8,128)(2,1)S(1)}, u32[]{:S(2)}) copy-start(bf16[2048,768]{1,0:T(8,128)(2,1)S(1)} %convolution_convert_fusion.3.packed_ref) | copy-start | bytes 9437188
  175.3 7.3 %copy-start.5 = (bf16[2048,256]{1,0:T(8,128)(2,1)}, bf16[2048,256]{1,0:T(8,128)(2,1)S(1)}, u32[]{:S(2)}) copy-start(bf16[2048,256]{1,0:T(8,128)(2,1)S(1)} %get-tuple-element.65.out_ref) | copy-start | bytes 3145732
  290.7 8.8 %copy-start.30 = (bf16[2048,1024]{1,0:T(8,128)(2,1)S(1)}, bf16[2048,1024]{1,0:T(8,128)(2,1)}, u32[]{:S(2)}) copy-start(bf16[2048,1024]{1,0:T(8,128)(2,1)} %get-tuple-element.71.left_ref) | copy-start | bytes 12582916
  339.5 224.6 %reduce-scatter.6.cloned.1.call-start = ((), (), s32[]{:S(2)}) async-start(), calls=%async_computation.7 | async-start | bytes 7864320 | tf_op jit(solution)/shard_map/reduce_scatter | solution.py:970
  358.8 9.3 %copy-start.3 = (bf16[2048,512]{1,0:T(8,128)(2,1)}, bf16[2048,512]{1,0:T(8,128)(2,1)S(1)}, u32[]{:S(2)}) copy-start(bf16[2048,512]{1,0:T(8,128)(2,1)S(1)} %get-tuple-element.91.left_ref) | copy-start | bytes 6291460
  358.8 9.3 %copy-start.26 = (bf16[2048,1024]{1,0:T(8,128)(2,1)S(1)}, bf16[2048,1024]{1,0:T(8,128)(2,1)}, u32[]{:S(2)}) copy-start(bf16[2048,1024]{1,0:T(8,128)(2,1)} %get-tuple-element.74.left_ref) | copy-start | bytes 12582916
  398.7 257.9 %reduce-scatter.8.cloned.1.call-start = ((), (), s32[]{:S(2)}) async-start(), calls=%async_computation.8 | async-start | bytes 5242880 | tf_op jit(solution)/shard_map/reduce_scatter | solution.py:970
  483.5 6.3 copy-start.6
  483.5 31.3 %collective-permute-start.2 = (bf16[256,1536]{1,0:T(8,128)(2,1)S(1)}, bf16[256,1536]{1,0:T(8,128)(2,1)S(1)}, u32[]{:S(2)}, u32[]{:S(2)}) collective-permute-start(bf16[256,1536]{1,0:T(8,128)(2,1)S(1)} %constant_dynamic-slice_fusion.2), channel_id=1, source_target_pairs={{0,4},{4,0},{8,12},{12,8},{16,20},{20,16},{24,28},{28,24},{1,5},{5... | collective-permute-start | bytes 2359304 | tf_op jit(solution)/shard_map/ppermute | solution.py:958
  507.6 7.2 %copy-start.24 = (bf16[2048,768]{1,0:T(8,128)(2,1)}, bf16[2048,768]{1,0:T(8,128)(2,1)S(1)}, u32[]{:S(2)}) copy-start(bf16[2048,768]{1,0:T(8,128)(2,1)S(1)} %attend_back.1.grad_ref) | copy-start | bytes 9437188
  507.6 7.2 %copy-start.14 = (f32[1,2048]{1,0:T(1,128)S(1)}, f32[1,2048]{1,0:T(1,128)}, u32[]{:S(2)}) copy-start(f32[1,2048]{1,0:T(1,128)} %copy-done.13) | copy-start | bytes 24580
  507.6 7.2 %copy-start.33 = (f32[2048]{0:T(1024)S(1)}, f32[2048]{0:T(1024)}, u32[]{:S(2)}) copy-start(f32[2048]{0:T(1024)} %copy-done.32) | copy-start | bytes 24580
  514.8 10.2 %copy-start.11 = (bf16[256,1536]{1,0:T(8,128)(2,1)}, bf16[256,1536]{1,0:T(8,128)(2,1)S(1)}, u32[]{:S(2)}) copy-start(bf16[256,1536]{1,0:T(8,128)(2,1)S(1)} %collective-permute-done.2.refs_2_) | copy-start | bytes 2359300
  531.1 18.0 %copy-start.4 = (bf16[2048,512]{1,0:T(8,128)(2,1)S(1)}, bf16[2048,512]{1,0:T(8,128)(2,1)}, u32[]{:S(2)}) copy-start(bf16[2048,512]{1,0:T(8,128)(2,1)} %copy-done.3) | copy-start | bytes 6291460
  566.2 93.8 %collective-permute-start.4 = (bf16[256,1536]{1,0:T(8,128)(2,1)}, bf16[256,1536]{1,0:T(8,128)(2,1)}, u32[]{:S(2)}, u32[]{:S(2)}) collective-permute-start(bf16[256,1536]{1,0:T(8,128)(2,1)} %constant_dynamic-slice_fusion), channel_id=1, source_target_pairs={{0,4},{4,0},{8,12},{12,8},{16,20},{20,16},{24,28},{28,24},{1,5},{5... | collective-permute-start | bytes 2359304 | tf_op jit(solution)/shard_map/ppermute | solution.py:958
  567.6 92.3 %copy-start = (bf16[512,1536]{1,0:T(8,128)(2,1)S(1)}, bf16[512,1536]{1,0:T(8,128)(2,1)}, u32[]{:S(2)}) copy-start(bf16[512,1536]{1,0:T(8,128)(2,1)} %reduce-scatter.4.cloned.1.call-done.refs_0_) | copy-start | bytes 4718596
  567.7 92.3 %copy-start.1 = (bf16[512,1536]{1,0:T(8,128)(2,1)S(1)}, bf16[512,1536]{1,0:T(8,128)(2,1)}, u32[]{:S(2)}) copy-start(bf16[512,1536]{1,0:T(8,128)(2,1)} %reduce-scatter.6.cloned.1.call-done.refs_1_) | copy-start | bytes 4718596
  656.6 14.2 %copy-start.2 = (bf16[512,1024]{1,0:T(8,128)(2,1)S(1)}, bf16[512,1024]{1,0:T(8,128)(2,1)}, u32[]{:S(2)}) copy-start(bf16[512,1024]{1,0:T(8,128)(2,1)} %reduce-scatter.8.cloned.1.call-done.refs_0_) | copy-start | bytes 3145732
  656.6 15.6 %copy-start.10 = (bf16[1024,512]{1,0:T(8,128)(2,1)S(1)}, bf16[1024,512]{1,0:T(8,128)(2,1)}, u32[]{:S(2)}) copy-start(bf16[1024,512]{1,0:T(8,128)(2,1)} %copy-done.9) | copy-start | bytes 3145732
  656.6 16.6 %copy-start.8 = (bf16[1024,512]{1,0:T(8,128)(2,1)S(1)}, bf16[1024,512]{1,0:T(8,128)(2,1)}, u32[]{:S(2)}) copy-start(bf16[1024,512]{1,0:T(8,128)(2,1)} %copy-done.7) | copy-start | bytes 3145732
  657.8 12.9 %collective-permute-start.3 = (bf16[256,1024]{1,0:T(8,128)(2,1)S(1)}, bf16[256,1024]{1,0:T(8,128)(2,1)S(1)}, u32[]{:S(2)}, u32[]{:S(2)}) collective-permute-start(bf16[256,1024]{1,0:T(8,128)(2,1)S(1)} %constant_dynamic-slice_fusion.1), channel_id=1, source_target_pairs={{0,4},{4,0},{8,12},{12,8},{16,20},{20,16},{24,28},{28,24},{1,5},{5... | collective-permute-start | bytes 1572872 | tf_op jit(solution)/shard_map/ppermute | solution.py:958
  (15 other events, 21.6 us)
Sparse Core Ops, SparseCore 0:
  27.7 81.0 all-gather.3
  110.4 113.8 all-gather.7
  225.8 113.5 all-gather.5
  341.6 108.9 reduce-scatter.3
  452.8 111.2 reduce-scatter.5
  566.2 78.3 reduce-scatter.7

commit v5 on v4

--- a/solution.py
+++ b/solution.py
@@ -11,10 +11,12 @@
 BF16 = jnp.bfloat16
 F32 = jnp.float32
 MESH = pl.DeviceIdType.MESH
+HBM = pltpu.MemorySpace.HBM
 VMEM = 48 << 20
-CHUNKS = 2
 FORWARD_BLOCK = 512
 BACK_BLOCK = 256
+WHOLE_VMEM = 62 << 20
+CHUNKS = (3, 1)
 
 
 def left_trans(left, right):
@@ -746,7 +748,7 @@
     )
 
 
-def assemble(plan, flipped_out, totals, others):
+def assemble(plan, flipped_out, totals, others, passed=()):
     count = len(totals)
     size = others[0].shape[0]
     shapes = []
@@ -756,7 +758,9 @@
 
     def assemble_grads(*refs):
         member = lax.rem(lax.axis_index("tok"), 2)
-        outs = refs[2 * count :]
+        outs = refs[2 * count + len(passed) :]
+        for i in range(len(passed)):
+            outs[len(plan) + i][...] = refs[2 * count + i][...]
         for index, pieces in enumerate(plan):
             half = sum(piece[2] for piece in pieces)
             for source, column, width, target in pieces:
@@ -772,15 +776,16 @@
 
     return pl.pallas_call(
         assemble_grads,
-        out_shape=[jax.ShapeDtypeStruct(shape, F32) for shape in shapes],
-        in_specs=[pl.BlockSpec(memory_space=pltpu.VMEM)] * (2 * count),
-        out_specs=[pl.BlockSpec(memory_space=pltpu.VMEM)] * len(plan),
+        out_shape=[jax.ShapeDtypeStruct(shape, F32) for shape in shapes]
+        + [jax.ShapeDtypeStruct(array.shape, array.dtype) for array in passed],
+        in_specs=[pl.BlockSpec(memory_space=pltpu.VMEM)] * (2 * count + len(passed)),
+        out_specs=[pl.BlockSpec(memory_space=pltpu.VMEM)] * (len(plan) + len(passed)),
         compiler_params=pltpu.CompilerParams(vmem_limit_bytes=VMEM),
         cost_estimate=pl.CostEstimate(
             flops=0, transcendentals=0, bytes_accessed=8 * size * 2 * sum(t.shape[1] for t in totals)
         ),
         name="assemble_grads",
-    )(*totals, *others)
+    )(*totals, *others, *passed)
 
 
 def input_terms(grad_packed, weights, x_all, gain, grad_middle, own):
@@ -976,7 +981,9 @@
         return swap(lax.dynamic_slice_in_dim(total, (1 - member) * size, size, 0))
 
     heads_wide = w_query.shape[1] // 2
-    chunk = w_gate.shape[1] // 2 // CHUNKS
+    hidden_wide = w_gate.shape[1] // 2
+    chunks = [hidden_wide * part // sum(CHUNKS) for part in CHUNKS]
+    lefts = [sum(chunks[:c]) for c in range(len(chunks))]
     attention_pieces = [
         (part, left, pair_width, 3 * left + part * pair_width)
         for left in range(0, heads_wide, pair_width)
@@ -992,7 +999,7 @@
     for c, shard in enumerate((tokens_after, cotangent)):
         if c:
             shard, wholes[0] = lax.optimization_barrier((shard, wholes[0]))
-        pieces = [(part, c * chunk, chunk, part * chunk) for part in range(3)]
+        pieces = [(part, lefts[c], chunks[c], part * chunks[c]) for part in range(3)]
         start, whole = swap_and_gather(1 + c, feed, pieces, shard)
         wholes.append(whole)
         feed_weights.append(ring_gather(start))
@@ -1020,34 +1027,40 @@
     own = (member * 4 + feat).astype(jnp.int32).reshape(1)
     feed_sums = []
     grad_normed_two = out_rows = None
-    for c in range(CHUNKS):
-        if c:
-            feed_weights[c], feed_terms, grad_normed_two, out_rows = lax.optimization_barrier(
-                (feed_weights[c], feed_terms, grad_normed_two, out_rows)
-            )
-            feed_sums.append(ring_scatter(feed_terms))
-        hidden, grad_both = feed_forward(normed_two, cot_rows, feed_weights[c], chunk)
-        grad_normed_two = columns_back(grad_both, feed_weights[c], 0, grad_normed_two, own)
-        feed_terms = jnp.concatenate(
+
+    def terms_of(grad_both, hidden):
+        return jnp.concatenate(
             [
                 left_trans(normed_two, grad_both).astype(BF16),
                 left_trans(cot_rows, hidden).astype(BF16),
             ],
             axis=1,
         )
-        if c + 1 < CHUNKS:
-            out_rows = columns_back(hidden, feed_weights[c], 2, out_rows, own)
-    grad_normed_two, feed_terms = lax.optimization_barrier((grad_normed_two, feed_terms))
-    feed_sums.append(ring_scatter(feed_terms))
+
+    hiddens = []
+    for c in range(len(chunks)):
+        if c:
+            feed_weights[c], grad_normed_two = lax.optimization_barrier(
+                (feed_weights[c], grad_normed_two)
+            )
+        hidden, grad_both = feed_forward(normed_two, cot_rows, feed_weights[c], chunks[c])
+        hiddens.append(hidden)
+        if c + 1 < len(chunks):
+            feed_terms = terms_of(grad_both, hidden)
+            feed_terms, grad_both = lax.optimization_barrier((feed_terms, grad_both))
+            feed_sums.append(ring_scatter(feed_terms))
+        grad_normed_two = columns_back(grad_both, feed_weights[c], 0, grad_normed_two, own)
     grad_mid_rows, grad_middle, gain_ffn_part = middle_back(
         4, grad_normed_two, cot_rows, middle, factor_two, gain_two
     )
 
-    grad_mid_rows, feed_sums[0] = lax.optimization_barrier((grad_mid_rows, feed_sums[0]))
+    hidden, grad_both, grad_mid_rows = lax.optimization_barrier((hidden, grad_both, grad_mid_rows))
+    feed_terms = terms_of(grad_both, hidden)
+    grad_mid_rows, feed_terms = lax.optimization_barrier((grad_mid_rows, feed_terms))
+    feed_sums.append(ring_scatter(feed_terms))
+
     grad_attended = product(grad_mid_rows, out_proj).astype(BF16)
     grad_packed = attend_back(packed, attended, grad_attended, log_sums)
-    first_other = other_half(feed_sums[0])
-    grad_packed, first_other = lax.optimization_barrier((grad_packed, first_other))
     attention_terms = jnp.concatenate(
         [
             left_trans(normed, grad_packed).astype(BF16),
@@ -1058,19 +1071,23 @@
     attention_terms, grad_packed = lax.optimization_barrier((attention_terms, grad_packed))
     attention_sum = ring_scatter(attention_terms)
     terms, gain_attn_part = input_terms(grad_packed, attention_weights, x_all, gain_one, grad_middle, own)
-    hidden, terms = lax.optimization_barrier((hidden, terms))
-    out_rows = columns_back(hidden, feed_weights[-1], 2, out_rows, own, middle)
-    out_rows, feed_sums[1] = lax.optimization_barrier((out_rows, feed_sums[1]))
+    hiddens[0], terms, feed_sums[0] = lax.optimization_barrier((hiddens[0], terms, feed_sums[0]))
+    for c in range(len(chunks)):
+        last = middle if c + 1 == len(chunks) else None
+        out_rows = columns_back(hiddens[c], feed_weights[c], 2, out_rows, own, last)
     outcome, input_grad, gain_grads = scatter_blocks(
         5, tok_size // 2, jnp.concatenate([gain_attn_part, gain_ffn_part]), out_rows, terms
     )
-    outcome, attention_sum = lax.optimization_barrier((outcome, attention_sum))
-
+    feed_others = [other_half(feed_sums[0])]
+    outcome, feed_sums[1] = lax.optimization_barrier((outcome, feed_sums[1]))
+    feed_others.append(other_half(feed_sums[1]))
+    feed_others[1], attention_sum = lax.optimization_barrier((feed_others[1], attention_sum))
     feed_plan = [
-        [(c, part * chunk, chunk, c * chunk) for c in range(CHUNKS)] for part in range(3)
+        [(c, part * chunks[c], chunks[c], lefts[c]) for c in range(len(chunks))]
+        for part in range(3)
     ]
-    gate_grad, up_grad, down_grad = assemble(
-        feed_plan, 2, feed_sums, [first_other, other_half(feed_sums[1])]
+    gate_grad, up_grad, down_grad, outcome, input_grad = assemble(
+        feed_plan, 2, feed_sums, feed_others, (outcome, input_grad)
     )
     attention_plan = [
         [
@@ -1080,7 +1097,11 @@
         for part in range(3)
     ]
     attention_plan.append([(0, 3 * heads_wide, heads_wide, 0)])
-    part_grads = assemble(attention_plan, 3, [attention_sum], [other_half(attention_sum)])
+    attention_other = other_half(attention_sum)
+    attention_other, gate_grad, up_grad, down_grad, outcome, input_grad = lax.optimization_barrier(
+        (attention_other, gate_grad, up_grad, down_grad, outcome, input_grad)
+    )
+    part_grads = assemble(attention_plan, 3, [attention_sum], [attention_other])
     return (
         outcome,
         input_grad,

time: 685 us -> 678 us (0.990)
  Pallas kernels: 513 us -> 505 us
  waiting for transfers between devices: 22.8 us -> 29.8 us
  local copies, waits for them, and re-layouts: 28.5 us -> 21.6 us
    pallas_call x6, Pallas kernels: 377 us -> 365 us  [call(): pl.pallas_call(kernel, out_shape=outputs, in_specs=[pl.BlockSpec(memory_s...]
    unnamed x76 -> x72, local copies, waits for them, and re-layouts: 23.4 us -> 15.7 us
  transfers between devices with their start and end apart: 11 -> 11, of which waited for: 4 -> 5; matrix products, arithmetic and copies ran while one was open for 15% -> 15% of each run, Pallas kernels for 73% -> 73%
where the time goes in v5:
time: 678 us; the launch traced here: 669 us
  Pallas kernels  505 us (74%)
  matrix products  78.4 us (12%)
  waiting for transfers between devices  29.8 us (4%)
  local copies, waits for them, and re-layouts  21.6 us (3%)
  between operations  14.9 us (2%)
  other arithmetic  14.6 us (2%)
    pallas_call x6, Pallas kernels, call(): pl.pallas_call(kernel, out_shape=outputs, in_specs=[pl.BlockSpec(memory_s...  365 us
    dot_general x6, matrix products, left_trans(): lax.dot_general(left, right, (((0,), (0,)), ((), ())), preferred_element_...  54.7 us
    pallas_call x4, Pallas kernels, columns_back(): pl.pallas_call(columns_step, grid_spec=pltpu.PrefetchScalarGridSpec(num_s...  47.9 us
    pallas_call x2, Pallas kernels, feed_forward(): pl.pallas_call(feed_step, grid=(total // tile,), in_specs=[rows, rows, we...  38.2 us
    pallas_call x1, Pallas kernels, input_terms(): pl.pallas_call(input_terms_step, grid_spec=pltpu.PrefetchScalarGridSpec(n...  18 us
    pallas_call x1, Pallas kernels, attend_back(): pl.pallas_call(attend_back_kernel, grid=(sequences, pairs), out_shape=jax...  17.9 us
    dot_general x2, matrix products, product(): return jnp.dot(left, right, preferred_element_type=F32)  16.4 us
    unnamed x72, local copies, waits for them, and re-layouts  15.7 us
  transfers between devices with their start and end apart: 11, of which 5 were waited for; matrix products, arithmetic and copies ran while one was open for 15% of the time, Pallas kernels for 73%

profile of v5, /device:TPU:0, one launch (start us, length us, event | category | flops | bytes accessed | tf_op | source)
XLA Modules:
  0.0 669.0 jit_solution(12620477616786437037)
XLA Ops:
  11.2 16.4 %swap_gather.3 = bf16[512,1024]{1,0:T(8,128)(2,1)} custom-call(bf16[256,512]{1,0:T(8,128)(2,1)S(1)} %copy-done.17, bf16[256,512]{1,0:T(8,128)(2,1)S(1)} %copy-done.18, bf16[256,512]{1,0:T(8,128)(2,1)S(1)} %copy-done.19, bf16[256,512]{1,0:T(8,128)(2,1)S(1)} %bitcast.34), custom_call_target="tpu_custom_call" | custom-call | flops 15000000512 | bytes 150000000 | tf_op jit(solution)/shard_map/swap_gather/pallas_call | solution.py:416
  30.4 63.2 %swap_gather.4 = (bf16[512,2304]{1,0:T(8,128)(2,1)}, bf16[2048,2048]{1,0:T(8,128)(2,1)}) custom-call(bf16[256,2048]{1,0:T(8,128)(2,1)S(1)} %copy-done.13, bf16[256,2048]{1,0:T(8,128)(2,1)S(1)} %copy-done.14, bf16[256,2048]{1,0:T(8,128)(2,1)S(1)} %bitcast.32, bf16[1024,512]{1,0:T(8,128)(2,1)S(1)} %copy-done.12), custom_call_target="tpu_custom_call" | custom-call | flops 49999998976 | bytes 500000000 | tf_op jit(solution)/shard_map/swap_gather/pallas_call | solution.py:416
  96.7 47.6 %swap_gather.5 = (bf16[512,768]{1,0:T(8,128)(2,1)}, bf16[2048,2048]{1,0:T(8,128)(2,1)}) custom-call(bf16[256,2048]{1,0:T(8,128)(2,1)S(1)} %copy-done.13, bf16[256,2048]{1,0:T(8,128)(2,1)S(1)} %copy-done.15, bf16[256,2048]{1,0:T(8,128)(2,1)S(1)} %bitcast.33, bf16[1024,512]{1,0:T(8,128)(2,1)S(1)} %copy-done.16), custom_call_target="tpu_custom_call" | custom-call | flops 49999998976 | bytes 500000000 | tf_op jit(solution)/shard_map/swap_gather/pallas_call | solution.py:416
  144.4 5.2 fusion
  150.7 2.6 collective-permute-done.1
  153.4 10.2 %convolution_convert_fusion.2.packed_ref = bf16[2048,768]{1,0:T(8,128)(2,1)S(1)} fusion(bf16[2048,1024]{1,0:T(8,128)(2,1)} %all-gather.4.cloned.1.call-done.qkv_ref, bf16[2048,2048]{1,0:T(8,128)(2,1)} %get-tuple-element.71.x_ref, f32[2048]{0:T(1024)S(1)} %bitcast.35, f32[2048]{0:T(1024)S(1)} %add_rsqrt_fusion), kind=kOutput, calls=%fused_computation.9 | convolution fusion | flops 6460801024 | bytes 14696448 | tf_op jit(solution)/shard_map/dot_general | solution.py:35
  163.7 11.3 %attend.1 = (bf16[2048,256]{1,0:T(8,128)(2,1)S(1)}, f32[2,2,2,1024]{3,2,1,0:T(2,128)S(1)}) custom-call(bf16[2048,768]{1,0:T(8,128)(2,1)S(1)} %convolution_convert_fusion.2.packed_ref), custom_call_target="tpu_custom_call" | custom-call | flops 1073741824 | bytes 6291456 | tf_op jit(solution)/shard_map/attend/pallas_call | solution.py:108
  175.0 7.3 %convolution_convert_fusion.terms_ref = bf16[2048,2048]{1,0:T(8,128)(2,1)} fusion(bf16[2048,256]{1,0:T(8,128)(2,1)S(1)} %get-tuple-element.73.out_ref, bf16[2048,1024]{1,0:T(8,128)(2,1)} %all-gather.4.cloned.1.call-done.qkv_ref), kind=kOutput, calls=%fused_computation.6 | convolution fusion | flops 2151677952 | bytes 10485760 | tf_op jit(solution)/shard_map/dot_general | solution.py:29
  182.3 80.5 %middle_step.1 = (bf16[2048,2048]{1,0:T(8,128)(2,1)}, f32[256,2048]{1,0:T(8,128)S(1)}, f32[256,128]{1,0:T(8,128)S(1)}) custom-call(bf16[2048,2048]{1,0:T(8,128)(2,1)} %convolution_convert_fusion.terms_ref, bf16[2048,2048]{1,0:T(8,128)(2,1)} %get-tuple-element.71.x_ref, f32[1,2048]{1,0:T(1,128)S(1)} %get-tuple-element.127.gain_ref), custom_call_target="tpu_custom_call" | custom-call | flops 70000001024 | bytes 700000000 | tf_op jit(solution)/shard_map/middle_step/pallas_call | solution.py:416
  264.2 11.5 %all-gather.8.cloned.1.call-done.gate_ref.up_ref.down_ref.right_ref = bf16[2048,2304]{1,0:T(8,128)(2,1)} async-done(((bf16[512,2304]{1,0:T(8,128)(2,1)}), bf16[2048,2304]{1,0:T(8,128)(2,1)}) %all-gather.8.cloned.1.call-update) | async-done | bytes 9437200 | tf_op jit(solution)/shard_map/all_gather | solution.py:972
  275.7 27.0 %feed_forward.2 = (bf16[2048,768]{1,0:T(8,128)(2,1)S(1)}, bf16[2048,1536]{1,0:T(8,128)(2,1)}) custom-call(bf16[2048,2048]{1,0:T(8,128)(2,1)} %get-tuple-element.74.normed_ref, bf16[2048,2048]{1,0:T(8,128)(2,1)} %get-tuple-element.76.cot_ref, bf16[2048,2304]{1,0:T(8,128)(2,1)} %all-gather.8.cloned.1.call-done.gate_ref.up_ref.down_ref.right_ref, ...), custom_call_target="tpu_custom_call" | custom-call | flops 19327352832 | bytes 35651584 | tf_op jit(solution)/shard_map/feed_forward/pallas_call | solution.py:874
  302.7 10.4 %convolution_convert_fusion.4 = bf16[2048,768]{1,0:T(8,128)(2,1)S(1)} fusion(bf16[2048,2048]{1,0:T(8,128)(2,1)} %get-tuple-element.76.cot_ref, bf16[2048,768]{1,0:T(8,128)(2,1)S(1)} %get-tuple-element.100.left_ref), kind=kOutput, calls=%fused_computation.11 | convolution fusion | flops 6444023808 | bytes 14680064 | tf_op jit(solution)/shard_map/dot_general | solution.py:23
  313.2 14.3 %convolution_convert_fusion.1 = bf16[2048,1536]{1,0:T(8,128)(2,1)S(1)} fusion(bf16[2048,2048]{1,0:T(8,128)(2,1)S(1)} %copy-done.27, bf16[2048,1536]{1,0:T(8,128)(2,1)S(1)} %copy-done.32), kind=kOutput, calls=%fused_computation.7 | convolution fusion | flops 12888047616 | bytes 20971520 | tf_op jit(solution)/shard_map/dot_general | solution.py:23
  327.5 4.9 pad_maximum_fusion
  332.6 18.7 %columns_back.4.refs_0_ = bf16[2048,2048]{1,0:T(8,128)(2,1)} custom-call(s32[1]{0:T(128)} %bitcast.own_ref, bf16[2048,1536]{1,0:T(8,128)(2,1)} %get-tuple-element.81.left_ref, bf16[2048,2304]{1,0:T(8,128)(2,1)} %all-gather.8.cloned.1.call-done.gate_ref.up_ref.down_ref.right_ref), custom_call_target="tpu_custom_call" | custom-call | flops 12884901888 | bytes 20971520 | tf_op jit(solution)/shard_map/columns_back/pallas_call | solution.py:930
  351.2 11.1 %feed_forward.3 = (bf16[2048,256]{1,0:T(8,128)(2,1)S(1)}, bf16[2048,512]{1,0:T(8,128)(2,1)S(1)}) custom-call(bf16[2048,2048]{1,0:T(8,128)(2,1)} %get-tuple-element.74.normed_ref, bf16[2048,2048]{1,0:T(8,128)(2,1)} %get-tuple-element.76.cot_ref, bf16[2048,768]{1,0:T(8,128)(2,1)} %all-gather.6.cloned.1.call-done.gate_ref.up_ref.down_ref.right_ref, ...), custom_call_target="tpu_custom_call" | custom-call | flops 6442450944 | bytes 23068672 | tf_op jit(solution)/shard_map/feed_forward/pallas_call | solution.py:874
  362.4 9.8 %columns_back.5.terms_ref = bf16[2048,2048]{1,0:T(8,128)(2,1)} custom-call(s32[1]{0:T(128)} %bitcast.own_ref, bf16[2048,512]{1,0:T(8,128)(2,1)S(1)} %get-tuple-element.90.left_ref, bf16[2048,768]{1,0:T(8,128)(2,1)S(1)} %copy-done, bf16[2048,2048]{1,0:T(8,128)(2,1)} %columns_back.4.refs_0_), custom_call_target="tpu_custom_call" | custom-call | flops 4294967296 | bytes 12582912 | tf_op jit(solution)/shard_map/columns_back/pallas_call | solution.py:930
  372.3 81.8 %middle_back_step.1 = (bf16[2048,2048]{1,0:T(8,128)(2,1)}, f32[256,2048]{1,0:T(8,128)S(1)}, f32[1,2048]{1,0:T(1,128)S(1)}) custom-call(bf16[2048,2048]{1,0:T(8,128)(2,1)} %columns_back.5.terms_ref, bf16[2048,2048]{1,0:T(8,128)(2,1)} %get-tuple-element.76.cot_ref, f32[256,2048]{1,0:T(8,128)S(1)} %copy-done.3, f32[256,128]{1,0:T(8,128)S(1)} %get-tuple-element.87.factor_ref, ...), custom_call_target="tpu_custom_call" | custom-call | flops 70000001024 | bytes 700000000 | tf_op jit(solution)/shard_map/middle_back_step/pallas_call | solution.py:416
  454.1 6.7 convolution_convert_fusion.8
  460.8 8.5 %convolution_convert_fusion.5 = bf16[2048,512]{1,0:T(8,128)(2,1)S(1)} fusion(bf16[2048,2048]{1,0:T(8,128)(2,1)} %get-tuple-element.74.normed_ref, bf16[2048,512]{1,0:T(8,128)(2,1)S(1)} %get-tuple-element.90.left_ref), kind=kOutput, calls=%fused_computation.14 | convolution fusion | flops 4296015872 | bytes 12582912 | tf_op jit(solution)/shard_map/dot_general | solution.py:23
  471.4 6.2 convolution_convert_fusion.7.grad_ref
  477.6 17.9 %attend_back.1.grad_ref = bf16[2048,768]{1,0:T(8,128)(2,1)S(1)} custom-call(bf16[2048,768]{1,0:T(8,128)(2,1)} %copy-done.20, bf16[2048,256]{1,0:T(8,128)(2,1)S(1)} %copy-done.6, bf16[2048,256]{1,0:T(8,128)(2,1)S(1)} %convolution_convert_fusion.7.grad_ref, f32[2,2,2,1024]{3,2,1,0:T(2,128)S(1)} %get-tuple-element.93.lse_ref), custom_call_target="tpu_custom_call" | custom-call | flops 2684354560 | bytes 9437184 | tf_op jit(solution)/shard_map/attend_back/pallas_call | solution.py:135
  495.6 7.0 %convolution_convert_fusion.6 = bf16[2048,256]{1,0:T(8,128)(2,1)S(1)} fusion(bf16[2048,2048]{1,0:T(8,128)(2,1)} %get-tuple-element.92, bf16[2048,256]{1,0:T(8,128)(2,1)S(1)} %copy-done.6), kind=kOutput, calls=%fused_computation.15 | convolution fusion | flops 2148007936 | bytes 10485760 | tf_op jit(solution)/shard_map/dot_general | solution.py:23
  502.7 7.7 %convolution_convert_fusion.3 = bf16[2048,768]{1,0:T(8,128)(2,1)S(1)} fusion(bf16[2048,768]{1,0:T(8,128)(2,1)S(1)} %attend_back.1.grad_ref, bf16[2048,2048]{1,0:T(8,128)(2,1)S(1)} %bitcast.38, f32[2048]{0:T(1024)S(1)} %bitcast.36, f32[2048]{0:T(1024)S(1)} %copy-done.29), kind=kOutput, calls=%fused_computation.10 | convolution fusion | flops 6460801024 | bytes 14696448 | tf_op jit(solution)/shard_map/dot_general | solution.py:23
  510.4 2.6 pad_maximum_fusion.1
  514.9 18.0 %input_terms.1 = (bf16[2048,2048]{1,0:T(8,128)(2,1)}, f32[1,2048]{1,0:T(1,128)S(1)}) custom-call(s32[1]{0:T(128)} %bitcast.own_ref, bf16[2048,768]{1,0:T(8,128)(2,1)S(1)} %copy-done.22, bf16[2048,1024]{1,0:T(8,128)(2,1)} %all-gather.4.cloned.1.call-done.qkv_ref, bf16[2048,2048]{1,0:T(8,128)(2,1)} %get-tuple-element.71.x_ref, f32[1,2048]{1,0:T(1,128)S(1)} %copy-done.11, ...), custom_call_target="tpu_custom_call" | custom-call | flops 6442450944 | bytes 25165824 | tf_op jit(solution)/shard_map/input_terms/pallas_call | solution.py:819
  537.9 10.6 %columns_back.6.refs_0_ = bf16[2048,2048]{1,0:T(8,128)(2,1)} custom-call(s32[1]{0:T(128)} %bitcast.own_ref, bf16[2048,768]{1,0:T(8,128)(2,1)S(1)} %copy-done.24, bf16[2048,2304]{1,0:T(8,128)(2,1)} %all-gather.8.cloned.1.call-done.gate_ref.up_ref.down_ref.right_ref), custom_call_target="tpu_custom_call" | custom-call | flops 6442450944 | bytes 14680064 | tf_op jit(solution)/shard_map/columns_back/pallas_call | solution.py:930
  548.5 8.8 %columns_back.7.refs_0_ = bf16[2048,2048]{1,0:T(8,128)(2,1)} custom-call(s32[1]{0:T(128)} %bitcast.own_ref, bf16[2048,256]{1,0:T(8,128)(2,1)S(1)} %copy-done.9, bf16[2048,768]{1,0:T(8,128)(2,1)} %all-gather.6.cloned.1.call-done.gate_ref.up_ref.down_ref.right_ref, bf16[2048,2048]{1,0:T(8,128)(2,1)} %columns_back.6.refs_0_, f32[256,2048]{1,0:T(8,128)S(1)} %copy-done.4), custom_call_target="tpu_custom_call" | custom-call | flops 2147483648 | bytes 10485760 | tf_op jit(solution)/shard_map/columns_back/pallas_call | solution.py:930
  557.3 75.2 %scatter_outputs.1 = (bf16[1024,512]{1,0:T(8,128)(2,1)S(1)}, bf16[1024,512]{1,0:T(8,128)(2,1)S(1)}, f32[2,512]{1,0:T(2,128)S(1)}) custom-call(f32[2,2048]{1,0:T(2,128)S(1)} %pad_maximum_fusion.5.vector_ref, bf16[2048,2048]{1,0:T(8,128)(2,1)} %columns_back.7.refs_0_, bf16[2048,2048]{1,0:T(8,128)(2,1)} %get-tuple-element.101.refs_1_), custom_call_target="tpu_custom_call" | custom-call | flops 60000002048 | bytes 600000000 | tf_op jit(solution)/shard_map/scatter_outputs/pallas_call | solution.py:416
  635.5 9.0 %reduce-scatter.8.cloned.1.call-done.refs_0_ = bf16[512,1024]{1,0:T(8,128)(2,1)} async-done(((bf16[2048,1024]{1,0:T(8,128)(2,1)}), bf16[512,1024]{1,0:T(8,128)(2,1)}) %reduce-scatter.8.cloned.1.call-update) | async-done | bytes 1048592 | tf_op jit(solution)/shard_map/reduce_scatter | solution.py:975
  650.0 5.5 assemble_grads.2
  655.5 5.0 collective-permute-done.3.refs_1_
  (111 shorter events, 31.4 us)
Async XLA Ops:
  7.2 146.2 %all-gather.4.cloned.1.call-start = ((), (), s32[]{:S(2)}) async-start(), calls=%async_computation.3 | async-start | bytes 5242880 | tf_op jit(solution)/shard_map/all_gather | solution.py:972
  11.2 18.0 %copy-start.12 = (bf16[1024,512]{1,0:T(8,128)(2,1)S(1)}, bf16[1024,512]{1,0:T(8,128)(2,1)}, u32[]{:S(2)}) copy-start(bf16[1024,512]{1,0:T(8,128)(2,1)} %refs_3_) | copy-start | bytes 3145732
  11.2 18.0 %copy-start.13 = (bf16[256,2048]{1,0:T(8,128)(2,1)S(1)}, bf16[256,2048]{1,0:T(8,128)(2,1)}, u32[]{:S(2)}) copy-start(bf16[256,2048]{1,0:T(8,128)(2,1)} %refs_0_.5) | copy-start | bytes 3145732
  27.6 248.1 %all-gather.8.cloned.1.call-start = ((), (), s32[]{:S(2)}) async-start(), calls=%async_computation.5 | async-start | bytes 11796480 | tf_op jit(solution)/shard_map/all_gather | solution.py:972
  30.4 63.3 %copy-start.30 = (f32[512]{0:T(512)S(1)}, f32[512]{0:T(512)}, u32[]{:S(2)}) copy-start(f32[512]{0:T(512)} %param.17) | copy-start | bytes 6148
  30.4 63.3 %copy-start.31 = (f32[512]{0:T(512)S(1)}, f32[512]{0:T(512)}, u32[]{:S(2)}) copy-start(f32[512]{0:T(512)} %param.12) | copy-start | bytes 6148
  93.7 257.6 %all-gather.6.cloned.1.call-start = ((), (), s32[]{:S(2)}) async-start(), calls=%async_computation.4 | async-start | bytes 3932160 | tf_op jit(solution)/shard_map/all_gather | solution.py:972
  93.7 55.8 %collective-permute-start = (f32[2,512]{1,0:T(2,128)S(1)}, f32[2,512]{1,0:T(2,128)S(1)}, u32[]{:S(2)}, u32[]{:S(2)}) collective-permute-start(f32[2,512]{1,0:T(2,128)S(1)} %get-tuple-element.136), channel_id=1, source_target_pairs={{0,1},{1,0},{2,3},{3,2},{4,5},{5,4},{6,7},{7,6},{8,9},{9,8},{10,11... | collective-permute-start | bytes 12296 | tf_op jit(solution)/shard_map/ppermute | solution.py:969
  144.3 388.6 %reduce-scatter.4.cloned.1.call-start = ((), (), s32[]{:S(2)}) async-start(), calls=%async_computation.6 | async-start | bytes 11796480 | tf_op jit(solution)/shard_map/reduce_scatter | solution.py:975
  149.5 3.7 collective-permute-start.1
  153.4 10.3 %copy-start.10 = (f32[1,2048]{1,0:T(1,128)}, f32[1,2048]{1,0:T(1,128)S(1)}, u32[]{:S(2)}) copy-start(f32[1,2048]{1,0:T(1,128)S(1)} %get-tuple-element.128.gain_ref) | copy-start | bytes 24580
  163.6 18.7 %copy-start.20 = (bf16[2048,768]{1,0:T(8,128)(2,1)}, bf16[2048,768]{1,0:T(8,128)(2,1)S(1)}, u32[]{:S(2)}) copy-start(bf16[2048,768]{1,0:T(8,128)(2,1)S(1)} %convolution_convert_fusion.2.packed_ref) | copy-start | bytes 9437188
  175.0 7.3 %copy-start.5 = (bf16[2048,256]{1,0:T(8,128)(2,1)}, bf16[2048,256]{1,0:T(8,128)(2,1)S(1)}, u32[]{:S(2)}) copy-start(bf16[2048,256]{1,0:T(8,128)(2,1)S(1)} %get-tuple-element.73.out_ref) | copy-start | bytes 3145732
  302.7 10.5 %copy-start.23 = (bf16[2048,768]{1,0:T(8,128)(2,1)}, bf16[2048,768]{1,0:T(8,128)(2,1)S(1)}, u32[]{:S(2)}) copy-start(bf16[2048,768]{1,0:T(8,128)(2,1)S(1)} %get-tuple-element.100.left_ref) | copy-start | bytes 9437188
  302.7 10.5 %copy-start.27 = (bf16[2048,2048]{1,0:T(8,128)(2,1)S(1)}, bf16[2048,2048]{1,0:T(8,128)(2,1)}, u32[]{:S(2)}) copy-start(bf16[2048,2048]{1,0:T(8,128)(2,1)} %get-tuple-element.74.normed_ref) | copy-start | bytes 25165828
  302.7 10.5 %copy-start.32 = (bf16[2048,1536]{1,0:T(8,128)(2,1)S(1)}, bf16[2048,1536]{1,0:T(8,128)(2,1)}, u32[]{:S(2)}) copy-start(bf16[2048,1536]{1,0:T(8,128)(2,1)} %get-tuple-element.81.left_ref) | copy-start | bytes 18874372
  332.5 300.0 %reduce-scatter.6.cloned.1.call-start = ((), (), s32[]{:S(2)}) async-start(), calls=%async_computation.7 | async-start | bytes 3932160 | tf_op jit(solution)/shard_map/reduce_scatter | solution.py:975
  351.2 11.2 %copy-start = (bf16[2048,768]{1,0:T(8,128)(2,1)S(1)}, bf16[2048,768]{1,0:T(8,128)(2,1)}, u32[]{:S(2)}) copy-start(bf16[2048,768]{1,0:T(8,128)(2,1)} %all-gather.6.cloned.1.call-done.gate_ref.up_ref.down_ref.right_ref) | copy-start | bytes 9437188
  362.4 91.7 %copy-start.8 = (bf16[2048,256]{1,0:T(8,128)(2,1)}, bf16[2048,256]{1,0:T(8,128)(2,1)S(1)}, u32[]{:S(2)}) copy-start(bf16[2048,256]{1,0:T(8,128)(2,1)S(1)} %get-tuple-element.91.left_ref) | copy-start | bytes 3145732
  362.4 9.8 %copy-start.3 = (f32[256,2048]{1,0:T(8,128)S(1)}, f32[256,2048]{1,0:T(8,128)}, u32[]{:S(2)}) copy-start(f32[256,2048]{1,0:T(8,128)} %copy-done.2) | copy-start | bytes 6291460
  471.2 173.2 %reduce-scatter.8.cloned.1.call-start = ((), (), s32[]{:S(2)}) async-start(), calls=%async_computation.8 | async-start | bytes 5242880 | tf_op jit(solution)/shard_map/reduce_scatter | solution.py:975
  477.6 25.0 %slice-start = ((s8[8388608]{0:T(1024)(128)(4,1)}), s8[4194304]{0:T(1024)(128)(4,1)S(1)}, s32[]{:S(2)}) async-start(s8[8388608]{0:T(1024)(128)(4,1)} %bitcast.37), calls=%async_computation.9 | async-start | bytes 8388608
  495.5 7.1 %copy-start.21 = (bf16[2048,768]{1,0:T(8,128)(2,1)}, bf16[2048,768]{1,0:T(8,128)(2,1)S(1)}, u32[]{:S(2)}) copy-start(bf16[2048,768]{1,0:T(8,128)(2,1)S(1)} %attend_back.1.grad_ref) | copy-start | bytes 9437188
  495.5 7.1 %copy-start.11 = (f32[1,2048]{1,0:T(1,128)S(1)}, f32[1,2048]{1,0:T(1,128)}, u32[]{:S(2)}) copy-start(f32[1,2048]{1,0:T(1,128)} %copy-done.10) | copy-start | bytes 24580
  495.5 7.1 %slice-start.1 = ((s8[8388608]{0:T(1024)(128)(4,1)}), s8[4194304]{0:T(1024)(128)(4,1)S(1)}, s32[]{:S(2)}) async-start(s8[8388608]{0:T(1024)(128)(4,1)} %bitcast.37), calls=%async_computation.10 | async-start | bytes 8388608
  495.6 7.1 %copy-start.29 = (f32[2048]{0:T(1024)S(1)}, f32[2048]{0:T(1024)}, u32[]{:S(2)}) copy-start(f32[2048]{0:T(1024)} %copy-done.28) | copy-start | bytes 24580
  535.3 13.2 %copy-start.4 = (f32[256,2048]{1,0:T(8,128)S(1)}, f32[256,2048]{1,0:T(8,128)}, u32[]{:S(2)}) copy-start(f32[256,2048]{1,0:T(8,128)} %copy-done.2) | copy-start | bytes 6291460
  535.3 13.2 %copy-start.9 = (bf16[2048,256]{1,0:T(8,128)(2,1)S(1)}, bf16[2048,256]{1,0:T(8,128)(2,1)}, u32[]{:S(2)}) copy-start(bf16[2048,256]{1,0:T(8,128)(2,1)} %copy-done.8) | copy-start | bytes 3145732
  535.3 113.6 %collective-permute-start.4 = (bf16[256,2304]{1,0:T(8,128)(2,1)}, bf16[256,2304]{1,0:T(8,128)(2,1)S(1)}, u32[]{:S(2)}, u32[]{:S(2)}) collective-permute-start(bf16[256,2304]{1,0:T(8,128)(2,1)} %constant_dynamic-slice_fusion), channel_id=1, source_target_pairs={{0,4},{4,0},{8,12},{12,8},{16,20},{20,16},{24,28},{28,24},{1,5},{5... | collective-permute-start | bytes 3538952 | tf_op jit(solution)/shard_map/ppermute | solution.py:963
  634.4 11.7 %collective-permute-start.2 = (bf16[256,768]{1,0:T(8,128)(2,1)}, bf16[256,768]{1,0:T(8,128)(2,1)}, u32[]{:S(2)}, u32[]{:S(2)}) collective-permute-start(bf16[256,768]{1,0:T(8,128)(2,1)} %constant_dynamic-slice_fusion.2), channel_id=1, source_target_pairs={{0,4},{4,0},{8,12},{12,8},{16,20},{20,16},{24,28},{28,24},{1,5},{5... | collective-permute-start | bytes 1179656 | tf_op jit(solution)/shard_map/ppermute | solution.py:963
  644.5 16.0 %copy-start.1 = (bf16[512,1024]{1,0:T(8,128)(2,1)S(1)}, bf16[512,1024]{1,0:T(8,128)(2,1)}, u32[]{:S(2)}) copy-start(bf16[512,1024]{1,0:T(8,128)(2,1)} %reduce-scatter.8.cloned.1.call-done.refs_0_) | copy-start | bytes 3145732
  647.1 13.4 %collective-permute-start.3 = (bf16[256,1024]{1,0:T(8,128)(2,1)S(1)}, bf16[256,1024]{1,0:T(8,128)(2,1)S(1)}, u32[]{:S(2)}, u32[]{:S(2)}) collective-permute-start(bf16[256,1024]{1,0:T(8,128)(2,1)S(1)} %constant_dynamic-slice_fusion.1), channel_id=1, source_target_pairs={{0,4},{4,0},{8,12},{12,8},{16,20},{20,16},{24,28},{28,24},{1,5},{5... | collective-permute-start | bytes 1572872 | tf_op jit(solution)/shard_map/ppermute | solution.py:963
  (14 other events, 31.4 us)
Sparse Core Ops, SparseCore 0:
  27.7 81.0 all-gather.3
  110.3 165.2 all-gather.7
  277.3 61.6 all-gather.5
  341.2 159.9 reduce-scatter.3
  503.3 61.0 reduce-scatter.5
  566.6 77.8 reduce-scatter.7

commit v6 on v5

--- a/solution.py
+++ b/solution.py
@@ -11,11 +11,9 @@
 BF16 = jnp.bfloat16
 F32 = jnp.float32
 MESH = pl.DeviceIdType.MESH
-HBM = pltpu.MemorySpace.HBM
 VMEM = 48 << 20
 FORWARD_BLOCK = 512
 BACK_BLOCK = 256
-WHOLE_VMEM = 62 << 20
 CHUNKS = (3, 1)
 
 
@@ -893,18 +891,21 @@
     )(normed, cot, weights, weights, weights)
 
 
-def columns_back(left, weights, place, base=None, own=None, middle=None):
-    total, inner = left.shape
-    model = weights.shape[0]
+def columns_back(lefts, weights, place, own, base=None, middle=None):
+    count = len(lefts)
+    total = lefts[0].shape[0]
+    model = weights[0].shape[0]
     tile, part = 512, 512
 
-    def columns_step(own_ref, left_ref, right_ref, *refs):
+    def columns_step(own_ref, *refs):
         out_ref = refs[-1]
         for start in range(0, model, part):
             here = slice(start, start + part)
-            value = right_trans(left_ref[...], right_ref[here, :])
+            value = sum(
+                right_trans(refs[i][...], refs[count + i][here, :]) for i in range(count)
+            )
             if base is not None:
-                value = value + refs[0][:, here].astype(F32)
+                value = value + refs[2 * count][:, here].astype(F32)
             out_ref[:, here] = value.astype(BF16)
         if middle is not None:
             middle_ref = refs[-2]
@@ -916,17 +917,21 @@
                 rows = pl.ds(pl.multiple_of(inside, size), size)
                 out_ref[rows, :] = (out_ref[rows, :].astype(F32) + middle_ref[...]).astype(BF16)
 
-    in_specs = [
-        pl.BlockSpec((tile, inner), lambda i, own: (i, 0)),
-        pl.BlockSpec((model, inner), lambda i, own: (0, place), pipeline_mode=pl.Buffered(1)),
+    in_specs = [pl.BlockSpec((tile, left.shape[1]), lambda i, own: (i, 0)) for left in lefts]
+    in_specs += [
+        pl.BlockSpec(
+            (model, left.shape[1]), lambda i, own: (0, place), pipeline_mode=pl.Buffered(1)
+        )
+        for left in lefts
     ]
-    operands = [own, left, weights]
+    operands = [own, *lefts, *weights]
     if base is not None:
         in_specs.append(pl.BlockSpec((tile, model), lambda i, own: (i, 0)))
         operands.append(base)
     if middle is not None:
         in_specs.append(pl.BlockSpec(middle.shape, lambda i, own: (0, 0)))
         operands.append(middle)
+    inner = sum(left.shape[1] for left in lefts)
     return pl.pallas_call(
         columns_step,
         grid_spec=pltpu.PrefetchScalarGridSpec(
@@ -944,6 +949,40 @@
         ),
         name="columns_back",
     )(*operands)
+
+
+def weight_terms(pairs, tile=256):
+    rows, model = pairs[0][0].shape
+    count = len(pairs)
+    widths = [right.shape[1] for _, right in pairs]
+
+    def terms_step(*refs):
+        out_ref = refs[-1]
+        start = 0
+        for i, width in enumerate(widths):
+            out_ref[:, start : start + width] = left_trans(refs[i][...], refs[count + i][...]).astype(
+                BF16
+            )
+            start += width
+
+    return pl.pallas_call(
+        terms_step,
+        grid=(model // tile,),
+        in_specs=[pl.BlockSpec((rows, tile), lambda i: (0, i))] * count
+        + [
+            pl.BlockSpec((rows, width), lambda i: (0, 0), pipeline_mode=pl.Buffered(1))
+            for width in widths
+        ],
+        out_specs=pl.BlockSpec((tile, sum(widths)), lambda i: (i, 0)),
+        out_shape=jax.ShapeDtypeStruct((model, sum(widths)), BF16),
+        compiler_params=pltpu.CompilerParams(vmem_limit_bytes=VMEM),
+        cost_estimate=pl.CostEstimate(
+            flops=2 * rows * model * sum(widths),
+            transcendentals=0,
+            bytes_accessed=2 * (rows * model * count + (rows + model) * sum(widths)),
+        ),
+        name="weight_terms",
+    )(*[left for left, _ in pairs], *[right for _, right in pairs])
 
 
 def program(
@@ -1028,15 +1067,6 @@
     feed_sums = []
     grad_normed_two = out_rows = None
 
-    def terms_of(grad_both, hidden):
-        return jnp.concatenate(
-            [
-                left_trans(normed_two, grad_both).astype(BF16),
-                left_trans(cot_rows, hidden).astype(BF16),
-            ],
-            axis=1,
-        )
-
     hiddens = []
     for c in range(len(chunks)):
         if c:
@@ -1046,35 +1076,31 @@
         hidden, grad_both = feed_forward(normed_two, cot_rows, feed_weights[c], chunks[c])
         hiddens.append(hidden)
         if c + 1 < len(chunks):
-            feed_terms = terms_of(grad_both, hidden)
+            feed_terms = weight_terms([(normed_two, grad_both), (cot_rows, hidden)])
             feed_terms, grad_both = lax.optimization_barrier((feed_terms, grad_both))
             feed_sums.append(ring_scatter(feed_terms))
-        grad_normed_two = columns_back(grad_both, feed_weights[c], 0, grad_normed_two, own)
+        grad_normed_two = columns_back(
+            [grad_both], [feed_weights[c]], 0, own, grad_normed_two
+        )
     grad_mid_rows, grad_middle, gain_ffn_part = middle_back(
         4, grad_normed_two, cot_rows, middle, factor_two, gain_two
     )
 
     hidden, grad_both, grad_mid_rows = lax.optimization_barrier((hidden, grad_both, grad_mid_rows))
-    feed_terms = terms_of(grad_both, hidden)
+    feed_terms = weight_terms(
+        [(normed_two, grad_both), (cot_rows, hidden), (grad_mid_rows, attended)]
+    )
     grad_mid_rows, feed_terms = lax.optimization_barrier((grad_mid_rows, feed_terms))
     feed_sums.append(ring_scatter(feed_terms))
 
     grad_attended = product(grad_mid_rows, out_proj).astype(BF16)
     grad_packed = attend_back(packed, attended, grad_attended, log_sums)
-    attention_terms = jnp.concatenate(
-        [
-            left_trans(normed, grad_packed).astype(BF16),
-            left_trans(grad_mid_rows, attended).astype(BF16),
-        ],
-        axis=1,
-    )
+    attention_terms = left_trans(normed, grad_packed).astype(BF16)
     attention_terms, grad_packed = lax.optimization_barrier((attention_terms, grad_packed))
     attention_sum = ring_scatter(attention_terms)
     terms, gain_attn_part = input_terms(grad_packed, attention_weights, x_all, gain_one, grad_middle, own)
     hiddens[0], terms, feed_sums[0] = lax.optimization_barrier((hiddens[0], terms, feed_sums[0]))
-    for c in range(len(chunks)):
-        last = middle if c + 1 == len(chunks) else None
-        out_rows = columns_back(hiddens[c], feed_weights[c], 2, out_rows, own, last)
+    out_rows = columns_back(hiddens, feed_weights, 2, own, None, middle)
     outcome, input_grad, gain_grads = scatter_blocks(
         5, tok_size // 2, jnp.concatenate([gain_attn_part, gain_ffn_part]), out_rows, terms
     )
@@ -1086,7 +1112,8 @@
         [(c, part * chunks[c], chunks[c], lefts[c]) for c in range(len(chunks))]
         for part in range(3)
     ]
-    gate_grad, up_grad, down_grad, outcome, input_grad = assemble(
+    feed_plan.append([(len(chunks) - 1, 3 * chunks[-1], heads_wide, 0)])
+    gate_grad, up_grad, down_grad, out_grad, outcome, input_grad = assemble(
         feed_plan, 2, feed_sums, feed_others, (outcome, input_grad)
     )
     attention_plan = [
@@ -1096,7 +1123,6 @@
         ]
         for part in range(3)
     ]
-    attention_plan.append([(0, 3 * heads_wide, heads_wide, 0)])
     attention_other = other_half(attention_sum)
     attention_other, gate_grad, up_grad, down_grad, outcome, input_grad = lax.optimization_barrier(
         (attention_other, gate_grad, up_grad, down_grad, outcome, input_grad)
@@ -1108,6 +1134,7 @@
         gain_grads[0],
         gain_grads[1],
         *part_grads,
+        out_grad,
         gate_grad,
         up_grad,
         down_grad,

time: 678 us -> 674 us (level)
  matrix products: 78.4 us -> 34.5 us
  Pallas kernels: 505 us -> 548 us
  other arithmetic: 14.6 us -> 5.22 us
  local copies, waits for them, and re-layouts: 21.6 us -> 28.4 us
    dot_general x6 -> x1, matrix products: 54.7 us -> 11.1 us  [left_trans(): lax.dot_general(left, right, (((0,), (0,)), ((), ())), preferred_element_...]
    pallas_call x0 -> x2, Pallas kernels: none -> 41.8 us  [weight_terms(): pl.pallas_call(terms_step, grid=(model // tile,), in_specs=[pl.BlockSpec(...]
    concatenate x3 -> x0, other arithmetic: 9.39 us -> none  [the longest x2 6.81 us: terms_of(): jnp.concatenate([left_trans(normed_two, grad_both).astype(BF16), left_tra...]
    unnamed x72 -> x62, local copies, waits for them, and re-layouts: 15.7 us -> 22.5 us
    pallas_call x4 -> x3, Pallas kernels: 47.9 us -> 42.1 us  [columns_back(): pl.pallas_call(columns_step, grid_spec=pltpu.PrefetchScalarGridSpec(num_s...]
  transfers between devices with their start and end apart: 11 -> 11, of which waited for: 5 -> 4; matrix products, arithmetic and copies ran while one was open for 15% -> 7% of each run, Pallas kernels for 73% -> 80%
where the time goes in v6:
time: 674 us; the launch traced here: 665 us
  Pallas kernels  548 us (81%)
  matrix products  34.5 us (5%)
  waiting for transfers between devices  29.8 us (4%)
  local copies, waits for them, and re-layouts  28.4 us (4%)
  between operations  14.9 us (2%)
    pallas_call x6, Pallas kernels, call(): pl.pallas_call(kernel, out_shape=outputs, in_specs=[pl.BlockSpec(memory_s...  371 us
    pallas_call x3, Pallas kernels, columns_back(): pl.pallas_call(columns_step, grid_spec=pltpu.PrefetchScalarGridSpec(num_s...  42.1 us
    pallas_call x2, Pallas kernels, weight_terms(): pl.pallas_call(terms_step, grid=(model // tile,), in_specs=[pl.BlockSpec(...  41.8 us
    pallas_call x2, Pallas kernels, feed_forward(): pl.pallas_call(feed_step, grid=(total // tile,), in_specs=[rows, rows, we...  38.2 us
    unnamed x62, local copies, waits for them, and re-layouts  22.5 us
    pallas_call x1, Pallas kernels, input_terms(): pl.pallas_call(input_terms_step, grid_spec=pltpu.PrefetchScalarGridSpec(n...  18.2 us
    pallas_call x1, Pallas kernels, attend_back(): pl.pallas_call(attend_back_kernel, grid=(sequences, pairs), out_shape=jax...  18 us
    dot_general x2, matrix products, product(): return jnp.dot(left, right, preferred_element_type=F32)  16.4 us
  transfers between devices with their start and end apart: 11, of which 4 were waited for; matrix products, arithmetic and copies ran while one was open for 7% of the time, Pallas kernels for 80%

profile of v6, /device:TPU:0, one launch (start us, length us, event | category | flops | bytes accessed | tf_op | source)
XLA Modules:
  0.0 665.4 jit_solution(12945283059585495664)
XLA Ops:
  11.2 16.4 %swap_gather.3 = bf16[512,1024]{1,0:T(8,128)(2,1)} custom-call(bf16[256,512]{1,0:T(8,128)(2,1)S(1)} %copy-done.14, bf16[256,512]{1,0:T(8,128)(2,1)S(1)} %copy-done.15, bf16[256,512]{1,0:T(8,128)(2,1)S(1)} %copy-done.16, bf16[256,512]{1,0:T(8,128)(2,1)S(1)} %bitcast.24), custom_call_target="tpu_custom_call" | custom-call | flops 15000000512 | bytes 150000000 | tf_op jit(solution)/shard_map/swap_gather/pallas_call | solution.py:414
  30.4 63.2 %swap_gather.4 = (bf16[512,2304]{1,0:T(8,128)(2,1)}, bf16[2048,2048]{1,0:T(8,128)(2,1)}) custom-call(bf16[256,2048]{1,0:T(8,128)(2,1)S(1)} %copy-done.10, bf16[256,2048]{1,0:T(8,128)(2,1)S(1)} %copy-done.11, bf16[256,2048]{1,0:T(8,128)(2,1)S(1)} %bitcast.22, bf16[1024,512]{1,0:T(8,128)(2,1)S(1)} %copy-done.9), custom_call_target="tpu_custom_call" | custom-call | flops 49999998976 | bytes 500000000 | tf_op jit(solution)/shard_map/swap_gather/pallas_call | solution.py:414
  96.7 47.6 %swap_gather.5 = (bf16[512,768]{1,0:T(8,128)(2,1)}, bf16[2048,2048]{1,0:T(8,128)(2,1)}) custom-call(bf16[256,2048]{1,0:T(8,128)(2,1)S(1)} %copy-done.10, bf16[256,2048]{1,0:T(8,128)(2,1)S(1)} %copy-done.12, bf16[256,2048]{1,0:T(8,128)(2,1)S(1)} %bitcast.23, bf16[1024,512]{1,0:T(8,128)(2,1)S(1)} %copy-done.13), custom_call_target="tpu_custom_call" | custom-call | flops 49999998976 | bytes 500000000 | tf_op jit(solution)/shard_map/swap_gather/pallas_call | solution.py:414
  144.4 5.2 fusion
  150.7 2.6 collective-permute-done.1
  153.4 10.2 %convolution_convert_fusion.1.packed_ref = bf16[2048,768]{1,0:T(8,128)(2,1)S(1)} fusion(bf16[2048,1024]{1,0:T(8,128)(2,1)} %all-gather.4.cloned.1.call-done.qkv_ref, bf16[2048,2048]{1,0:T(8,128)(2,1)} %get-tuple-element.71.x_ref, f32[2048]{0:T(1024)S(1)} %bitcast.25, f32[2048]{0:T(1024)S(1)} %add_rsqrt_fusion), kind=kOutput, calls=%fused_computation.6 | convolution fusion | flops 6460801024 | bytes 14696448 | tf_op jit(solution)/shard_map/dot_general | solution.py:33
  163.7 11.3 %attend.1 = (bf16[2048,256]{1,0:T(8,128)(2,1)S(1)}, f32[2,2,2,1024]{3,2,1,0:T(2,128)S(1)}) custom-call(bf16[2048,768]{1,0:T(8,128)(2,1)S(1)} %convolution_convert_fusion.1.packed_ref), custom_call_target="tpu_custom_call" | custom-call | flops 1073741824 | bytes 6291456 | tf_op jit(solution)/shard_map/attend/pallas_call | solution.py:106
  174.9 6.9 %convolution_convert_fusion.terms_ref = bf16[2048,2048]{1,0:T(8,128)(2,1)} fusion(bf16[2048,256]{1,0:T(8,128)(2,1)S(1)} %get-tuple-element.73.refs_5_.out_ref, bf16[2048,1024]{1,0:T(8,128)(2,1)} %all-gather.4.cloned.1.call-done.qkv_ref), kind=kOutput, calls=%fused_computation.5 | convolution fusion | flops 2151677952 | bytes 10485760 | tf_op jit(solution)/shard_map/dot_general | solution.py:27
  182.9 80.5 %middle_step.1 = (bf16[2048,2048]{1,0:T(8,128)(2,1)}, f32[256,2048]{1,0:T(8,128)S(1)}, f32[256,128]{1,0:T(8,128)S(1)}) custom-call(bf16[2048,2048]{1,0:T(8,128)(2,1)} %convolution_convert_fusion.terms_ref, bf16[2048,2048]{1,0:T(8,128)(2,1)} %get-tuple-element.71.x_ref, f32[1,2048]{1,0:T(1,128)S(1)} %get-tuple-element.127.gain_ref), custom_call_target="tpu_custom_call" | custom-call | flops 70000001024 | bytes 700000000 | tf_op jit(solution)/shard_map/middle_step/pallas_call | solution.py:414
  264.7 11.0 %all-gather.8.cloned.1.call-done.gate_ref.up_ref.down_ref.refs_1_.refs_2_ = bf16[2048,2304]{1,0:T(8,128)(2,1)} async-done(((bf16[512,2304]{1,0:T(8,128)(2,1)}), bf16[2048,2304]{1,0:T(8,128)(2,1)}) %all-gather.8.cloned.1.call-update) | async-done | bytes 9437200 | tf_op jit(solution)/shard_map/all_gather | solution.py:1011
  275.7 27.0 %feed_forward.2 = (bf16[2048,768]{1,0:T(8,128)(2,1)S(1)}, bf16[2048,1536]{1,0:T(8,128)(2,1)}) custom-call(bf16[2048,2048]{1,0:T(8,128)(2,1)} %get-tuple-element.74.normed_ref.refs_0_, bf16[2048,2048]{1,0:T(8,128)(2,1)} %get-tuple-element.76.cot_ref.refs_1_, bf16[2048,2304]{1,0:T(8,128)(2,1)} %all-gather.8.cloned.1.call-done.gate_ref.up_ref.down_ref.refs_1_.refs_2_, ...), custom_call_target="tpu_custom_call" | custom-call | flops 19327352832 | bytes 35651584 | tf_op jit(solution)/shard_map/feed_forward/pallas_call | solution.py:872
  302.7 25.9 %weight_terms.2 = bf16[2048,2304]{1,0:T(8,128)(2,1)} custom-call(bf16[2048,2048]{1,0:T(8,128)(2,1)} %get-tuple-element.74.normed_ref.refs_0_, bf16[2048,2048]{1,0:T(8,128)(2,1)} %get-tuple-element.76.cot_ref.refs_1_, bf16[2048,1536]{1,0:T(8,128)(2,1)} %get-tuple-element.81.refs_2_.refs_0_, bf16[2048,768]{1,0:T(8,128)(2,1)S(1)} %get-tuple-element.100.refs_3_.refs_0_), custom_call_target="tpu_custom_call" | custom-call | flops 19327352832 | bytes 35651584 | tf_op jit(solution)/shard_map/weight_terms/pallas_call | solution.py:968
  328.6 1.7 copy-done.20
  330.4 18.8 %columns_back.3.refs_2_ = bf16[2048,2048]{1,0:T(8,128)(2,1)} custom-call(s32[1]{0:T(128)} %bitcast.own_ref, bf16[2048,1536]{1,0:T(8,128)(2,1)} %get-tuple-element.81.refs_2_.refs_0_, bf16[2048,2304]{1,0:T(8,128)(2,1)} %all-gather.8.cloned.1.call-done.gate_ref.up_ref.down_ref.refs_1_.refs_2_), custom_call_target="tpu_custom_call" | custom-call | flops 12884901888 | bytes 20971520 | tf_op jit(solution)/shard_map/columns_back/pallas_call | solution.py:935
  349.2 11.2 %feed_forward.3 = (bf16[2048,256]{1,0:T(8,128)(2,1)S(1)}, bf16[2048,512]{1,0:T(8,128)(2,1)S(1)}) custom-call(bf16[2048,2048]{1,0:T(8,128)(2,1)} %get-tuple-element.74.normed_ref.refs_0_, bf16[2048,2048]{1,0:T(8,128)(2,1)} %get-tuple-element.76.cot_ref.refs_1_, bf16[2048,768]{1,0:T(8,128)(2,1)} %all-gather.6.cloned.1.call-done.gate_ref.up_ref.down_ref.refs_1_.refs_3_, ...), custom_call_target="tpu_custom_call" | custom-call | flops 6442450944 | bytes 23068672 | tf_op jit(solution)/shard_map/feed_forward/pallas_call | solution.py:872
  360.4 9.8 %columns_back.4.terms_ref = bf16[2048,2048]{1,0:T(8,128)(2,1)} custom-call(s32[1]{0:T(128)} %bitcast.own_ref, bf16[2048,512]{1,0:T(8,128)(2,1)S(1)} %get-tuple-element.90.refs_0_.refs_3_, bf16[2048,768]{1,0:T(8,128)(2,1)S(1)} %copy-done, bf16[2048,2048]{1,0:T(8,128)(2,1)} %columns_back.3.refs_2_), custom_call_target="tpu_custom_call" | custom-call | flops 4294967296 | bytes 12582912 | tf_op jit(solution)/shard_map/columns_back/pallas_call | solution.py:935
  370.3 81.8 %middle_back_step.1 = (bf16[2048,2048]{1,0:T(8,128)(2,1)}, f32[256,2048]{1,0:T(8,128)S(1)}, f32[1,2048]{1,0:T(1,128)S(1)}) custom-call(bf16[2048,2048]{1,0:T(8,128)(2,1)} %columns_back.4.terms_ref, bf16[2048,2048]{1,0:T(8,128)(2,1)} %get-tuple-element.76.cot_ref.refs_1_, f32[256,2048]{1,0:T(8,128)S(1)} %copy-done.22, ...), custom_call_target="tpu_custom_call" | custom-call | flops 70000001024 | bytes 700000000 | tf_op jit(solution)/shard_map/middle_back_step/pallas_call | solution.py:414
  453.4 15.9 %weight_terms.3 = bf16[2048,1024]{1,0:T(8,128)(2,1)} custom-call(bf16[2048,2048]{1,0:T(8,128)(2,1)} %get-tuple-element.74.normed_ref.refs_0_, bf16[2048,2048]{1,0:T(8,128)(2,1)} %get-tuple-element.76.cot_ref.refs_1_, bf16[2048,2048]{1,0:T(8,128)(2,1)} %get-tuple-element.92.refs_2_, bf16[2048,512]{1,0:T(8,128)(2,1)S(1)} %get-tuple-element.90.refs_0_.refs_3_, ...), custom_call_target="tpu_custom_call" | custom-call | flops 8589934592 | bytes 33554432 | tf_op jit(solution)/shard_map/weight_terms/pallas_call | solution.py:968
  469.4 6.2 convolution_convert_fusion.3.grad_ref
  475.6 18.0 %attend_back.1.grad_ref = bf16[2048,768]{1,0:T(8,128)(2,1)S(1)} custom-call(bf16[2048,768]{1,0:T(8,128)(2,1)} %copy-done.17, bf16[2048,256]{1,0:T(8,128)(2,1)S(1)} %copy-done.2, bf16[2048,256]{1,0:T(8,128)(2,1)S(1)} %convolution_convert_fusion.3.grad_ref, f32[2,2,2,1024]{3,2,1,0:T(2,128)S(1)} %get-tuple-element.93.lse_ref), custom_call_target="tpu_custom_call" | custom-call | flops 2684354560 | bytes 9437184 | tf_op jit(solution)/shard_map/attend_back/pallas_call | solution.py:133
  493.7 11.1 %convolution_convert_fusion.2 = bf16[2048,768]{1,0:T(8,128)(2,1)} fusion(bf16[2048,768]{1,0:T(8,128)(2,1)S(1)} %attend_back.1.grad_ref, bf16[2048,2048]{1,0:T(8,128)(2,1)} %get-tuple-element.71.x_ref, f32[2048]{0:T(1024)S(1)} %bitcast.26, f32[2048]{0:T(1024)S(1)} %copy-done.27), kind=kOutput, calls=%fused_computation.7 | convolution fusion | flops 6460801024 | bytes 14696448 | tf_op jit(solution)/shard_map/dot_general | solution.py:21
  504.8 1.7 copy-done.18
  506.5 1.9 copy-done.19
  510.0 18.2 %input_terms.1 = (bf16[2048,2048]{1,0:T(8,128)(2,1)}, f32[1,2048]{1,0:T(1,128)S(1)}) custom-call(s32[1]{0:T(128)} %bitcast.own_ref, bf16[2048,768]{1,0:T(8,128)(2,1)S(1)} %copy-done.19, bf16[2048,1024]{1,0:T(8,128)(2,1)} %all-gather.4.cloned.1.call-done.qkv_ref, bf16[2048,2048]{1,0:T(8,128)(2,1)} %get-tuple-element.71.x_ref, f32[1,2048]{1,0:T(1,128)S(1)} %copy-done.8, ...), custom_call_target="tpu_custom_call" | custom-call | flops 6442450944 | bytes 25165824 | tf_op jit(solution)/shard_map/input_terms/pallas_call | solution.py:817
  528.3 2.4 constant_dynamic-slice_fusion
  532.6 13.5 %columns_back.5.refs_0_ = bf16[2048,2048]{1,0:T(8,128)(2,1)} custom-call(s32[1]{0:T(128)} %bitcast.own_ref, bf16[2048,768]{1,0:T(8,128)(2,1)} %copy-done.20, bf16[2048,256]{1,0:T(8,128)(2,1)S(1)} %copy-done.6, bf16[2048,2304]{1,0:T(8,128)(2,1)} %all-gather.8.cloned.1.call-done.gate_ref.up_ref.down_ref.refs_1_.refs_2_, ...), custom_call_target="tpu_custom_call" | custom-call | flops 8589934592 | bytes 16777216 | tf_op jit(solution)/shard_map/columns_back/pallas_call | solution.py:935
  546.1 81.9 %scatter_outputs.1 = (bf16[1024,512]{1,0:T(8,128)(2,1)S(1)}, bf16[1024,512]{1,0:T(8,128)(2,1)S(1)}, f32[2,512]{1,0:T(2,128)S(1)}) custom-call(f32[2,2048]{1,0:T(2,128)S(1)} %pad_maximum_fusion.2.vector_ref, bf16[2048,2048]{1,0:T(8,128)(2,1)} %columns_back.5.refs_0_, bf16[2048,2048]{1,0:T(8,128)(2,1)} %get-tuple-element.101.refs_1_), custom_call_target="tpu_custom_call" | custom-call | flops 60000002048 | bytes 600000000 | tf_op jit(solution)/shard_map/scatter_outputs/pallas_call | solution.py:414
  628.0 1.9 constant_dynamic-slice_fusion.2
  630.6 14.4 %reduce-scatter.8.cloned.1.call-done.refs_0_ = bf16[512,768]{1,0:T(8,128)(2,1)} async-done(((bf16[2048,768]{1,0:T(8,128)(2,1)}), bf16[512,768]{1,0:T(8,128)(2,1)}) %reduce-scatter.8.cloned.1.call-update) | async-done | bytes 786448 | tf_op jit(solution)/shard_map/reduce_scatter | solution.py:1014
  646.1 1.6 collective-permute-start.3
  649.5 5.7 assemble_grads.2
  655.2 1.7 collective-permute-done.3.refs_1_
  (93 shorter events, 23.4 us)
Async XLA Ops:
  7.2 146.2 %all-gather.4.cloned.1.call-start = ((), (), s32[]{:S(2)}) async-start(), calls=%async_computation.3 | async-start | bytes 5242880 | tf_op jit(solution)/shard_map/all_gather | solution.py:1011
  11.2 18.0 %copy-start.9 = (bf16[1024,512]{1,0:T(8,128)(2,1)S(1)}, bf16[1024,512]{1,0:T(8,128)(2,1)}, u32[]{:S(2)}) copy-start(bf16[1024,512]{1,0:T(8,128)(2,1)} %refs_3_) | copy-start | bytes 3145732
  11.2 18.0 %copy-start.10 = (bf16[256,2048]{1,0:T(8,128)(2,1)S(1)}, bf16[256,2048]{1,0:T(8,128)(2,1)}, u32[]{:S(2)}) copy-start(bf16[256,2048]{1,0:T(8,128)(2,1)} %refs_0_.5) | copy-start | bytes 3145732
  27.6 248.1 %all-gather.8.cloned.1.call-start = ((), (), s32[]{:S(2)}) async-start(), calls=%async_computation.5 | async-start | bytes 11796480 | tf_op jit(solution)/shard_map/all_gather | solution.py:1011
  30.4 63.3 %copy-start.28 = (f32[512]{0:T(512)S(1)}, f32[512]{0:T(512)}, u32[]{:S(2)}) copy-start(f32[512]{0:T(512)} %param.17) | copy-start | bytes 6148
  30.4 63.3 %copy-start.29 = (f32[512]{0:T(512)S(1)}, f32[512]{0:T(512)}, u32[]{:S(2)}) copy-start(f32[512]{0:T(512)} %param.12) | copy-start | bytes 6148
  93.7 255.6 %all-gather.6.cloned.1.call-start = ((), (), s32[]{:S(2)}) async-start(), calls=%async_computation.4 | async-start | bytes 3932160 | tf_op jit(solution)/shard_map/all_gather | solution.py:1011
  93.7 55.8 %collective-permute-start = (f32[2,512]{1,0:T(2,128)S(1)}, f32[2,512]{1,0:T(2,128)S(1)}, u32[]{:S(2)}, u32[]{:S(2)}) collective-permute-start(f32[2,512]{1,0:T(2,128)S(1)} %get-tuple-element.136), channel_id=1, source_target_pairs={{0,1},{1,0},{2,3},{3,2},{4,5},{5,4},{6,7},{7,6},{8,9},{9,8},{10,11... | collective-permute-start | bytes 12296 | tf_op jit(solution)/shard_map/ppermute | solution.py:1008
  144.3 383.9 %reduce-scatter.4.cloned.1.call-start = ((), (), s32[]{:S(2)}) async-start(), calls=%async_computation.6 | async-start | bytes 11796480 | tf_op jit(solution)/shard_map/reduce_scatter | solution.py:1014
  149.5 3.7 collective-permute-start.1
  150.7 2.7 copy-start.26
  153.4 10.3 %copy-start.7 = (f32[1,2048]{1,0:T(1,128)}, f32[1,2048]{1,0:T(1,128)S(1)}, u32[]{:S(2)}) copy-start(f32[1,2048]{1,0:T(1,128)S(1)} %get-tuple-element.128.gain_ref) | copy-start | bytes 24580
  163.6 18.2 %copy-start.17 = (bf16[2048,768]{1,0:T(8,128)(2,1)}, bf16[2048,768]{1,0:T(8,128)(2,1)S(1)}, u32[]{:S(2)}) copy-start(bf16[2048,768]{1,0:T(8,128)(2,1)S(1)} %convolution_convert_fusion.1.packed_ref) | copy-start | bytes 9437188
  263.4 1.3 copy-start.21
  328.6 1.7 copy-start.20
  330.3 297.6 %reduce-scatter.6.cloned.1.call-start = ((), (), s32[]{:S(2)}) async-start(), calls=%async_computation.7 | async-start | bytes 5242880 | tf_op jit(solution)/shard_map/reduce_scatter | solution.py:1014
  349.2 11.2 %copy-start = (bf16[2048,768]{1,0:T(8,128)(2,1)S(1)}, bf16[2048,768]{1,0:T(8,128)(2,1)}, u32[]{:S(2)}) copy-start(bf16[2048,768]{1,0:T(8,128)(2,1)} %all-gather.6.cloned.1.call-done.gate_ref.up_ref.down_ref.refs_1_.refs_3_) | copy-start | bytes 9437188
  360.4 93.0 %copy-start.5 = (bf16[2048,256]{1,0:T(8,128)(2,1)}, bf16[2048,256]{1,0:T(8,128)(2,1)S(1)}, u32[]{:S(2)}) copy-start(bf16[2048,256]{1,0:T(8,128)(2,1)S(1)} %get-tuple-element.91.refs_4_.refs_1_) | copy-start | bytes 3145732
  360.4 9.8 %copy-start.22 = (f32[256,2048]{1,0:T(8,128)S(1)}, f32[256,2048]{1,0:T(8,128)}, u32[]{:S(2)}) copy-start(f32[256,2048]{1,0:T(8,128)} %copy-done.21) | copy-start | bytes 6291460
  370.3 83.1 %copy-start.2 = (bf16[2048,256]{1,0:T(8,128)(2,1)S(1)}, bf16[2048,256]{1,0:T(8,128)(2,1)}, u32[]{:S(2)}) copy-start(bf16[2048,256]{1,0:T(8,128)(2,1)} %copy-done.1) | copy-start | bytes 3145732
  469.4 175.7 %reduce-scatter.8.cloned.1.call-start = ((), (), s32[]{:S(2)}) async-start(), calls=%async_computation.8 | async-start | bytes 3932160 | tf_op jit(solution)/shard_map/reduce_scatter | solution.py:1014
  475.6 18.0 %copy-start.8 = (f32[1,2048]{1,0:T(1,128)S(1)}, f32[1,2048]{1,0:T(1,128)}, u32[]{:S(2)}) copy-start(f32[1,2048]{1,0:T(1,128)} %copy-done.7) | copy-start | bytes 24580
  475.6 18.0 %copy-start.27 = (f32[2048]{0:T(1024)S(1)}, f32[2048]{0:T(1024)}, u32[]{:S(2)}) copy-start(f32[2048]{0:T(1024)} %copy-done.26) | copy-start | bytes 24580
  504.8 1.7 copy-start.18
  506.5 1.9 copy-start.19
  508.4 1.6 copy-start.25
  510.0 21.0 %copy-start.6 = (bf16[2048,256]{1,0:T(8,128)(2,1)S(1)}, bf16[2048,256]{1,0:T(8,128)(2,1)}, u32[]{:S(2)}) copy-start(bf16[2048,256]{1,0:T(8,128)(2,1)} %copy-done.5) | copy-start | bytes 3145732
  530.6 117.7 %collective-permute-start.4 = (bf16[256,2304]{1,0:T(8,128)(2,1)}, bf16[256,2304]{1,0:T(8,128)(2,1)S(1)}, u32[]{:S(2)}, u32[]{:S(2)}) collective-permute-start(bf16[256,2304]{1,0:T(8,128)(2,1)} %constant_dynamic-slice_fusion), channel_id=1, source_target_pairs={{0,4},{4,0},{8,12},{12,8},{16,20},{20,16},{24,28},{28,24},{1,5},{5... | collective-permute-start | bytes 3538952 | tf_op jit(solution)/shard_map/ppermute | solution.py:1002
  531.0 1.6 copy-start.23
  629.9 15.2 %collective-permute-start.2 = (bf16[256,1024]{1,0:T(8,128)(2,1)}, bf16[256,1024]{1,0:T(8,128)(2,1)}, u32[]{:S(2)}, u32[]{:S(2)}) collective-permute-start(bf16[256,1024]{1,0:T(8,128)(2,1)} %constant_dynamic-slice_fusion.2), channel_id=1, source_target_pairs={{0,4},{4,0},{8,12},{12,8},{16,20},{20,16},{24,28},{28,24},{1,5},{5... | collective-permute-start | bytes 1572872 | tf_op jit(solution)/shard_map/ppermute | solution.py:1002
  645.0 11.9 %copy-start.4 = (bf16[512,768]{1,0:T(8,128)(2,1)S(1)}, bf16[512,768]{1,0:T(8,128)(2,1)}, u32[]{:S(2)}) copy-start(bf16[512,768]{1,0:T(8,128)(2,1)} %reduce-scatter.8.cloned.1.call-done.refs_0_) | copy-start | bytes 2359300
  646.1 10.8 %collective-permute-start.3 = (bf16[256,768]{1,0:T(8,128)(2,1)S(1)}, bf16[256,768]{1,0:T(8,128)(2,1)S(1)}, u32[]{:S(2)}, u32[]{:S(2)}) collective-permute-start(bf16[256,768]{1,0:T(8,128)(2,1)S(1)} %constant_dynamic-slice_fusion.1), channel_id=1, source_target_pairs={{0,4},{4,0},{8,12},{12,8},{16,20},{20,16},{24,28},{28,24},{1,5},{5... | collective-permute-start | bytes 1179656 | tf_op jit(solution)/shard_map/ppermute | solution.py:1002
  (9 other events, 10.0 us)
Sparse Core Ops, SparseCore 0:
  27.7 81.0 all-gather.3
  110.3 165.2 all-gather.7
  277.3 61.6 all-gather.5
  341.2 159.9 reduce-scatter.3
  503.3 77.5 reduce-scatter.5
  583.2 61.7 reduce-scatter.7

commit v7 on v6

--- a/solution.py
+++ b/solution.py
@@ -290,10 +290,8 @@
             if after is None and which == half:
                 self.copy(k).start()
 
-    def forward(self):
-        for first in range(8):
-            if first in (4, 5):
-                continue
+    def forward(self, arrivals=(0, 1, 2, 3, 6, 7)):
+        for first in arrivals:
             self.arrival(first).wait_recv()
             for k, (_, _, _, after) in enumerate(SPREAD):
                 if after == first:
@@ -308,6 +306,26 @@
 
 
 SPREAD_SEMS = [pltpu.SemaphoreType.DMA((len(SPREAD),))] * 2
+
+
+def block_spread(shard_ref, out_ref, local, send, recv):
+    rows, wide = shard_ref.shape
+    half = rows // 2
+
+    def own(which):
+        return shard_ref.at[pl.ds(which * half, half)]
+
+    def region(r, which):
+        member, slot = owner(r)
+        return out_ref.at[
+            pl.ds(pl.multiple_of(member * rows + which * half, half), half),
+            pl.ds(pl.multiple_of(slot * wide, wide), wide),
+        ]
+
+    copies = [
+        pltpu.make_async_copy(own(which), region(0, which), local.at[which]) for which in range(2)
+    ]
+    return Spread(own, region, send, recv), copies
 
 
 class Collect:
@@ -425,6 +443,81 @@
     )(*operands)
 
 
+class RingBlocks:
+    def __init__(self, ring, source, out_ref, send, recv):
+        self.ring, self.source, self.out, self.send, self.recv = ring, source, out_ref, send, recv
+        self.count = out_ref.shape[0]
+        self.stage = 0
+
+    def copy(self, k):
+        source = self.source if k == 0 else self.out.at[k - 1]
+        return pltpu.make_async_remote_copy(
+            source, self.out.at[k], self.send.at[k], self.recv.at[k],
+            device_id=ring_peer(self.ring, 1), device_id_type=MESH,
+        )
+
+    def start(self):
+        self.copy(0).start()
+
+    def advance(self):
+        if self.stage + 1 < self.count:
+            self.copy(self.stage).wait_recv()
+            self.stage += 1
+            self.copy(self.stage).start()
+
+    def finish(self):
+        while self.stage + 1 < self.count:
+            self.advance()
+        self.copy(self.count - 1).wait_recv()
+        for k in range(self.count):
+            self.copy(k).wait_send()
+
+
+class RowsSwap:
+    def __init__(self, ring, blocks, out_ref, local, send, recv):
+        self.ring, self.blocks, self.out = ring, blocks, out_ref
+        self.local, self.send, self.recv = local, send, recv
+        token = lax.axis_index("tok")
+        self.place, self.member = lax.div(token, 2), lax.rem(token, 2)
+        self.peer = neighbours()["y"]
+
+    def block(self, s, half):
+        width = self.out.shape[1]
+        return self.blocks[s].at[:, pl.ds(pl.multiple_of(half * width, width), width)]
+
+    def target(self, s, member):
+        size = self.out.shape[0] // self.ring // 2
+        place = lax.rem(self.place + self.ring - s, self.ring)
+        return self.out.at[pl.ds(pl.multiple_of((2 * place + member) * size, size), size)]
+
+    def remote(self, s, source, member):
+        return pltpu.make_async_remote_copy(
+            source, self.target(s, member), self.send.at[s], self.recv.at[s],
+            device_id=self.peer, device_id_type=MESH,
+        )
+
+    def own(self, s):
+        return pltpu.make_async_copy(
+            self.block(s, self.member), self.target(s, self.member), self.local.at[s]
+        )
+
+    def away(self, s):
+        return self.remote(s, self.block(s, 1 - self.member), self.member)
+
+    def start(self):
+        for s in range(self.ring):
+            self.away(s).start()
+        for s in range(self.ring):
+            self.own(s).start()
+
+    def finish(self):
+        for s in range(self.ring):
+            other = 1 - self.member
+            self.remote(s, self.target(s, other), other).wait_recv()
+            self.away(s).wait_send()
+            self.own(s).wait()
+
+
 class PairSwap:
     def __init__(self, sources, out_ref, pieces, local, send, recv):
         self.sources, self.out, self.pieces = sources, out_ref, pieces
@@ -471,62 +564,138 @@
             self.own(i).wait()
 
 
-def swap_and_gather(identity, weights, pieces, shard=None):
+def swap_first(identity, weights, pieces, ring, block, count):
+    size = weights[0].shape[0]
+    outputs = [
+        jax.ShapeDtypeStruct((2 * size, sum(piece[2] for piece in pieces)), weights[0].dtype),
+        jax.ShapeDtypeStruct((count, *block.shape), block.dtype),
+    ]
+
+    def swap_start(*refs):
+        sources, (block_ref, start_ref, blocks_ref, *sems) = refs[: len(weights)], refs[len(weights) :]
+        greet([ring_peer(ring, 1), ring_peer(ring, ring - 1)])
+        around = RingBlocks(ring, block_ref, blocks_ref, *sems[3:])
+        pair = PairSwap(sources, start_ref, pieces, *sems[:3])
+        around.start()
+        pair.start()
+        around.finish()
+        pair.finish()
+
+    operands = (*weights, block)
+    return call(
+        swap_start, identity, operands, (pl.ANY,) * len(operands),
+        outputs, [pl.ANY] * len(outputs),
+        [pltpu.SemaphoreType.DMA((len(pieces),))] * 3 + [pltpu.SemaphoreType.DMA((count,))] * 2,
+        15_000_000_000,
+    )
+
+
+def swap_and_gather(identity, weights, pieces, shard, ring, blocks, steps, small):
     count = len(weights)
     size = weights[0].shape[0]
     columns = sum(piece[2] for piece in pieces)
-    operands = tuple(weights)
-    outputs = [jax.ShapeDtypeStruct((2 * size, columns), weights[0].dtype)]
-    scratch = [pltpu.SemaphoreType.DMA((len(pieces),))] * 3
-    if shard is not None:
-        rows, wide = shard.shape
-        half = rows // 2
-        operands += (shard,)
-        outputs.append(jax.ShapeDtypeStruct((2 * rows, 4 * wide), shard.dtype))
-        scratch += [pltpu.SemaphoreType.DMA((2,))] + SPREAD_SEMS
+    rows, wide = shard.shape
+    operands = (*weights, shard, blocks, small)
+    small_rows, small_wide = small.shape
+    outputs = [
+        jax.ShapeDtypeStruct((2 * size, columns), weights[0].dtype),
+        jax.ShapeDtypeStruct((2 * rows, 4 * wide), shard.dtype),
+        jax.ShapeDtypeStruct((steps, *blocks.shape[1:]), shard.dtype),
+        jax.ShapeDtypeStruct((small_rows, 4 * small_wide), small.dtype),
+    ]
 
     def swap_gather(*refs):
         sources, refs = refs[:count], refs[count:]
-        if shard is not None:
-            shard_ref, start_ref, out_ref, *sems = refs
-        else:
-            start_ref, *sems = refs
-        greet()
+        shard_ref, blocks_ref, small_ref, start_ref, out_ref, around_ref, whole_ref, *sems = refs
+        small_send, small_recv = sems[8:]
+        greet([ring_peer(ring, 1), ring_peer(ring, ring - 1)])
+
+        def small_place(r):
+            _, slot = owner(r)
+            return whole_ref.at[:, pl.ds(pl.multiple_of(slot * small_wide, small_wide), small_wide)]
+
+        def small_copy(k, source, place):
+            return pltpu.make_async_remote_copy(
+                source, place, small_send.at[k], small_recv.at[k],
+                device_id=neighbours()[("core", "x", "core")[k]], device_id_type=MESH,
+            )
+
+        small_copies = [
+            small_copy(0, small_ref, small_place(0)),
+            small_copy(1, small_ref, small_place(0)),
+            small_copy(2, small_place(2), small_place(2)),
+        ]
+        small_copies[0].start()
+        small_copies[1].start()
+        last = blocks_ref.at[blocks.shape[0] - 1]
+        around = RingBlocks(ring, last, around_ref, *sems[6:8])
+        around.start()
         pair = PairSwap(sources, start_ref, pieces, *sems[:3])
         pair.start()
-        if shard is None:
-            pair.finish()
-            return
-
-        def own(which):
-            return shard_ref.at[pl.ds(which * half, half)]
-
-        def region(r, which):
-            member, slot = owner(r)
-            return out_ref.at[
-                pl.ds(pl.multiple_of(member * rows + which * half, half), half),
-                pl.ds(pl.multiple_of(slot * wide, wide), wide),
-            ]
-
-        spread = Spread(own, region, *sems[4:])
+        spread, copies = block_spread(shard_ref, out_ref, *sems[3:6])
         spread.start(0)
         spread.start(1)
-        copies = [
-            pltpu.make_async_copy(own(which), region(0, which), sems[3].at[which])
-            for which in range(2)
-        ]
         for copy in copies:
             copy.start()
-        spread.forward()
+        small_copy(1, small_place(2), small_place(2)).wait_recv()
+        small_copies[2].start()
+        whole_ref[:, pl.ds(pl.multiple_of(owner(0)[1] * small_wide, small_wide), small_wide)] = (
+            small_ref[...]
+        )
+        spread.forward((0, 1, 2, 3))
+        around.advance()
+        spread.forward((6, 7))
         spread.finish()
         pair.finish()
+        around.finish()
+        small_copy(0, small_place(1), small_place(1)).wait_recv()
+        small_copy(2, small_place(3), small_place(3)).wait_recv()
+        for copy in small_copies:
+            copy.wait_send()
         for copy in copies:
             copy.wait()
 
     return call(
-        swap_gather, identity, operands, (pl.ANY,) * len(operands),
-        outputs, [pl.ANY] * len(outputs), scratch,
-        15_000_000_000 if shard is None else 50_000_000_000,
+        swap_gather, identity, operands, (pl.ANY,) * (len(operands) - 1) + (pltpu.VMEM,),
+        outputs, [pl.ANY] * (len(outputs) - 1) + [pltpu.VMEM],
+        [pltpu.SemaphoreType.DMA((len(pieces),))] * 3
+        + [pltpu.SemaphoreType.DMA((2,))]
+        + SPREAD_SEMS
+        + [pltpu.SemaphoreType.DMA((steps,))] * 2
+        + [pltpu.SemaphoreType.DMA((3,))] * 2,
+        50_000_000_000,
+    )
+
+
+def swap_pairs(identity, weights, pieces, ring, blocks):
+    count = len(weights)
+    size = weights[0].shape[0]
+    columns = sum(piece[2] for piece in pieces)
+    block_size, block_wide = blocks[0].shape[-2:]
+    operands = (*weights, *blocks)
+    outputs = [
+        jax.ShapeDtypeStruct((2 * size, columns), weights[0].dtype),
+        jax.ShapeDtypeStruct((2 * ring * block_size, block_wide // 2), weights[0].dtype),
+    ]
+
+    def swap_last(*refs):
+        greet()
+        start_ref, out_ref, *sems = refs[len(operands) :]
+        parts = []
+        for ref in refs[count : len(operands)]:
+            parts += [ref] if len(ref.shape) == 2 else [ref.at[k] for k in range(ref.shape[0])]
+        around = RowsSwap(ring, parts, out_ref, *sems[3:])
+        around.start()
+        pair = PairSwap(refs[:count], start_ref, pieces, *sems[:3])
+        pair.start()
+        around.finish()
+        pair.finish()
+
+    return call(
+        swap_last, identity, operands, (pl.ANY,) * len(operands),
+        outputs, [pl.ANY] * len(outputs),
+        [pltpu.SemaphoreType.DMA((len(pieces),))] * 3 + [pltpu.SemaphoreType.DMA((ring,))] * 3,
+        20_000_000_000,
     )
 
 
@@ -605,16 +774,17 @@
     return region
 
 
-def middle_norm(identity, terms, x_all, gain):
+def middle_norm(identity, terms, x_all, gain, cotangent):
     total, model = terms.shape
     quarter = total // 8
     half = quarter // 2
 
     def middle_step(
-        terms_ref, x_ref, gain_ref, out_ref, middle_ref, factor_ref,
-        x_own, normed, local, send, recv, *scratch
+        terms_ref, x_ref, gain_ref, shard_ref, out_ref, middle_ref, factor_ref, cot_ref,
+        x_own, normed, local, send, recv, cot_local, cot_send, cot_recv, *scratch
     ):
         greet()
+        beside, copies = block_spread(shard_ref, cot_ref, cot_local, cot_send, cot_recv)
         x_copy = pltpu.make_async_copy(row_parts(x_ref, quarter)(0), x_own, local.at[0])
         x_copy.start()
         collect = Collect(row_parts(terms_ref, quarter), quarter, *scratch[:6], scratch[6:])
@@ -623,10 +793,14 @@
             lambda which: normed.at[pl.ds(which * half, half)], region, send, recv
         )
         collect.start()
+        beside.start(0)
+        beside.start(1)
+        for copy in copies:
+            copy.start()
         collect.first()
+        beside.forward((0, 1, 2, 3))
         collect.second()
         x_copy.wait()
-        copies = []
         for which in range(2):
             collect.ready(which)
 
@@ -646,28 +820,34 @@
             )
             copy.start()
             copies.append(copy)
+        beside.forward((6, 7))
         spread.forward()
         spread.finish()
+        beside.finish()
         collect.finish()
         for copy in copies:
             copy.wait()
 
     return call(
-        middle_step, identity, (terms, x_all, gain), (pl.ANY, pl.ANY, pltpu.VMEM),
+        middle_step, identity, (terms, x_all, gain, cotangent),
+        (pl.ANY, pl.ANY, pltpu.VMEM, pl.ANY),
         (
             jax.ShapeDtypeStruct((total, model), BF16),
             jax.ShapeDtypeStruct((quarter, model), F32),
             jax.ShapeDtypeStruct((quarter, 128), F32),
+            jax.ShapeDtypeStruct((total, model), BF16),
         ),
-        (pl.ANY, pltpu.VMEM, pltpu.VMEM),
+        (pl.ANY, pltpu.VMEM, pltpu.VMEM, pl.ANY),
         [
             pltpu.VMEM((quarter, model), BF16),
             pltpu.VMEM((quarter, model), BF16),
             pltpu.SemaphoreType.DMA((3,)),
         ]
         + SPREAD_SEMS
+        + [pltpu.SemaphoreType.DMA((2,))]
+        + SPREAD_SEMS
         + Collect.scratch(quarter, model),
-        70_000_000_000,
+        100_000_000_000,
     )
 
 
@@ -1001,12 +1181,6 @@
     def swap(value):
         return lax.ppermute(value, "tok", [(i, i ^ 1) for i in range(tok_size)])
 
-    def x_swap(value):
-        return lax.ppermute(value, "feat", [(i, i ^ 2) for i in range(4)])
-
-    def core_swap(value):
-        return lax.ppermute(value, "feat", [(i, i ^ 1) for i in range(4)])
-
     def ring_gather(shard):
         return lax.all_gather(shard, "tok", axis=0, tiled=True, axis_index_groups=groups)
 
@@ -1028,39 +1202,43 @@
         for left in range(0, heads_wide, pair_width)
         for part in range(3)
     ]
-    attention_pieces.append((3, 0, heads_wide, 3 * heads_wide))
-    (attention_start,) = swap_and_gather(0, (w_query, w_key, w_value, w_out.T), attention_pieces)
+    ring = tok_size // 2
+    early = 1
+    out_blocks = [w_out.T]
+    attention_start, block = swap_first(
+        0, (w_query, w_key, w_value), attention_pieces, ring, out_blocks[0], early
+    )
+    out_blocks.append(block)
     feed = (w_gate, w_up, w_down.T)
     tokens_after, attention_start = lax.optimization_barrier((tokens, attention_start))
-    attention_weights = ring_gather(attention_start)
-    feed_weights = []
-    wholes = []
-    for c, shard in enumerate((tokens_after, cotangent)):
-        if c:
-            shard, wholes[0] = lax.optimization_barrier((shard, wholes[0]))
-        pieces = [(part, lefts[c], chunks[c], part * chunks[c]) for part in range(3)]
-        start, whole = swap_and_gather(1 + c, feed, pieces, shard)
-        wholes.append(whole)
-        feed_weights.append(ring_gather(start))
-    x_all, cot_rows = wholes
-    qkv = attention_weights[:, : 3 * heads_wide]
-    out_proj = attention_weights[:, 3 * heads_wide :]
-
-    gains = jnp.stack([gain_attn, gain_ffn])
-    gains = jnp.stack([gains, core_swap(gains)])
-    gains = jnp.concatenate([gains, x_swap(gains)])
-    gains = jnp.concatenate(
-        [lax.dynamic_index_in_dim(gains, feat ^ j, 0, keepdims=False) for j in range(4)], axis=1
+    qkv = ring_gather(attention_start)
+    plans = [
+        [(part, left, size, part * size) for part in range(3)] for left, size in zip(lefts, chunks)
+    ]
+    first_start, x_all, block, gains = swap_and_gather(
+        1,
+        feed,
+        plans[0],
+        tokens_after,
+        ring,
+        out_blocks[-1],
+        ring - 1 - early,
+        jnp.stack([gain_attn, gain_ffn]),
     )
     gain_one, gain_two = gains[:1], gains[1:]
+    out_blocks.append(block)
+    feed_weights = [ring_gather(first_start)]
+    w_gate, x_all = lax.optimization_barrier((w_gate, x_all))
+    last_start, out_proj = swap_pairs(2, (w_gate, *feed[1:]), plans[1], ring, out_blocks)
+    feed_weights.append(ring_gather(last_start))
 
     x_wide = x_all.astype(F32)
     factor_one = lax.rsqrt(jnp.mean(x_wide * x_wide, axis=1, keepdims=True) + EPSILON)
     normed = (x_wide * factor_one * gain_one).astype(BF16)
     packed = product(normed, qkv).astype(BF16)
     attended, log_sums = attend(packed)
-    normed_two, middle, factor_two = middle_norm(
-        3, right_trans(attended, out_proj).astype(BF16), x_all, gain_two
+    normed_two, middle, factor_two, cot_rows = middle_norm(
+        3, right_trans(attended, out_proj).astype(BF16), x_all, gain_two, cotangent
     )
 
     own = (member * 4 + feat).astype(jnp.int32).reshape(1)
@@ -1098,7 +1276,7 @@
     attention_terms = left_trans(normed, grad_packed).astype(BF16)
     attention_terms, grad_packed = lax.optimization_barrier((attention_terms, grad_packed))
     attention_sum = ring_scatter(attention_terms)
-    terms, gain_attn_part = input_terms(grad_packed, attention_weights, x_all, gain_one, grad_middle, own)
+    terms, gain_attn_part = input_terms(grad_packed, qkv, x_all, gain_one, grad_middle, own)
     hiddens[0], terms, feed_sums[0] = lax.optimization_barrier((hiddens[0], terms, feed_sums[0]))
     out_rows = columns_back(hiddens, feed_weights, 2, own, None, middle)
     outcome, input_grad, gain_grads = scatter_blocks(

time: 674 us -> 664 us (0.985)
  waiting for transfers between devices: 29.8 us -> 14.4 us
    all_gather x3, waiting for transfers between devices: 11 us -> 0.02 us  [ring_gather(): lax.all_gather(shard, 'tok', axis=0, tiled=True, axis_index_groups=groups)]
    unnamed x62 -> x76, local copies, waits for them, and re-layouts: 22.5 us -> 26.9 us
  transfers between devices with their start and end apart: 11 -> 9, of which waited for: 4 -> 3; matrix products, arithmetic and copies ran while one was open for 7% -> 7% of each run, Pallas kernels for 80% -> 82%
where the time goes in v7:
time: 664 us; the launch traced here: 655 us
  Pallas kernels  551 us (83%)
  local copies, waits for them, and re-layouts  32.8 us (5%)
  matrix products  32.7 us (5%)
  between operations  15 us (2%)
  waiting for transfers between devices  14.4 us (2%)
    pallas_call x6, Pallas kernels, call(): pl.pallas_call(kernel, out_shape=outputs, in_specs=[pl.BlockSpec(memory_s...  375 us
    pallas_call x3, Pallas kernels, columns_back(): pl.pallas_call(columns_step, grid_spec=pltpu.PrefetchScalarGridSpec(num_s...  42.1 us
    pallas_call x2, Pallas kernels, weight_terms(): pl.pallas_call(terms_step, grid=(model // tile,), in_specs=[pl.BlockSpec(...  41.9 us
    pallas_call x2, Pallas kernels, feed_forward(): pl.pallas_call(feed_step, grid=(total // tile,), in_specs=[rows, rows, we...  38.6 us
    unnamed x76, local copies, waits for them, and re-layouts  26.9 us
    pallas_call x1, Pallas kernels, attend_back(): pl.pallas_call(attend_back_kernel, grid=(sequences, pairs), out_shape=jax...  18 us
    pallas_call x1, Pallas kernels, input_terms(): pl.pallas_call(input_terms_step, grid_spec=pltpu.PrefetchScalarGridSpec(n...  17.9 us
    dot_general x2, matrix products, product(): return jnp.dot(left, right, preferred_element_type=F32)  15.9 us
  transfers between devices with their start and end apart: 9, of which 3 were waited for; matrix products, arithmetic and copies ran while one was open for 7% of the time, Pallas kernels for 82%

profile of v7, /device:TPU:0, one launch (start us, length us, event | category | flops | bytes accessed | tf_op | source)
XLA Modules:
  0.0 655.3 jit_solution(824397267476603806)
XLA Ops:
  11.2 15.7 %swap_start.1 = (bf16[512,768]{1,0:T(8,128)(2,1)}, bf16[1,256,512]{2,1,0:T(8,128)(2,1)S(1)}) custom-call(bf16[256,512]{1,0:T(8,128)(2,1)S(1)} %copy-done.17, bf16[256,512]{1,0:T(8,128)(2,1)S(1)} %copy-done.18, bf16[256,512]{1,0:T(8,128)(2,1)S(1)} %copy-done.19, bf16[256,512]{1,0:T(8,128)(2,1)S(1)} %bitcast.16), custom_call_target="tpu_custom_call" | custom-call | flops 15000000512 | bytes 150000000 | tf_op jit(solution)/shard_map/swap_start/pallas_call | solution.py:432
  27.0 1.5 copy.22
  31.0 65.4 %swap_gather.1 = (bf16[512,2304]{1,0:T(8,128)(2,1)}, bf16[2048,2048]{1,0:T(8,128)(2,1)}, bf16[2,256,512]{2,1,0:T(8,128)(2,1)S(1)}, f32[2,2048]{1,0:T(2,128)S(1)}) custom-call(bf16[256,2048]{1,0:T(8,128)(2,1)S(1)} %copy-done.12, bf16[256,2048]{1,0:T(8,128)(2,1)S(1)} %copy-done.14, bf16[256,2048]{1,0:T(8,128)(2,1)S(1)} %bitcast.14, ...), custom_call_target="tpu_custom_call" | custom-call | flops 49999998976 | bytes 500000000 | tf_op jit(solution)/shard_map/swap_gather/pallas_call | solution.py:432
  101.6 22.5 %swap_last.1 = (bf16[512,768]{1,0:T(8,128)(2,1)}, bf16[2048,256]{1,0:T(8,128)(2,1)S(1)}) custom-call(bf16[256,2048]{1,0:T(8,128)(2,1)S(1)} %copy-done.13, bf16[256,2048]{1,0:T(8,128)(2,1)S(1)} %copy-done.15, bf16[256,2048]{1,0:T(8,128)(2,1)S(1)} %bitcast.15, bf16[256,512]{1,0:T(8,128)(2,1)S(1)} %bitcast.17, bf16[1,256,512]{2,1,0:T(8,128)(2,1)S(1)} %copy-done.32, ...), custom_call_target="tpu_custom_call" | custom-call | flops 20000000000 | bytes 200000000 | tf_op jit(solution)/shard_map/swap_last/pallas_call | solution.py:432
  124.3 5.5 fusion
  130.3 10.2 %convolution_convert_fusion.1.packed_ref = bf16[2048,768]{1,0:T(8,128)(2,1)S(1)} fusion(bf16[2048,768]{1,0:T(8,128)(2,1)} %all-gather.4.cloned.1.call-done.qkv_ref, bf16[2048,2048]{1,0:T(8,128)(2,1)} %get-tuple-element.78.x_ref, f32[2048]{0:T(1024)S(1)} %bitcast.18, f32[2048]{0:T(1024)S(1)} %add_rsqrt_fusion), kind=kOutput, calls=%fused_computation.6 | convolution fusion | flops 6460801024 | bytes 14696448 | tf_op jit(solution)/shard_map/dot_general | solution.py:33
  140.5 11.3 %attend.1 = (bf16[2048,256]{1,0:T(8,128)(2,1)S(1)}, f32[2,2,2,1024]{3,2,1,0:T(2,128)S(1)}) custom-call(bf16[2048,768]{1,0:T(8,128)(2,1)S(1)} %convolution_convert_fusion.1.packed_ref), custom_call_target="tpu_custom_call" | custom-call | flops 1073741824 | bytes 6291456 | tf_op jit(solution)/shard_map/attend/pallas_call | solution.py:106
  151.8 5.7 convolution_convert_fusion.terms_ref
  158.5 109.3 %middle_step.1 = (bf16[2048,2048]{1,0:T(8,128)(2,1)}, f32[256,2048]{1,0:T(8,128)S(1)}, f32[256,128]{1,0:T(8,128)S(1)}, bf16[2048,2048]{1,0:T(8,128)(2,1)}) custom-call(bf16[2048,2048]{1,0:T(8,128)(2,1)} %convolution_convert_fusion.terms_ref, bf16[2048,2048]{1,0:T(8,128)(2,1)} %get-tuple-element.78.x_ref, f32[1,2048]{1,0:T(1,128)S(1)} %get-tuple-element.137.gain_ref, ...), custom_call_target="tpu_custom_call" | custom-call | flops 99999997952 | bytes 1000000000 | tf_op jit(solution)/shard_map/middle_step/pallas_call | solution.py:432
  269.2 27.5 %feed_forward.2 = (bf16[2048,768]{1,0:T(8,128)(2,1)S(1)}, bf16[2048,1536]{1,0:T(8,128)(2,1)}) custom-call(bf16[2048,2048]{1,0:T(8,128)(2,1)} %get-tuple-element.85.normed_ref.refs_0_, bf16[2048,2048]{1,0:T(8,128)(2,1)} %get-tuple-element.86.cot_ref.refs_1_, bf16[2048,2304]{1,0:T(8,128)(2,1)} %all-gather.8.cloned.1.call-done.gate_ref.up_ref.down_ref.refs_1_.refs_2_, ...), custom_call_target="tpu_custom_call" | custom-call | flops 19327352832 | bytes 35651584 | tf_op jit(solution)/shard_map/feed_forward/pallas_call | solution.py:1052
  296.6 25.9 %weight_terms.2 = bf16[2048,2304]{1,0:T(8,128)(2,1)} custom-call(bf16[2048,2048]{1,0:T(8,128)(2,1)} %get-tuple-element.85.normed_ref.refs_0_, bf16[2048,2048]{1,0:T(8,128)(2,1)} %get-tuple-element.86.cot_ref.refs_1_, bf16[2048,1536]{1,0:T(8,128)(2,1)} %get-tuple-element.91.refs_2_.refs_0_, bf16[2048,768]{1,0:T(8,128)(2,1)S(1)} %get-tuple-element.110.refs_3_.refs_0_), custom_call_target="tpu_custom_call" | custom-call | flops 19327352832 | bytes 35651584 | tf_op jit(solution)/shard_map/weight_terms/pallas_call | solution.py:1148
  322.6 1.7 copy-done.23
  324.3 18.6 %columns_back.3.refs_2_ = bf16[2048,2048]{1,0:T(8,128)(2,1)} custom-call(s32[1]{0:T(128)} %bitcast.own_ref, bf16[2048,1536]{1,0:T(8,128)(2,1)} %get-tuple-element.91.refs_2_.refs_0_, bf16[2048,2304]{1,0:T(8,128)(2,1)} %all-gather.8.cloned.1.call-done.gate_ref.up_ref.down_ref.refs_1_.refs_2_), custom_call_target="tpu_custom_call" | custom-call | flops 12884901888 | bytes 20971520 | tf_op jit(solution)/shard_map/columns_back/pallas_call | solution.py:1115
  342.9 11.2 %feed_forward.3 = (bf16[2048,256]{1,0:T(8,128)(2,1)S(1)}, bf16[2048,512]{1,0:T(8,128)(2,1)S(1)}) custom-call(bf16[2048,2048]{1,0:T(8,128)(2,1)} %get-tuple-element.85.normed_ref.refs_0_, bf16[2048,2048]{1,0:T(8,128)(2,1)} %get-tuple-element.86.cot_ref.refs_1_, bf16[2048,768]{1,0:T(8,128)(2,1)} %all-gather.6.cloned.1.call-done.gate_ref.up_ref.down_ref.refs_1_.refs_3_, ...), custom_call_target="tpu_custom_call" | custom-call | flops 6442450944 | bytes 23068672 | tf_op jit(solution)/shard_map/feed_forward/pallas_call | solution.py:1052
  354.2 9.8 %columns_back.4.terms_ref = bf16[2048,2048]{1,0:T(8,128)(2,1)} custom-call(s32[1]{0:T(128)} %bitcast.own_ref, bf16[2048,512]{1,0:T(8,128)(2,1)S(1)} %get-tuple-element.100.refs_0_.refs_3_, bf16[2048,768]{1,0:T(8,128)(2,1)S(1)} %copy-done, bf16[2048,2048]{1,0:T(8,128)(2,1)} %columns_back.3.refs_2_), custom_call_target="tpu_custom_call" | custom-call | flops 4294967296 | bytes 12582912 | tf_op jit(solution)/shard_map/columns_back/pallas_call | solution.py:1115
  364.0 80.5 %middle_back_step.1 = (bf16[2048,2048]{1,0:T(8,128)(2,1)}, f32[256,2048]{1,0:T(8,128)S(1)}, f32[1,2048]{1,0:T(1,128)S(1)}) custom-call(bf16[2048,2048]{1,0:T(8,128)(2,1)} %columns_back.4.terms_ref, bf16[2048,2048]{1,0:T(8,128)(2,1)} %get-tuple-element.86.cot_ref.refs_1_, f32[256,2048]{1,0:T(8,128)S(1)} %copy-done.25, ...), custom_call_target="tpu_custom_call" | custom-call | flops 70000001024 | bytes 700000000 | tf_op jit(solution)/shard_map/middle_back_step/pallas_call | solution.py:432
  445.9 16.0 %weight_terms.3 = bf16[2048,1024]{1,0:T(8,128)(2,1)} custom-call(bf16[2048,2048]{1,0:T(8,128)(2,1)} %get-tuple-element.85.normed_ref.refs_0_, bf16[2048,2048]{1,0:T(8,128)(2,1)} %get-tuple-element.86.cot_ref.refs_1_, bf16[2048,2048]{1,0:T(8,128)(2,1)} %get-tuple-element.102.refs_2_, bf16[2048,512]{1,0:T(8,128)(2,1)S(1)} %get-tuple-element.100.refs_0_.refs_3_, ...), custom_call_target="tpu_custom_call" | custom-call | flops 8589934592 | bytes 33554432 | tf_op jit(solution)/shard_map/weight_terms/pallas_call | solution.py:1148
  461.9 5.8 convolution_convert_fusion.3.grad_ref
  467.7 18.0 %attend_back.1.grad_ref = bf16[2048,768]{1,0:T(8,128)(2,1)S(1)} custom-call(bf16[2048,768]{1,0:T(8,128)(2,1)} %copy-done.20, bf16[2048,256]{1,0:T(8,128)(2,1)S(1)} %copy-done.2, bf16[2048,256]{1,0:T(8,128)(2,1)S(1)} %convolution_convert_fusion.3.grad_ref, f32[2,2,2,1024]{3,2,1,0:T(2,128)S(1)} %get-tuple-element.103.lse_ref), custom_call_target="tpu_custom_call" | custom-call | flops 2684354560 | bytes 9437184 | tf_op jit(solution)/shard_map/attend_back/pallas_call | solution.py:133
  485.8 11.0 %convolution_convert_fusion.2 = bf16[2048,768]{1,0:T(8,128)(2,1)} fusion(bf16[2048,768]{1,0:T(8,128)(2,1)S(1)} %attend_back.1.grad_ref, bf16[2048,2048]{1,0:T(8,128)(2,1)} %get-tuple-element.78.x_ref, f32[2048]{0:T(1024)S(1)} %bitcast.19, f32[2048]{0:T(1024)S(1)} %copy-done.34), kind=kOutput, calls=%fused_computation.7 | convolution fusion | flops 6460801024 | bytes 14696448 | tf_op jit(solution)/shard_map/dot_general | solution.py:21
  496.8 1.7 copy-done.21
  498.5 1.9 copy-done.22
  500.4 1.6 copy-done.28
  502.0 17.9 %input_terms.1 = (bf16[2048,2048]{1,0:T(8,128)(2,1)}, f32[1,2048]{1,0:T(1,128)S(1)}) custom-call(s32[1]{0:T(128)} %bitcast.own_ref, bf16[2048,768]{1,0:T(8,128)(2,1)S(1)} %copy-done.22, bf16[2048,768]{1,0:T(8,128)(2,1)} %all-gather.4.cloned.1.call-done.qkv_ref, bf16[2048,2048]{1,0:T(8,128)(2,1)} %get-tuple-element.78.x_ref, f32[1,2048]{1,0:T(1,128)S(1)} %copy-done.10, ...), custom_call_target="tpu_custom_call" | custom-call | flops 6442450944 | bytes 25165824 | tf_op jit(solution)/shard_map/input_terms/pallas_call | solution.py:997
  520.0 2.4 constant_dynamic-slice_fusion
  523.6 1.6 copy-done.26
  525.1 13.6 %columns_back.5.refs_0_ = bf16[2048,2048]{1,0:T(8,128)(2,1)} custom-call(s32[1]{0:T(128)} %bitcast.own_ref, bf16[2048,768]{1,0:T(8,128)(2,1)} %copy-done.23, bf16[2048,256]{1,0:T(8,128)(2,1)S(1)} %copy-done.6, bf16[2048,2304]{1,0:T(8,128)(2,1)} %all-gather.8.cloned.1.call-done.gate_ref.up_ref.down_ref.refs_1_.refs_2_, ...), custom_call_target="tpu_custom_call" | custom-call | flops 8589934592 | bytes 16777216 | tf_op jit(solution)/shard_map/columns_back/pallas_call | solution.py:1115
  538.7 81.1 %scatter_outputs.1 = (bf16[1024,512]{1,0:T(8,128)(2,1)S(1)}, bf16[1024,512]{1,0:T(8,128)(2,1)S(1)}, f32[2,512]{1,0:T(2,128)S(1)}) custom-call(f32[2,2048]{1,0:T(2,128)S(1)} %pad_maximum_fusion.vector_ref, bf16[2048,2048]{1,0:T(8,128)(2,1)} %columns_back.5.refs_0_, bf16[2048,2048]{1,0:T(8,128)(2,1)} %get-tuple-element.111.refs_1_), custom_call_target="tpu_custom_call" | custom-call | flops 60000002048 | bytes 600000000 | tf_op jit(solution)/shard_map/scatter_outputs/pallas_call | solution.py:432
  619.8 1.9 constant_dynamic-slice_fusion.2
  622.9 9.1 %reduce-scatter.8.cloned.1.call-done.refs_0_ = bf16[512,768]{1,0:T(8,128)(2,1)} async-done(((bf16[2048,768]{1,0:T(8,128)(2,1)}), bf16[512,768]{1,0:T(8,128)(2,1)}) %reduce-scatter.8.cloned.1.call-update) | async-done | bytes 786448 | tf_op jit(solution)/shard_map/reduce_scatter | solution.py:1188
  632.0 3.7 collective-permute-done.refs_3_
  639.7 5.7 assemble_grads.2
  (99 shorter events, 25.3 us)
Async XLA Ops:
  7.2 122.6 %all-gather.4.cloned.1.call-start = ((), (), s32[]{:S(2)}) async-start(), calls=%async_computation.3 | async-start | bytes 3932160 | tf_op jit(solution)/shard_map/all_gather | solution.py:1185
  11.2 15.8 %copy-start.35 = (f32[512]{0:T(512)S(1)}, f32[512]{0:T(512)}, u32[]{:S(2)}) copy-start(f32[512]{0:T(512)} %param.17) | copy-start | bytes 6148
  11.2 15.8 %copy-start.36 = (f32[512]{0:T(512)S(1)}, f32[512]{0:T(512)}, u32[]{:S(2)}) copy-start(f32[512]{0:T(512)} %param.12) | copy-start | bytes 6148
  11.2 17.3 %copy-start.11 = (bf16[1024,512]{1,0:T(8,128)(2,1)S(1)}, bf16[1024,512]{1,0:T(8,128)(2,1)}, u32[]{:S(2)}) copy-start(bf16[1024,512]{1,0:T(8,128)(2,1)} %refs_3_) | copy-start | bytes 3145732
  26.9 69.5 %copy-start.31 = (bf16[1,256,512]{2,1,0:T(8,128)(2,1)}, bf16[1,256,512]{2,1,0:T(8,128)(2,1)S(1)}, u32[]{:S(2)}) copy-start(bf16[1,256,512]{2,1,0:T(8,128)(2,1)S(1)} %get-tuple-element.76.refs_4_) | copy-start | bytes 786436
  26.9 242.2 %all-gather.8.cloned.1.call-start = ((), (), s32[]{:S(2)}) async-start(), calls=%async_computation.5 | async-start | bytes 11796480 | tf_op jit(solution)/shard_map/all_gather | solution.py:1185
  96.4 246.5 %all-gather.6.cloned.1.call-start = ((), (), s32[]{:S(2)}) async-start(), calls=%async_computation.4 | async-start | bytes 3932160 | tf_op jit(solution)/shard_map/all_gather | solution.py:1185
  124.2 27.6 %copy-start.7 = (bf16[2048,256]{1,0:T(8,128)(2,1)}, bf16[2048,256]{1,0:T(8,128)(2,1)S(1)}, u32[]{:S(2)}) copy-start(bf16[2048,256]{1,0:T(8,128)(2,1)S(1)} %get-tuple-element.84) | copy-start | bytes 3145732
  124.2 395.7 %reduce-scatter.4.cloned.1.call-start = ((), (), s32[]{:S(2)}) async-start(), calls=%async_computation.6 | async-start | bytes 11796480 | tf_op jit(solution)/shard_map/reduce_scatter | solution.py:1188
  129.8 10.7 %copy-start.9 = (f32[1,2048]{1,0:T(1,128)}, f32[1,2048]{1,0:T(1,128)S(1)}, u32[]{:S(2)}) copy-start(f32[1,2048]{1,0:T(1,128)S(1)} %get-tuple-element.138.gain_ref) | copy-start | bytes 24580
  140.5 17.0 %copy-start.20 = (bf16[2048,768]{1,0:T(8,128)(2,1)}, bf16[2048,768]{1,0:T(8,128)(2,1)S(1)}, u32[]{:S(2)}) copy-start(bf16[2048,768]{1,0:T(8,128)(2,1)S(1)} %convolution_convert_fusion.1.packed_ref) | copy-start | bytes 9437188
  151.8 6.7 %copy-start.16 = (bf16[1024,512]{1,0:T(8,128)(2,1)S(1)}, bf16[1024,512]{1,0:T(8,128)(2,1)}, u32[]{:S(2)}) copy-start(bf16[1024,512]{1,0:T(8,128)(2,1)} %shard_ref.1) | copy-start | bytes 3145732
  267.8 1.3 copy-start.24
  322.6 1.7 copy-start.23
  324.2 295.6 %reduce-scatter.6.cloned.1.call-start = ((), (), s32[]{:S(2)}) async-start(), calls=%async_computation.7 | async-start | bytes 5242880 | tf_op jit(solution)/shard_map/reduce_scatter | solution.py:1188
  342.9 11.2 %copy-start = (bf16[2048,768]{1,0:T(8,128)(2,1)S(1)}, bf16[2048,768]{1,0:T(8,128)(2,1)}, u32[]{:S(2)}) copy-start(bf16[2048,768]{1,0:T(8,128)(2,1)} %all-gather.6.cloned.1.call-done.gate_ref.up_ref.down_ref.refs_1_.refs_3_) | copy-start | bytes 9437188
  354.1 91.7 %copy-start.5 = (bf16[2048,256]{1,0:T(8,128)(2,1)}, bf16[2048,256]{1,0:T(8,128)(2,1)S(1)}, u32[]{:S(2)}) copy-start(bf16[2048,256]{1,0:T(8,128)(2,1)S(1)} %get-tuple-element.101.refs_4_.refs_1_) | copy-start | bytes 3145732
  354.1 9.9 %copy-start.25 = (f32[256,2048]{1,0:T(8,128)S(1)}, f32[256,2048]{1,0:T(8,128)}, u32[]{:S(2)}) copy-start(f32[256,2048]{1,0:T(8,128)} %copy-done.24) | copy-start | bytes 6291460
  364.0 81.8 %copy-start.2 = (bf16[2048,256]{1,0:T(8,128)(2,1)S(1)}, bf16[2048,256]{1,0:T(8,128)(2,1)}, u32[]{:S(2)}) copy-start(bf16[2048,256]{1,0:T(8,128)(2,1)} %copy-done.1) | copy-start | bytes 3145732
  445.9 16.1 %copy-start.8 = (bf16[2048,256]{1,0:T(8,128)(2,1)S(1)}, bf16[2048,256]{1,0:T(8,128)(2,1)}, u32[]{:S(2)}) copy-start(bf16[2048,256]{1,0:T(8,128)(2,1)} %copy-done.7) | copy-start | bytes 3145732
  461.9 170.1 %reduce-scatter.8.cloned.1.call-start = ((), (), s32[]{:S(2)}) async-start(), calls=%async_computation.8 | async-start | bytes 3932160 | tf_op jit(solution)/shard_map/reduce_scatter | solution.py:1188
  467.7 18.0 %copy-start.10 = (f32[1,2048]{1,0:T(1,128)S(1)}, f32[1,2048]{1,0:T(1,128)}, u32[]{:S(2)}) copy-start(f32[1,2048]{1,0:T(1,128)} %copy-done.9) | copy-start | bytes 24580
  467.7 18.0 %copy-start.34 = (f32[2048]{0:T(1024)S(1)}, f32[2048]{0:T(1024)}, u32[]{:S(2)}) copy-start(f32[2048]{0:T(1024)} %copy-done.33) | copy-start | bytes 24580
  496.8 1.7 copy-start.21
  498.5 1.9 copy-start.22
  500.4 1.6 copy-start.28
  502.0 21.5 %copy-start.6 = (bf16[2048,256]{1,0:T(8,128)(2,1)S(1)}, bf16[2048,256]{1,0:T(8,128)(2,1)}, u32[]{:S(2)}) copy-start(bf16[2048,256]{1,0:T(8,128)(2,1)} %copy-done.5) | copy-start | bytes 3145732
  522.3 116.2 %collective-permute-start.2 = (bf16[256,2304]{1,0:T(8,128)(2,1)}, bf16[256,2304]{1,0:T(8,128)(2,1)S(1)}, u32[]{:S(2)}, u32[]{:S(2)}) collective-permute-start(bf16[256,2304]{1,0:T(8,128)(2,1)} %constant_dynamic-slice_fusion), channel_id=1, source_target_pairs={{0,4},{4,0},{8,12},{12,8},{16,20},{20,16},{24,28},{28,24},{1,5},{5... | collective-permute-start | bytes 3538952 | tf_op jit(solution)/shard_map/ppermute | solution.py:1182
  523.6 1.6 copy-start.26
  621.7 14.0 %collective-permute-start = (bf16[256,1024]{1,0:T(8,128)(2,1)}, bf16[256,1024]{1,0:T(8,128)(2,1)}, u32[]{:S(2)}, u32[]{:S(2)}) collective-permute-start(bf16[256,1024]{1,0:T(8,128)(2,1)} %constant_dynamic-slice_fusion.2), channel_id=1, source_target_pairs={{0,4},{4,0},{8,12},{12,8},{16,20},{20,16},{24,28},{28,24},{1,5},{5... | collective-permute-start | bytes 1572872 | tf_op jit(solution)/shard_map/ppermute | solution.py:1182
  631.9 14.8 %copy-start.4 = (bf16[512,768]{1,0:T(8,128)(2,1)S(1)}, bf16[512,768]{1,0:T(8,128)(2,1)}, u32[]{:S(2)}) copy-start(bf16[512,768]{1,0:T(8,128)(2,1)} %reduce-scatter.8.cloned.1.call-done.refs_0_) | copy-start | bytes 2359300
  636.7 10.0 %collective-permute-start.1 = (bf16[256,768]{1,0:T(8,128)(2,1)S(1)}, bf16[256,768]{1,0:T(8,128)(2,1)S(1)}, u32[]{:S(2)}, u32[]{:S(2)}) collective-permute-start(bf16[256,768]{1,0:T(8,128)(2,1)S(1)} %constant_dynamic-slice_fusion.1), channel_id=1, source_target_pairs={{0,4},{4,0},{8,12},{12,8},{16,20},{20,16},{24,28},{28,24},{1,5},{5... | collective-permute-start | bytes 1179656 | tf_op jit(solution)/shard_map/ppermute | solution.py:1182
  (14 other events, 14.7 us)
Sparse Core Ops, SparseCore 0:
  27.0 69.8 all-gather.3
  98.5 164.0 all-gather.7
  264.1 61.6 all-gather.5
  328.1 159.9 reduce-scatter.3
  490.2 77.5 reduce-scatter.5
  570.1 61.8 reduce-scatter.7

commit v8 on v7

--- a/solution.py
+++ b/solution.py
@@ -564,16 +564,18 @@
             self.own(i).wait()
 
 
-def swap_first(identity, weights, pieces, ring, block, count):
+def swap_ring(identity, weights, pieces, ring, block, count):
     size = weights[0].shape[0]
     outputs = [
         jax.ShapeDtypeStruct((2 * size, sum(piece[2] for piece in pieces)), weights[0].dtype),
-        jax.ShapeDtypeStruct((count, *block.shape), block.dtype),
+        jax.ShapeDtypeStruct((count, *block.shape[-2:]), block.dtype),
     ]
 
     def swap_start(*refs):
         sources, (block_ref, start_ref, blocks_ref, *sems) = refs[: len(weights)], refs[len(weights) :]
         greet([ring_peer(ring, 1), ring_peer(ring, ring - 1)])
+        if len(block.shape) == 3:
+            block_ref = block_ref.at[block.shape[0] - 1]
         around = RingBlocks(ring, block_ref, blocks_ref, *sems[3:])
         pair = PairSwap(sources, start_ref, pieces, *sems[:3])
         around.start()
@@ -590,25 +592,29 @@
     )
 
 
-def swap_and_gather(identity, weights, pieces, shard, ring, blocks, steps, small):
+def swap_and_gather(identity, weights, pieces, shard, ring, blocks, small):
     count = len(weights)
     size = weights[0].shape[0]
     columns = sum(piece[2] for piece in pieces)
     rows, wide = shard.shape
-    operands = (*weights, shard, blocks, small)
+    operands = (*weights, shard, *blocks, small)
     small_rows, small_wide = small.shape
+    block_size, block_wide = blocks[0].shape[-2:]
     outputs = [
         jax.ShapeDtypeStruct((2 * size, columns), weights[0].dtype),
         jax.ShapeDtypeStruct((2 * rows, 4 * wide), shard.dtype),
-        jax.ShapeDtypeStruct((steps, *blocks.shape[1:]), shard.dtype),
+        jax.ShapeDtypeStruct((2 * ring * block_size, block_wide // 2), shard.dtype),
         jax.ShapeDtypeStruct((small_rows, 4 * small_wide), small.dtype),
     ]
 
     def swap_gather(*refs):
-        sources, refs = refs[:count], refs[count:]
-        shard_ref, blocks_ref, small_ref, start_ref, out_ref, around_ref, whole_ref, *sems = refs
-        small_send, small_recv = sems[8:]
-        greet([ring_peer(ring, 1), ring_peer(ring, ring - 1)])
+        sources, shard_ref = refs[:count], refs[count]
+        block_refs = refs[count + 1 : count + 1 + len(blocks)]
+        small_ref, start_ref, out_ref, around_ref, whole_ref, *sems = refs[
+            count + 1 + len(blocks) :
+        ]
+        small_send, small_recv = sems[9:]
+        greet()
 
         def small_place(r):
             _, slot = owner(r)
@@ -627,14 +633,14 @@
         ]
         small_copies[0].start()
         small_copies[1].start()
-        last = blocks_ref.at[blocks.shape[0] - 1]
-        around = RingBlocks(ring, last, around_ref, *sems[6:8])
-        around.start()
-        pair = PairSwap(sources, start_ref, pieces, *sems[:3])
-        pair.start()
         spread, copies = block_spread(shard_ref, out_ref, *sems[3:6])
         spread.start(0)
         spread.start(1)
+        pair = PairSwap(sources, start_ref, pieces, *sems[:3])
+        parts = []
+        for ref in block_refs:
+            parts += [ref] if len(ref.shape) == 2 else [ref.at[k] for k in range(ref.shape[0])]
+        around = RowsSwap(ring, parts, around_ref, *sems[6:9])
         for copy in copies:
             copy.start()
         small_copy(1, small_place(2), small_place(2)).wait_recv()
@@ -643,11 +649,12 @@
             small_ref[...]
         )
         spread.forward((0, 1, 2, 3))
-        around.advance()
+        around.start()
+        pair.start()
         spread.forward((6, 7))
         spread.finish()
+        around.finish()
         pair.finish()
-        around.finish()
         small_copy(0, small_place(1), small_place(1)).wait_recv()
         small_copy(2, small_place(3), small_place(3)).wait_recv()
         for copy in small_copies:
@@ -661,41 +668,9 @@
         [pltpu.SemaphoreType.DMA((len(pieces),))] * 3
         + [pltpu.SemaphoreType.DMA((2,))]
         + SPREAD_SEMS
-        + [pltpu.SemaphoreType.DMA((steps,))] * 2
+        + [pltpu.SemaphoreType.DMA((ring,))] * 3
         + [pltpu.SemaphoreType.DMA((3,))] * 2,
-        50_000_000_000,
-    )
-
-
-def swap_pairs(identity, weights, pieces, ring, blocks):
-    count = len(weights)
-    size = weights[0].shape[0]
-    columns = sum(piece[2] for piece in pieces)
-    block_size, block_wide = blocks[0].shape[-2:]
-    operands = (*weights, *blocks)
-    outputs = [
-        jax.ShapeDtypeStruct((2 * size, columns), weights[0].dtype),
-        jax.ShapeDtypeStruct((2 * ring * block_size, block_wide // 2), weights[0].dtype),
-    ]
-
-    def swap_last(*refs):
-        greet()
-        start_ref, out_ref, *sems = refs[len(operands) :]
-        parts = []
-        for ref in refs[count : len(operands)]:
-            parts += [ref] if len(ref.shape) == 2 else [ref.at[k] for k in range(ref.shape[0])]
-        around = RowsSwap(ring, parts, out_ref, *sems[3:])
-        around.start()
-        pair = PairSwap(refs[:count], start_ref, pieces, *sems[:3])
-        pair.start()
-        around.finish()
-        pair.finish()
-
-    return call(
-        swap_last, identity, operands, (pl.ANY,) * len(operands),
-        outputs, [pl.ANY] * len(outputs),
-        [pltpu.SemaphoreType.DMA((len(pieces),))] * 3 + [pltpu.SemaphoreType.DMA((ring,))] * 3,
-        20_000_000_000,
+        55_000_000_000,
     )
 
 
@@ -851,16 +826,67 @@
     )
 
 
-def middle_back(identity, terms, cot, middle, factor, gain):
+def middle_back(identity, terms, cot, middle, factor, gain, hiddens, weights):
     total, model = terms.shape
+    widths = [hidden.shape[1] for hidden in hiddens]
+    inner_width = sum(widths)
+    count = len(hiddens)
     quarter = total // 8
     half = quarter // 2
 
     def middle_back_step(
-        terms_ref, cot_ref, middle_ref, factor_ref, gain_ref, out_ref, grad_ref, gain_grad_ref,
-        cot_own, rounded, local, send, recv, *scratch
+        terms_ref, cot_ref, middle_ref, factor_ref, gain_ref, *refs
     ):
+        parts_refs, refs = refs[: 2 * count], refs[2 * count :]
+        out_ref, grad_ref, gain_grad_ref, rows_ref, *refs = refs
+        hidden_all, down_all, tiles, load_sems, tile_sems, *refs = refs
+        cot_own, rounded, local, send, recv, *scratch = refs
         greet()
+        loads = []
+        left = 0
+        for k, width in enumerate(widths):
+            place = pl.ds(left, width)
+            loads.append(
+                pltpu.make_async_copy(parts_refs[k], hidden_all.at[:, place], load_sems.at[2 * k])
+            )
+            down = parts_refs[count + k].at[:, pl.ds(2 * width, width)]
+            loads.append(
+                pltpu.make_async_copy(down, down_all.at[:, place], load_sems.at[2 * k + 1])
+            )
+            left += width
+        for load in loads:
+            load.start()
+        member, slot = owner(0)
+
+        def tile_copy(index):
+            start = pl.multiple_of(index * quarter, quarter)
+            kept = lax.rem(index, 2)
+            return pltpu.make_async_copy(
+                tiles.at[kept], rows_ref.at[pl.ds(start, quarter)], tile_sems.at[kept]
+            )
+
+        def result_tiles(first, last):
+            def step(index, carry):
+                @pl.when(index >= 2)
+                def _():
+                    tile_copy(index - 2).wait()
+
+                kept = lax.rem(index, 2)
+                rows = pl.ds(pl.multiple_of(index * quarter, quarter), quarter)
+                for start in range(0, model, 512):
+                    here = slice(start, start + 512)
+                    value = right_trans(hidden_all[rows, :], down_all[here, :])
+                    tiles[kept, :, here] = value.astype(BF16)
+
+                @pl.when(index == member * 4 + slot)
+                def _():
+                    tiles[kept] = (tiles[kept].astype(F32) + middle_ref[...]).astype(BF16)
+
+                tile_copy(index).start()
+                return carry
+
+            lax.fori_loop(first, last, step, 0)
+
         cot_copy = pltpu.make_async_copy(row_parts(cot_ref, quarter)(0), cot_own, local.at[0])
         cot_copy.start()
         collect = Collect(row_parts(terms_ref, quarter), quarter, *scratch[:6], scratch[6:])
@@ -870,7 +896,11 @@
         )
         collect.start()
         collect.first()
+        for load in loads:
+            load.wait()
+        result_tiles(0, 4)
         collect.second()
+        result_tiles(4, 6)
         cot_copy.wait()
         gain_grad_ref[...] = jnp.zeros_like(gain_grad_ref)
         copies = []
@@ -900,22 +930,31 @@
             )
             copy.start()
             copies.append(copy)
+        result_tiles(6, 8)
         spread.forward()
         spread.finish()
         collect.finish()
+        tile_copy(6).wait()
+        tile_copy(7).wait()
         for copy in copies:
             copy.wait()
 
     return call(
-        middle_back_step, identity, (terms, cot, middle, factor, gain),
-        (pl.ANY, pl.ANY, pltpu.VMEM, pltpu.VMEM, pltpu.VMEM),
+        middle_back_step, identity, (terms, cot, middle, factor, gain, *hiddens, *weights),
+        (pl.ANY, pl.ANY, pltpu.VMEM, pltpu.VMEM, pltpu.VMEM) + (pl.ANY,) * (2 * count),
         (
             jax.ShapeDtypeStruct((total, model), BF16),
             jax.ShapeDtypeStruct((quarter, model), F32),
             jax.ShapeDtypeStruct((1, model), F32),
+            jax.ShapeDtypeStruct((total, model), BF16),
         ),
-        (pl.ANY, pltpu.VMEM, pltpu.VMEM),
+        (pl.ANY, pltpu.VMEM, pltpu.VMEM, pl.ANY),
         [
+            pltpu.VMEM((total, inner_width), BF16),
+            pltpu.VMEM((model, inner_width), BF16),
+            pltpu.VMEM((2, quarter, model), BF16),
+            pltpu.SemaphoreType.DMA((2 * count,)),
+            pltpu.SemaphoreType.DMA((2,)),
             pltpu.VMEM((quarter, model), BF16),
             pltpu.VMEM((quarter, model), BF16),
             pltpu.SemaphoreType.DMA((3,)),
@@ -1027,7 +1066,7 @@
 
 def feed_forward(normed, cot, weights, chunk):
     total, model = normed.shape
-    tile = 512
+    tile = 256
     part = 256 if chunk % 256 == 0 else 128
 
     def feed_step(normed_ref, cot_ref, gate_ref, up_ref, down_ref, hidden_ref, grads_ref):
@@ -1205,31 +1244,24 @@
     ring = tok_size // 2
     early = 1
     out_blocks = [w_out.T]
-    attention_start, block = swap_first(
+    attention_start, block = swap_ring(
         0, (w_query, w_key, w_value), attention_pieces, ring, out_blocks[0], early
     )
     out_blocks.append(block)
     feed = (w_gate, w_up, w_down.T)
-    tokens_after, attention_start = lax.optimization_barrier((tokens, attention_start))
+    block, attention_start = lax.optimization_barrier((block, attention_start))
     qkv = ring_gather(attention_start)
     plans = [
         [(part, left, size, part * size) for part in range(3)] for left, size in zip(lefts, chunks)
     ]
-    first_start, x_all, block, gains = swap_and_gather(
-        1,
-        feed,
-        plans[0],
-        tokens_after,
-        ring,
-        out_blocks[-1],
-        ring - 1 - early,
-        jnp.stack([gain_attn, gain_ffn]),
-    )
-    gain_one, gain_two = gains[:1], gains[1:]
+    first_start, block = swap_ring(1, feed, plans[0], ring, block, ring - 1 - early)
     out_blocks.append(block)
     feed_weights = [ring_gather(first_start)]
-    w_gate, x_all = lax.optimization_barrier((w_gate, x_all))
-    last_start, out_proj = swap_pairs(2, (w_gate, *feed[1:]), plans[1], ring, out_blocks)
+    tokens, block = lax.optimization_barrier((tokens, block))
+    last_start, x_all, out_proj, gains = swap_and_gather(
+        2, feed, plans[1], tokens, ring, out_blocks, jnp.stack([gain_attn, gain_ffn])
+    )
+    gain_one, gain_two = gains[:1], gains[1:]
     feed_weights.append(ring_gather(last_start))
 
     x_wide = x_all.astype(F32)
@@ -1260,8 +1292,8 @@
         grad_normed_two = columns_back(
             [grad_both], [feed_weights[c]], 0, own, grad_normed_two
         )
-    grad_mid_rows, grad_middle, gain_ffn_part = middle_back(
-        4, grad_normed_two, cot_rows, middle, factor_two, gain_two
+    grad_mid_rows, grad_middle, gain_ffn_part, out_rows = middle_back(
+        4, grad_normed_two, cot_rows, middle, factor_two, gain_two, hiddens, feed_weights
     )
 
     hidden, grad_both, grad_mid_rows = lax.optimization_barrier((hidden, grad_both, grad_mid_rows))
@@ -1276,13 +1308,14 @@
     attention_terms = left_trans(normed, grad_packed).astype(BF16)
     attention_terms, grad_packed = lax.optimization_barrier((attention_terms, grad_packed))
     attention_sum = ring_scatter(attention_terms)
+    grad_packed, feed_sums[0] = lax.optimization_barrier((grad_packed, feed_sums[0]))
+    first_other = other_half(feed_sums[0])
     terms, gain_attn_part = input_terms(grad_packed, qkv, x_all, gain_one, grad_middle, own)
-    hiddens[0], terms, feed_sums[0] = lax.optimization_barrier((hiddens[0], terms, feed_sums[0]))
-    out_rows = columns_back(hiddens, feed_weights, 2, own, None, middle)
+    terms, first_other = lax.optimization_barrier((terms, first_other))
     outcome, input_grad, gain_grads = scatter_blocks(
         5, tok_size // 2, jnp.concatenate([gain_attn_part, gain_ffn_part]), out_rows, terms
     )
-    feed_others = [other_half(feed_sums[0])]
+    feed_others = [first_other]
     outcome, feed_sums[1] = lax.optimization_barrier((outcome, feed_sums[1]))
     feed_others.append(other_half(feed_sums[1]))
     feed_others[1], attention_sum = lax.optimization_barrier((feed_others[1], attention_sum))

time: 664 us -> 655 us (0.986)
  Pallas kernels: 551 us -> 534 us
  waiting for transfers between devices: 14.4 us -> 29.5 us
    pallas_call x3 -> x2, Pallas kernels: 42.1 us -> 28.2 us  [columns_back(): pl.pallas_call(columns_step, grid_spec=pltpu.PrefetchScalarGridSpec(num_s...]
    reduce_scatter x3, waiting for transfers between devices: 9.1 us -> 22.1 us  [ring_scatter(): lax.psum_scatter(terms, 'tok', scatter_dimension=0, tiled=True, axis_inde...]
    unnamed x76 -> x68, local copies, waits for them, and re-layouts: 26.9 us -> 25.2 us
  transfers between devices with their start and end apart: 9 -> 9, of which waited for: 3 -> 3; matrix products, arithmetic and copies ran while one was open for 7% -> 7% of each run, Pallas kernels for 82% -> 79%
where the time goes in v8:
time: 655 us; the launch traced here: 652 us
  Pallas kernels  534 us (82%)
  matrix products  32.8 us (5%)
  local copies, waits for them, and re-layouts  30.1 us (5%)
  waiting for transfers between devices  29.5 us (5%)
  between operations  14.7 us (2%)
    pallas_call x6, Pallas kernels, call(): pl.pallas_call(kernel, out_shape=outputs, in_specs=[pl.BlockSpec(memory_s...  369 us
    pallas_call x2, Pallas kernels, weight_terms(): pl.pallas_call(terms_step, grid=(model // tile,), in_specs=[pl.BlockSpec(...  42.4 us
    pallas_call x2, Pallas kernels, feed_forward(): pl.pallas_call(feed_step, grid=(total // tile,), in_specs=[rows, rows, we...  40.3 us
    pallas_call x2, Pallas kernels, columns_back(): pl.pallas_call(columns_step, grid_spec=pltpu.PrefetchScalarGridSpec(num_s...  28.2 us
    unnamed x68, local copies, waits for them, and re-layouts  25.2 us
    reduce_scatter x3, waiting for transfers between devices, ring_scatter(): lax.psum_scatter(terms, 'tok', scatter_dimension=0, tiled=True, axis_inde...  22.1 us
    pallas_call x1, Pallas kernels, input_terms(): pl.pallas_call(input_terms_step, grid_spec=pltpu.PrefetchScalarGridSpec(n...  17.8 us
    pallas_call x1, Pallas kernels, attend_back(): pl.pallas_call(attend_back_kernel, grid=(sequences, pairs), out_shape=jax...  17.7 us
  transfers between devices with their start and end apart: 9, of which 3 were waited for; matrix products, arithmetic and copies ran while one was open for 7% of the time, Pallas kernels for 79%

profile of v8, /device:TPU:0, one launch (start us, length us, event | category | flops | bytes accessed | tf_op | source)
XLA Modules:
  0.0 651.5 jit_solution(8472714262977098018)
XLA Ops:
  11.2 15.7 %swap_start.2 = (bf16[512,768]{1,0:T(8,128)(2,1)}, bf16[1,256,512]{2,1,0:T(8,128)(2,1)S(1)}) custom-call(bf16[256,512]{1,0:T(8,128)(2,1)S(1)} %copy-done.13, bf16[256,512]{1,0:T(8,128)(2,1)S(1)} %copy-done.14, bf16[256,512]{1,0:T(8,128)(2,1)S(1)} %copy-done.15, bf16[256,512]{1,0:T(8,128)(2,1)S(1)} %bitcast.16), custom_call_target="tpu_custom_call" | custom-call | flops 15000000512 | bytes 150000000 | tf_op jit(solution)/shard_map/swap_start/pallas_call | solution.py:432
  30.1 27.4 %swap_start.3 = (bf16[512,2304]{1,0:T(8,128)(2,1)}, bf16[2,256,512]{2,1,0:T(8,128)(2,1)S(1)}) custom-call(bf16[256,2048]{1,0:T(8,128)(2,1)S(1)} %copy-done.9, bf16[256,2048]{1,0:T(8,128)(2,1)S(1)} %copy-done.10, bf16[256,2048]{1,0:T(8,128)(2,1)S(1)} %bitcast.14, bf16[1,256,512]{2,1,0:T(8,128)(2,1)S(1)} %copy-done.25), custom_call_target="tpu_custom_call" | custom-call | flops 15000000512 | bytes 150000000 | tf_op jit(solution)/shard_map/swap_start/pallas_call | solution.py:432
  61.6 59.3 %swap_gather.1 = (bf16[512,768]{1,0:T(8,128)(2,1)}, bf16[2048,2048]{1,0:T(8,128)(2,1)}, bf16[2048,256]{1,0:T(8,128)(2,1)S(1)}, f32[2,2048]{1,0:T(2,128)S(1)}) custom-call(bf16[256,2048]{1,0:T(8,128)(2,1)S(1)} %copy-done.9, bf16[256,2048]{1,0:T(8,128)(2,1)S(1)} %copy-done.11, bf16[256,2048]{1,0:T(8,128)(2,1)S(1)} %bitcast.15, bf16[1024,512]{1,0:T(8,128)(2,1)} %refs_3_, ...), custom_call_target="tpu_custom_call" | custom-call | flops 54999998464 | bytes 550000000 | tf_op jit(solution)/shard_map/swap_gather/pallas_call | solution.py:432
  121.1 5.4 fusion
  127.1 10.4 %convolution_convert_fusion.1.packed_ref = bf16[2048,768]{1,0:T(8,128)(2,1)S(1)} fusion(bf16[2048,768]{1,0:T(8,128)(2,1)} %all-gather.4.cloned.1.call-done.qkv_ref, bf16[2048,2048]{1,0:T(8,128)(2,1)} %get-tuple-element.80.x_ref, f32[2048]{0:T(1024)S(1)} %bitcast.18, f32[2048]{0:T(1024)S(1)} %add_rsqrt_fusion), kind=kOutput, calls=%fused_computation.6 | convolution fusion | flops 6460801024 | bytes 14696448 | tf_op jit(solution)/shard_map/dot_general | solution.py:33
  137.4 11.3 %attend.1 = (bf16[2048,256]{1,0:T(8,128)(2,1)S(1)}, f32[2,2,2,1024]{3,2,1,0:T(2,128)S(1)}) custom-call(bf16[2048,768]{1,0:T(8,128)(2,1)S(1)} %convolution_convert_fusion.1.packed_ref), custom_call_target="tpu_custom_call" | custom-call | flops 1073741824 | bytes 6291456 | tf_op jit(solution)/shard_map/attend/pallas_call | solution.py:106
  148.7 1.7 copy-done.16
  150.4 5.7 convolution_convert_fusion.terms_ref
  157.1 108.9 %middle_step.1 = (bf16[2048,2048]{1,0:T(8,128)(2,1)}, f32[256,2048]{1,0:T(8,128)S(1)}, f32[256,128]{1,0:T(8,128)S(1)}, bf16[2048,2048]{1,0:T(8,128)(2,1)}) custom-call(bf16[2048,2048]{1,0:T(8,128)(2,1)} %convolution_convert_fusion.terms_ref, bf16[2048,2048]{1,0:T(8,128)(2,1)} %get-tuple-element.80.x_ref, f32[1,2048]{1,0:T(1,128)S(1)} %get-tuple-element.139.gain_ref, ...), custom_call_target="tpu_custom_call" | custom-call | flops 99999997952 | bytes 1000000000 | tf_op jit(solution)/shard_map/middle_step/pallas_call | solution.py:432
  267.3 27.6 %feed_forward.2 = (bf16[2048,768]{1,0:T(8,128)(2,1)S(1)}, bf16[2048,1536]{1,0:T(8,128)(2,1)}) custom-call(bf16[2048,2048]{1,0:T(8,128)(2,1)} %get-tuple-element.85.normed_ref.refs_0_, bf16[2048,2048]{1,0:T(8,128)(2,1)} %get-tuple-element.86.cot_ref.refs_1_, bf16[2048,2304]{1,0:T(8,128)(2,1)} %all-gather.8.cloned.1.call-done.gate_ref.up_ref.down_ref.refs_1_.refs_2_, ...), custom_call_target="tpu_custom_call" | custom-call | flops 19327352832 | bytes 35651584 | tf_op jit(solution)/shard_map/feed_forward/pallas_call | solution.py:1091
  294.9 26.3 %weight_terms.2 = bf16[2048,2304]{1,0:T(8,128)(2,1)} custom-call(bf16[2048,2048]{1,0:T(8,128)(2,1)} %get-tuple-element.85.normed_ref.refs_0_, bf16[2048,2048]{1,0:T(8,128)(2,1)} %get-tuple-element.86.cot_ref.refs_1_, bf16[2048,1536]{1,0:T(8,128)(2,1)} %get-tuple-element.91.refs_2_.refs_0_, bf16[2048,768]{1,0:T(8,128)(2,1)S(1)} %get-tuple-element.90.refs_3_.refs_0_), custom_call_target="tpu_custom_call" | custom-call | flops 19327352832 | bytes 35651584 | tf_op jit(solution)/shard_map/weight_terms/pallas_call | solution.py:1187
  321.2 1.8 copy-done.21
  323.0 18.6 %columns_back.2.refs_2_ = bf16[2048,2048]{1,0:T(8,128)(2,1)} custom-call(s32[1]{0:T(128)} %bitcast.own_ref, bf16[2048,1536]{1,0:T(8,128)(2,1)} %get-tuple-element.91.refs_2_.refs_0_, bf16[2048,2304]{1,0:T(8,128)(2,1)} %all-gather.8.cloned.1.call-done.gate_ref.up_ref.down_ref.refs_1_.refs_2_), custom_call_target="tpu_custom_call" | custom-call | flops 12884901888 | bytes 20971520 | tf_op jit(solution)/shard_map/columns_back/pallas_call | solution.py:1154
  341.6 12.8 %feed_forward.3 = (bf16[2048,256]{1,0:T(8,128)(2,1)S(1)}, bf16[2048,512]{1,0:T(8,128)(2,1)S(1)}) custom-call(bf16[2048,2048]{1,0:T(8,128)(2,1)} %get-tuple-element.85.normed_ref.refs_0_, bf16[2048,2048]{1,0:T(8,128)(2,1)} %get-tuple-element.86.cot_ref.refs_1_, bf16[2048,768]{1,0:T(8,128)(2,1)} %all-gather.6.cloned.1.call-done.gate_ref.up_ref.down_ref.refs_1_.refs_3_, ...), custom_call_target="tpu_custom_call" | custom-call | flops 6442450944 | bytes 23068672 | tf_op jit(solution)/shard_map/feed_forward/pallas_call | solution.py:1091
  354.4 9.6 %columns_back.3.terms_ref = bf16[2048,2048]{1,0:T(8,128)(2,1)} custom-call(s32[1]{0:T(128)} %bitcast.own_ref, bf16[2048,512]{1,0:T(8,128)(2,1)S(1)} %get-tuple-element.100.refs_0_.refs_3_, bf16[2048,768]{1,0:T(8,128)(2,1)S(1)} %copy-done, bf16[2048,2048]{1,0:T(8,128)(2,1)} %columns_back.2.refs_2_), custom_call_target="tpu_custom_call" | custom-call | flops 4294967296 | bytes 12582912 | tf_op jit(solution)/shard_map/columns_back/pallas_call | solution.py:1154
  364.0 81.5 %middle_back_step.1 = (bf16[2048,2048]{1,0:T(8,128)(2,1)}, f32[256,2048]{1,0:T(8,128)S(1)}, f32[1,2048]{1,0:T(1,128)S(1)}, bf16[2048,2048]{1,0:T(8,128)(2,1)}) custom-call(bf16[2048,2048]{1,0:T(8,128)(2,1)} %columns_back.3.terms_ref, bf16[2048,2048]{1,0:T(8,128)(2,1)} %get-tuple-element.86.cot_ref.refs_1_, f32[256,2048]{1,0:T(8,128)S(1)} %copy-done.28, ...), custom_call_target="tpu_custom_call" | custom-call | flops 70000001024 | bytes 700000000 | tf_op jit(solution)/shard_map/middle_back_step/pallas_call | solution.py:432
  446.9 16.1 %weight_terms.3 = bf16[2048,1024]{1,0:T(8,128)(2,1)} custom-call(bf16[2048,2048]{1,0:T(8,128)(2,1)} %get-tuple-element.85.normed_ref.refs_0_, bf16[2048,2048]{1,0:T(8,128)(2,1)} %get-tuple-element.86.cot_ref.refs_1_, bf16[2048,2048]{1,0:T(8,128)(2,1)} %get-tuple-element.102.refs_2_, bf16[2048,512]{1,0:T(8,128)(2,1)S(1)} %get-tuple-element.100.refs_0_.refs_3_, ...), custom_call_target="tpu_custom_call" | custom-call | flops 8589934592 | bytes 33554432 | tf_op jit(solution)/shard_map/weight_terms/pallas_call | solution.py:1187
  463.3 5.7 convolution_convert_fusion.3.grad_ref
  469.0 17.7 %attend_back.1.grad_ref = bf16[2048,768]{1,0:T(8,128)(2,1)S(1)} custom-call(bf16[2048,768]{1,0:T(8,128)(2,1)} %copy-done.16, bf16[2048,256]{1,0:T(8,128)(2,1)S(1)} %copy-done.2, bf16[2048,256]{1,0:T(8,128)(2,1)S(1)} %convolution_convert_fusion.3.grad_ref, f32[2,2,2,1024]{3,2,1,0:T(2,128)S(1)} %get-tuple-element.103.lse_ref), custom_call_target="tpu_custom_call" | custom-call | flops 2684354560 | bytes 9437184 | tf_op jit(solution)/shard_map/attend_back/pallas_call | solution.py:133
  486.8 11.1 %convolution_convert_fusion.2 = bf16[2048,768]{1,0:T(8,128)(2,1)} fusion(bf16[2048,768]{1,0:T(8,128)(2,1)S(1)} %attend_back.1.grad_ref, bf16[2048,2048]{1,0:T(8,128)(2,1)} %get-tuple-element.80.x_ref, f32[2048]{0:T(1024)S(1)} %bitcast.19, f32[2048]{0:T(1024)S(1)} %copy-done.30), kind=kOutput, calls=%fused_computation.7 | convolution fusion | flops 6460801024 | bytes 14696448 | tf_op jit(solution)/shard_map/dot_general | solution.py:21
  497.9 1.7 copy-done.17
  502.4 1.9 copy-done.18
  504.3 1.6 copy-done.20
  505.9 17.8 %input_terms.1 = (bf16[2048,2048]{1,0:T(8,128)(2,1)}, f32[1,2048]{1,0:T(1,128)S(1)}) custom-call(s32[1]{0:T(128)} %bitcast.own_ref, bf16[2048,768]{1,0:T(8,128)(2,1)S(1)} %copy-done.18, bf16[2048,768]{1,0:T(8,128)(2,1)} %all-gather.4.cloned.1.call-done.qkv_ref, bf16[2048,2048]{1,0:T(8,128)(2,1)} %get-tuple-element.80.x_ref, f32[1,2048]{1,0:T(1,128)S(1)} %copy-done.8, ...), custom_call_target="tpu_custom_call" | custom-call | flops 6442450944 | bytes 25165824 | tf_op jit(solution)/shard_map/input_terms/pallas_call | solution.py:1036
  523.7 5.5 collective-permute-done.refs_2_
  529.2 76.6 %scatter_outputs.1 = (bf16[1024,512]{1,0:T(8,128)(2,1)S(1)}, bf16[1024,512]{1,0:T(8,128)(2,1)S(1)}, f32[2,512]{1,0:T(2,128)S(1)}) custom-call(f32[2,2048]{1,0:T(2,128)S(1)} %pad_maximum_fusion.vector_ref, bf16[2048,2048]{1,0:T(8,128)(2,1)} %get-tuple-element.110.refs_0_, bf16[2048,2048]{1,0:T(8,128)(2,1)} %get-tuple-element.113.refs_1_), custom_call_target="tpu_custom_call" | custom-call | flops 60000002048 | bytes 600000000 | tf_op jit(solution)/shard_map/scatter_outputs/pallas_call | solution.py:432
  605.8 1.9 constant_dynamic-slice_fusion.1
  607.7 1.6 collective-permute-start.1
  609.3 22.1 %reduce-scatter.8.cloned.1.call-done.refs_0_ = bf16[512,768]{1,0:T(8,128)(2,1)} async-done(((bf16[2048,768]{1,0:T(8,128)(2,1)}), bf16[512,768]{1,0:T(8,128)(2,1)}) %reduce-scatter.8.cloned.1.call-update) | async-done | bytes 786448 | tf_op jit(solution)/shard_map/reduce_scatter | solution.py:1227
  632.5 1.5 collective-permute-start.2
  635.8 5.7 assemble_grads.2
  641.5 1.7 collective-permute-done.2.refs_1_
  (90 shorter events, 22.9 us)
Async XLA Ops:
  7.2 119.3 %all-gather.4.cloned.1.call-start = ((), (), s32[]{:S(2)}) async-start(), calls=%async_computation.3 | async-start | bytes 3932160 | tf_op jit(solution)/shard_map/all_gather | solution.py:1224
  11.2 18.0 %copy-start.9 = (bf16[256,2048]{1,0:T(8,128)(2,1)S(1)}, bf16[256,2048]{1,0:T(8,128)(2,1)}, u32[]{:S(2)}) copy-start(bf16[256,2048]{1,0:T(8,128)(2,1)} %refs_0_.5) | copy-start | bytes 3145732
  11.2 18.0 %copy-start.10 = (bf16[256,2048]{1,0:T(8,128)(2,1)S(1)}, bf16[256,2048]{1,0:T(8,128)(2,1)}, u32[]{:S(2)}) copy-start(bf16[256,2048]{1,0:T(8,128)(2,1)} %refs_1_.5) | copy-start | bytes 3145732
  27.6 239.7 %all-gather.8.cloned.1.call-start = ((), (), s32[]{:S(2)}) async-start(), calls=%async_computation.5 | async-start | bytes 11796480 | tf_op jit(solution)/shard_map/all_gather | solution.py:1224
  30.1 28.3 %copy-start.31 = (f32[512]{0:T(512)S(1)}, f32[512]{0:T(512)}, u32[]{:S(2)}) copy-start(f32[512]{0:T(512)} %param.17) | copy-start | bytes 6148
  30.1 28.3 %copy-start.32 = (f32[512]{0:T(512)S(1)}, f32[512]{0:T(512)}, u32[]{:S(2)}) copy-start(f32[512]{0:T(512)} %param.12) | copy-start | bytes 6148
  58.3 283.3 %all-gather.6.cloned.1.call-start = ((), (), s32[]{:S(2)}) async-start(), calls=%async_computation.4 | async-start | bytes 3932160 | tf_op jit(solution)/shard_map/all_gather | solution.py:1224
  58.4 1.2 copy-start.11
  120.9 29.5 %copy-start.5 = (bf16[2048,256]{1,0:T(8,128)(2,1)}, bf16[2048,256]{1,0:T(8,128)(2,1)S(1)}, u32[]{:S(2)}) copy-start(bf16[2048,256]{1,0:T(8,128)(2,1)S(1)} %get-tuple-element.84) | copy-start | bytes 3145732
  121.0 378.6 %reduce-scatter.4.cloned.1.call-start = ((), (), s32[]{:S(2)}) async-start(), calls=%async_computation.6 | async-start | bytes 11796480 | tf_op jit(solution)/shard_map/reduce_scatter | solution.py:1227
  121.1 16.4 %copy-start.7 = (f32[1,2048]{1,0:T(1,128)}, f32[1,2048]{1,0:T(1,128)S(1)}, u32[]{:S(2)}) copy-start(f32[1,2048]{1,0:T(1,128)S(1)} %get-tuple-element.140.gain_ref) | copy-start | bytes 24580
  148.7 1.7 copy-start.16
  150.4 6.7 %copy-start.12 = (bf16[1024,512]{1,0:T(8,128)(2,1)S(1)}, bf16[1024,512]{1,0:T(8,128)(2,1)}, u32[]{:S(2)}) copy-start(bf16[1024,512]{1,0:T(8,128)(2,1)} %shard_ref.1) | copy-start | bytes 3145732
  266.0 1.3 copy-start.27
  321.2 1.8 copy-start.21
  323.0 282.9 %reduce-scatter.6.cloned.1.call-start = ((), (), s32[]{:S(2)}) async-start(), calls=%async_computation.7 | async-start | bytes 5242880 | tf_op jit(solution)/shard_map/reduce_scatter | solution.py:1227
  341.6 12.8 %copy-start = (bf16[2048,768]{1,0:T(8,128)(2,1)S(1)}, bf16[2048,768]{1,0:T(8,128)(2,1)}, u32[]{:S(2)}) copy-start(bf16[2048,768]{1,0:T(8,128)(2,1)} %all-gather.6.cloned.1.call-done.gate_ref.up_ref.down_ref.refs_1_.refs_3_) | copy-start | bytes 9437188
  354.4 9.6 %copy-start.28 = (f32[256,2048]{1,0:T(8,128)S(1)}, f32[256,2048]{1,0:T(8,128)}, u32[]{:S(2)}) copy-start(f32[256,2048]{1,0:T(8,128)} %copy-done.27) | copy-start | bytes 6291460
  364.0 82.9 %copy-start.2 = (bf16[2048,256]{1,0:T(8,128)(2,1)S(1)}, bf16[2048,256]{1,0:T(8,128)(2,1)}, u32[]{:S(2)}) copy-start(bf16[2048,256]{1,0:T(8,128)(2,1)} %copy-done.1) | copy-start | bytes 3145732
  445.6 1.3 copy-start.19
  446.9 16.3 %copy-start.6 = (bf16[2048,256]{1,0:T(8,128)(2,1)S(1)}, bf16[2048,256]{1,0:T(8,128)(2,1)}, u32[]{:S(2)}) copy-start(bf16[2048,256]{1,0:T(8,128)(2,1)} %copy-done.5) | copy-start | bytes 3145732
  463.0 168.4 %reduce-scatter.8.cloned.1.call-start = ((), (), s32[]{:S(2)}) async-start(), calls=%async_computation.8 | async-start | bytes 3932160 | tf_op jit(solution)/shard_map/reduce_scatter | solution.py:1227
  469.0 17.8 %copy-start.8 = (f32[1,2048]{1,0:T(1,128)S(1)}, f32[1,2048]{1,0:T(1,128)}, u32[]{:S(2)}) copy-start(f32[1,2048]{1,0:T(1,128)} %copy-done.7) | copy-start | bytes 24580
  469.0 17.8 %copy-start.30 = (f32[2048]{0:T(1024)S(1)}, f32[2048]{0:T(1024)}, u32[]{:S(2)}) copy-start(f32[2048]{0:T(1024)} %copy-done.29) | copy-start | bytes 24580
  497.8 1.7 copy-start.17
  500.9 28.3 %collective-permute-start = (bf16[256,2304]{1,0:T(8,128)(2,1)S(1)}, bf16[256,2304]{1,0:T(8,128)(2,1)S(1)}, u32[]{:S(2)}, u32[]{:S(2)}) collective-permute-start(bf16[256,2304]{1,0:T(8,128)(2,1)S(1)} %constant_dynamic-slice_fusion.2), channel_id=1, source_target_pairs={{0,4},{4,0},{8,12},{12,8},{16,20},{20,16},{24,28},{28,24},{1,5},{5... | collective-permute-start | bytes 3538952 | tf_op jit(solution)/shard_map/ppermute | solution.py:1221
  502.4 1.9 copy-start.18
  504.3 1.6 copy-start.20
  607.7 23.7 %collective-permute-start.1 = (bf16[256,1024]{1,0:T(8,128)(2,1)}, bf16[256,1024]{1,0:T(8,128)(2,1)}, u32[]{:S(2)}, u32[]{:S(2)}) collective-permute-start(bf16[256,1024]{1,0:T(8,128)(2,1)} %constant_dynamic-slice_fusion.1), channel_id=1, source_target_pairs={{0,4},{4,0},{8,12},{12,8},{16,20},{20,16},{24,28},{28,24},{1,5},{5... | collective-permute-start | bytes 1572872 | tf_op jit(solution)/shard_map/ppermute | solution.py:1221
  631.4 11.8 %copy-start.4 = (bf16[512,768]{1,0:T(8,128)(2,1)S(1)}, bf16[512,768]{1,0:T(8,128)(2,1)}, u32[]{:S(2)}) copy-start(bf16[512,768]{1,0:T(8,128)(2,1)} %reduce-scatter.8.cloned.1.call-done.refs_0_) | copy-start | bytes 2359300
  632.5 10.7 %collective-permute-start.2 = (bf16[256,768]{1,0:T(8,128)(2,1)S(1)}, bf16[256,768]{1,0:T(8,128)(2,1)S(1)}, u32[]{:S(2)}, u32[]{:S(2)}) collective-permute-start(bf16[256,768]{1,0:T(8,128)(2,1)S(1)} %constant_dynamic-slice_fusion), channel_id=1, source_target_pairs={{0,4},{4,0},{8,12},{12,8},{16,20},{20,16},{24,28},{28,24},{1,5},{5... | collective-permute-start | bytes 1179656 | tf_op jit(solution)/shard_map/ppermute | solution.py:1221
  634.6 1.2 copy-start.3
  (10 other events, 8.9 us)
Sparse Core Ops, SparseCore 0:
  27.7 68.3 all-gather.3
  97.7 164.2 all-gather.7
  263.6 61.6 all-gather.5
  327.5 159.9 reduce-scatter.3
  489.6 77.5 reduce-scatter.5
  569.5 61.8 reduce-scatter.7

commit v9 on v8

--- a/solution.py
+++ b/solution.py
@@ -428,7 +428,7 @@
     lax.fori_loop(0, count // 32, step, 0)
 
 
-def call(kernel, identity, operands, spaces, outputs, out_spaces, scratch, cost):
+def call(kernel, identity, operands, spaces, outputs, out_spaces, scratch, cost, limit=VMEM):
     return pl.pallas_call(
         kernel,
         out_shape=outputs,
@@ -436,7 +436,7 @@
         out_specs=jax.tree.map(lambda space: pl.BlockSpec(memory_space=space), out_spaces),
         scratch_shapes=scratch,
         compiler_params=pltpu.CompilerParams(
-            collective_id=identity, has_side_effects=True, vmem_limit_bytes=VMEM
+            collective_id=identity, has_side_effects=True, vmem_limit_bytes=limit
         ),
         cost_estimate=pl.CostEstimate(flops=cost, bytes_accessed=cost // 100, transcendentals=0),
         name=kernel.__name__,
@@ -564,7 +564,7 @@
             self.own(i).wait()
 
 
-def swap_ring(identity, weights, pieces, ring, block, count):
+def swap_ring(identity, weights, pieces, ring, block, count, load=False):
     size = weights[0].shape[0]
     outputs = [
         jax.ShapeDtypeStruct((2 * size, sum(piece[2] for piece in pieces)), weights[0].dtype),
@@ -573,22 +573,38 @@
 
     def swap_start(*refs):
         sources, (block_ref, start_ref, blocks_ref, *sems) = refs[: len(weights)], refs[len(weights) :]
+        if load:
+            held, load_sems = sems[5:-1], sems[-1]
+            loads = [
+                pltpu.make_async_copy(source, kept, load_sems.at[k])
+                for k, (source, kept) in enumerate(zip(sources, held))
+            ]
+            for copy in loads:
+                copy.start()
+            sources = held
         greet([ring_peer(ring, 1), ring_peer(ring, ring - 1)])
         if len(block.shape) == 3:
             block_ref = block_ref.at[block.shape[0] - 1]
-        around = RingBlocks(ring, block_ref, blocks_ref, *sems[3:])
+        around = RingBlocks(ring, block_ref, blocks_ref, *sems[3:5])
         pair = PairSwap(sources, start_ref, pieces, *sems[:3])
         around.start()
+        if load:
+            for copy in loads:
+                copy.wait()
         pair.start()
         around.finish()
         pair.finish()
 
     operands = (*weights, block)
+    scratch = [pltpu.SemaphoreType.DMA((len(pieces),))] * 3
+    scratch += [pltpu.SemaphoreType.DMA((count,))] * 2
+    if load:
+        scratch += [pltpu.VMEM(weight.shape, weight.dtype) for weight in weights]
+        scratch.append(pltpu.SemaphoreType.DMA((len(weights),)))
     return call(
         swap_start, identity, operands, (pl.ANY,) * len(operands),
         outputs, [pl.ANY] * len(outputs),
-        [pltpu.SemaphoreType.DMA((len(pieces),))] * 3 + [pltpu.SemaphoreType.DMA((count,))] * 2,
-        15_000_000_000,
+        scratch, 15_000_000_000, (62 << 20) if load else VMEM,
     )
 
 
@@ -1242,10 +1258,10 @@
         for part in range(3)
     ]
     ring = tok_size // 2
-    early = 1
+    early = min(2, ring - 2)
     out_blocks = [w_out.T]
     attention_start, block = swap_ring(
-        0, (w_query, w_key, w_value), attention_pieces, ring, out_blocks[0], early
+        0, (w_query, w_key, w_value), attention_pieces, ring, out_blocks[0], early, True
     )
     out_blocks.append(block)
     feed = (w_gate, w_up, w_down.T)

time: 655 us -> 654 us (level)
    unnamed x68 -> x62, local copies, waits for them, and re-layouts: 25.2 us -> 23.1 us
where the time goes in v9:
time: 654 us; the launch traced here: 650 us
  Pallas kernels  536 us (82%)
  matrix products  32.9 us (5%)
  waiting for transfers between devices  28.8 us (4%)
  local copies, waits for them, and re-layouts  28 us (4%)
  between operations  14.7 us (2%)
    pallas_call x6, Pallas kernels, call(): pl.pallas_call(kernel, out_shape=outputs, in_specs=[pl.BlockSpec(memory_s...  372 us
    pallas_call x2, Pallas kernels, weight_terms(): pl.pallas_call(terms_step, grid=(model // tile,), in_specs=[pl.BlockSpec(...  42.4 us
    pallas_call x2, Pallas kernels, feed_forward(): pl.pallas_call(feed_step, grid=(total // tile,), in_specs=[rows, rows, we...  40.1 us
    pallas_call x2, Pallas kernels, columns_back(): pl.pallas_call(columns_step, grid_spec=pltpu.PrefetchScalarGridSpec(num_s...  28 us
    unnamed x62, local copies, waits for them, and re-layouts  23.1 us
    reduce_scatter x3, waiting for transfers between devices, ring_scatter(): lax.psum_scatter(terms, 'tok', scatter_dimension=0, tiled=True, axis_inde...  20.7 us
    pallas_call x1, Pallas kernels, input_terms(): pl.pallas_call(input_terms_step, grid_spec=pltpu.PrefetchScalarGridSpec(n...  18.1 us
    pallas_call x1, Pallas kernels, attend_back(): pl.pallas_call(attend_back_kernel, grid=(sequences, pairs), out_shape=jax...  17.7 us
  transfers between devices with their start and end apart: 9, of which 3 were waited for; matrix products, arithmetic and copies ran while one was open for 7% of the time, Pallas kernels for 79%

profile of v9, /device:TPU:0, one launch (start us, length us, event | category | flops | bytes accessed | tf_op | source)
XLA Modules:
  0.0 649.9 jit_solution(10575844532952304050)
XLA Ops:
  7.2 1.8 copy.23
  9.0 19.4 %swap_start.2 = (bf16[512,768]{1,0:T(8,128)(2,1)}, bf16[2,256,512]{2,1,0:T(8,128)(2,1)}) custom-call(bf16[256,512]{1,0:T(8,128)(2,1)} %refs_0_.3, bf16[256,512]{1,0:T(8,128)(2,1)} %refs_1_.3, bf16[256,512]{1,0:T(8,128)(2,1)} %refs_2_.1, bf16[256,512]{1,0:T(8,128)(2,1)} %bitcast.16), custom_call_target="tpu_custom_call" | custom-call | flops 15000000512 | bytes 150000000 | tf_op jit(solution)/shard_map/swap_start/pallas_call | solution.py:432
  32.3 28.4 %swap_start.3 = (bf16[512,2304]{1,0:T(8,128)(2,1)}, bf16[1,256,512]{2,1,0:T(8,128)(2,1)S(1)}) custom-call(bf16[256,2048]{1,0:T(8,128)(2,1)S(1)} %copy-done.10, bf16[256,2048]{1,0:T(8,128)(2,1)S(1)} %copy-done.11, bf16[256,2048]{1,0:T(8,128)(2,1)S(1)} %bitcast.14, bf16[2,256,512]{2,1,0:T(8,128)(2,1)S(1)} %copy-done.20), custom_call_target="tpu_custom_call" | custom-call | flops 15000000512 | bytes 150000000 | tf_op jit(solution)/shard_map/swap_start/pallas_call | solution.py:432
  64.7 57.2 %swap_gather.1 = (bf16[512,768]{1,0:T(8,128)(2,1)}, bf16[2048,2048]{1,0:T(8,128)(2,1)}, bf16[2048,256]{1,0:T(8,128)(2,1)S(1)}, f32[2,2048]{1,0:T(2,128)S(1)}) custom-call(bf16[256,2048]{1,0:T(8,128)(2,1)S(1)} %copy-done.10, bf16[256,2048]{1,0:T(8,128)(2,1)S(1)} %copy-done.12, bf16[256,2048]{1,0:T(8,128)(2,1)S(1)} %bitcast.15, bf16[1024,512]{1,0:T(8,128)(2,1)} %refs_3_, ...), custom_call_target="tpu_custom_call" | custom-call | flops 54999998464 | bytes 550000000 | tf_op jit(solution)/shard_map/swap_gather/pallas_call | solution.py:432
  122.1 5.4 fusion
  127.5 10.3 %convolution_convert_fusion.1.packed_ref = bf16[2048,768]{1,0:T(8,128)(2,1)S(1)} fusion(bf16[2048,768]{1,0:T(8,128)(2,1)} %all-gather.4.cloned.1.call-done.qkv_ref, bf16[2048,2048]{1,0:T(8,128)(2,1)} %get-tuple-element.80.x_ref, f32[2048]{0:T(1024)S(1)} %bitcast.18, f32[2048]{0:T(1024)S(1)} %add_rsqrt_fusion), kind=kOutput, calls=%fused_computation.6 | convolution fusion | flops 6460801024 | bytes 14696448 | tf_op jit(solution)/shard_map/dot_general | solution.py:33
  137.9 11.3 %attend.1 = (bf16[2048,256]{1,0:T(8,128)(2,1)S(1)}, f32[2,2,2,1024]{3,2,1,0:T(2,128)S(1)}) custom-call(bf16[2048,768]{1,0:T(8,128)(2,1)S(1)} %convolution_convert_fusion.1.packed_ref), custom_call_target="tpu_custom_call" | custom-call | flops 1073741824 | bytes 6291456 | tf_op jit(solution)/shard_map/attend/pallas_call | solution.py:106
  149.2 1.7 copy-done.14
  150.9 5.7 convolution_convert_fusion.terms_ref
  157.6 107.8 %middle_step.1 = (bf16[2048,2048]{1,0:T(8,128)(2,1)}, f32[256,2048]{1,0:T(8,128)S(1)}, f32[256,128]{1,0:T(8,128)S(1)}, bf16[2048,2048]{1,0:T(8,128)(2,1)}) custom-call(bf16[2048,2048]{1,0:T(8,128)(2,1)} %convolution_convert_fusion.terms_ref, bf16[2048,2048]{1,0:T(8,128)(2,1)} %get-tuple-element.80.x_ref, f32[1,2048]{1,0:T(1,128)S(1)} %get-tuple-element.139.gain_ref, ...), custom_call_target="tpu_custom_call" | custom-call | flops 99999997952 | bytes 1000000000 | tf_op jit(solution)/shard_map/middle_step/pallas_call | solution.py:432
  266.7 27.4 %feed_forward.2 = (bf16[2048,768]{1,0:T(8,128)(2,1)S(1)}, bf16[2048,1536]{1,0:T(8,128)(2,1)}) custom-call(bf16[2048,2048]{1,0:T(8,128)(2,1)} %get-tuple-element.85.normed_ref.refs_0_, bf16[2048,2048]{1,0:T(8,128)(2,1)} %get-tuple-element.86.cot_ref.refs_1_, bf16[2048,2304]{1,0:T(8,128)(2,1)} %all-gather.8.cloned.1.call-done.gate_ref.up_ref.down_ref.refs_1_.refs_2_, ...), custom_call_target="tpu_custom_call" | custom-call | flops 19327352832 | bytes 35651584 | tf_op jit(solution)/shard_map/feed_forward/pallas_call | solution.py:1107
  294.1 26.3 %weight_terms.2 = bf16[2048,2304]{1,0:T(8,128)(2,1)} custom-call(bf16[2048,2048]{1,0:T(8,128)(2,1)} %get-tuple-element.85.normed_ref.refs_0_, bf16[2048,2048]{1,0:T(8,128)(2,1)} %get-tuple-element.86.cot_ref.refs_1_, bf16[2048,1536]{1,0:T(8,128)(2,1)} %get-tuple-element.91.refs_2_.refs_0_, bf16[2048,768]{1,0:T(8,128)(2,1)S(1)} %get-tuple-element.90.refs_3_.refs_0_), custom_call_target="tpu_custom_call" | custom-call | flops 19327352832 | bytes 35651584 | tf_op jit(solution)/shard_map/weight_terms/pallas_call | solution.py:1203
  320.4 1.8 copy-done.19
  322.2 18.4 %columns_back.2.refs_2_ = bf16[2048,2048]{1,0:T(8,128)(2,1)} custom-call(s32[1]{0:T(128)} %bitcast.own_ref, bf16[2048,1536]{1,0:T(8,128)(2,1)} %get-tuple-element.91.refs_2_.refs_0_, bf16[2048,2304]{1,0:T(8,128)(2,1)} %all-gather.8.cloned.1.call-done.gate_ref.up_ref.down_ref.refs_1_.refs_2_), custom_call_target="tpu_custom_call" | custom-call | flops 12884901888 | bytes 20971520 | tf_op jit(solution)/shard_map/columns_back/pallas_call | solution.py:1170
  340.7 12.7 %feed_forward.3 = (bf16[2048,256]{1,0:T(8,128)(2,1)S(1)}, bf16[2048,512]{1,0:T(8,128)(2,1)S(1)}) custom-call(bf16[2048,2048]{1,0:T(8,128)(2,1)} %get-tuple-element.85.normed_ref.refs_0_, bf16[2048,2048]{1,0:T(8,128)(2,1)} %get-tuple-element.86.cot_ref.refs_1_, bf16[2048,768]{1,0:T(8,128)(2,1)} %all-gather.6.cloned.1.call-done.gate_ref.up_ref.down_ref.refs_1_.refs_3_, ...), custom_call_target="tpu_custom_call" | custom-call | flops 6442450944 | bytes 23068672 | tf_op jit(solution)/shard_map/feed_forward/pallas_call | solution.py:1107
  353.4 9.5 %columns_back.3.terms_ref = bf16[2048,2048]{1,0:T(8,128)(2,1)} custom-call(s32[1]{0:T(128)} %bitcast.own_ref, bf16[2048,512]{1,0:T(8,128)(2,1)S(1)} %get-tuple-element.100.refs_0_.refs_3_, bf16[2048,768]{1,0:T(8,128)(2,1)S(1)} %copy-done, bf16[2048,2048]{1,0:T(8,128)(2,1)} %columns_back.2.refs_2_), custom_call_target="tpu_custom_call" | custom-call | flops 4294967296 | bytes 12582912 | tf_op jit(solution)/shard_map/columns_back/pallas_call | solution.py:1170
  363.0 84.6 %middle_back_step.1 = (bf16[2048,2048]{1,0:T(8,128)(2,1)}, f32[256,2048]{1,0:T(8,128)S(1)}, f32[1,2048]{1,0:T(1,128)S(1)}, bf16[2048,2048]{1,0:T(8,128)(2,1)}) custom-call(bf16[2048,2048]{1,0:T(8,128)(2,1)} %columns_back.3.terms_ref, bf16[2048,2048]{1,0:T(8,128)(2,1)} %get-tuple-element.86.cot_ref.refs_1_, f32[256,2048]{1,0:T(8,128)S(1)} %copy-done.25, ...), custom_call_target="tpu_custom_call" | custom-call | flops 70000001024 | bytes 700000000 | tf_op jit(solution)/shard_map/middle_back_step/pallas_call | solution.py:432
  448.9 16.1 %weight_terms.3 = bf16[2048,1024]{1,0:T(8,128)(2,1)} custom-call(bf16[2048,2048]{1,0:T(8,128)(2,1)} %get-tuple-element.85.normed_ref.refs_0_, bf16[2048,2048]{1,0:T(8,128)(2,1)} %get-tuple-element.86.cot_ref.refs_1_, bf16[2048,2048]{1,0:T(8,128)(2,1)} %get-tuple-element.102.refs_2_, bf16[2048,512]{1,0:T(8,128)(2,1)S(1)} %get-tuple-element.100.refs_0_.refs_3_, ...), custom_call_target="tpu_custom_call" | custom-call | flops 8589934592 | bytes 33554432 | tf_op jit(solution)/shard_map/weight_terms/pallas_call | solution.py:1203
  465.2 5.8 convolution_convert_fusion.3.grad_ref
  471.1 17.7 %attend_back.1.grad_ref = bf16[2048,768]{1,0:T(8,128)(2,1)S(1)} custom-call(bf16[2048,768]{1,0:T(8,128)(2,1)} %copy-done.14, bf16[2048,256]{1,0:T(8,128)(2,1)S(1)} %copy-done.2, bf16[2048,256]{1,0:T(8,128)(2,1)S(1)} %convolution_convert_fusion.3.grad_ref, f32[2,2,2,1024]{3,2,1,0:T(2,128)S(1)} %get-tuple-element.103.lse_ref), custom_call_target="tpu_custom_call" | custom-call | flops 2684354560 | bytes 9437184 | tf_op jit(solution)/shard_map/attend_back/pallas_call | solution.py:133
  488.9 11.0 %convolution_convert_fusion.2 = bf16[2048,768]{1,0:T(8,128)(2,1)} fusion(bf16[2048,768]{1,0:T(8,128)(2,1)S(1)} %attend_back.1.grad_ref, bf16[2048,2048]{1,0:T(8,128)(2,1)} %get-tuple-element.80.x_ref, f32[2048]{0:T(1024)S(1)} %bitcast.19, f32[2048]{0:T(1024)S(1)} %copy-done.27), kind=kOutput, calls=%fused_computation.7 | convolution fusion | flops 6460801024 | bytes 14696448 | tf_op jit(solution)/shard_map/dot_general | solution.py:21
  499.9 1.7 copy-done.15
  503.4 2.0 copy-done.16
  505.4 1.6 copy-done.18
  507.0 18.1 %input_terms.1 = (bf16[2048,2048]{1,0:T(8,128)(2,1)}, f32[1,2048]{1,0:T(1,128)S(1)}) custom-call(s32[1]{0:T(128)} %bitcast.own_ref, bf16[2048,768]{1,0:T(8,128)(2,1)S(1)} %copy-done.16, bf16[2048,768]{1,0:T(8,128)(2,1)} %all-gather.4.cloned.1.call-done.qkv_ref, bf16[2048,2048]{1,0:T(8,128)(2,1)} %get-tuple-element.80.x_ref, f32[1,2048]{1,0:T(1,128)S(1)} %copy-done.9, ...), custom_call_target="tpu_custom_call" | custom-call | flops 6442450944 | bytes 25165824 | tf_op jit(solution)/shard_map/input_terms/pallas_call | solution.py:1052
  525.1 6.2 collective-permute-done.refs_2_
  531.4 74.5 %scatter_outputs.1 = (bf16[1024,512]{1,0:T(8,128)(2,1)S(1)}, bf16[1024,512]{1,0:T(8,128)(2,1)S(1)}, f32[2,512]{1,0:T(2,128)S(1)}) custom-call(f32[2,2048]{1,0:T(2,128)S(1)} %pad_maximum_fusion.vector_ref, bf16[2048,2048]{1,0:T(8,128)(2,1)} %get-tuple-element.110.refs_0_, bf16[2048,2048]{1,0:T(8,128)(2,1)} %get-tuple-element.113.refs_1_), custom_call_target="tpu_custom_call" | custom-call | flops 60000002048 | bytes 600000000 | tf_op jit(solution)/shard_map/scatter_outputs/pallas_call | solution.py:432
  605.9 1.9 constant_dynamic-slice_fusion.1
  609.1 20.6 %reduce-scatter.8.cloned.1.call-done.refs_0_ = bf16[512,768]{1,0:T(8,128)(2,1)} async-done(((bf16[2048,768]{1,0:T(8,128)(2,1)}), bf16[512,768]{1,0:T(8,128)(2,1)}) %reduce-scatter.8.cloned.1.call-update) | async-done | bytes 786448 | tf_op jit(solution)/shard_map/reduce_scatter | solution.py:1243
  630.8 1.5 collective-permute-start.2
  634.2 5.7 assemble_grads.2
  639.9 1.7 collective-permute-done.2.refs_1_
  (84 shorter events, 19.2 us)
Async XLA Ops:
  7.2 120.4 %all-gather.4.cloned.1.call-start = ((), (), s32[]{:S(2)}) async-start(), calls=%async_computation.3 | async-start | bytes 3932160 | tf_op jit(solution)/shard_map/all_gather | solution.py:1240
  9.0 21.0 %copy-start.10 = (bf16[256,2048]{1,0:T(8,128)(2,1)S(1)}, bf16[256,2048]{1,0:T(8,128)(2,1)}, u32[]{:S(2)}) copy-start(bf16[256,2048]{1,0:T(8,128)(2,1)} %refs_0_.5) | copy-start | bytes 3145732
  28.5 238.3 %all-gather.8.cloned.1.call-start = ((), (), s32[]{:S(2)}) async-start(), calls=%async_computation.5 | async-start | bytes 11796480 | tf_op jit(solution)/shard_map/all_gather | solution.py:1240
  30.0 1.2 copy-start.11
  32.3 29.2 %copy-start.28 = (f32[512]{0:T(512)S(1)}, f32[512]{0:T(512)}, u32[]{:S(2)}) copy-start(f32[512]{0:T(512)} %param.17) | copy-start | bytes 6148
  32.3 29.2 %copy-start.29 = (f32[512]{0:T(512)S(1)}, f32[512]{0:T(512)}, u32[]{:S(2)}) copy-start(f32[512]{0:T(512)} %param.12) | copy-start | bytes 6148
  32.3 29.2 %copy-start.7 = (bf16[512,256]{0,1:T(8,128)(2,1)S(1)}, bf16[512,256]{0,1:T(8,128)(2,1)}, u32[]{:S(2)}) copy-start(bf16[512,256]{0,1:T(8,128)(2,1)} %copy.23) | copy-start | bytes 786436
  61.4 279.3 %all-gather.6.cloned.1.call-start = ((), (), s32[]{:S(2)}) async-start(), calls=%async_computation.4 | async-start | bytes 3932160 | tf_op jit(solution)/shard_map/all_gather | solution.py:1240
  122.0 28.9 %copy-start.5 = (bf16[2048,256]{1,0:T(8,128)(2,1)}, bf16[2048,256]{1,0:T(8,128)(2,1)S(1)}, u32[]{:S(2)}) copy-start(bf16[2048,256]{1,0:T(8,128)(2,1)S(1)} %get-tuple-element.84) | copy-start | bytes 3145732
  122.0 379.6 %reduce-scatter.4.cloned.1.call-start = ((), (), s32[]{:S(2)}) async-start(), calls=%async_computation.6 | async-start | bytes 11796480 | tf_op jit(solution)/shard_map/reduce_scatter | solution.py:1243
  122.1 15.8 %copy-start.8 = (f32[1,2048]{1,0:T(1,128)}, f32[1,2048]{1,0:T(1,128)S(1)}, u32[]{:S(2)}) copy-start(f32[1,2048]{1,0:T(1,128)S(1)} %get-tuple-element.140.gain_ref) | copy-start | bytes 24580
  127.5 10.4 %copy-start.26 = (f32[2048]{0:T(1024)}, f32[2048]{0:T(1024)S(1)}, u32[]{:S(2)}) copy-start(f32[2048]{0:T(1024)S(1)} %add_rsqrt_fusion) | copy-start | bytes 24580
  149.2 1.7 copy-start.14
  150.9 6.7 %copy-start.13 = (bf16[1024,512]{1,0:T(8,128)(2,1)S(1)}, bf16[1024,512]{1,0:T(8,128)(2,1)}, u32[]{:S(2)}) copy-start(bf16[1024,512]{1,0:T(8,128)(2,1)} %shard_ref.1) | copy-start | bytes 3145732
  265.4 1.3 copy-start.24
  320.4 1.8 copy-start.19
  322.2 283.7 %reduce-scatter.6.cloned.1.call-start = ((), (), s32[]{:S(2)}) async-start(), calls=%async_computation.7 | async-start | bytes 5242880 | tf_op jit(solution)/shard_map/reduce_scatter | solution.py:1243
  340.7 12.7 %copy-start = (bf16[2048,768]{1,0:T(8,128)(2,1)S(1)}, bf16[2048,768]{1,0:T(8,128)(2,1)}, u32[]{:S(2)}) copy-start(bf16[2048,768]{1,0:T(8,128)(2,1)} %all-gather.6.cloned.1.call-done.gate_ref.up_ref.down_ref.refs_1_.refs_3_) | copy-start | bytes 9437188
  353.4 9.6 %copy-start.25 = (f32[256,2048]{1,0:T(8,128)S(1)}, f32[256,2048]{1,0:T(8,128)}, u32[]{:S(2)}) copy-start(f32[256,2048]{1,0:T(8,128)} %copy-done.24) | copy-start | bytes 6291460
  363.0 85.9 %copy-start.2 = (bf16[2048,256]{1,0:T(8,128)(2,1)S(1)}, bf16[2048,256]{1,0:T(8,128)(2,1)}, u32[]{:S(2)}) copy-start(bf16[2048,256]{1,0:T(8,128)(2,1)} %copy-done.1) | copy-start | bytes 3145732
  447.6 1.3 copy-start.17
  448.9 16.3 %copy-start.6 = (bf16[2048,256]{1,0:T(8,128)(2,1)S(1)}, bf16[2048,256]{1,0:T(8,128)(2,1)}, u32[]{:S(2)}) copy-start(bf16[2048,256]{1,0:T(8,128)(2,1)} %copy-done.5) | copy-start | bytes 3145732
  465.0 164.7 %reduce-scatter.8.cloned.1.call-start = ((), (), s32[]{:S(2)}) async-start(), calls=%async_computation.8 | async-start | bytes 3932160 | tf_op jit(solution)/shard_map/reduce_scatter | solution.py:1243
  471.1 17.8 %copy-start.9 = (f32[1,2048]{1,0:T(1,128)S(1)}, f32[1,2048]{1,0:T(1,128)}, u32[]{:S(2)}) copy-start(f32[1,2048]{1,0:T(1,128)} %copy-done.8) | copy-start | bytes 24580
  471.1 17.8 %copy-start.27 = (f32[2048]{0:T(1024)S(1)}, f32[2048]{0:T(1024)}, u32[]{:S(2)}) copy-start(f32[2048]{0:T(1024)} %copy-done.26) | copy-start | bytes 24580
  499.9 1.7 copy-start.15
  503.0 28.4 %collective-permute-start = (bf16[256,2304]{1,0:T(8,128)(2,1)S(1)}, bf16[256,2304]{1,0:T(8,128)(2,1)S(1)}, u32[]{:S(2)}, u32[]{:S(2)}) collective-permute-start(bf16[256,2304]{1,0:T(8,128)(2,1)S(1)} %constant_dynamic-slice_fusion.2), channel_id=1, source_target_pairs={{0,4},{4,0},{8,12},{12,8},{16,20},{20,16},{24,28},{28,24},{1,5},{5... | collective-permute-start | bytes 3538952 | tf_op jit(solution)/shard_map/ppermute | solution.py:1237
  503.4 2.0 copy-start.16
  505.4 1.6 copy-start.18
  607.8 22.0 %collective-permute-start.1 = (bf16[256,1024]{1,0:T(8,128)(2,1)}, bf16[256,1024]{1,0:T(8,128)(2,1)}, u32[]{:S(2)}, u32[]{:S(2)}) collective-permute-start(bf16[256,1024]{1,0:T(8,128)(2,1)} %constant_dynamic-slice_fusion.1), channel_id=1, source_target_pairs={{0,4},{4,0},{8,12},{12,8},{16,20},{20,16},{24,28},{28,24},{1,5},{5... | collective-permute-start | bytes 1572872 | tf_op jit(solution)/shard_map/ppermute | solution.py:1237
  629.7 11.9 %copy-start.4 = (bf16[512,768]{1,0:T(8,128)(2,1)S(1)}, bf16[512,768]{1,0:T(8,128)(2,1)}, u32[]{:S(2)}) copy-start(bf16[512,768]{1,0:T(8,128)(2,1)} %reduce-scatter.8.cloned.1.call-done.refs_0_) | copy-start | bytes 2359300
  630.8 10.8 %collective-permute-start.2 = (bf16[256,768]{1,0:T(8,128)(2,1)S(1)}, bf16[256,768]{1,0:T(8,128)(2,1)S(1)}, u32[]{:S(2)}, u32[]{:S(2)}) collective-permute-start(bf16[256,768]{1,0:T(8,128)(2,1)S(1)} %constant_dynamic-slice_fusion), channel_id=1, source_target_pairs={{0,4},{4,0},{8,12},{12,8},{16,20},{20,16},{24,28},{28,24},{1,5},{5... | collective-permute-start | bytes 1179656 | tf_op jit(solution)/shard_map/ppermute | solution.py:1237
  (7 other events, 7.2 us)
Sparse Core Ops, SparseCore 0:
  28.6 63.4 all-gather.3
  93.7 166.7 all-gather.7
  262.0 61.6 all-gather.5
  325.9 159.9 reduce-scatter.3
  488.0 77.5 reduce-scatter.5
  567.9 61.7 reduce-scatter.7

commit v10 on v9

--- a/solution.py
+++ b/solution.py
@@ -566,22 +566,25 @@
 
 def swap_ring(identity, weights, pieces, ring, block, count, load=False):
     size = weights[0].shape[0]
+    block_shape = block.shape[::-1] if load else block.shape[-2:]
     outputs = [
         jax.ShapeDtypeStruct((2 * size, sum(piece[2] for piece in pieces)), weights[0].dtype),
-        jax.ShapeDtypeStruct((count, *block.shape[-2:]), block.dtype),
+        jax.ShapeDtypeStruct((count, *block_shape), block.dtype),
     ]
 
     def swap_start(*refs):
         sources, (block_ref, start_ref, blocks_ref, *sems) = refs[: len(weights)], refs[len(weights) :]
         if load:
-            held, load_sems = sems[5:-1], sems[-1]
+            held, raw, turned, load_sems = sems[5:-3], sems[-3], sems[-2], sems[-1]
             loads = [
                 pltpu.make_async_copy(source, kept, load_sems.at[k])
-                for k, (source, kept) in enumerate(zip(sources, held))
+                for k, (source, kept) in enumerate(zip([*sources, block_ref], [*held, raw]))
             ]
             for copy in loads:
                 copy.start()
-            sources = held
+            sources, block_ref = held, turned
+            loads.pop().wait()
+            turned[...] = raw[...].T
         greet([ring_peer(ring, 1), ring_peer(ring, ring - 1)])
         if len(block.shape) == 3:
             block_ref = block_ref.at[block.shape[0] - 1]
@@ -600,7 +603,8 @@
     scratch += [pltpu.SemaphoreType.DMA((count,))] * 2
     if load:
         scratch += [pltpu.VMEM(weight.shape, weight.dtype) for weight in weights]
-        scratch.append(pltpu.SemaphoreType.DMA((len(weights),)))
+        scratch += [pltpu.VMEM(block.shape, block.dtype), pltpu.VMEM(block_shape, block.dtype)]
+        scratch.append(pltpu.SemaphoreType.DMA((len(weights) + 1,)))
     return call(
         swap_start, identity, operands, (pl.ANY,) * len(operands),
         outputs, [pl.ANY] * len(outputs),
@@ -1261,7 +1265,7 @@
     early = min(2, ring - 2)
     out_blocks = [w_out.T]
     attention_start, block = swap_ring(
-        0, (w_query, w_key, w_value), attention_pieces, ring, out_blocks[0], early, True
+        0, (w_query, w_key, w_value), attention_pieces, ring, w_out, early, True
     )
     out_blocks.append(block)
     feed = (w_gate, w_up, w_down.T)

time: 654 us -> 654 us (level)
    unnamed x62 -> x60, local copies, waits for them, and re-layouts: 23.1 us -> 22.2 us
where the time goes in v10:
time: 654 us; the launch traced here: 650 us
  Pallas kernels  538 us (82%)
  matrix products  32.9 us (5%)
  waiting for transfers between devices  28.2 us (4%)
  local copies, waits for them, and re-layouts  27.2 us (4%)
  between operations  14.7 us (2%)
    pallas_call x6, Pallas kernels, call(): pl.pallas_call(kernel, out_shape=outputs, in_specs=[pl.BlockSpec(memory_s...  374 us
    pallas_call x2, Pallas kernels, weight_terms(): pl.pallas_call(terms_step, grid=(model // tile,), in_specs=[pl.BlockSpec(...  42.4 us
    pallas_call x2, Pallas kernels, feed_forward(): pl.pallas_call(feed_step, grid=(total // tile,), in_specs=[rows, rows, we...  39.8 us
    pallas_call x2, Pallas kernels, columns_back(): pl.pallas_call(columns_step, grid_spec=pltpu.PrefetchScalarGridSpec(num_s...  28 us
    unnamed x60, local copies, waits for them, and re-layouts  22.2 us
    reduce_scatter x3, waiting for transfers between devices, ring_scatter(): lax.psum_scatter(terms, 'tok', scatter_dimension=0, tiled=True, axis_inde...  20 us
    pallas_call x1, Pallas kernels, input_terms(): pl.pallas_call(input_terms_step, grid_spec=pltpu.PrefetchScalarGridSpec(n...  18.1 us
    pallas_call x1, Pallas kernels, attend_back(): pl.pallas_call(attend_back_kernel, grid=(sequences, pairs), out_shape=jax...  17.7 us
  transfers between devices with their start and end apart: 9, of which 3 were waited for; matrix products, arithmetic and copies ran while one was open for 7% of the time, Pallas kernels for 79%

profile of v10, /device:TPU:0, one launch (start us, length us, event | category | flops | bytes accessed | tf_op | source)
XLA Modules:
  0.0 649.7 jit_solution(17119054991110112090)
XLA Ops:
  7.2 20.6 %swap_start.2 = (bf16[512,768]{1,0:T(8,128)(2,1)}, bf16[2,256,512]{2,1,0:T(8,128)(2,1)}) custom-call(bf16[256,512]{1,0:T(8,128)(2,1)} %refs_0_.3, bf16[256,512]{1,0:T(8,128)(2,1)} %refs_1_.3, bf16[256,512]{1,0:T(8,128)(2,1)} %refs_2_.1, bf16[512,256]{1,0:T(8,128)(2,1)} %refs_3_.1), custom_call_target="tpu_custom_call" | custom-call | flops 15000000512 | bytes 150000000 | tf_op jit(solution)/shard_map/swap_start/pallas_call | solution.py:432
  27.9 1.5 copy.22
  31.7 28.4 %swap_start.3 = (bf16[512,2304]{1,0:T(8,128)(2,1)}, bf16[1,256,512]{2,1,0:T(8,128)(2,1)S(1)}) custom-call(bf16[256,2048]{1,0:T(8,128)(2,1)S(1)} %copy-done.9, bf16[256,2048]{1,0:T(8,128)(2,1)S(1)} %copy-done.10, bf16[256,2048]{1,0:T(8,128)(2,1)S(1)} %bitcast.14, bf16[2,256,512]{2,1,0:T(8,128)(2,1)S(1)} %copy-done.19), custom_call_target="tpu_custom_call" | custom-call | flops 15000000512 | bytes 150000000 | tf_op jit(solution)/shard_map/swap_start/pallas_call | solution.py:432
  65.1 57.2 %swap_gather.1 = (bf16[512,768]{1,0:T(8,128)(2,1)}, bf16[2048,2048]{1,0:T(8,128)(2,1)}, bf16[2048,256]{1,0:T(8,128)(2,1)S(1)}, f32[2,2048]{1,0:T(2,128)S(1)}) custom-call(bf16[256,2048]{1,0:T(8,128)(2,1)S(1)} %copy-done.9, bf16[256,2048]{1,0:T(8,128)(2,1)S(1)} %copy-done.11, bf16[256,2048]{1,0:T(8,128)(2,1)S(1)} %bitcast.15, bf16[1024,512]{1,0:T(8,128)(2,1)} %refs_3_.2, ...), custom_call_target="tpu_custom_call" | custom-call | flops 54999998464 | bytes 550000000 | tf_op jit(solution)/shard_map/swap_gather/pallas_call | solution.py:432
  122.5 5.4 fusion
  127.9 10.3 %convolution_convert_fusion.1.packed_ref = bf16[2048,768]{1,0:T(8,128)(2,1)S(1)} fusion(bf16[2048,768]{1,0:T(8,128)(2,1)} %all-gather.4.cloned.1.call-done.qkv_ref, bf16[2048,2048]{1,0:T(8,128)(2,1)} %get-tuple-element.80.x_ref, f32[2048]{0:T(1024)S(1)} %bitcast.17, f32[2048]{0:T(1024)S(1)} %add_rsqrt_fusion), kind=kOutput, calls=%fused_computation.6 | convolution fusion | flops 6460801024 | bytes 14696448 | tf_op jit(solution)/shard_map/dot_general | solution.py:33
  138.3 11.3 %attend.1 = (bf16[2048,256]{1,0:T(8,128)(2,1)S(1)}, f32[2,2,2,1024]{3,2,1,0:T(2,128)S(1)}) custom-call(bf16[2048,768]{1,0:T(8,128)(2,1)S(1)} %convolution_convert_fusion.1.packed_ref), custom_call_target="tpu_custom_call" | custom-call | flops 1073741824 | bytes 6291456 | tf_op jit(solution)/shard_map/attend/pallas_call | solution.py:106
  149.6 1.6 copy-done.13
  151.3 5.7 convolution_convert_fusion.terms_ref
  157.9 107.9 %middle_step.1 = (bf16[2048,2048]{1,0:T(8,128)(2,1)}, f32[256,2048]{1,0:T(8,128)S(1)}, f32[256,128]{1,0:T(8,128)S(1)}, bf16[2048,2048]{1,0:T(8,128)(2,1)}) custom-call(bf16[2048,2048]{1,0:T(8,128)(2,1)} %convolution_convert_fusion.terms_ref, bf16[2048,2048]{1,0:T(8,128)(2,1)} %get-tuple-element.80.x_ref, f32[1,2048]{1,0:T(1,128)S(1)} %get-tuple-element.139.gain_ref, ...), custom_call_target="tpu_custom_call" | custom-call | flops 99999997952 | bytes 1000000000 | tf_op jit(solution)/shard_map/middle_step/pallas_call | solution.py:432
  267.1 27.1 %feed_forward.2 = (bf16[2048,768]{1,0:T(8,128)(2,1)S(1)}, bf16[2048,1536]{1,0:T(8,128)(2,1)}) custom-call(bf16[2048,2048]{1,0:T(8,128)(2,1)} %get-tuple-element.85.normed_ref.refs_0_, bf16[2048,2048]{1,0:T(8,128)(2,1)} %get-tuple-element.86.cot_ref.refs_1_, bf16[2048,2304]{1,0:T(8,128)(2,1)} %all-gather.8.cloned.1.call-done.gate_ref.up_ref.down_ref.refs_1_.refs_2_, ...), custom_call_target="tpu_custom_call" | custom-call | flops 19327352832 | bytes 35651584 | tf_op jit(solution)/shard_map/feed_forward/pallas_call | solution.py:1111
  294.3 26.3 %weight_terms.2 = bf16[2048,2304]{1,0:T(8,128)(2,1)} custom-call(bf16[2048,2048]{1,0:T(8,128)(2,1)} %get-tuple-element.85.normed_ref.refs_0_, bf16[2048,2048]{1,0:T(8,128)(2,1)} %get-tuple-element.86.cot_ref.refs_1_, bf16[2048,1536]{1,0:T(8,128)(2,1)} %get-tuple-element.91.refs_2_.refs_0_, bf16[2048,768]{1,0:T(8,128)(2,1)S(1)} %get-tuple-element.90.refs_3_.refs_0_), custom_call_target="tpu_custom_call" | custom-call | flops 19327352832 | bytes 35651584 | tf_op jit(solution)/shard_map/weight_terms/pallas_call | solution.py:1207
  320.6 1.7 copy-done.18
  322.4 18.5 %columns_back.2.refs_2_ = bf16[2048,2048]{1,0:T(8,128)(2,1)} custom-call(s32[1]{0:T(128)} %bitcast.own_ref, bf16[2048,1536]{1,0:T(8,128)(2,1)} %get-tuple-element.91.refs_2_.refs_0_, bf16[2048,2304]{1,0:T(8,128)(2,1)} %all-gather.8.cloned.1.call-done.gate_ref.up_ref.down_ref.refs_1_.refs_2_), custom_call_target="tpu_custom_call" | custom-call | flops 12884901888 | bytes 20971520 | tf_op jit(solution)/shard_map/columns_back/pallas_call | solution.py:1174
  340.9 12.7 %feed_forward.3 = (bf16[2048,256]{1,0:T(8,128)(2,1)S(1)}, bf16[2048,512]{1,0:T(8,128)(2,1)S(1)}) custom-call(bf16[2048,2048]{1,0:T(8,128)(2,1)} %get-tuple-element.85.normed_ref.refs_0_, bf16[2048,2048]{1,0:T(8,128)(2,1)} %get-tuple-element.86.cot_ref.refs_1_, bf16[2048,768]{1,0:T(8,128)(2,1)} %all-gather.6.cloned.1.call-done.gate_ref.up_ref.down_ref.refs_1_.refs_3_, ...), custom_call_target="tpu_custom_call" | custom-call | flops 6442450944 | bytes 23068672 | tf_op jit(solution)/shard_map/feed_forward/pallas_call | solution.py:1111
  353.6 9.6 %columns_back.3.terms_ref = bf16[2048,2048]{1,0:T(8,128)(2,1)} custom-call(s32[1]{0:T(128)} %bitcast.own_ref, bf16[2048,512]{1,0:T(8,128)(2,1)S(1)} %get-tuple-element.100.refs_0_.refs_3_, bf16[2048,768]{1,0:T(8,128)(2,1)S(1)} %copy-done, bf16[2048,2048]{1,0:T(8,128)(2,1)} %columns_back.2.refs_2_), custom_call_target="tpu_custom_call" | custom-call | flops 4294967296 | bytes 12582912 | tf_op jit(solution)/shard_map/columns_back/pallas_call | solution.py:1174
  363.2 85.2 %middle_back_step.1 = (bf16[2048,2048]{1,0:T(8,128)(2,1)}, f32[256,2048]{1,0:T(8,128)S(1)}, f32[1,2048]{1,0:T(1,128)S(1)}, bf16[2048,2048]{1,0:T(8,128)(2,1)}) custom-call(bf16[2048,2048]{1,0:T(8,128)(2,1)} %columns_back.3.terms_ref, bf16[2048,2048]{1,0:T(8,128)(2,1)} %get-tuple-element.86.cot_ref.refs_1_, f32[256,2048]{1,0:T(8,128)S(1)} %copy-done.24, ...), custom_call_target="tpu_custom_call" | custom-call | flops 70000001024 | bytes 700000000 | tf_op jit(solution)/shard_map/middle_back_step/pallas_call | solution.py:432
  449.7 16.1 %weight_terms.3 = bf16[2048,1024]{1,0:T(8,128)(2,1)} custom-call(bf16[2048,2048]{1,0:T(8,128)(2,1)} %get-tuple-element.85.normed_ref.refs_0_, bf16[2048,2048]{1,0:T(8,128)(2,1)} %get-tuple-element.86.cot_ref.refs_1_, bf16[2048,2048]{1,0:T(8,128)(2,1)} %get-tuple-element.102.refs_2_, bf16[2048,512]{1,0:T(8,128)(2,1)S(1)} %get-tuple-element.100.refs_0_.refs_3_, ...), custom_call_target="tpu_custom_call" | custom-call | flops 8589934592 | bytes 33554432 | tf_op jit(solution)/shard_map/weight_terms/pallas_call | solution.py:1207
  466.0 5.8 convolution_convert_fusion.3.grad_ref
  471.9 17.7 %attend_back.1.grad_ref = bf16[2048,768]{1,0:T(8,128)(2,1)S(1)} custom-call(bf16[2048,768]{1,0:T(8,128)(2,1)} %copy-done.13, bf16[2048,256]{1,0:T(8,128)(2,1)S(1)} %copy-done.2, bf16[2048,256]{1,0:T(8,128)(2,1)S(1)} %convolution_convert_fusion.3.grad_ref, f32[2,2,2,1024]{3,2,1,0:T(2,128)S(1)} %get-tuple-element.103.lse_ref), custom_call_target="tpu_custom_call" | custom-call | flops 2684354560 | bytes 9437184 | tf_op jit(solution)/shard_map/attend_back/pallas_call | solution.py:133
  489.6 11.0 %convolution_convert_fusion.2 = bf16[2048,768]{1,0:T(8,128)(2,1)} fusion(bf16[2048,768]{1,0:T(8,128)(2,1)S(1)} %attend_back.1.grad_ref, bf16[2048,2048]{1,0:T(8,128)(2,1)} %get-tuple-element.80.x_ref, f32[2048]{0:T(1024)S(1)} %bitcast.18, f32[2048]{0:T(1024)S(1)} %copy-done.26), kind=kOutput, calls=%fused_computation.7 | convolution fusion | flops 6460801024 | bytes 14696448 | tf_op jit(solution)/shard_map/dot_general | solution.py:21
  500.7 1.8 copy-done.14
  504.1 1.9 copy-done.15
  506.0 1.6 copy-done.17
  507.6 18.1 %input_terms.1 = (bf16[2048,2048]{1,0:T(8,128)(2,1)}, f32[1,2048]{1,0:T(1,128)S(1)}) custom-call(s32[1]{0:T(128)} %bitcast.own_ref, bf16[2048,768]{1,0:T(8,128)(2,1)S(1)} %copy-done.15, bf16[2048,768]{1,0:T(8,128)(2,1)} %all-gather.4.cloned.1.call-done.qkv_ref, bf16[2048,2048]{1,0:T(8,128)(2,1)} %get-tuple-element.80.x_ref, f32[1,2048]{1,0:T(1,128)S(1)} %copy-done.8, ...), custom_call_target="tpu_custom_call" | custom-call | flops 6442450944 | bytes 25165824 | tf_op jit(solution)/shard_map/input_terms/pallas_call | solution.py:1056
  525.8 6.3 collective-permute-done.refs_2_
  532.1 74.6 %scatter_outputs.1 = (bf16[1024,512]{1,0:T(8,128)(2,1)S(1)}, bf16[1024,512]{1,0:T(8,128)(2,1)S(1)}, f32[2,512]{1,0:T(2,128)S(1)}) custom-call(f32[2,2048]{1,0:T(2,128)S(1)} %pad_maximum_fusion.vector_ref, bf16[2048,2048]{1,0:T(8,128)(2,1)} %get-tuple-element.110.refs_0_, bf16[2048,2048]{1,0:T(8,128)(2,1)} %get-tuple-element.113.refs_1_), custom_call_target="tpu_custom_call" | custom-call | flops 60000002048 | bytes 600000000 | tf_op jit(solution)/shard_map/scatter_outputs/pallas_call | solution.py:432
  606.7 1.9 constant_dynamic-slice_fusion.1
  609.6 20.0 %reduce-scatter.8.cloned.1.call-done.refs_0_ = bf16[512,768]{1,0:T(8,128)(2,1)} async-done(((bf16[2048,768]{1,0:T(8,128)(2,1)}), bf16[512,768]{1,0:T(8,128)(2,1)}) %reduce-scatter.8.cloned.1.call-update) | async-done | bytes 786448 | tf_op jit(solution)/shard_map/reduce_scatter | solution.py:1247
  630.7 1.5 collective-permute-start.2
  634.0 5.7 assemble_grads.2
  639.7 1.7 collective-permute-done.2.refs_1_
  (82 shorter events, 18.4 us)
Async XLA Ops:
  7.2 22.2 %copy-start.9 = (bf16[256,2048]{1,0:T(8,128)(2,1)S(1)}, bf16[256,2048]{1,0:T(8,128)(2,1)}, u32[]{:S(2)}) copy-start(bf16[256,2048]{1,0:T(8,128)(2,1)} %refs_0_.5) | copy-start | bytes 3145732
  7.2 120.7 %all-gather.4.cloned.1.call-start = ((), (), s32[]{:S(2)}) async-start(), calls=%async_computation.3 | async-start | bytes 3932160 | tf_op jit(solution)/shard_map/all_gather | solution.py:1244
  27.9 239.3 %all-gather.8.cloned.1.call-start = ((), (), s32[]{:S(2)}) async-start(), calls=%async_computation.5 | async-start | bytes 11796480 | tf_op jit(solution)/shard_map/all_gather | solution.py:1244
  29.4 1.2 copy-start.10
  31.7 30.2 %copy-start.27 = (f32[512]{0:T(512)S(1)}, f32[512]{0:T(512)}, u32[]{:S(2)}) copy-start(f32[512]{0:T(512)} %param.17) | copy-start | bytes 6148
  31.7 30.2 %copy-start.28 = (f32[512]{0:T(512)S(1)}, f32[512]{0:T(512)}, u32[]{:S(2)}) copy-start(f32[512]{0:T(512)} %param.12) | copy-start | bytes 6148
  60.8 280.1 %all-gather.6.cloned.1.call-start = ((), (), s32[]{:S(2)}) async-start(), calls=%async_computation.4 | async-start | bytes 3932160 | tf_op jit(solution)/shard_map/all_gather | solution.py:1244
  61.9 1.2 copy-start.11
  122.4 28.9 %copy-start.5 = (bf16[2048,256]{1,0:T(8,128)(2,1)}, bf16[2048,256]{1,0:T(8,128)(2,1)S(1)}, u32[]{:S(2)}) copy-start(bf16[2048,256]{1,0:T(8,128)(2,1)S(1)} %get-tuple-element.84) | copy-start | bytes 3145732
  122.4 380.0 %reduce-scatter.4.cloned.1.call-start = ((), (), s32[]{:S(2)}) async-start(), calls=%async_computation.6 | async-start | bytes 11796480 | tf_op jit(solution)/shard_map/reduce_scatter | solution.py:1247
  122.5 15.8 %copy-start.7 = (f32[1,2048]{1,0:T(1,128)}, f32[1,2048]{1,0:T(1,128)S(1)}, u32[]{:S(2)}) copy-start(f32[1,2048]{1,0:T(1,128)S(1)} %get-tuple-element.140.gain_ref) | copy-start | bytes 24580
  127.9 10.4 %copy-start.25 = (f32[2048]{0:T(1024)}, f32[2048]{0:T(1024)S(1)}, u32[]{:S(2)}) copy-start(f32[2048]{0:T(1024)S(1)} %add_rsqrt_fusion) | copy-start | bytes 24580
  149.6 1.7 copy-start.13
  151.3 6.7 %copy-start.12 = (bf16[1024,512]{1,0:T(8,128)(2,1)S(1)}, bf16[1024,512]{1,0:T(8,128)(2,1)}, u32[]{:S(2)}) copy-start(bf16[1024,512]{1,0:T(8,128)(2,1)} %shard_ref.1) | copy-start | bytes 3145732
  265.8 1.3 copy-start.23
  320.6 1.7 copy-start.18
  322.3 284.3 %reduce-scatter.6.cloned.1.call-start = ((), (), s32[]{:S(2)}) async-start(), calls=%async_computation.7 | async-start | bytes 5242880 | tf_op jit(solution)/shard_map/reduce_scatter | solution.py:1247
  340.9 12.7 %copy-start = (bf16[2048,768]{1,0:T(8,128)(2,1)S(1)}, bf16[2048,768]{1,0:T(8,128)(2,1)}, u32[]{:S(2)}) copy-start(bf16[2048,768]{1,0:T(8,128)(2,1)} %all-gather.6.cloned.1.call-done.gate_ref.up_ref.down_ref.refs_1_.refs_3_) | copy-start | bytes 9437188
  353.6 9.6 %copy-start.24 = (f32[256,2048]{1,0:T(8,128)S(1)}, f32[256,2048]{1,0:T(8,128)}, u32[]{:S(2)}) copy-start(f32[256,2048]{1,0:T(8,128)} %copy-done.23) | copy-start | bytes 6291460
  363.2 86.5 %copy-start.2 = (bf16[2048,256]{1,0:T(8,128)(2,1)S(1)}, bf16[2048,256]{1,0:T(8,128)(2,1)}, u32[]{:S(2)}) copy-start(bf16[2048,256]{1,0:T(8,128)(2,1)} %copy-done.1) | copy-start | bytes 3145732
  448.4 1.3 copy-start.16
  449.7 16.3 %copy-start.6 = (bf16[2048,256]{1,0:T(8,128)(2,1)S(1)}, bf16[2048,256]{1,0:T(8,128)(2,1)}, u32[]{:S(2)}) copy-start(bf16[2048,256]{1,0:T(8,128)(2,1)} %copy-done.5) | copy-start | bytes 3145732
  465.8 163.8 %reduce-scatter.8.cloned.1.call-start = ((), (), s32[]{:S(2)}) async-start(), calls=%async_computation.8 | async-start | bytes 3932160 | tf_op jit(solution)/shard_map/reduce_scatter | solution.py:1247
  471.8 17.8 %copy-start.8 = (f32[1,2048]{1,0:T(1,128)S(1)}, f32[1,2048]{1,0:T(1,128)}, u32[]{:S(2)}) copy-start(f32[1,2048]{1,0:T(1,128)} %copy-done.7) | copy-start | bytes 24580
  471.9 17.8 %copy-start.26 = (f32[2048]{0:T(1024)S(1)}, f32[2048]{0:T(1024)}, u32[]{:S(2)}) copy-start(f32[2048]{0:T(1024)} %copy-done.25) | copy-start | bytes 24580
  500.7 1.8 copy-start.14
  503.8 28.3 %collective-permute-start = (bf16[256,2304]{1,0:T(8,128)(2,1)S(1)}, bf16[256,2304]{1,0:T(8,128)(2,1)S(1)}, u32[]{:S(2)}, u32[]{:S(2)}) collective-permute-start(bf16[256,2304]{1,0:T(8,128)(2,1)S(1)} %constant_dynamic-slice_fusion.2), channel_id=1, source_target_pairs={{0,4},{4,0},{8,12},{12,8},{16,20},{20,16},{24,28},{28,24},{1,5},{5... | collective-permute-start | bytes 3538952 | tf_op jit(solution)/shard_map/ppermute | solution.py:1241
  504.1 1.9 copy-start.15
  506.0 1.6 copy-start.17
  608.5 21.0 %collective-permute-start.1 = (bf16[256,1024]{1,0:T(8,128)(2,1)}, bf16[256,1024]{1,0:T(8,128)(2,1)}, u32[]{:S(2)}, u32[]{:S(2)}) collective-permute-start(bf16[256,1024]{1,0:T(8,128)(2,1)} %constant_dynamic-slice_fusion.1), channel_id=1, source_target_pairs={{0,4},{4,0},{8,12},{12,8},{16,20},{20,16},{24,28},{28,24},{1,5},{5... | collective-permute-start | bytes 1572872 | tf_op jit(solution)/shard_map/ppermute | solution.py:1241
  629.6 11.9 %copy-start.4 = (bf16[512,768]{1,0:T(8,128)(2,1)S(1)}, bf16[512,768]{1,0:T(8,128)(2,1)}, u32[]{:S(2)}) copy-start(bf16[512,768]{1,0:T(8,128)(2,1)} %reduce-scatter.8.cloned.1.call-done.refs_0_) | copy-start | bytes 2359300
  630.7 10.8 %collective-permute-start.2 = (bf16[256,768]{1,0:T(8,128)(2,1)S(1)}, bf16[256,768]{1,0:T(8,128)(2,1)S(1)}, u32[]{:S(2)}, u32[]{:S(2)}) collective-permute-start(bf16[256,768]{1,0:T(8,128)(2,1)S(1)} %constant_dynamic-slice_fusion), channel_id=1, source_target_pairs={{0,4},{4,0},{8,12},{12,8},{16,20},{20,16},{24,28},{28,24},{1,5},{5... | collective-permute-start | bytes 1179656 | tf_op jit(solution)/shard_map/ppermute | solution.py:1241
  (6 other events, 5.9 us)
Sparse Core Ops, SparseCore 0:
  28.0 63.4 all-gather.3
  93.1 166.7 all-gather.7
  261.4 61.6 all-gather.5
  325.3 160.3 reduce-scatter.3
  487.9 77.5 reduce-scatter.5
  567.8 61.7 reduce-scatter.7
